TPU v7x, 256 devices: a whole 4x4x8 slice. The times are simulated.
256 devices in a mesh: node: 64 (over z, y, core), feat: 4 (over x).
Axes of the slice: x: 4, y: 4, z: 8, core: 2. Of those that a mesh axis runs over, the one named last changes fastest.
Arguments:
- features: bfloat16 [262144, 256], P(('node', 'feat')), may hold values from -6 to 6
- weight: bfloat16 [256, 256], replicated, may hold values from -1.5 to 1.5
- grad_out: bfloat16 [262144, 256], P(('node', 'feat')), may hold values from -6 to 6
- local_rows: int32 [64, 4, 32], P('node', 'feat'), may hold values from 0 to 7
- local_cols: int32 [64, 4, 32], P('node', 'feat'), may hold values from 0 to 31
- local_values: bfloat16 [64, 4, 32, 128, 128], P('node', 'feat'), may hold values from 0 to 3, as said below
- remote_rows: int32 [64, 4, 3, 16], P('node', 'feat'), may hold values from 0 to 7
- remote_slots: int32 [64, 4, 3, 16], P('node', 'feat'), may hold values from 0 to 15
- remote_values: bfloat16 [64, 4, 3, 16, 128, 128], P('node', 'feat'), may hold values from 0 to 3, as said below
- send_blocks: int32 [64, 3, 16], P('node'), may hold values from 0 to 31, as said below
- tile_counts: int32 [64, 4, 4], P('node', 'feat'), may hold values from 1 to 32, as said below
Outputs:
- output: bfloat16 [262144, 256], P(('node', 'feat'))
- grad_features: bfloat16 [262144, 256], P(('node', 'feat'))
Inputs may be any that keep to these rules, and one draw needn't show every extreme that they name: `tile_counts`: column 0 is at most 32 and every other column at most 16; each column reaches its bound on some device, and other devices hold all, a half or a quarter of it, at least 1. `send_blocks`: the 16 blocks of one part and round are distinct. `local_values`: each entry is zero or a positive edge weight. `remote_values`: each entry is zero or a positive edge weight.
All inputs are finite; a program needn't handle non-finite values.
Results may differ from a plain program's by a relative error of at most 0.0049.
Values may be sent and summed in bfloat16 or wider, within the bound.
No kernel may reach another device: no remote copies, remote signals or barrier semaphores. Data moves between devices by JAX's collectives and lax.ppermute only.
A program may use at most 128 MiB of HBM per device.

v0:
```python
import jax
import jax.numpy as jnp
from jax import lax
from jax.sharding import PartitionSpec as P


def swapped(array, axis, apart):
    return lax.ppermute(array, axis, [(i, i ^ 1 << apart) for i in range(lax.axis_size(axis))])


def spread(one_hot, values):
    return jnp.einsum("tb,tif->bif", one_hot, values, precision=lax.Precision.HIGHEST)


def masked_hot(targets, width, live):
    target_ids = jnp.arange(width, dtype=jnp.int32)
    return ((targets[:, None] == target_ids[None, :]) & live[:, None]).astype(jnp.float32)


def body(
    features,
    weight,
    grad_out,
    local_rows,
    local_cols,
    local_values,
    remote_rows,
    remote_slots,
    remote_values,
    send_blocks,
    tile_counts,
):
    rows_dev, feat_cols = features.shape
    block_rows = local_values.shape[-1]
    own_count = rows_dev // block_rows
    rounds = send_blocks.shape[1]
    log_nodes = lax.axis_size("node").bit_length() - 1
    own_blocks = features.reshape(own_count, block_rows, feat_cols)
    gathered = lax.all_gather(features, "feat", axis=0, tiled=True)
    part_count = gathered.shape[0] // block_rows
    part_feats = gathered.reshape(part_count, block_rows, feat_cols)
    counts = tile_counts[0, 0]
    dests = local_rows[0, 0]
    sources_ids = local_cols[0, 0]
    local_vals = local_values[0, 0]
    local_live = jnp.arange(local_vals.shape[0], dtype=jnp.int32) < counts[0]
    local_hot = masked_hot(dests, own_count, local_live)
    local_prod = jnp.einsum(
        "tij,tjf->tif", local_vals, part_feats[sources_ids], preferred_element_type=jnp.float32
    )
    totals = own_blocks.astype(jnp.float32) + spread(local_hot, local_prod)
    rowsum = jnp.einsum(
        "tb,ti->bi",
        local_hot,
        jnp.sum(local_vals, axis=-1, dtype=jnp.float32),
        precision=lax.Precision.HIGHEST,
    )
    kept_ids = []
    round_live = []
    for round_no in range(rounds):
        bit_no = round_no * log_nodes // rounds
        send_order = send_blocks[0, round_no]
        slots = remote_slots[0, 0, round_no]
        arrived, arrived_ids = swapped(
            (part_feats, send_order.astype(jnp.bfloat16)), "node", bit_no
        )
        source_ids = arrived_ids.astype(jnp.int32)[slots]
        sources = arrived[source_ids]
        kept_ids.append(source_ids)
        remote_vals = remote_values[0, 0, round_no]
        remote_live = jnp.arange(remote_vals.shape[0], dtype=jnp.int32) < counts[round_no + 1]
        round_live.append(remote_live)
        remote_hot = masked_hot(remote_rows[0, 0, round_no], own_count, remote_live)
        remote_prod = jnp.einsum(
            "tij,tjf->tif", remote_vals, sources, preferred_element_type=jnp.float32
        )
        totals = totals + spread(remote_hot, remote_prod)
        rowsum = rowsum + jnp.einsum(
            "tb,ti->bi",
            remote_hot,
            jnp.sum(remote_vals, axis=-1, dtype=jnp.float32),
            precision=lax.Precision.HIGHEST,
        )
    degree = 1.0 + rowsum
    hidden = (totals / degree[:, :, None]).astype(jnp.bfloat16).reshape(rows_dev, feat_cols)
    degree_flat = degree.reshape(rows_dev)
    output = jnp.dot(hidden, weight, preferred_element_type=jnp.float32).astype(jnp.bfloat16)
    grad_dense = lax.dot_general(
        grad_out, weight, (((1,), (1,)), ((), ())), preferred_element_type=jnp.float32
    )
    grad_hidden = (grad_dense / degree_flat[:, None]).astype(jnp.bfloat16)
    grad_blocks = grad_hidden.reshape(own_count, block_rows, feat_cols)
    local_back = jnp.einsum(
        "tij,tif->tjf", local_vals, grad_blocks[dests], preferred_element_type=jnp.float32
    )
    part_acc = spread(masked_hot(sources_ids, part_count, local_live), local_back)
    for round_no in range(rounds):
        bit_no = round_no * log_nodes // rounds
        remote_vals = remote_values[0, 0, round_no]
        remote_live = round_live[round_no]
        remote_back = jnp.einsum(
            "tij,tif->tjf",
            remote_vals,
            grad_blocks[remote_rows[0, 0, round_no]],
            preferred_element_type=jnp.float32,
        )
        parcel = spread(masked_hot(kept_ids[round_no], part_count, remote_live), remote_back)
        returned = swapped(parcel, "node", bit_no)
        part_acc = part_acc + returned
    shares = lax.psum_scatter(
        part_acc.reshape(part_count * block_rows, feat_cols),
        "feat",
        scatter_dimension=0,
        tiled=True,
    )
    grad_features = (grad_hidden.astype(jnp.float32) + shares).astype(jnp.bfloat16)
    return (output, grad_features)


def solution(mesh):
    in_specs = (
        P(("node", "feat"), None),
        P(),
        P(("node", "feat"), None),
        P("node", "feat", None),
        P("node", "feat", None),
        P("node", "feat", None, None, None),
        P("node", "feat", None, None),
        P("node", "feat", None, None),
        P("node", "feat", None, None, None, None),
        P("node", None, None),
        P("node", "feat", None),
    )
    out_specs = (P(("node", "feat"), None), P(("node", "feat"), None))
    return jax.shard_map(body, mesh=mesh, in_specs=in_specs, out_specs=out_specs, check_vma=False)
```

profile of v0, /device:TPU:146, one launch (start us, length us, event | category | flops | bytes accessed | tf_op | source)
XLA Modules:
  0.0 392.5 jit_solution(1151144169308127243)
XLA Ops:
  7.2 0.7 convert.6
  8.3 1.5 collective-permute-start.5
  10.5 0.7 fusion.121
  11.2 1.5 fusion.124
  13.3 1.6 convert_reduce_fusion
  15.5 1.8 convert_reduce_fusion.1
  19.6 1.6 gather_fusion.9
  21.2 3.0 fusion.46
  24.2 3.2 copy.25
  27.4 1.6 gather_fusion.10
  29.0 3.0 fusion.42
  32.0 3.1 copy.26
  35.1 1.6 gather_fusion.8
  36.7 3.0 fusion.50
  39.7 3.2 copy.24
  43.6 5.5 %fusion.8 = f32[32,128,256]{2,0,1:T(8,128)} fusion(f32[16,256,128]{1,0,2:T(8,128)} %copy.25, s32[16]{0:T(128)S(1)} %gather_fusion.3, pred[16]{0:T(512)(128)(4,1)S(1)} %iota_compare_fusion.9), kind=kOutput, calls=%fused_computation.18 | convolution fusion | flops 201327616 | bytes 6291536 | tf_op jit(solution)/shard_map/tb,tif->bif/dot_general | solution.py:12
  49.0 3.2 collective-permute-start.7
  52.9 5.4 %fusion.6 = f32[32,128,256]{2,0,1:T(8,128)} fusion(f32[16,256,128]{1,0,2:T(8,128)} %copy.26, s32[16]{0:T(128)S(1)} %gather_fusion.5, pred[16]{0:T(512)(128)(4,1)S(1)} %iota_compare_fusion.8), kind=kOutput, calls=%fused_computation.16 | convolution fusion | flops 201327616 | bytes 6291536 | tf_op jit(solution)/shard_map/tb,tif->bif/dot_general | solution.py:12
  58.3 1.4 collective-permute-start.8
  60.5 5.5 %fusion.10 = f32[32,128,256]{2,0,1:T(8,128)} fusion(f32[16,256,128]{1,0,2:T(8,128)} %copy.24, s32[16]{0:T(128)S(1)} %gather_fusion.1, pred[16]{0:T(512)(128)(4,1)S(1)} %iota_compare_fusion.10), kind=kOutput, calls=%fused_computation.20 | convolution fusion | flops 201327616 | bytes 6291536 | tf_op jit(solution)/shard_map/tb,tif->bif/dot_general | solution.py:12
  66.1 2.1 gather_fusion.7
  68.1 4.5 %fusion.38 = f32[32,256,128]{2,1,0:T(8,128)} fusion(bf16[32,128,256]{2,1,0:T(8,128)(2,1)} %gather_fusion.7, bf16[1,1,32,128,128]{4,3,2,1,0:T(8,128)(2,1)} %param.16), kind=kOutput, calls=%fused_computation.42 | convolution fusion | flops 268435456 | bytes 7340032 | tf_op jit(solution)/shard_map/tij,tif->tjf/dot_general | solution.py:93
  72.7 5.5 %copy.23 = f32[32,256,128]{1,0,2:T(8,128)} copy(f32[32,256,128]{2,1,0:T(8,128)} %fusion.38) | data formatting | bytes 8388608 | tf_op jit(solution)/shard_map/tij,tif->tjf/dot_general | solution.py:93
  78.2 65.7 %collective-permute-done.7 = f32[32,128,256]{2,0,1:T(8,128)} collective-permute-done((f32[32,128,256]{2,0,1:T(8,128)}, f32[32,128,256]{2,0,1:T(8,128)}, u32[]{:S(2)}, u32[]{:S(2)}) %collective-permute-start.7) | collective-permute-done | bytes 4194336 | tf_op jit(solution)/shard_map/ppermute | solution.py:8
  143.8 98.3 %collective-permute-done.8 = f32[32,128,256]{2,0,1:T(8,128)} collective-permute-done((f32[32,128,256]{2,0,1:T(8,128)}, f32[32,128,256]{2,0,1:T(8,128)}, u32[]{:S(2)}, u32[]{:S(2)}) %collective-permute-start.8) | collective-permute-done | bytes 4194336 | tf_op jit(solution)/shard_map/ppermute | solution.py:8
  242.2 8.7 %add_add_fusion = f32[32,128,256]{2,0,1:T(8,128)S(1)} fusion(f32[32,128,256]{2,0,1:T(8,128)} %collective-permute-done.8, f32[32,128,256]{2,0,1:T(8,128)} %collective-permute-done.7, f32[32,128,256]{2,0,1:T(8,128)} %collective-permute-done.6, f32[32,256,128]{1,0,2:T(8,128)} %copy.23, s32[32]{0:T(128)S(1)} %bitcast.185, pred[32]{0:T(512)(128)(4,1)S(1)} %iota_compare_fusion.11), kind=kOutput, calls=%fused_computation.15 | convolution fusion | flops 405800960 | bytes 20971680 | tf_op jit(solution)/shard_map/tb,tif->bif/dot_general | solution.py:12
  250.9 4.4 %copy.18 = f32[32,128,256]{2,1,0:T(8,128)} copy(f32[32,128,256]{2,0,1:T(8,128)S(1)} %add_add_fusion) | data formatting | bytes 8388608 | tf_op jit(solution)/shard_map/add | solution.py:109
  255.4 0.9 copy-done.5
  256.3 1.1 convert.7
  258.3 3.6 gather_fusion
  261.9 4.6 %fusion.40 = f32[32,256,128]{2,1,0:T(8,128)} fusion(bf16[32,128,256]{2,1,0:T(8,128)(2,1)} %gather_fusion, bf16[1,1,32,128,128]{4,3,2,1,0:T(8,128)(2,1)} %param.16), kind=kOutput, calls=%fused_computation.44 | convolution fusion | flops 268435456 | bytes 7340032 | tf_op jit(solution)/shard_map/tij,tjf->tif/dot_general | solution.py:48
  266.5 5.5 %copy.19 = f32[32,256,128]{1,0,2:T(8,128)} copy(f32[32,256,128]{2,1,0:T(8,128)} %fusion.40) | data formatting | bytes 8388608 | tf_op jit(solution)/shard_map/tij,tjf->tif/dot_general | solution.py:48
  272.0 5.4 %fusion.30 = f32[8,128,256]{2,0,1:T(8,128)} fusion(f32[32,256,128]{1,0,2:T(8,128)} %copy.19, f32[8,128,256]{2,1,0:T(8,128)} %convert.7, s32[32]{0:T(128)S(1)} %bitcast.184, pred[32]{0:T(512)(128)(4,1)S(1)} %iota_compare_fusion.11), kind=kOutput, calls=%fused_computation.33 | convolution fusion | flops 100925952 | bytes 6291616 | tf_op jit(solution)/shard_map/tb,tif->bif/dot_general | solution.py:12
  277.4 72.6 %collective-permute-done.4 = bf16[32,128,256]{2,1,0:T(8,128)(2,1)} collective-permute-done((bf16[32,128,256]{2,1,0:T(8,128)(2,1)}, bf16[32,128,256]{2,1,0:T(8,128)(2,1)}, u32[]{:S(2)}, u32[]{:S(2)}) %collective-permute-start.4) | collective-permute-done | bytes 2097184 | tf_op jit(solution)/shard_map/ppermute | solution.py:8
  350.0 3.2 gather_fusion.6
  353.2 3.1 fusion.44
  356.2 3.2 copy.22
  359.4 3.2 gather_fusion.4
  362.6 3.1 fusion.48
  365.7 3.1 copy.21
  368.8 3.2 gather_fusion.2
  372.0 3.1 fusion.52
  375.1 2.2 copy.20
  377.4 2.6 fusion.12
  380.0 0.8 fusion.14
  381.2 1.1 fusion.34
  382.4 1.1 convolution_convert_fusion
  383.5 2.1 add_convert_fusion
  (72 shorter events, 8.0 us)
Async XLA Ops:
  7.2 12.0 %copy-start = (bf16[1024,256]{1,0:T(8,128)(2,1)S(1)}, bf16[1024,256]{1,0:T(8,128)(2,1)}, u32[]{:S(2)}) copy-start(bf16[1024,256]{1,0:T(8,128)(2,1)} %param.13) | copy-start | bytes 1572868
  7.2 11.5 %copy-start.7 = (s32[1,1,32]{2,1,0:T(1,128)S(1)}, s32[1,1,32]{2,1,0:T(1,128)}, u32[]{:S(2)}) copy-start(s32[1,1,32]{2,1,0:T(1,128)} %param.14) | copy-start | bytes 388
  7.2 12.0 %copy-start.6 = (bf16[256,256]{1,0:T(8,128)(2,1)S(1)}, bf16[256,256]{1,0:T(8,128)(2,1)}, u32[]{:S(2)}) copy-start(bf16[256,256]{1,0:T(8,128)(2,1)} %param.12) | copy-start | bytes 393220
  7.2 250.2 %all-gather.2.cloned.1.call-start = ((), (), s32[]{:S(2)}) async-start(), calls=%async_computation.1 | async-start | bytes 2621440 | tf_op jit(solution)/shard_map/all_gather | solution.py:39
  8.0 34.9 %collective-permute-start.3 = (bf16[16]{0:T(256)(128)(2,1)S(1)}, bf16[16]{0:T(256)(128)(2,1)S(1)}, u32[]{:S(2)}, u32[]{:S(2)}) collective-permute-start(bf16[16]{0:T(256)(128)(2,1)S(1)} %get-tuple-element.16), channel_id=1, source_target_pairs={{0,16},{4,20},{8,24},{12,28},{16,0},{20,4},{24,8},{28,12},{32,48},... | collective-permute-start | bytes 104 | tf_op jit(solution)/shard_map/ppermute | solution.py:8
  8.3 43.9 %collective-permute-start.5 = (bf16[16]{0:T(256)(128)(2,1)S(1)}, bf16[16]{0:T(256)(128)(2,1)S(1)}, u32[]{:S(2)}, u32[]{:S(2)}) collective-permute-start(bf16[16]{0:T(256)(128)(2,1)S(1)} %get-tuple-element.15), channel_id=1, source_target_pairs={{0,64},{4,68},{8,72},{12,76},{16,80},{20,84},{24,88},{28,92},{32,9... | collective-permute-start | bytes 104 | tf_op jit(solution)/shard_map/ppermute | solution.py:8
  9.8 50.0 %collective-permute-start.1 = (bf16[16]{0:T(256)(128)(2,1)S(1)}, bf16[16]{0:T(256)(128)(2,1)S(1)}, u32[]{:S(2)}, u32[]{:S(2)}) collective-permute-start(bf16[16]{0:T(256)(128)(2,1)S(1)} %get-tuple-element.14), channel_id=1, source_target_pairs={{0,4},{4,0},{8,12},{12,8},{16,20},{20,16},{24,28},{28,24},{32,36},... | collective-permute-start | bytes 104 | tf_op jit(solution)/shard_map/ppermute | solution.py:8
  19.6 1.6 copy-start.2
  24.2 3.2 copy-start.8
  49.0 94.8 %collective-permute-start.7 = (f32[32,128,256]{2,0,1:T(8,128)}, f32[32,128,256]{2,0,1:T(8,128)}, u32[]{:S(2)}, u32[]{:S(2)}) collective-permute-start(f32[32,128,256]{2,0,1:T(8,128)} %fusion.8), channel_id=1, source_target_pairs={{0,16},{4,20},{8,24},{12,28},{16,0},{20,4},{24,8},{28,12},{32,48},... | collective-permute-start | bytes 12582920 | tf_op jit(solution)/shard_map/ppermute | solution.py:8
  58.3 183.8 %collective-permute-start.8 = (f32[32,128,256]{2,0,1:T(8,128)}, f32[32,128,256]{2,0,1:T(8,128)}, u32[]{:S(2)}, u32[]{:S(2)}) collective-permute-start(f32[32,128,256]{2,0,1:T(8,128)} %fusion.6), channel_id=1, source_target_pairs={{0,64},{4,68},{8,72},{12,76},{16,80},{20,84},{24,88},{28,92},{32,9... | collective-permute-start | bytes 12582920 | tf_op jit(solution)/shard_map/ppermute | solution.py:8
  65.9 176.2 %collective-permute-start.6 = (f32[32,128,256]{2,0,1:T(8,128)}, f32[32,128,256]{2,0,1:T(8,128)}, u32[]{:S(2)}, u32[]{:S(2)}) collective-permute-start(f32[32,128,256]{2,0,1:T(8,128)} %fusion.10), channel_id=1, source_target_pairs={{0,4},{4,0},{8,12},{12,8},{16,20},{20,16},{24,28},{28,24},{32,36},... | collective-permute-start | bytes 12582920 | tf_op jit(solution)/shard_map/ppermute | solution.py:8
  66.0 317.5 %reduce-scatter.2.cloned.1.call-start = ((), (), s32[]{:S(2)}) async-start(), calls=%async_computation.2 | async-start | bytes 5242880 | tf_op jit(solution)/shard_map/reduce_scatter | solution.py:110
  72.7 169.5 %copy-start.9 = (s32[1,1,32]{2,1,0:T(1,128)S(1)}, s32[1,1,32]{2,1,0:T(1,128)}, u32[]{:S(2)}) copy-start(s32[1,1,32]{2,1,0:T(1,128)} %param.15) | copy-start | bytes 388
  255.3 1.0 copy-start.5
  257.4 92.5 %collective-permute-start.4 = (bf16[32,128,256]{2,1,0:T(8,128)(2,1)}, bf16[32,128,256]{2,1,0:T(8,128)(2,1)}, u32[]{:S(2)}, u32[]{:S(2)}) collective-permute-start(bf16[32,128,256]{2,1,0:T(8,128)(2,1)} %bitcast.177), channel_id=1, source_target_pairs={{0,64},{4,68},{8,72},{12,76},{16,80},{20,84},{24,88},{28,92},{32,9... | collective-permute-start | bytes 6291464 | tf_op jit(solution)/shard_map/ppermute | solution.py:8
  257.5 101.9 %collective-permute-start.2 = (bf16[32,128,256]{2,1,0:T(8,128)(2,1)}, bf16[32,128,256]{2,1,0:T(8,128)(2,1)}, u32[]{:S(2)}, u32[]{:S(2)}) collective-permute-start(bf16[32,128,256]{2,1,0:T(8,128)(2,1)} %bitcast.178), channel_id=1, source_target_pairs={{0,16},{4,20},{8,24},{12,28},{16,0},{20,4},{24,8},{28,12},{32,48},... | collective-permute-start | bytes 6291464 | tf_op jit(solution)/shard_map/ppermute | solution.py:8
  257.9 110.9 %collective-permute-start = (bf16[32,128,256]{2,1,0:T(8,128)(2,1)}, bf16[32,128,256]{2,1,0:T(8,128)(2,1)}, u32[]{:S(2)}, u32[]{:S(2)}) collective-permute-start(bf16[32,128,256]{2,1,0:T(8,128)(2,1)} %bitcast.179), channel_id=1, source_target_pairs={{0,4},{4,0},{8,12},{12,8},{16,20},{20,16},{24,28},{28,24},{32,36},... | collective-permute-start | bytes 6291464 | tf_op jit(solution)/shard_map/ppermute | solution.py:8
  377.4 2.6 copy-start.3
  380.0 1.2 copy-start.4
  381.2 4.4 %copy-start.1 = (bf16[1024,256]{1,0:T(8,128)(2,1)S(1)}, bf16[1024,256]{1,0:T(8,128)(2,1)}, u32[]{:S(2)}) copy-start(bf16[1024,256]{1,0:T(8,128)(2,1)} %param.13) | copy-start | bytes 1572868
Sparse Core Ops, SparseCore 0:
  66.1 33.8 all-gather.1
  255.4 49.4 reduce-scatter.1
where the time goes:
time: 396 us; the launch traced here: 392 us
  waiting for transfers between devices  237 us (60%)
  matrix products  64.4 us (16%)
  local copies, waits for them, and re-layouts  59.1 us (15%)
  between operations  14.3 us (4%)
  other arithmetic  10.7 us (3%)
  starting transfers between devices  7.28 us (2%)
    ppermute x9, waiting for transfers between devices, swapped(): lax.ppermute(array, axis, [(i, i ^ 1 << apart) for i in range(lax.axis_si...  237 us
    dot_general x8, matrix products, spread(): jnp.einsum('tb,tif->bif', one_hot, values, precision=lax.Precision.HIGHEST)  35.1 us
    gather x3, local copies, waits for them, and re-layouts, body(): sources = arrived[source_ids]  9.62 us
    dot_general x3, local copies, waits for them, and re-layouts, body(): jnp.einsum('tij,tif->tjf', remote_vals, grad_blocks[remote_rows[0, 0, rou...  9.39 us
    dot_general x3, matrix products, body(): jnp.einsum('tij,tjf->tif', remote_vals, sources, preferred_element_type=j...  9.22 us
    dot_general x3, matrix products, body(): jnp.einsum('tij,tif->tjf', remote_vals, grad_blocks[remote_rows[0, 0, rou...  9.09 us
    dot_general x3, local copies, waits for them, and re-layouts, body(): jnp.einsum('tij,tjf->tif', remote_vals, sources, preferred_element_type=j...  8.53 us
  transfers between devices with their start and end apart: 11, of which 3 were waited for; matrix products, arithmetic and copies ran while one was open for 33% of the time, Pallas kernels for 0%

commit v1 on v0

v1 whole, which is shorter than its diff:
```python
import jax
import jax.numpy as jnp
from jax import lax
from jax.experimental import pallas as pl
from jax.experimental.pallas import tpu as pltpu
from jax.sharding import PartitionSpec as P

UNROLL = 4
F32 = jnp.float32
BF16 = jnp.bfloat16
SMEM = pl.BlockSpec(memory_space=pltpu.SMEM)
VMEM = pl.BlockSpec(memory_space=pltpu.VMEM)
ANY = pl.BlockSpec(memory_space=pl.ANY)


def swapped(array, bit):
    return lax.ppermute(array, "node", [(i, i ^ 1 << bit) for i in range(lax.axis_size("node"))])


def shifted(array, step):
    size = lax.axis_size("feat")
    return lax.ppermute(array, "feat", [(i, (i + step) % size) for i in range(size)])


def spread_out(mine):
    half = mine.shape[0] // 2
    before = shifted(mine, 1)
    after = shifted(mine, -1)
    far_low = shifted(before[:half], 1)
    far_high = shifted(after[half:], -1)
    return (mine, after, far_low, far_high, before)


def start_all(pairs, sems):
    copies = [pltpu.make_async_copy(a, b, sems.at[i]) for i, (a, b) in enumerate(pairs)]
    for copy in copies:
        copy.start()
    return copies


def wait_all(copies):
    for copy in copies:
        copy.wait()


def pieces_into(pieces, dst, base):
    pairs = []
    for piece in pieces:
        pairs.append((piece, dst.at[pl.ds(base, piece.shape[0])]))
        base += piece.shape[0]
    return pairs


def for_live(count, step):
    def group(k, carry):
        for u in range(UNROLL):
            t = k * UNROLL + u
            step(t, t < count)
        return carry

    lax.fori_loop(0, pl.cdiv(count, UNROLL), group, 0)


def forward_tiles(count, base, vals, row_of, source_of, acc):
    trash = acc.shape[0] - 1

    def step(t, live):
        row = jnp.where(live, row_of(t), trash)
        acc[row] += jnp.dot(vals[base + t], source_of(t), preferred_element_type=F32)

    for_live(count, step)


def backward_tiles(count, base, vals, row_of, target_of, grads, acc):
    trash = acc.shape[0] - 1

    def step(t, live):
        target = jnp.where(live, target_of(t), trash)
        acc[target] += lax.dot_general(
            vals[base + t], grads[row_of(t)], (((0,), (0,)), ((), ())), preferred_element_type=F32
        )

    for_live(count, step)


def degree_kernel(counts, lrows, rrows, rslots, me, lv_hbm, rv_hbm, go_hbm, w_ref,
                  deg_ref, gh_ref, right_ref, left_ref, keep_r_ref, keep_l_ref, own_ref,
                  lv, rv, go, dacc, acc, sems):
    copies = start_all([(lv_hbm, lv), (rv_hbm, rv), (go_hbm, go)], sems)
    own = deg_ref.shape[0]
    cap = rrows.shape[1]
    dacc[...] = jnp.zeros_like(dacc)
    acc[...] = jnp.zeros_like(acc)
    copies[0].wait()

    def add_rows(vals, base, row_of):
        def step(t, live):
            row = jnp.where(live, row_of(t), own)
            dacc[row] += vals[base + t].astype(F32)
        return step

    for_live(counts[0], add_rows(lv, 0, lambda t: lrows[t]))
    copies[1].wait()
    for r in range(rrows.shape[0]):
        for_live(counts[r + 1], add_rows(rv, r * cap, lambda t: rrows[r, t]))
    copies[2].wait()
    for b in range(own):
        degree = 1.0 + jnp.broadcast_to(jnp.sum(dacc[b], axis=1, keepdims=True), dacc.shape[1:])
        deg_ref[b] = degree
        dense = lax.dot_general(go[b], w_ref[...], (((1,), (1,)), ((), ())), preferred_element_type=F32)
        width = degree.shape[1]
        for k in range(dense.shape[1] // width):
            gh_ref[b, :, k * width:(k + 1) * width] = (
                dense[:, k * width:(k + 1) * width] / degree
            ).astype(BF16)
    last = rrows.shape[0] - 1
    share = own_ref.shape[0]
    shift = me[0] * share
    backward_tiles(
        counts[last + 1], last * cap, rv, lambda t: rrows[last, t],
        lambda t: lax.rem(rslots[last, t] - shift + cap, cap), gh_ref, acc,
    )
    split_out(acc, share, right_ref, left_ref, keep_r_ref, keep_l_ref, own_ref)


def split_out(acc, n, right_ref, left_ref, keep_r_ref, keep_l_ref, own_ref):
    h = n // 2
    right_ref[:h] = acc[2 * n:2 * n + h].astype(BF16)
    right_ref[h:] = acc[n + h:2 * n].astype(BF16)
    left_ref[:h] = acc[2 * n + h:3 * n].astype(BF16)
    left_ref[h:] = acc[3 * n:3 * n + h].astype(BF16)
    keep_r_ref[...] = acc[n:n + h]
    keep_l_ref[...] = acc[3 * n + h:4 * n]
    own_ref[...] = acc[:n]


def parcels_kernel(counts, rrows, rslots, rv_ref, gh_ref, out_a, out_b, acc):
    cap = rrows.shape[1]
    for r, out in ((1, out_b), (0, out_a)):
        acc[...] = jnp.zeros_like(acc)
        backward_tiles(
            counts[r + 1], r * cap, rv_ref, lambda t: rrows[r, t], lambda t: rslots[r, t], gh_ref, acc
        )
        out[...] = acc[:out.shape[0]].astype(BF16)


def local_back_kernel(counts, lrows, lcols, me, lv_ref, gh_ref, out_ref, acc):
    total = out_ref.shape[0]
    own = gh_ref.shape[0]
    acc[...] = jnp.zeros_like(acc)
    shift = me[0] * own
    backward_tiles(
        counts[0], 0, lv_ref, lambda t: lrows[t],
        lambda t: lax.rem(lcols[t] - shift + total, total), gh_ref, acc,
    )
    acc[:own] += gh_ref[...].astype(F32)
    out_ref[...] = acc[:total]


def combine_kernel(keep_r, keep_l, from_left, from_right, out_r, out_l):
    h = keep_r.shape[0]
    out_r[...] = (keep_r[...] + from_left[:h].astype(F32)).astype(BF16)
    out_l[...] = (keep_l[...] + from_right[:h].astype(F32)).astype(BF16)


def finish_kernel(own, a_left, a_right, b_left, b_right, out):
    h = own.shape[0] // 2
    out[:h] = (own[:h] + a_right[h:].astype(F32) + b_left[...].astype(F32)).astype(BF16)
    out[h:] = (own[h:] + a_left[h:].astype(F32) + b_right[...].astype(F32)).astype(BF16)


def merge_kernel(sends, me, part_hbm, got_a, got_b, got_c,
                 right_ref, left_ref, keep_r_ref, keep_l_ref, own_ref, acc, sems):
    copies = start_all([(part_hbm, acc)], sems)
    total = acc.shape[0]
    own = own_ref.shape[0]
    shift = me[0] * own
    wait_all(copies)

    def add(got, r, base):
        for s in range(got.shape[0]):
            block = lax.rem(sends[r, base + s] - shift + total, total)
            acc[block] += got[s].astype(F32)

    add(got_a, 0, 0)
    add(got_b, 1, 0)
    add(got_c, 2, me[0] * got_c.shape[0])
    split_out(acc, own, right_ref, left_ref, keep_r_ref, keep_l_ref, own_ref)


def pick_kernel(sends, me, p0, p1, p2, p3, p4, out_a, out_b, out_c, src, sems):
    pieces = (p0, p1, p2, p3, p4)
    wait_all(start_all(pieces_into(pieces, src, 0), sems))
    total = src.shape[0]
    shift = me[0] * p0.shape[0]

    def put(out, r, base):
        for s in range(out.shape[0]):
            out[s] = src[lax.rem(sends[r, base + s] - shift + total, total)]

    put(out_c, 2, me[0] * out_c.shape[0])
    put(out_b, 1, 0)
    put(out_a, 0, 0)


def near_forward_kernel(counts, lrows, lcols, rrows, rslots, me, p0, p1, p2, p3, p4, got_hbm, lv_hbm, rv_hbm,
                        out_ref, src, vals, acc, sems):
    total = out_ref.shape[0]
    cap = rrows.shape[1]
    lcap = lcols.shape[0]
    pieces = (p0, p1, p2, p3, p4)
    part = src.shape[0] - got_hbm.shape[0]
    pairs = pieces_into(pieces + (got_hbm,), src, 0)
    pairs += [(lv_hbm, vals.at[pl.ds(0, lcap)]), (rv_hbm.at[pl.ds(0, cap)], vals.at[pl.ds(lcap, cap)])]
    wait_all(start_all(pairs, sems))
    acc[:total] = src[:total].astype(F32)
    shift = me[0] * total
    forward_tiles(
        counts[0], 0, vals, lambda t: lrows[t],
        lambda t: src[lax.rem(lcols[t] - shift + part, part)], acc,
    )
    forward_tiles(counts[1], lcap, vals, lambda t: rrows[0, t], lambda t: src[part + rslots[0, t]], acc)
    out_ref[...] = acc[:total]


def far_forward_kernel(counts, rrows, rslots, me, p0, p1, p2, p3, p4, got_hbm, rv_hbm, near_hbm, deg_hbm, w_ref,
                       out_ref, src, vals, acc, deg, sems):
    total = out_ref.shape[0]
    cap = rrows.shape[1]
    pieces = (p0, p1, p2, p3, p4)
    pairs = pieces_into((got_hbm,) + pieces, src, 0)
    pairs += [(rv_hbm.at[pl.ds(cap, 2 * cap)], vals), (near_hbm, acc.at[pl.ds(0, total)]), (deg_hbm, deg)]
    wait_all(start_all(pairs, sems))
    forward_tiles(counts[2], 0, vals, lambda t: rrows[1, t], lambda t: src[rslots[1, t]], acc)
    shift = me[0] * p0.shape[0]
    forward_tiles(
        counts[3], cap, vals, lambda t: rrows[2, t],
        lambda t: src[cap + lax.rem(rslots[2, t] - shift + cap, cap)], acc,
    )
    width = deg.shape[2]
    for b in range(total):
        hidden = jnp.concatenate(
            [acc[b, :, k:k + width] / deg[b] for k in range(0, acc.shape[2], width)], axis=1
        ).astype(BF16)
        out_ref[b] = jnp.dot(hidden, w_ref[...], preferred_element_type=F32).astype(BF16)


def body(
    features,
    weight,
    grad_out,
    local_rows,
    local_cols,
    local_values,
    remote_rows,
    remote_slots,
    remote_values,
    send_blocks,
    tile_counts,
):
    rows_dev, width = features.shape
    lcap, rows = local_values.shape[2:4]
    own = rows_dev // rows
    rounds, cap = remote_rows.shape[2:]
    slices = lax.axis_size("feat")
    part = own * slices
    share = cap // slices
    log_nodes = lax.axis_size("node").bit_length() - 1
    bits = [r * log_nodes // rounds for r in range(rounds)]
    tail = (rows, width)

    me = lax.axis_index("feat").astype(jnp.int32).reshape(1)
    counts = tile_counts[0, 0]
    lrows, lcols = local_rows[0, 0], local_cols[0, 0]
    rrows, rslots = remote_rows[0, 0], remote_slots[0, 0]
    sends = send_blocks[0]
    lv = local_values.reshape(lcap, rows, rows)
    rv = remote_values.reshape(rounds * cap, rows, rows)
    feats = features.reshape((own,) + tail)
    go = grad_out.reshape((own,) + tail)

    def blocks(n, kind):
        return jax.ShapeDtypeStruct((n,) + tail, kind)

    def room(n, kind):
        return pltpu.VMEM((n,) + tail, kind)

    def tiles(n, kind=BF16):
        return pltpu.VMEM((n, rows, rows), kind)

    def call(kernel, scalars, specs, args, outs, scratch, flops):
        size = sum(a.size * a.dtype.itemsize for a in args)
        size += sum(o.size * o.dtype.itemsize for o in outs)
        return pl.pallas_call(
            kernel,
            out_shape=tuple(outs),
            in_specs=[SMEM] * len(scalars) + specs,
            out_specs=tuple([VMEM] * len(outs)),
            scratch_shapes=scratch,
            cost_estimate=pl.CostEstimate(flops=flops, bytes_accessed=size, transcendentals=0),
        )(*scalars, *args)

    def sems(n):
        return pltpu.SemaphoreType.DMA((n,))

    tile_flops = 2 * rows * rows * width

    def split_shapes(n):
        return [blocks(n, BF16), blocks(n, BF16), blocks(n // 2, F32), blocks(n // 2, F32), blocks(n, F32)]

    part_feats = spread_out(feats)

    deg, gh, z_right, z_left, z_keep_r, z_keep_l, z_own = call(
        degree_kernel, (counts, lrows, rrows, rslots, me), [ANY, ANY, ANY, VMEM], (lv, rv, go, weight),
        [jax.ShapeDtypeStruct((own, rows, rows), F32), blocks(own, BF16)] + split_shapes(share),
        [tiles(lcap), tiles(rounds * cap), room(own, BF16), tiles(own + 1, F32), room(cap + 1, F32), sems(3)],
        cap * tile_flops,
    )

    def scattered(right, left, keep_r, keep_l):
        a_left = shifted(right, 1)
        a_right = shifted(left, -1)
        h = keep_r.shape[0]
        out_r, out_l = call(
            combine_kernel, (), [VMEM] * 4, (keep_r, keep_l, a_left, a_right),
            [blocks(h, BF16), blocks(h, BF16)], [], 0,
        )
        return a_left, a_right, shifted(out_r, 1), shifted(out_l, -1)

    def finished(own_part, parts):
        return call(finish_kernel, (), [VMEM] * 5, (own_part,) + parts, [blocks(own_part.shape[0], BF16)], [], 0)[0]

    z_parts = scattered(z_right, z_left, z_keep_r, z_keep_l)
    back_a, back_b = call(
        parcels_kernel, (counts, rrows, rslots), [VMEM, VMEM], (rv, gh),
        [blocks(cap, BF16), blocks(cap, BF16)], [room(cap + 1, F32)], 2 * cap * tile_flops,
    )
    got_back_b = swapped(back_b, bits[1])
    got_back_a = swapped(back_a, bits[0])
    got_back_c = swapped(finished(z_own, z_parts), bits[2])

    part_back = call(
        local_back_kernel, (counts, lrows, lcols, me), [VMEM, VMEM], (lv, gh),
        [blocks(part, F32)], [room(part + 1, F32)], lcap * tile_flops,
    )[0]

    need_a, need_b, need_c = call(
        pick_kernel, (sends, me), [ANY] * 5, part_feats,
        [blocks(cap, BF16), blocks(cap, BF16), blocks(share, BF16)], [room(part, BF16), sems(5)], 0,
    )
    got_c = swapped(need_c, bits[2])
    got_b = swapped(need_b, bits[1])
    got_a = swapped(need_a, bits[0])
    far_feats = spread_out(got_c)

    near = call(
        near_forward_kernel, (counts, lrows, lcols, rrows, rslots, me), [ANY] * 8,
        part_feats + (got_a, lv, rv), [blocks(own, F32)],
        [room(part + cap, BF16), tiles(lcap + cap), room(own + 1, F32), sems(8)], (lcap + cap) * tile_flops,
    )[0]

    right, left, keep_r, keep_l, own_part = call(
        merge_kernel, (sends, me), [ANY, VMEM, VMEM, VMEM], (part_back, got_back_a, got_back_b, got_back_c),
        split_shapes(own), [room(part, F32), sems(1)], 0,
    )
    grad_features = finished(own_part, scattered(right, left, keep_r, keep_l))

    output = call(
        far_forward_kernel, (counts, rrows, rslots, me), [ANY] * 9 + [VMEM],
        far_feats + (got_b, rv, near, deg, weight), [blocks(own, BF16)],
        [room(2 * cap, BF16), tiles(2 * cap), room(own + 1, F32), tiles(own, F32), sems(9)],
        2 * cap * tile_flops,
    )[0]
    return (output.reshape(rows_dev, width), grad_features.reshape(rows_dev, width))


def solution(mesh):
    in_specs = (
        P(("node", "feat"), None),
        P(),
        P(("node", "feat"), None),
        P("node", "feat", None),
        P("node", "feat", None),
        P("node", "feat", None, None, None),
        P("node", "feat", None, None),
        P("node", "feat", None, None),
        P("node", "feat", None, None, None, None),
        P("node", None, None),
        P("node", "feat", None),
    )
    out_specs = (P(("node", "feat"), None), P(("node", "feat"), None))
    return jax.shard_map(body, mesh=mesh, in_specs=in_specs, out_specs=out_specs, check_vma=False)
```

time: 396 us -> 130 us (0.33)
  waiting for transfers between devices: 237 us -> 44.9 us
  matrix products: 64.4 us -> 0 us
  local copies, waits for them, and re-layouts: 59.1 us -> 7.32 us
  Pallas kernels: 0 us -> 45.2 us
  starting transfers between devices: 7.28 us -> 29 us
  between operations: 14.3 us -> 1.05 us
  other arithmetic: 10.7 us -> 0 us
    ppermute x9 -> x22, waiting for transfers between devices: 237 us -> 44.9 us  [the longest x16 31.2 us: shifted(): lax.ppermute(array, 'feat', [(i, (i + step) % size) for i in range(size)])]
    dot_general x22 -> x0, matrix products: 64.4 us -> none  [the longest x8 35.1 us: spread(): jnp.einsum('tb,tif->bif', one_hot, values, precision=lax.Precision.HIGHEST)]
    pallas_call x0 -> x11, Pallas kernels: none -> 45.2 us  [call(): pl.pallas_call(kernel, out_shape=tuple(outs), in_specs=[SMEM] * len(scala...]
    dot_general x8 -> x0, local copies, waits for them, and re-layouts: 28.9 us -> none  [the longest x3 9.39 us: body(): jnp.einsum('tij,tif->tjf', remote_vals, grad_blocks[remote_rows[0, 0, rou...]
    gather x11 -> x0, local copies, waits for them, and re-layouts: 22.1 us -> none  [the longest x3 9.62 us: body(): sources = arrived[source_ids]]
    ppermute x9 -> x22, starting transfers between devices: 7.2 us -> 29 us  [the longest x16 21.6 us: shifted(): lax.ppermute(array, 'feat', [(i, (i + step) % size) for i in range(size)])]
    unnamed x20 -> x46, local copies, waits for them, and re-layouts: 1.33 us -> 7.26 us
    add x2 -> x0, local copies, waits for them, and re-layouts: 4.49 us -> none  [the longest x1 4.39 us: body(): part_acc = part_acc + returned]
  transfers between devices with their start and end apart: 11 -> 22, of which waited for: 3 -> 6; matrix products, arithmetic and copies ran while one was open for 33% -> 1% of each run, Pallas kernels for 0% -> 26%
where the time goes in v1:
time: 130 us; the launch traced here: 127 us
  Pallas kernels  45.2 us (35%)
  waiting for transfers between devices  44.9 us (35%)
  starting transfers between devices  29 us (22%)
  local copies, waits for them, and re-layouts  7.32 us (6%)
    pallas_call x11, Pallas kernels, call(): pl.pallas_call(kernel, out_shape=tuple(outs), in_specs=[SMEM] * len(scala...  45.2 us
    ppermute x16, waiting for transfers between devices, shifted(): lax.ppermute(array, 'feat', [(i, (i + step) % size) for i in range(size)])  31.2 us
    ppermute x16, starting transfers between devices, shifted(): lax.ppermute(array, 'feat', [(i, (i + step) % size) for i in range(size)])  21.6 us
    ppermute x6, waiting for transfers between devices, swapped(): lax.ppermute(array, 'node', [(i, i ^ 1 << bit) for i in range(lax.axis_si...  13.7 us
    ppermute x6, starting transfers between devices, swapped(): lax.ppermute(array, 'node', [(i, i ^ 1 << bit) for i in range(lax.axis_si...  7.4 us
    unnamed x46, local copies, waits for them, and re-layouts  7.26 us
  transfers between devices with their start and end apart: 22, of which 6 were waited for; matrix products, arithmetic and copies ran while one was open for 1% of the time, Pallas kernels for 26%

profile of v1, /device:TPU:146, one launch (start us, length us, event | category | flops | bytes accessed | tf_op | source)
XLA Modules:
  0.0 127.5 jit_solution(14600425291697153939)
XLA Ops:
  0.6 1.4 %copy_bitcast_fusion.1 = (s32[3,16]{1,0:T(4,128)}, s32[3,16]{1,0:T(4,128)}) fusion(s32[1,1,3,16]{3,1,2,0:T(1,128)} %param.18, s32[1,1,3,16]{3,1,2,0:T(1,128)} %param.17), kind=kLoop, calls=%fused_computation.1 | loop fusion | bytes 768
  2.0 6.0 %shard_map.124 = (f32[8,128,128]{2,1,0:T(8,128)}, bf16[8,128,256]{2,1,0:T(8,128)(2,1)}, bf16[4,128,256]{2,1,0:T(8,128)(2,1)}, bf16[4,128,256]{2,1,0:T(8,128)(2,1...) custom-call(s32[4]{0:T(128)} %bitcast.33, s32[32]{0:T(128)} %bitcast.38, ...), custom_call_target="tpu_custom_call" | custom-call | flops 134217728 | bytes 5898240 | tf_op jit(solution)/shard_map/pallas_call | solution.py:294
  8.0 0.6 collective-permute-start.13
  8.6 4.5 %shard_map.127 = (bf16[16,128,256]{2,1,0:T(8,128)(2,1)}, bf16[16,128,256]{2,1,0:T(8,128)(2,1)}) custom-call(s32[4]{0:T(128)} %bitcast.34, s32[3,16]{1,0:T(4,128)} %get-tuple-element.45.rrows, s32[3,16]{1,0:T(4,128)} %get-tuple-element.44.rslots, bf16[48,128,128]{2,1,0:T(8,128)(2,1)} %bitcast.18, bf16[8,128,256]{2,1,0:T(8,128)(2,1)} %get-tuple-element.27.gh_ref), custom_call_target="tpu_custom_call" | custom-call | flops 268435456 | bytes 4194304 | tf_op jit(solution)/shard_map/pallas_call | solution.py:294
  13.2 1.1 collective-permute-start.12
  14.3 1.4 %collective-permute-start.1 = (bf16[8,128,256]{2,1,0:T(8,128)(2,1)S(1)}, bf16[8,128,256]{2,1,0:T(8,128)(2,1)S(1)}, u32[]{:S(2)}, u32[]{:S(2)}) collective-permute-start(bf16[8,128,256]{2,1,0:T(8,128)(2,1)S(1)} %bitcast.26), channel_id=1, source_target_pairs={{0,1},{1,2},{2,3},{3,0},{4,5},{5,6},{6,7},{7,4},{8,9},{9,10},{10,1... | collective-permute-start | bytes 1572872 | tf_op jit(solution)/shard_map/ppermute | solution.py:22
  15.7 0.7 collective-permute-start
  16.3 1.9 %collective-permute-start.14 = (bf16[4,128,256]{2,1,0:T(8,128)(2,1)}, bf16[4,128,256]{2,1,0:T(8,128)(2,1)S(1)}, u32[]{:S(2)}, u32[]{:S(2)}) collective-permute-start(bf16[4,128,256]{2,1,0:T(8,128)(2,1)} %get-tuple-element.32), channel_id=1, source_target_pairs={{0,3},{1,0},{2,1},{3,2},{4,7},{5,4},{6,5},{7,6},{8,11},{9,8},{10,9... | collective-permute-start | bytes 786440 | tf_op jit(solution)/shard_map/ppermute | solution.py:22
  18.3 16.8 %collective-permute-done.14.from_right.a_right = bf16[4,128,256]{2,1,0:T(8,128)(2,1)S(1)} collective-permute-done((bf16[4,128,256]{2,1,0:T(8,128)(2,1)}, bf16[4,128,256]{2,1,0:T(8,128)(2,1)S(1)}, u32[]{:S(2)}, u32[]{:S(2)}) %collective-permute-start.14) | collective-permute-done | bytes 262176 | tf_op jit(solution)/shard_map/ppermute | solution.py:22
  35.1 0.7 copy-done.9
  35.7 1.9 %shard_map.128 = (bf16[2,128,256]{2,1,0:T(8,128)(2,1)}, bf16[2,128,256]{2,1,0:T(8,128)(2,1)}) custom-call(f32[2,128,256]{2,1,0:T(8,128)} %get-tuple-element.33.keep_r, f32[2,128,256]{2,1,0:T(8,128)} %get-tuple-element.34.keep_l, bf16[4,128,256]{2,1,0:T(8,128)(2,1)} %copy-done.8, bf16[4,128,256]{2,1,0:T(8,128)(2,1)} %copy-done.9), custom_call_target="tpu_custom_call" | custom-call | bytes 1310720 | tf_op jit(solution)/shard_map/pallas_call | solution.py:294
  37.7 0.4 collective-permute-start.15
  38.1 3.0 %collective-permute-start.2 = (bf16[4,128,256]{2,1,0:T(8,128)(2,1)S(1)}, bf16[4,128,256]{2,1,0:T(8,128)(2,1)S(1)}, u32[]{:S(2)}, u32[]{:S(2)}) collective-permute-start(bf16[4,128,256]{2,1,0:T(8,128)(2,1)S(1)} %slice.16), channel_id=1, source_target_pairs={{0,1},{1,2},{2,3},{3,0},{4,5},{5,6},{6,7},{7,4},{8,9},{9,10},{10,1... | collective-permute-start | bytes 786440 | tf_op jit(solution)/shard_map/ppermute | solution.py:22
  41.2 0.1 collective-permute-start.3
  41.3 3.0 %collective-permute-done.15.b_left = bf16[2,128,256]{2,1,0:T(8,128)(2,1)S(1)} collective-permute-done((bf16[2,128,256]{2,1,0:T(8,128)(2,1)}, bf16[2,128,256]{2,1,0:T(8,128)(2,1)S(1)}, u32[]{:S(2)}, u32[]{:S(2)}) %collective-permute-start.15) | collective-permute-done | bytes 131104 | tf_op jit(solution)/shard_map/ppermute | solution.py:22
  44.3 2.0 %collective-permute-start.16 = (bf16[2,128,256]{2,1,0:T(8,128)(2,1)}, bf16[2,128,256]{2,1,0:T(8,128)(2,1)S(1)}, u32[]{:S(2)}, u32[]{:S(2)}) collective-permute-start(bf16[2,128,256]{2,1,0:T(8,128)(2,1)} %get-tuple-element.36), channel_id=1, source_target_pairs={{0,3},{1,0},{2,1},{3,2},{4,7},{5,4},{6,5},{7,6},{8,11},{9,8},{10,9... | collective-permute-start | bytes 393224 | tf_op jit(solution)/shard_map/ppermute | solution.py:22
  46.2 4.8 %collective-permute-done.16.b_right = bf16[2,128,256]{2,1,0:T(8,128)(2,1)S(1)} collective-permute-done((bf16[2,128,256]{2,1,0:T(8,128)(2,1)}, bf16[2,128,256]{2,1,0:T(8,128)(2,1)S(1)}, u32[]{:S(2)}, u32[]{:S(2)}) %collective-permute-start.16) | collective-permute-done | bytes 131104 | tf_op jit(solution)/shard_map/ppermute | solution.py:22
  51.0 0.6 copy-done.19
  51.7 2.1 %shard_map.129 = bf16[4,128,256]{2,1,0:T(8,128)(2,1)} custom-call(f32[4,128,256]{2,1,0:T(8,128)} %get-tuple-element.30.own, bf16[4,128,256]{2,1,0:T(8,128)(2,1)} %copy-done.8, bf16[4,128,256]{2,1,0:T(8,128)(2,1)} %copy-done.9, bf16[2,128,256]{2,1,0:T(8,128)(2,1)} %copy-done.18, bf16[2,128,256]{2,1,0:T(8,128)(2,1)} %copy-done.19), custom_call_target="tpu_custom_call" | custom-call | bytes 1572864 | tf_op jit(solution)/shard_map/pallas_call | solution.py:294
  53.7 1.1 collective-permute-start.17
  54.9 0.6 copy.19
  55.5 0.7 copy-done.6
  56.3 3.8 %shard_map.122 = (bf16[16,128,256]{2,1,0:T(8,128)(2,1)}, bf16[16,128,256]{2,1,0:T(8,128)(2,1)}, bf16[4,128,256]{2,1,0:T(8,128)(2,1)}) custom-call(s32[3,16]{1,0:T(4,128)} %bitcast.31, s32[1]{0:T(128)} %bitcast.1.me, bf16[8,128,256]{2,1,0:T(8,128)(2,1)} %bitcast.24, bf16[8,128,256]{2,1,0:T(8,128)(2,1)} %copy-done.1, bf16[4,128,256]{2,1,0:T(8,128)(2,1)} %copy-done.6, ...), custom_call_target="tpu_custom_call" | custom-call | bytes 4456448 | tf_op jit(solution)/shard_map/pallas_call | solution.py:294
  60.1 0.1 collective-permute-start.10
  60.2 3.2 %collective-permute-start.9 = (bf16[16,128,256]{2,1,0:T(8,128)(2,1)}, bf16[16,128,256]{2,1,0:T(8,128)(2,1)}, u32[]{:S(2)}, u32[]{:S(2)}) collective-permute-start(bf16[16,128,256]{2,1,0:T(8,128)(2,1)} %get-tuple-element.24), channel_id=1, source_target_pairs={{0,16},{4,20},{8,24},{12,28},{16,0},{20,4},{24,8},{28,12},{32,48},... | collective-permute-start | bytes 3145736 | tf_op jit(solution)/shard_map/ppermute | solution.py:17
  63.5 4.7 %shard_map.126.part_hbm = f32[32,128,256]{2,1,0:T(8,128)} custom-call(s32[4]{0:T(128)} %bitcast.35, s32[32]{0:T(128)} %bitcast.39, s32[32]{0:T(128)} %bitcast.41, s32[1]{0:T(128)} %bitcast.1.me, bf16[32,128,128]{2,1,0:T(8,128)(2,1)} %bitcast.22, bf16[8,128,256]{2,1,0:T(8,128)(2,1)} %get-tuple-element.27.gh_ref), custom_call_target="tpu_custom_call" | custom-call | flops 268435456 | bytes 5767168 | tf_op jit(solution)/shard_map/pallas_call | solution.py:294
  68.2 0.7 copy-done.13
  68.9 0.3 copy-done.5
  69.2 6.0 %shard_map.130 = (bf16[8,128,256]{2,1,0:T(8,128)(2,1)}, bf16[8,128,256]{2,1,0:T(8,128)(2,1)}, f32[4,128,256]{2,1,0:T(8,128)}, f32[4,128,256]{2,1,0:T(8,128)}, f32[8,128,256]{2,1,0:T(8,128)}) custom-call(s32[3,16]{1,0:T(4,128)} %bitcast.32, s32[1]{0:T(128)} %bitcast.1.me, f32[32,128,256]{2,1,0:T(8,128)} %shard_map.126.part_hbm, ...), custom_call_target="tpu_custom_call" | custom-call | bytes 9699328 | tf_op jit(solution)/shard_map/pallas_call | solution.py:294
  75.2 1.1 collective-permute-start.18
  76.3 1.0 collective-permute-start.19
  77.3 1.8 %collective-permute-start.4 = (bf16[4,128,256]{2,1,0:T(8,128)(2,1)S(1)}, bf16[4,128,256]{2,1,0:T(8,128)(2,1)S(1)}, u32[]{:S(2)}, u32[]{:S(2)}) collective-permute-start(bf16[4,128,256]{2,1,0:T(8,128)(2,1)S(1)} %copy-done.21), channel_id=1, source_target_pairs={{0,64},{4,68},{8,72},{12,76},{16,80},{20,84},{24,88},{28,92},{32,9... | collective-permute-start | bytes 786440 | tf_op jit(solution)/shard_map/ppermute | solution.py:17
  79.1 13.7 %collective-permute-done.4.p0 = bf16[4,128,256]{2,1,0:T(8,128)(2,1)S(1)} collective-permute-done((bf16[4,128,256]{2,1,0:T(8,128)(2,1)S(1)}, bf16[4,128,256]{2,1,0:T(8,128)(2,1)S(1)}, u32[]{:S(2)}, u32[]{:S(2)}) %collective-permute-start.4) | collective-permute-done | bytes 262176 | tf_op jit(solution)/shard_map/ppermute | solution.py:17
  92.8 0.8 collective-permute-start.6
  93.6 1.9 %collective-permute-start.5 = (bf16[4,128,256]{2,1,0:T(8,128)(2,1)S(1)}, bf16[4,128,256]{2,1,0:T(8,128)(2,1)S(1)}, u32[]{:S(2)}, u32[]{:S(2)}) collective-permute-start(bf16[4,128,256]{2,1,0:T(8,128)(2,1)S(1)} %collective-permute-done.4.p0), channel_id=1, source_target_pairs={{0,3},{1,0},{2,1},{3,2},{4,7},{5,4},{6,5},{7,6},{8,11},{9,8},{10,9... | collective-permute-start | bytes 786440 | tf_op jit(solution)/shard_map/ppermute | solution.py:22
  95.5 0.8 copy-done.3
  96.3 2.4 %shard_map.131 = (bf16[4,128,256]{2,1,0:T(8,128)(2,1)}, bf16[4,128,256]{2,1,0:T(8,128)(2,1)}) custom-call(f32[4,128,256]{2,1,0:T(8,128)} %get-tuple-element.40.keep_r, f32[4,128,256]{2,1,0:T(8,128)} %get-tuple-element.41.keep_l, bf16[8,128,256]{2,1,0:T(8,128)(2,1)} %copy-done.2, bf16[8,128,256]{2,1,0:T(8,128)(2,1)} %copy-done.3), custom_call_target="tpu_custom_call" | custom-call | bytes 2621440 | tf_op jit(solution)/shard_map/pallas_call | solution.py:294
  98.6 0.7 collective-permute-start.20
  99.4 2.2 %collective-permute-done.6.p4 = bf16[4,128,256]{2,1,0:T(8,128)(2,1)S(1)} collective-permute-done((bf16[4,128,256]{2,1,0:T(8,128)(2,1)S(1)}, bf16[4,128,256]{2,1,0:T(8,128)(2,1)S(1)}, u32[]{:S(2)}, u32[]{:S(2)}) %collective-permute-start.6) | collective-permute-done | bytes 262176 | tf_op jit(solution)/shard_map/ppermute | solution.py:22
  101.6 3.0 %collective-permute-start.21 = (bf16[4,128,256]{2,1,0:T(8,128)(2,1)}, bf16[4,128,256]{2,1,0:T(8,128)(2,1)S(1)}, u32[]{:S(2)}, u32[]{:S(2)}) collective-permute-start(bf16[4,128,256]{2,1,0:T(8,128)(2,1)} %get-tuple-element.43), channel_id=1, source_target_pairs={{0,3},{1,0},{2,1},{3,2},{4,7},{5,4},{6,5},{7,6},{8,11},{9,8},{10,9... | collective-permute-start | bytes 786440 | tf_op jit(solution)/shard_map/ppermute | solution.py:22
  104.6 0.1 collective-permute-start.7
  104.7 4.4 %collective-permute-done.20.b_left = bf16[4,128,256]{2,1,0:T(8,128)(2,1)S(1)} collective-permute-done((bf16[4,128,256]{2,1,0:T(8,128)(2,1)}, bf16[4,128,256]{2,1,0:T(8,128)(2,1)S(1)}, u32[]{:S(2)}, u32[]{:S(2)}) %collective-permute-start.20) | collective-permute-done | bytes 262176 | tf_op jit(solution)/shard_map/ppermute | solution.py:22
  109.1 3.0 %collective-permute-start.8 = (bf16[2,128,256]{2,1,0:T(8,128)(2,1)S(1)}, bf16[2,128,256]{2,1,0:T(8,128)(2,1)S(1)}, u32[]{:S(2)}, u32[]{:S(2)}) collective-permute-start(bf16[2,128,256]{2,1,0:T(8,128)(2,1)S(1)} %slice.19), channel_id=1, source_target_pairs={{0,3},{1,0},{2,1},{3,2},{4,7},{5,4},{6,5},{7,6},{8,11},{9,8},{10,9... | collective-permute-start | bytes 393224 | tf_op jit(solution)/shard_map/ppermute | solution.py:22
  112.0 0.7 copy-done.15
  112.7 2.6 %shard_map.132 = bf16[8,128,256]{2,1,0:T(8,128)(2,1)} custom-call(f32[8,128,256]{2,1,0:T(8,128)} %get-tuple-element.37.own, bf16[8,128,256]{2,1,0:T(8,128)(2,1)} %copy-done.2, bf16[8,128,256]{2,1,0:T(8,128)(2,1)} %copy-done.3, bf16[4,128,256]{2,1,0:T(8,128)(2,1)} %copy-done.14, bf16[4,128,256]{2,1,0:T(8,128)(2,1)} %copy-done.15), custom_call_target="tpu_custom_call" | custom-call | bytes 3145728 | tf_op jit(solution)/shard_map/pallas_call | solution.py:294
  115.4 5.6 %shard_map.123.near_hbm = f32[8,128,256]{2,1,0:T(8,128)} custom-call(s32[4]{0:T(128)} %bitcast.36, s32[32]{0:T(128)} %bitcast.40, s32[32]{0:T(128)} %bitcast.42, s32[3,16]{1,0:T(4,128)} %get-tuple-element.45.rrows, s32[3,16]{1,0:T(4,128)} %get-tuple-element.44.rslots, s32[1]{0:T(128)} %bitcast.1.me, bf16[8,128,256]{2,1,0:T(8,128)(2,1)} %bitcast.25, ...), custom_call_target="tpu_custom_call" | custom-call | flops 402653184 | bytes 6815744 | tf_op jit(solution)/shard_map/pallas_call | solution.py:294
  121.1 0.6 copy-done.16
  121.7 5.6 %shard_map.125 = bf16[8,128,256]{2,1,0:T(8,128)(2,1)} custom-call(s32[4]{0:T(128)} %bitcast.37, s32[3,16]{1,0:T(4,128)} %get-tuple-element.45.rrows, s32[3,16]{1,0:T(4,128)} %get-tuple-element.44.rslots, s32[1]{0:T(128)} %bitcast.1.me, bf16[4,128,256]{2,1,0:T(8,128)(2,1)} %copy-done.12, bf16[4,128,256]{2,1,0:T(8,128)(2,1)} %copy-done.11, ...), custom_call_target="tpu_custom_call" | custom-call | flops 268435456 | bytes 5898240 | tf_op jit(solution)/shard_map/pallas_call | solution.py:294
  (57 shorter events, 0.3 us)
Async XLA Ops:
  0.6 13.7 %copy-start.4 = (bf16[1024,256]{1,0:T(8,128)(2,1)S(1)}, bf16[1024,256]{1,0:T(8,128)(2,1)}, u32[]{:S(2)}) copy-start(bf16[1024,256]{1,0:T(8,128)(2,1)} %param.11) | copy-start | bytes 1572868
  2.0 52.9 %copy-start.20 = (s32[1,3,16]{2,0,1:T(1,128)S(1)}, s32[1,3,16]{2,0,1:T(1,128)}, u32[]{:S(2)}) copy-start(s32[1,3,16]{2,0,1:T(1,128)} %param.20) | copy-start | bytes 580
  8.0 8.3 %collective-permute-start.13 = (bf16[4,128,256]{2,1,0:T(8,128)(2,1)}, bf16[4,128,256]{2,1,0:T(8,128)(2,1)S(1)}, u32[]{:S(2)}, u32[]{:S(2)}) collective-permute-start(bf16[4,128,256]{2,1,0:T(8,128)(2,1)} %get-tuple-element.31), channel_id=1, source_target_pairs={{0,1},{1,2},{2,3},{3,0},{4,5},{5,6},{6,7},{7,4},{8,9},{9,10},{10,1... | collective-permute-start | bytes 786440 | tf_op jit(solution)/shard_map/ppermute | solution.py:22
  13.2 55.0 %collective-permute-start.11 = (bf16[16,128,256]{2,1,0:T(8,128)(2,1)}, bf16[16,128,256]{2,1,0:T(8,128)(2,1)S(1)}, u32[]{:S(2)}, u32[]{:S(2)}) collective-permute-start(bf16[16,128,256]{2,1,0:T(8,128)(2,1)} %get-tuple-element.28), channel_id=1, source_target_pairs={{0,4},{4,0},{8,12},{12,8},{16,20},{20,16},{24,28},{28,24},{32,36},... | collective-permute-start | bytes 3145736 | tf_op jit(solution)/shard_map/ppermute | solution.py:17
  13.2 55.0 %collective-permute-start.12 = (bf16[16,128,256]{2,1,0:T(8,128)(2,1)}, bf16[16,128,256]{2,1,0:T(8,128)(2,1)}, u32[]{:S(2)}, u32[]{:S(2)}) collective-permute-start(bf16[16,128,256]{2,1,0:T(8,128)(2,1)} %get-tuple-element.29), channel_id=1, source_target_pairs={{0,16},{4,20},{8,24},{12,28},{16,0},{20,4},{24,8},{28,12},{32,48},... | collective-permute-start | bytes 3145736 | tf_op jit(solution)/shard_map/ppermute | solution.py:17
  14.3 23.8 %collective-permute-start.1 = (bf16[8,128,256]{2,1,0:T(8,128)(2,1)S(1)}, bf16[8,128,256]{2,1,0:T(8,128)(2,1)S(1)}, u32[]{:S(2)}, u32[]{:S(2)}) collective-permute-start(bf16[8,128,256]{2,1,0:T(8,128)(2,1)S(1)} %bitcast.26), channel_id=1, source_target_pairs={{0,1},{1,2},{2,3},{3,0},{4,5},{5,6},{6,7},{7,4},{8,9},{9,10},{10,1... | collective-permute-start | bytes 1572872 | tf_op jit(solution)/shard_map/ppermute | solution.py:22
  15.7 25.5 %collective-permute-start = (bf16[8,128,256]{2,1,0:T(8,128)(2,1)S(1)}, bf16[8,128,256]{2,1,0:T(8,128)(2,1)S(1)}, u32[]{:S(2)}, u32[]{:S(2)}) collective-permute-start(bf16[8,128,256]{2,1,0:T(8,128)(2,1)S(1)} %bitcast.27), channel_id=1, source_target_pairs={{0,3},{1,0},{2,1},{3,2},{4,7},{5,4},{6,5},{7,6},{8,11},{9,8},{10,9... | collective-permute-start | bytes 1572872 | tf_op jit(solution)/shard_map/ppermute | solution.py:22
  16.3 18.7 %copy-start.8 = (bf16[4,128,256]{2,1,0:T(8,128)(2,1)}, bf16[4,128,256]{2,1,0:T(8,128)(2,1)S(1)}, u32[]{:S(2)}) copy-start(bf16[4,128,256]{2,1,0:T(8,128)(2,1)S(1)} %collective-permute-done.13.from_left.a_left) | copy-start | bytes 786436
  16.3 18.7 %collective-permute-start.14 = (bf16[4,128,256]{2,1,0:T(8,128)(2,1)}, bf16[4,128,256]{2,1,0:T(8,128)(2,1)S(1)}, u32[]{:S(2)}, u32[]{:S(2)}) collective-permute-start(bf16[4,128,256]{2,1,0:T(8,128)(2,1)} %get-tuple-element.32), channel_id=1, source_target_pairs={{0,3},{1,0},{2,1},{3,2},{4,7},{5,4},{6,5},{7,6},{8,11},{9,8},{10,9... | collective-permute-start | bytes 786440 | tf_op jit(solution)/shard_map/ppermute | solution.py:22
  35.0 0.7 copy-start.9
  37.7 6.6 %collective-permute-start.15 = (bf16[2,128,256]{2,1,0:T(8,128)(2,1)}, bf16[2,128,256]{2,1,0:T(8,128)(2,1)S(1)}, u32[]{:S(2)}, u32[]{:S(2)}) collective-permute-start(bf16[2,128,256]{2,1,0:T(8,128)(2,1)} %get-tuple-element.35), channel_id=1, source_target_pairs={{0,1},{1,2},{2,3},{3,0},{4,5},{5,6},{6,7},{7,4},{8,9},{9,10},{10,1... | collective-permute-start | bytes 393224 | tf_op jit(solution)/shard_map/ppermute | solution.py:22
  38.1 17.4 %copy-start = (bf16[8,128,256]{2,1,0:T(8,128)(2,1)}, bf16[8,128,256]{2,1,0:T(8,128)(2,1)S(1)}, u32[]{:S(2)}) copy-start(bf16[8,128,256]{2,1,0:T(8,128)(2,1)S(1)} %collective-permute-done.1.p4) | copy-start | bytes 1572868
  38.1 17.3 %collective-permute-start.2 = (bf16[4,128,256]{2,1,0:T(8,128)(2,1)S(1)}, bf16[4,128,256]{2,1,0:T(8,128)(2,1)S(1)}, u32[]{:S(2)}, u32[]{:S(2)}) collective-permute-start(bf16[4,128,256]{2,1,0:T(8,128)(2,1)S(1)} %slice.16), channel_id=1, source_target_pairs={{0,1},{1,2},{2,3},{3,0},{4,5},{5,6},{6,7},{7,4},{8,9},{9,10},{10,1... | collective-permute-start | bytes 786440 | tf_op jit(solution)/shard_map/ppermute | solution.py:22
  41.2 14.3 %copy-start.1 = (bf16[8,128,256]{2,1,0:T(8,128)(2,1)}, bf16[8,128,256]{2,1,0:T(8,128)(2,1)S(1)}, u32[]{:S(2)}) copy-start(bf16[8,128,256]{2,1,0:T(8,128)(2,1)S(1)} %collective-permute-done.p1) | copy-start | bytes 1572868
  41.2 14.3 %collective-permute-start.3 = (bf16[4,128,256]{2,1,0:T(8,128)(2,1)S(1)}, bf16[4,128,256]{2,1,0:T(8,128)(2,1)S(1)}, u32[]{:S(2)}, u32[]{:S(2)}) collective-permute-start(bf16[4,128,256]{2,1,0:T(8,128)(2,1)S(1)} %slice.17), channel_id=1, source_target_pairs={{0,3},{1,0},{2,1},{3,2},{4,7},{5,4},{6,5},{7,6},{8,11},{9,8},{10,9... | collective-permute-start | bytes 786440 | tf_op jit(solution)/shard_map/ppermute | solution.py:22
  44.2 6.8 %copy-start.18 = (bf16[2,128,256]{2,1,0:T(8,128)(2,1)}, bf16[2,128,256]{2,1,0:T(8,128)(2,1)S(1)}, u32[]{:S(2)}) copy-start(bf16[2,128,256]{2,1,0:T(8,128)(2,1)S(1)} %collective-permute-done.15.b_left) | copy-start | bytes 393220
  44.3 6.8 %collective-permute-start.16 = (bf16[2,128,256]{2,1,0:T(8,128)(2,1)}, bf16[2,128,256]{2,1,0:T(8,128)(2,1)S(1)}, u32[]{:S(2)}, u32[]{:S(2)}) collective-permute-start(bf16[2,128,256]{2,1,0:T(8,128)(2,1)} %get-tuple-element.36), channel_id=1, source_target_pairs={{0,3},{1,0},{2,1},{3,2},{4,7},{5,4},{6,5},{7,6},{8,11},{9,8},{10,9... | collective-permute-start | bytes 393224 | tf_op jit(solution)/shard_map/ppermute | solution.py:22
  51.0 0.6 copy-start.19
  53.7 14.4 %collective-permute-start.17 = (bf16[4,128,256]{2,1,0:T(8,128)(2,1)}, bf16[4,128,256]{2,1,0:T(8,128)(2,1)S(1)}, u32[]{:S(2)}, u32[]{:S(2)}) collective-permute-start(bf16[4,128,256]{2,1,0:T(8,128)(2,1)} %shard_map.129), channel_id=1, source_target_pairs={{0,64},{4,68},{8,72},{12,76},{16,80},{20,84},{24,88},{28,92},{32,9... | collective-permute-start | bytes 786440 | tf_op jit(solution)/shard_map/ppermute | solution.py:17
  55.5 0.7 copy-start.6
  55.5 0.8 copy-start.7
  60.1 55.2 %collective-permute-start.10 = (bf16[16,128,256]{2,1,0:T(8,128)(2,1)}, bf16[16,128,256]{2,1,0:T(8,128)(2,1)}, u32[]{:S(2)}, u32[]{:S(2)}) collective-permute-start(bf16[16,128,256]{2,1,0:T(8,128)(2,1)} %get-tuple-element.25), channel_id=1, source_target_pairs={{0,4},{4,0},{8,12},{12,8},{16,20},{20,16},{24,28},{28,24},{32,36},... | collective-permute-start | bytes 3145736 | tf_op jit(solution)/shard_map/ppermute | solution.py:17
  60.2 60.8 %collective-permute-start.9 = (bf16[16,128,256]{2,1,0:T(8,128)(2,1)}, bf16[16,128,256]{2,1,0:T(8,128)(2,1)}, u32[]{:S(2)}, u32[]{:S(2)}) collective-permute-start(bf16[16,128,256]{2,1,0:T(8,128)(2,1)} %get-tuple-element.24), channel_id=1, source_target_pairs={{0,16},{4,20},{8,24},{12,28},{16,0},{20,4},{24,8},{28,12},{32,48},... | collective-permute-start | bytes 3145736 | tf_op jit(solution)/shard_map/ppermute | solution.py:17
  68.2 9.1 %copy-start.21 = (bf16[4,128,256]{2,1,0:T(8,128)(2,1)S(1)}, bf16[4,128,256]{2,1,0:T(8,128)(2,1)}, u32[]{:S(2)}) copy-start(bf16[4,128,256]{2,1,0:T(8,128)(2,1)} %get-tuple-element.23) | copy-start | bytes 786436
  68.2 0.7 copy-start.13
  68.2 1.0 copy-start.5
  75.2 18.4 %collective-permute-start.18 = (bf16[8,128,256]{2,1,0:T(8,128)(2,1)}, bf16[8,128,256]{2,1,0:T(8,128)(2,1)S(1)}, u32[]{:S(2)}, u32[]{:S(2)}) collective-permute-start(bf16[8,128,256]{2,1,0:T(8,128)(2,1)} %get-tuple-element.38), channel_id=1, source_target_pairs={{0,1},{1,2},{2,3},{3,0},{4,5},{5,6},{6,7},{7,4},{8,9},{9,10},{10,1... | collective-permute-start | bytes 1572872 | tf_op jit(solution)/shard_map/ppermute | solution.py:22
  76.3 19.2 %collective-permute-start.19 = (bf16[8,128,256]{2,1,0:T(8,128)(2,1)}, bf16[8,128,256]{2,1,0:T(8,128)(2,1)S(1)}, u32[]{:S(2)}, u32[]{:S(2)}) collective-permute-start(bf16[8,128,256]{2,1,0:T(8,128)(2,1)} %get-tuple-element.39), channel_id=1, source_target_pairs={{0,3},{1,0},{2,1},{3,2},{4,7},{5,4},{6,5},{7,6},{8,11},{9,8},{10,9... | collective-permute-start | bytes 1572872 | tf_op jit(solution)/shard_map/ppermute | solution.py:22
  77.3 15.5 %collective-permute-start.4 = (bf16[4,128,256]{2,1,0:T(8,128)(2,1)S(1)}, bf16[4,128,256]{2,1,0:T(8,128)(2,1)S(1)}, u32[]{:S(2)}, u32[]{:S(2)}) collective-permute-start(bf16[4,128,256]{2,1,0:T(8,128)(2,1)S(1)} %copy-done.21), channel_id=1, source_target_pairs={{0,64},{4,68},{8,72},{12,76},{16,80},{20,84},{24,88},{28,92},{32,9... | collective-permute-start | bytes 786440 | tf_op jit(solution)/shard_map/ppermute | solution.py:17
  92.8 28.3 %copy-start.12 = (bf16[4,128,256]{2,1,0:T(8,128)(2,1)}, bf16[4,128,256]{2,1,0:T(8,128)(2,1)S(1)}, u32[]{:S(2)}) copy-start(bf16[4,128,256]{2,1,0:T(8,128)(2,1)S(1)} %collective-permute-done.4.p0) | copy-start | bytes 786436
  92.8 8.8 %collective-permute-start.6 = (bf16[4,128,256]{2,1,0:T(8,128)(2,1)S(1)}, bf16[4,128,256]{2,1,0:T(8,128)(2,1)S(1)}, u32[]{:S(2)}, u32[]{:S(2)}) collective-permute-start(bf16[4,128,256]{2,1,0:T(8,128)(2,1)S(1)} %collective-permute-done.4.p0), channel_id=1, source_target_pairs={{0,1},{1,2},{2,3},{3,0},{4,5},{5,6},{6,7},{7,4},{8,9},{9,10},{10,1... | collective-permute-start | bytes 786440 | tf_op jit(solution)/shard_map/ppermute | solution.py:22
  93.6 1.9 %copy-start.2 = (bf16[8,128,256]{2,1,0:T(8,128)(2,1)}, bf16[8,128,256]{2,1,0:T(8,128)(2,1)S(1)}, u32[]{:S(2)}) copy-start(bf16[8,128,256]{2,1,0:T(8,128)(2,1)S(1)} %collective-permute-done.18.from_left.a_left) | copy-start | bytes 1572868
  93.6 11.0 %collective-permute-start.5 = (bf16[4,128,256]{2,1,0:T(8,128)(2,1)S(1)}, bf16[4,128,256]{2,1,0:T(8,128)(2,1)S(1)}, u32[]{:S(2)}, u32[]{:S(2)}) collective-permute-start(bf16[4,128,256]{2,1,0:T(8,128)(2,1)S(1)} %collective-permute-done.4.p0), channel_id=1, source_target_pairs={{0,3},{1,0},{2,1},{3,2},{4,7},{5,4},{6,5},{7,6},{8,11},{9,8},{10,9... | collective-permute-start | bytes 786440 | tf_op jit(solution)/shard_map/ppermute | solution.py:22
  95.5 0.8 copy-start.3
  98.6 10.4 %collective-permute-start.20 = (bf16[4,128,256]{2,1,0:T(8,128)(2,1)}, bf16[4,128,256]{2,1,0:T(8,128)(2,1)S(1)}, u32[]{:S(2)}, u32[]{:S(2)}) collective-permute-start(bf16[4,128,256]{2,1,0:T(8,128)(2,1)} %get-tuple-element.42), channel_id=1, source_target_pairs={{0,1},{1,2},{2,3},{3,0},{4,5},{5,6},{6,7},{7,4},{8,9},{9,10},{10,1... | collective-permute-start | bytes 786440 | tf_op jit(solution)/shard_map/ppermute | solution.py:22
  101.6 19.4 %copy-start.10 = (bf16[4,128,256]{2,1,0:T(8,128)(2,1)}, bf16[4,128,256]{2,1,0:T(8,128)(2,1)S(1)}, u32[]{:S(2)}) copy-start(bf16[4,128,256]{2,1,0:T(8,128)(2,1)S(1)} %collective-permute-done.6.p4) | copy-start | bytes 786436
  101.6 10.4 %collective-permute-start.21 = (bf16[4,128,256]{2,1,0:T(8,128)(2,1)}, bf16[4,128,256]{2,1,0:T(8,128)(2,1)S(1)}, u32[]{:S(2)}, u32[]{:S(2)}) collective-permute-start(bf16[4,128,256]{2,1,0:T(8,128)(2,1)} %get-tuple-element.43), channel_id=1, source_target_pairs={{0,3},{1,0},{2,1},{3,2},{4,7},{5,4},{6,5},{7,6},{8,11},{9,8},{10,9... | collective-permute-start | bytes 786440 | tf_op jit(solution)/shard_map/ppermute | solution.py:22
  104.6 16.4 %copy-start.11 = (bf16[4,128,256]{2,1,0:T(8,128)(2,1)}, bf16[4,128,256]{2,1,0:T(8,128)(2,1)S(1)}, u32[]{:S(2)}) copy-start(bf16[4,128,256]{2,1,0:T(8,128)(2,1)S(1)} %collective-permute-done.5.p1) | copy-start | bytes 786436
  104.6 16.4 %collective-permute-start.7 = (bf16[2,128,256]{2,1,0:T(8,128)(2,1)S(1)}, bf16[2,128,256]{2,1,0:T(8,128)(2,1)S(1)}, u32[]{:S(2)}, u32[]{:S(2)}) collective-permute-start(bf16[2,128,256]{2,1,0:T(8,128)(2,1)S(1)} %slice.18), channel_id=1, source_target_pairs={{0,1},{1,2},{2,3},{3,0},{4,5},{5,6},{6,7},{7,4},{8,9},{9,10},{10,1... | collective-permute-start | bytes 393224 | tf_op jit(solution)/shard_map/ppermute | solution.py:22
  109.1 3.0 %copy-start.14 = (bf16[4,128,256]{2,1,0:T(8,128)(2,1)}, bf16[4,128,256]{2,1,0:T(8,128)(2,1)S(1)}, u32[]{:S(2)}) copy-start(bf16[4,128,256]{2,1,0:T(8,128)(2,1)S(1)} %collective-permute-done.20.b_left) | copy-start | bytes 786436
  109.1 12.0 %collective-permute-start.8 = (bf16[2,128,256]{2,1,0:T(8,128)(2,1)S(1)}, bf16[2,128,256]{2,1,0:T(8,128)(2,1)S(1)}, u32[]{:S(2)}, u32[]{:S(2)}) collective-permute-start(bf16[2,128,256]{2,1,0:T(8,128)(2,1)S(1)} %slice.19), channel_id=1, source_target_pairs={{0,3},{1,0},{2,1},{3,2},{4,7},{5,4},{6,5},{7,6},{8,11},{9,8},{10,9... | collective-permute-start | bytes 393224 | tf_op jit(solution)/shard_map/ppermute | solution.py:22
  112.0 0.7 copy-start.15
  121.0 0.7 copy-start.16
  121.0 0.7 copy-start.17

commit v2 on v1

--- a/solution.py
+++ b/solution.py
@@ -1,3 +1,5 @@
+import functools
+
 import jax
 import jax.numpy as jnp
 from jax import lax
@@ -5,12 +7,14 @@
 from jax.experimental.pallas import tpu as pltpu
 from jax.sharding import PartitionSpec as P
 
+
 UNROLL = 4
 F32 = jnp.float32
 BF16 = jnp.bfloat16
 SMEM = pl.BlockSpec(memory_space=pltpu.SMEM)
 VMEM = pl.BlockSpec(memory_space=pltpu.VMEM)
 ANY = pl.BlockSpec(memory_space=pl.ANY)
+HBM = pl.BlockSpec(memory_space=pltpu.HBM)
 
 
 def swapped(array, bit):
@@ -97,6 +101,7 @@
         def step(t, live):
             row = jnp.where(live, row_of(t), own)
             dacc[row] += vals[base + t].astype(F32)
+
         return step
 
     for_live(counts[0], add_rows(lv, 0, lambda t: lrows[t]))
@@ -134,27 +139,24 @@
     own_ref[...] = acc[:n]
 
 
-def parcels_kernel(counts, rrows, rslots, rv_ref, gh_ref, out_a, out_b, acc):
-    cap = rrows.shape[1]
-    for r, out in ((1, out_b), (0, out_a)):
-        acc[...] = jnp.zeros_like(acc)
-        backward_tiles(
-            counts[r + 1], r * cap, rv_ref, lambda t: rrows[r, t], lambda t: rslots[r, t], gh_ref, acc
-        )
-        out[...] = acc[:out.shape[0]].astype(BF16)
-
-
-def local_back_kernel(counts, lrows, lcols, me, lv_ref, gh_ref, out_ref, acc):
-    total = out_ref.shape[0]
+def parcel_kernel(counts, rows, slots, vals, gh_ref, out, acc, *, r):
+    acc[...] = jnp.zeros_like(acc)
+    backward_tiles(
+        counts[r + 1], 0, vals, lambda t: rows[r, t], lambda t: slots[r, t], gh_ref, acc
+    )
+    out[...] = acc[:out.shape[0]].astype(BF16)
+
+
+def local_back_kernel(counts, lrows, lcols, me, lv_ref, gh_ref, out_ref):
     own = gh_ref.shape[0]
-    acc[...] = jnp.zeros_like(acc)
+    total = out_ref.shape[0] - 1
+    out_ref[:own] = gh_ref[...].astype(F32)
+    out_ref[own:] = jnp.zeros((total + 1 - own,) + out_ref.shape[1:], F32)
     shift = me[0] * own
     backward_tiles(
         counts[0], 0, lv_ref, lambda t: lrows[t],
-        lambda t: lax.rem(lcols[t] - shift + total, total), gh_ref, acc,
-    )
-    acc[:own] += gh_ref[...].astype(F32)
-    out_ref[...] = acc[:total]
+        lambda t: lax.rem(lcols[t] - shift + total, total), gh_ref, out_ref,
+    )
 
 
 def combine_kernel(keep_r, keep_l, from_left, from_right, out_r, out_l):
@@ -169,38 +171,84 @@
     out[h:] = (own[h:] + a_left[h:].astype(F32) + b_right[...].astype(F32)).astype(BF16)
 
 
-def merge_kernel(sends, me, part_hbm, got_a, got_b, got_c,
-                 right_ref, left_ref, keep_r_ref, keep_l_ref, own_ref, acc, sems):
-    copies = start_all([(part_hbm, acc)], sems)
-    total = acc.shape[0]
-    own = own_ref.shape[0]
-    shift = me[0] * own
-    wait_all(copies)
-
-    def add(got, r, base):
-        for s in range(got.shape[0]):
-            block = lax.rem(sends[r, base + s] - shift + total, total)
-            acc[block] += got[s].astype(F32)
-
-    add(got_a, 0, 0)
-    add(got_b, 1, 0)
-    add(got_c, 2, me[0] * got_c.shape[0])
-    split_out(acc, own, right_ref, left_ref, keep_r_ref, keep_l_ref, own_ref)
-
-
-def pick_kernel(sends, me, p0, p1, p2, p3, p4, out_a, out_b, out_c, src, sems):
+def add_arrived(sends, me, gots, own, total, first, count, acc):
+    for r, got in enumerate(gots):
+        n = got.shape[0]
+        base = me[0] * n if r == len(gots) - 1 else 0
+        for s in range(n):
+            at = lax.rem(sends[r, base + s] - me[0] * own - first + 2 * total, total)
+
+            @pl.when(at < count)
+            def _(got=got, s=s, at=at):
+                acc[at] += got[s].astype(F32)
+
+
+def merge_kernel(sends, me, part_hbm, got_a, got_b, got_c, right_ref, left_ref, acc, sems):
+    n = right_ref.shape[0]
+    h = n // 2
+    count = 2 * n
+    total = 4 * n
+    first = n + h
+    wait_all(start_all([(part_hbm.at[pl.ds(first, count)], acc)], sems))
+    add_arrived(sends, me, (got_a, got_b, got_c), n, total, first, count, acc)
+    right_ref[:h] = acc[h:n].astype(BF16)
+    right_ref[h:] = acc[:h].astype(BF16)
+    left_ref[:h] = acc[n:n + h].astype(BF16)
+    left_ref[h:] = acc[n + h:].astype(BF16)
+
+
+def rest_kernel(sends, me, part_hbm, got_a, got_b, got_c, keep_r_ref, keep_l_ref, own_ref, acc, sems):
+    n = own_ref.shape[0]
+    h = n // 2
+    total = 4 * n
+    first = total - h
+    pairs = [
+        (part_hbm.at[pl.ds(first, h)], acc.at[pl.ds(0, h)]),
+        (part_hbm.at[pl.ds(0, n + h)], acc.at[pl.ds(h, n + h)]),
+    ]
+    wait_all(start_all(pairs, sems))
+    add_arrived(sends, me, (got_a, got_b, got_c), n, total, first, 2 * n, acc)
+    keep_l_ref[...] = acc[:h]
+    own_ref[...] = acc[h:h + n]
+    keep_r_ref[...] = acc[h + n:]
+
+
+def pick_some(sends, r, base, me, pieces, out, sems):
+    own = pieces[0].shape[0]
+    total = 4 * own
+    count = out.shape[0]
+
+    def begin(s, carry):
+        at = lax.rem(sends[r, base + s] - me[0] * own + total, total)
+        low = 0
+        for piece in pieces:
+            size = piece.shape[0]
+
+            @pl.when((at >= low) & (at < low + size))
+            def _(piece=piece, low=low):
+                pltpu.make_async_copy(piece.at[at - low], out.at[s], sems.at[s]).start()
+
+            low += size
+        return carry
+
+    def end(s, carry):
+        pltpu.make_async_copy(pieces[0].at[0], out.at[s], sems.at[s]).wait()
+        return carry
+
+    lax.fori_loop(0, count, begin, 0)
+    return lambda: lax.fori_loop(0, count, end, 0)
+
+
+def pick_share_kernel(sends, me, p0, p1, p2, p3, p4, out_c, sems):
+    pick_some(sends, 2, me[0] * out_c.shape[0], me, (p0, p1, p2, p3, p4), out_c, sems)()
+
+
+def pick_kernel(sends, me, p0, p1, p2, p3, p4, out_a, out_b, sems_a, sems_b):
     pieces = (p0, p1, p2, p3, p4)
-    wait_all(start_all(pieces_into(pieces, src, 0), sems))
-    total = src.shape[0]
-    shift = me[0] * p0.shape[0]
-
-    def put(out, r, base):
-        for s in range(out.shape[0]):
-            out[s] = src[lax.rem(sends[r, base + s] - shift + total, total)]
-
-    put(out_c, 2, me[0] * out_c.shape[0])
-    put(out_b, 1, 0)
-    put(out_a, 0, 0)
+    end_b = pick_some(sends, 1, 0, me, pieces, out_b, sems_b)
+    end_a = pick_some(sends, 0, 0, me, pieces, out_a, sems_a)
+    end_b()
+    end_a()
 
 
 def near_forward_kernel(counts, lrows, lcols, rrows, rslots, me, p0, p1, p2, p3, p4, got_hbm, lv_hbm, rv_hbm,
@@ -308,6 +356,20 @@
     def split_shapes(n):
         return [blocks(n, BF16), blocks(n, BF16), blocks(n // 2, F32), blocks(n // 2, F32), blocks(n, F32)]
 
+    def first_round(right, left):
+        return shifted(right, 1), shifted(left, -1)
+
+    def second_round(a_left, a_right, keep_r, keep_l):
+        h = keep_r.shape[0]
+        out_r, out_l = call(
+            combine_kernel, (), [VMEM] * 4, (keep_r, keep_l, a_left, a_right),
+            [blocks(h, BF16), blocks(h, BF16)], [], 0,
+        )
+        return shifted(out_r, 1), shifted(out_l, -1)
+
+    def finished(own_part, parts):
+        return call(finish_kernel, (), [VMEM] * 5, (own_part,) + parts, [blocks(own_part.shape[0], BF16)], [], 0)[0]
+
     part_feats = spread_out(feats)
 
     deg, gh, z_right, z_left, z_keep_r, z_keep_l, z_own = call(
@@ -316,57 +378,64 @@
         [tiles(lcap), tiles(rounds * cap), room(own, BF16), tiles(own + 1, F32), room(cap + 1, F32), sems(3)],
         cap * tile_flops,
     )
-
-    def scattered(right, left, keep_r, keep_l):
-        a_left = shifted(right, 1)
-        a_right = shifted(left, -1)
-        h = keep_r.shape[0]
-        out_r, out_l = call(
-            combine_kernel, (), [VMEM] * 4, (keep_r, keep_l, a_left, a_right),
-            [blocks(h, BF16), blocks(h, BF16)], [], 0,
-        )
-        return a_left, a_right, shifted(out_r, 1), shifted(out_l, -1)
-
-    def finished(own_part, parts):
-        return call(finish_kernel, (), [VMEM] * 5, (own_part,) + parts, [blocks(own_part.shape[0], BF16)], [], 0)[0]
-
-    z_parts = scattered(z_right, z_left, z_keep_r, z_keep_l)
-    back_a, back_b = call(
-        parcels_kernel, (counts, rrows, rslots), [VMEM, VMEM], (rv, gh),
-        [blocks(cap, BF16), blocks(cap, BF16)], [room(cap + 1, F32)], 2 * cap * tile_flops,
-    )
-    got_back_b = swapped(back_b, bits[1])
-    got_back_a = swapped(back_a, bits[0])
+    z_first = first_round(z_right, z_left)
+
+    def parcel(r):
+        return pl.pallas_call(
+            functools.partial(parcel_kernel, r=r),
+            out_shape=blocks(cap, BF16),
+            grid=(1,),
+            in_specs=[SMEM] * 3 + [
+                pl.BlockSpec((cap, rows, rows), lambda i: (r, 0, 0)),
+                pl.BlockSpec((own,) + tail, lambda i: (0, 0, 0)),
+            ],
+            out_specs=pl.BlockSpec((cap,) + tail, lambda i: (0, 0, 0)),
+            scratch_shapes=[room(cap + 1, F32)],
+            cost_estimate=pl.CostEstimate(
+                flops=cap * tile_flops, bytes_accessed=2 * cap * rows * (rows + width), transcendentals=0
+            ),
+        )(counts, rrows, rslots, rv, gh)
+
+    got_back_b = swapped(parcel(1), bits[1])
+    got_back_a = swapped(parcel(0), bits[0])
+    z_parts = z_first + second_round(*z_first, z_keep_r, z_keep_l)
     got_back_c = swapped(finished(z_own, z_parts), bits[2])
 
     part_back = call(
         local_back_kernel, (counts, lrows, lcols, me), [VMEM, VMEM], (lv, gh),
-        [blocks(part, F32)], [room(part + 1, F32)], lcap * tile_flops,
+        [blocks(part + 1, F32)], [], lcap * tile_flops,
     )[0]
 
-    need_a, need_b, need_c = call(
-        pick_kernel, (sends, me), [ANY] * 5, part_feats,
-        [blocks(cap, BF16), blocks(cap, BF16), blocks(share, BF16)], [room(part, BF16), sems(5)], 0,
-    )
+    need_c = call(pick_share_kernel, (sends, me), [HBM] * 5, part_feats, [blocks(share, BF16)], [sems(share)], 0)[0]
     got_c = swapped(need_c, bits[2])
+    need_a, need_b = call(
+        pick_kernel, (sends, me), [HBM] * 5, part_feats,
+        [blocks(cap, BF16), blocks(cap, BF16)], [sems(cap), sems(cap)], 0,
+    )
     got_b = swapped(need_b, bits[1])
     got_a = swapped(need_a, bits[0])
     far_feats = spread_out(got_c)
 
     near = call(
-        near_forward_kernel, (counts, lrows, lcols, rrows, rslots, me), [ANY] * 8,
+        near_forward_kernel, (counts, lrows, lcols, rrows, rslots, me), [HBM] * 6 + [ANY] * 2,
         part_feats + (got_a, lv, rv), [blocks(own, F32)],
         [room(part + cap, BF16), tiles(lcap + cap), room(own + 1, F32), sems(8)], (lcap + cap) * tile_flops,
     )[0]
 
-    right, left, keep_r, keep_l, own_part = call(
-        merge_kernel, (sends, me), [ANY, VMEM, VMEM, VMEM], (part_back, got_back_a, got_back_b, got_back_c),
-        split_shapes(own), [room(part, F32), sems(1)], 0,
-    )
-    grad_features = finished(own_part, scattered(right, left, keep_r, keep_l))
+    arrived = (part_back, got_back_a, got_back_b, got_back_c)
+    right, left = call(
+        merge_kernel, (sends, me), [ANY, VMEM, VMEM, VMEM], arrived,
+        [blocks(own, BF16), blocks(own, BF16)], [room(2 * own, F32), sems(1)], 0,
+    )
+    first = first_round(right, left)
+    keep_r, keep_l, own_part = call(
+        rest_kernel, (sends, me), [ANY, VMEM, VMEM, VMEM], arrived,
+        [blocks(own // 2, F32), blocks(own // 2, F32), blocks(own, F32)], [room(2 * own, F32), sems(2)], 0,
+    )
+    grad_features = finished(own_part, first + second_round(*first, keep_r, keep_l))
 
     output = call(
-        far_forward_kernel, (counts, rrows, rslots, me), [ANY] * 9 + [VMEM],
+        far_forward_kernel, (counts, rrows, rslots, me), [HBM] * 6 + [ANY] * 3 + [VMEM],
         far_feats + (got_b, rv, near, deg, weight), [blocks(own, BF16)],
         [room(2 * cap, BF16), tiles(2 * cap), room(own + 1, F32), tiles(own, F32), sems(9)],
         2 * cap * tile_flops,

time: 130 us -> 138 us (1.062); the launches traced: 127 us -> 137 us
  Pallas kernels: 45.2 us -> 56.6 us
  waiting for transfers between devices: 44.9 us -> 43.1 us
    pallas_call x0 -> x2, Pallas kernels: none -> 6.98 us  [parcel(): pl.pallas_call(functools.partial(parcel_kernel, r=r), out_shape=blocks(ca...]
    pallas_call x11 -> x12, Pallas kernels: 45.2 us -> 49.7 us  [call(): pl.pallas_call(kernel, out_shape=tuple(outs), in_specs=[SMEM] * len(scala...]
    ppermute x6, starting transfers between devices: 7.4 us -> 4.6 us  [swapped(): lax.ppermute(array, 'node', [(i, i ^ 1 << bit) for i in range(lax.axis_si...]
    ppermute x16, starting transfers between devices: 21.6 us -> 24.3 us  [shifted(): lax.ppermute(array, 'feat', [(i, (i + step) % size) for i in range(size)])]
    ppermute x16, waiting for transfers between devices: 31.2 us -> 29.1 us  [shifted(): lax.ppermute(array, 'feat', [(i, (i + step) % size) for i in range(size)])]
  transfers between devices with their start and end apart: 22 -> 22, of which waited for: 6 -> 5; matrix products, arithmetic and copies ran while one was open for 1% -> 0% of each run, Pallas kernels for 26% -> 33%
where the time goes in v2:
time: 138 us; the launch traced here: 137 us
  Pallas kernels  56.6 us (41%)
  waiting for transfers between devices  43.1 us (31%)
  starting transfers between devices  28.9 us (21%)
  local copies, waits for them, and re-layouts  7.24 us (5%)
    pallas_call x12, Pallas kernels, call(): pl.pallas_call(kernel, out_shape=tuple(outs), in_specs=[SMEM] * len(scala...  49.7 us
    ppermute x16, waiting for transfers between devices, shifted(): lax.ppermute(array, 'feat', [(i, (i + step) % size) for i in range(size)])  29.1 us
    ppermute x16, starting transfers between devices, shifted(): lax.ppermute(array, 'feat', [(i, (i + step) % size) for i in range(size)])  24.3 us
    ppermute x6, waiting for transfers between devices, swapped(): lax.ppermute(array, 'node', [(i, i ^ 1 << bit) for i in range(lax.axis_si...  14.1 us
    unnamed x46, local copies, waits for them, and re-layouts  7.18 us
    pallas_call x2, Pallas kernels, parcel(): pl.pallas_call(functools.partial(parcel_kernel, r=r), out_shape=blocks(ca...  6.98 us
    ppermute x6, starting transfers between devices, swapped(): lax.ppermute(array, 'node', [(i, i ^ 1 << bit) for i in range(lax.axis_si...  4.6 us
  transfers between devices with their start and end apart: 22, of which 5 were waited for; matrix products, arithmetic and copies ran while one was open for 0% of the time, Pallas kernels for 33%

profile of v2, /device:TPU:146, one launch (start us, length us, event | category | flops | bytes accessed | tf_op | source)
XLA Modules:
  0.0 137.0 jit_solution(9443470138572567524)
XLA Ops:
  0.6 1.3 copy_bitcast_fusion.1
  1.9 5.6 %shard_map.125 = (f32[8,128,128]{2,1,0:T(8,128)}, bf16[8,128,256]{2,1,0:T(8,128)(2,1)}, bf16[4,128,256]{2,1,0:T(8,128)(2,1)}, bf16[4,128,256]{2,1,0:T(8,128)(2,1...) custom-call(s32[4]{0:T(128)} %bitcast.37, s32[32]{0:T(128)} %bitcast.43, ...), custom_call_target="tpu_custom_call" | custom-call | flops 134217728 | bytes 5898240 | tf_op jit(solution)/shard_map/pallas_call | solution.py:342
  7.5 2.0 %collective-permute-start.13 = (bf16[4,128,256]{2,1,0:T(8,128)(2,1)}, bf16[4,128,256]{2,1,0:T(8,128)(2,1)S(1)}, u32[]{:S(2)}, u32[]{:S(2)}) collective-permute-start(bf16[4,128,256]{2,1,0:T(8,128)(2,1)} %get-tuple-element.25), channel_id=1, source_target_pairs={{0,1},{1,2},{2,3},{3,0},{4,5},{5,6},{6,7},{7,4},{8,9},{9,10},{10,1... | collective-permute-start | bytes 786440 | tf_op jit(solution)/shard_map/ppermute | solution.py:26
  9.5 3.5 %shard_map.128 = bf16[16,128,256]{2,1,0:T(8,128)(2,1)} custom-call(s32[4]{0:T(128)} %bitcast.38, s32[3,16]{1,0:T(4,128)} %get-tuple-element.39.rrows.rows, s32[3,16]{1,0:T(4,128)} %get-tuple-element.38.rslots.slots, bf16[48,128,128]{2,1,0:T(8,128)(2,1)} %bitcast.18, bf16[8,128,256]{2,1,0:T(8,128)(2,1)} %get-tuple-element.23.gh_ref), custom_call_target="tpu_custom_call" | custom-call | flops 134217728 | bytes 1572864 | tf_op jit(solution)/shard_map/pallas_call | solution.py:384
  13.0 3.5 %shard_map.129 = bf16[16,128,256]{2,1,0:T(8,128)(2,1)} custom-call(s32[4]{0:T(128)} %bitcast.39, s32[3,16]{1,0:T(4,128)} %get-tuple-element.39.rrows.rows, s32[3,16]{1,0:T(4,128)} %get-tuple-element.38.rslots.slots, bf16[48,128,128]{2,1,0:T(8,128)(2,1)} %bitcast.19, bf16[8,128,256]{2,1,0:T(8,128)(2,1)} %get-tuple-element.23.gh_ref), custom_call_target="tpu_custom_call" | custom-call | flops 134217728 | bytes 1572864 | tf_op jit(solution)/shard_map/pallas_call | solution.py:384
  16.5 0.9 collective-permute-start.1
  17.4 1.2 collective-permute-start
  18.6 0.6 collective-permute-start.14
  19.2 16.8 %collective-permute-done.14.from_right.a_right = bf16[4,128,256]{2,1,0:T(8,128)(2,1)S(1)} collective-permute-done((bf16[4,128,256]{2,1,0:T(8,128)(2,1)S(1)}, bf16[4,128,256]{2,1,0:T(8,128)(2,1)S(1)}, u32[]{:S(2)}, u32[]{:S(2)}) %collective-permute-start.14) | collective-permute-done | bytes 262176 | tf_op jit(solution)/shard_map/ppermute | solution.py:26
  36.0 0.7 copy-done.10
  36.7 1.9 %shard_map.130 = (bf16[2,128,256]{2,1,0:T(8,128)(2,1)}, bf16[2,128,256]{2,1,0:T(8,128)(2,1)}) custom-call(f32[2,128,256]{2,1,0:T(8,128)} %get-tuple-element.27.keep_r, f32[2,128,256]{2,1,0:T(8,128)} %get-tuple-element.28.keep_l, bf16[4,128,256]{2,1,0:T(8,128)(2,1)} %copy-done.9, bf16[4,128,256]{2,1,0:T(8,128)(2,1)} %copy-done.10), custom_call_target="tpu_custom_call" | custom-call | bytes 1310720 | tf_op jit(solution)/shard_map/pallas_call | solution.py:342
  38.6 1.1 collective-permute-start.15
  39.7 2.4 %collective-permute-start.2 = (bf16[4,128,256]{2,1,0:T(8,128)(2,1)S(1)}, bf16[4,128,256]{2,1,0:T(8,128)(2,1)S(1)}, u32[]{:S(2)}, u32[]{:S(2)}) collective-permute-start(bf16[4,128,256]{2,1,0:T(8,128)(2,1)S(1)} %slice.16), channel_id=1, source_target_pairs={{0,1},{1,2},{2,3},{3,0},{4,5},{5,6},{6,7},{7,4},{8,9},{9,10},{10,1... | collective-permute-start | bytes 786440 | tf_op jit(solution)/shard_map/ppermute | solution.py:26
  42.3 3.0 %collective-permute-done.15.b_left = bf16[2,128,256]{2,1,0:T(8,128)(2,1)S(1)} collective-permute-done((bf16[2,128,256]{2,1,0:T(8,128)(2,1)}, bf16[2,128,256]{2,1,0:T(8,128)(2,1)S(1)}, u32[]{:S(2)}, u32[]{:S(2)}) %collective-permute-start.15) | collective-permute-done | bytes 131104 | tf_op jit(solution)/shard_map/ppermute | solution.py:26
  45.2 2.7 %collective-permute-start.16 = (bf16[2,128,256]{2,1,0:T(8,128)(2,1)}, bf16[2,128,256]{2,1,0:T(8,128)(2,1)S(1)}, u32[]{:S(2)}, u32[]{:S(2)}) collective-permute-start(bf16[2,128,256]{2,1,0:T(8,128)(2,1)} %get-tuple-element.30), channel_id=1, source_target_pairs={{0,3},{1,0},{2,1},{3,2},{4,7},{5,4},{6,5},{7,6},{8,11},{9,8},{10,9... | collective-permute-start | bytes 393224 | tf_op jit(solution)/shard_map/ppermute | solution.py:26
  47.9 4.2 %collective-permute-done.16.b_right = bf16[2,128,256]{2,1,0:T(8,128)(2,1)S(1)} collective-permute-done((bf16[2,128,256]{2,1,0:T(8,128)(2,1)}, bf16[2,128,256]{2,1,0:T(8,128)(2,1)S(1)}, u32[]{:S(2)}, u32[]{:S(2)}) %collective-permute-start.16) | collective-permute-done | bytes 131104 | tf_op jit(solution)/shard_map/ppermute | solution.py:26
  52.1 0.6 copy-done.19
  52.7 2.1 %shard_map.131 = bf16[4,128,256]{2,1,0:T(8,128)(2,1)} custom-call(f32[4,128,256]{2,1,0:T(8,128)} %get-tuple-element.24.own, bf16[4,128,256]{2,1,0:T(8,128)(2,1)} %copy-done.9, bf16[4,128,256]{2,1,0:T(8,128)(2,1)} %copy-done.10, bf16[2,128,256]{2,1,0:T(8,128)(2,1)} %copy-done.18, bf16[2,128,256]{2,1,0:T(8,128)(2,1)} %copy-done.19), custom_call_target="tpu_custom_call" | custom-call | bytes 1572864 | tf_op jit(solution)/shard_map/pallas_call | solution.py:342
  54.8 1.8 %collective-permute-start.17 = (bf16[4,128,256]{2,1,0:T(8,128)(2,1)}, bf16[4,128,256]{2,1,0:T(8,128)(2,1)S(1)}, u32[]{:S(2)}, u32[]{:S(2)}) collective-permute-start(bf16[4,128,256]{2,1,0:T(8,128)(2,1)} %shard_map.131), channel_id=1, source_target_pairs={{0,64},{4,68},{8,72},{12,76},{16,80},{20,84},{24,88},{28,92},{32,9... | collective-permute-start | bytes 786440 | tf_op jit(solution)/shard_map/ppermute | solution.py:21
  56.6 0.6 copy.19
  57.2 0.7 copy-done.4
  57.9 0.1 copy-done.5
  58.0 4.0 %shard_map.123 = (bf16[16,128,256]{2,1,0:T(8,128)(2,1)}, bf16[16,128,256]{2,1,0:T(8,128)(2,1)}) custom-call(s32[3,16]{1,0:T(4,128)} %bitcast.33, s32[1]{0:T(128)} %bitcast.1.me, bf16[8,128,256]{2,1,0:T(8,128)(2,1)} %bitcast.25, bf16[8,128,256]{2,1,0:T(8,128)(2,1)} %copy-done.1, bf16[4,128,256]{2,1,0:T(8,128)(2,1)} %copy-done.4, ...), custom_call_target="tpu_custom_call" | custom-call | bytes 4194304 | tf_op jit(solution)/shard_map/pallas_call | solution.py:342
  62.0 0.1 collective-permute-start.10
  62.1 2.3 %collective-permute-start.9 = (bf16[16,128,256]{2,1,0:T(8,128)(2,1)}, bf16[16,128,256]{2,1,0:T(8,128)(2,1)}, u32[]{:S(2)}, u32[]{:S(2)}) collective-permute-start(bf16[16,128,256]{2,1,0:T(8,128)(2,1)} %get-tuple-element.20), channel_id=1, source_target_pairs={{0,16},{4,20},{8,24},{12,28},{16,0},{20,4},{24,8},{28,12},{32,48},... | collective-permute-start | bytes 3145736 | tf_op jit(solution)/shard_map/ppermute | solution.py:21
  64.4 5.8 %shard_map.127.part_hbm = f32[33,128,256]{2,1,0:T(8,128)} custom-call(s32[4]{0:T(128)} %bitcast.40, s32[32]{0:T(128)} %bitcast.44, s32[32]{0:T(128)} %bitcast.46, s32[1]{0:T(128)} %bitcast.1.me, bf16[32,128,128]{2,1,0:T(8,128)(2,1)} %bitcast.23, bf16[8,128,256]{2,1,0:T(8,128)(2,1)} %get-tuple-element.23.gh_ref), custom_call_target="tpu_custom_call" | custom-call | flops 268435456 | bytes 5898240 | tf_op jit(solution)/shard_map/pallas_call | solution.py:342
  70.2 0.7 copy-done.8
  70.9 0.3 copy-done.3
  71.2 5.0 %shard_map.133 = (bf16[8,128,256]{2,1,0:T(8,128)(2,1)}, bf16[8,128,256]{2,1,0:T(8,128)(2,1)}) custom-call(s32[3,16]{1,0:T(4,128)} %bitcast.34, s32[1]{0:T(128)} %bitcast.1.me, f32[33,128,256]{2,1,0:T(8,128)} %shard_map.127.part_hbm, bf16[16,128,256]{2,1,0:T(8,128)(2,1)} %copy-done.3, bf16[16,128,256]{2,1,0:T(8,128)(2,1)} %collective-permute-done.12.got_b, ...), custom_call_target="tpu_custom_call" | custom-call | bytes 7733248 | tf_op jit(solution)/shard_map/pallas_call | solution.py:342
  76.2 0.8 collective-permute-start.18
  77.0 1.3 collective-permute-start.19
  78.3 2.4 %shard_map.122 = bf16[4,128,256]{2,1,0:T(8,128)(2,1)} custom-call(s32[3,16]{1,0:T(4,128)} %bitcast.35, s32[1]{0:T(128)} %bitcast.1.me, bf16[8,128,256]{2,1,0:T(8,128)(2,1)} %bitcast.26, bf16[8,128,256]{2,1,0:T(8,128)(2,1)} %copy-done.1, bf16[4,128,256]{2,1,0:T(8,128)(2,1)} %copy-done.4, bf16[4,128,256]{2,1,0:T(8,128)(2,1)} %copy-done.5, ...), custom_call_target="tpu_custom_call" | custom-call | bytes 2359296 | tf_op jit(solution)/shard_map/pallas_call | solution.py:342
  80.7 0.4 collective-permute-start.4
  81.2 14.1 %collective-permute-done.4.p0 = bf16[4,128,256]{2,1,0:T(8,128)(2,1)S(1)} collective-permute-done((bf16[4,128,256]{2,1,0:T(8,128)(2,1)}, bf16[4,128,256]{2,1,0:T(8,128)(2,1)S(1)}, u32[]{:S(2)}, u32[]{:S(2)}) %collective-permute-start.4) | collective-permute-done | bytes 262176 | tf_op jit(solution)/shard_map/ppermute | solution.py:21
  95.2 0.9 collective-permute-start.6
  96.1 5.1 %shard_map.132 = (f32[4,128,256]{2,1,0:T(8,128)}, f32[4,128,256]{2,1,0:T(8,128)}, f32[8,128,256]{2,1,0:T(8,128)}) custom-call(s32[3,16]{1,0:T(4,128)} %bitcast.36, s32[1]{0:T(128)} %bitcast.1.me, f32[33,128,256]{2,1,0:T(8,128)} %shard_map.127.part_hbm, bf16[16,128,256]{2,1,0:T(8,128)(2,1)} %copy-done.3, bf16[16,128,256]{2,1,0:T(8,128)(2,1)} %collective-permute-done.12.got_b, ...), custom_call_target="tpu_custom_call" | custom-call | bytes 8781824 | tf_op jit(solution)/shard_map/pallas_call | solution.py:342
  101.2 2.2 %collective-permute-start.5 = (bf16[4,128,256]{2,1,0:T(8,128)(2,1)S(1)}, bf16[4,128,256]{2,1,0:T(8,128)(2,1)S(1)}, u32[]{:S(2)}, u32[]{:S(2)}) collective-permute-start(bf16[4,128,256]{2,1,0:T(8,128)(2,1)S(1)} %collective-permute-done.4.p0), channel_id=1, source_target_pairs={{0,3},{1,0},{2,1},{3,2},{4,7},{5,4},{6,5},{7,6},{8,11},{9,8},{10,9... | collective-permute-start | bytes 786440 | tf_op jit(solution)/shard_map/ppermute | solution.py:26
  103.4 0.8 copy-done.7
  104.2 2.4 %shard_map.134 = (bf16[4,128,256]{2,1,0:T(8,128)(2,1)}, bf16[4,128,256]{2,1,0:T(8,128)(2,1)}) custom-call(f32[4,128,256]{2,1,0:T(8,128)} %get-tuple-element.34.keep_r, f32[4,128,256]{2,1,0:T(8,128)} %get-tuple-element.35.keep_l, bf16[8,128,256]{2,1,0:T(8,128)(2,1)} %copy-done.6, bf16[8,128,256]{2,1,0:T(8,128)(2,1)} %copy-done.7), custom_call_target="tpu_custom_call" | custom-call | bytes 2621440 | tf_op jit(solution)/shard_map/pallas_call | solution.py:342
  106.6 3.2 %collective-permute-start.21 = (bf16[4,128,256]{2,1,0:T(8,128)(2,1)}, bf16[4,128,256]{2,1,0:T(8,128)(2,1)S(1)}, u32[]{:S(2)}, u32[]{:S(2)}) collective-permute-start(bf16[4,128,256]{2,1,0:T(8,128)(2,1)} %get-tuple-element.37), channel_id=1, source_target_pairs={{0,3},{1,0},{2,1},{3,2},{4,7},{5,4},{6,5},{7,6},{8,11},{9,8},{10,9... | collective-permute-start | bytes 786440 | tf_op jit(solution)/shard_map/ppermute | solution.py:26
  109.8 2.1 %collective-permute-start.7 = (bf16[2,128,256]{2,1,0:T(8,128)(2,1)S(1)}, bf16[2,128,256]{2,1,0:T(8,128)(2,1)S(1)}, u32[]{:S(2)}, u32[]{:S(2)}) collective-permute-start(bf16[2,128,256]{2,1,0:T(8,128)(2,1)S(1)} %slice.18), channel_id=1, source_target_pairs={{0,1},{1,2},{2,3},{3,0},{4,5},{5,6},{6,7},{7,4},{8,9},{9,10},{10,1... | collective-permute-start | bytes 393224 | tf_op jit(solution)/shard_map/ppermute | solution.py:26
  111.9 5.1 %collective-permute-done.20.b_left = bf16[4,128,256]{2,1,0:T(8,128)(2,1)S(1)} collective-permute-done((bf16[4,128,256]{2,1,0:T(8,128)(2,1)}, bf16[4,128,256]{2,1,0:T(8,128)(2,1)S(1)}, u32[]{:S(2)}, u32[]{:S(2)}) %collective-permute-start.20) | collective-permute-done | bytes 262176 | tf_op jit(solution)/shard_map/ppermute | solution.py:26
  117.0 3.0 %collective-permute-start.8 = (bf16[2,128,256]{2,1,0:T(8,128)(2,1)S(1)}, bf16[2,128,256]{2,1,0:T(8,128)(2,1)S(1)}, u32[]{:S(2)}, u32[]{:S(2)}) collective-permute-start(bf16[2,128,256]{2,1,0:T(8,128)(2,1)S(1)} %slice.19), channel_id=1, source_target_pairs={{0,3},{1,0},{2,1},{3,2},{4,7},{5,4},{6,5},{7,6},{8,11},{9,8},{10,9... | collective-permute-start | bytes 393224 | tf_op jit(solution)/shard_map/ppermute | solution.py:26
  120.0 0.7 copy-done.15
  120.7 2.6 %shard_map.135 = bf16[8,128,256]{2,1,0:T(8,128)(2,1)} custom-call(f32[8,128,256]{2,1,0:T(8,128)} %get-tuple-element.31.own, bf16[8,128,256]{2,1,0:T(8,128)(2,1)} %copy-done.6, bf16[8,128,256]{2,1,0:T(8,128)(2,1)} %copy-done.7, bf16[4,128,256]{2,1,0:T(8,128)(2,1)} %copy-done.14, bf16[4,128,256]{2,1,0:T(8,128)(2,1)} %copy-done.15), custom_call_target="tpu_custom_call" | custom-call | bytes 3145728 | tf_op jit(solution)/shard_map/pallas_call | solution.py:342
  123.3 7.0 %shard_map.124.near_hbm = f32[8,128,256]{2,1,0:T(8,128)} custom-call(s32[4]{0:T(128)} %bitcast.41, s32[32]{0:T(128)} %bitcast.45, s32[32]{0:T(128)} %bitcast.47, s32[3,16]{1,0:T(4,128)} %get-tuple-element.39.rrows.rows, s32[3,16]{1,0:T(4,128)} %get-tuple-element.38.rslots.slots, s32[1]{0:T(128)} %bitcast.1.me, bf16[8,128,256]{2,1,0:T(8,128)(2,1)} %bitcast.27, ...), custom_call_target="tpu_custom_call" | custom-call | flops 402653184 | bytes 6815744 | tf_op jit(solution)/shard_map/pallas_call | solution.py:342
  130.4 0.6 copy-done.16
  131.1 5.8 %shard_map.126 = bf16[8,128,256]{2,1,0:T(8,128)(2,1)} custom-call(s32[4]{0:T(128)} %bitcast.42, s32[3,16]{1,0:T(4,128)} %get-tuple-element.39.rrows.rows, s32[3,16]{1,0:T(4,128)} %get-tuple-element.38.rslots.slots, s32[1]{0:T(128)} %bitcast.1.me, bf16[4,128,256]{2,1,0:T(8,128)(2,1)} %copy-done.13, bf16[4,128,256]{2,1,0:T(8,128)(2,1)} %copy-done.12, ...), custom_call_target="tpu_custom_call" | custom-call | flops 268435456 | bytes 5898240 | tf_op jit(solution)/shard_map/pallas_call | solution.py:342
  (60 shorter events, 0.3 us)
Async XLA Ops:
  1.9 14.6 %copy-start.2 = (bf16[1024,256]{1,0:T(8,128)(2,1)S(1)}, bf16[1024,256]{1,0:T(8,128)(2,1)}, u32[]{:S(2)}) copy-start(bf16[1024,256]{1,0:T(8,128)(2,1)} %param.11) | copy-start | bytes 1572868
  7.5 11.1 %copy-start.21 = (bf16[4,128,256]{2,1,0:T(8,128)(2,1)S(1)}, bf16[4,128,256]{2,1,0:T(8,128)(2,1)}, u32[]{:S(2)}) copy-start(bf16[4,128,256]{2,1,0:T(8,128)(2,1)} %get-tuple-element.26) | copy-start | bytes 786436
  7.5 11.1 %collective-permute-start.13 = (bf16[4,128,256]{2,1,0:T(8,128)(2,1)}, bf16[4,128,256]{2,1,0:T(8,128)(2,1)S(1)}, u32[]{:S(2)}, u32[]{:S(2)}) collective-permute-start(bf16[4,128,256]{2,1,0:T(8,128)(2,1)} %get-tuple-element.25), channel_id=1, source_target_pairs={{0,1},{1,2},{2,3},{3,0},{4,5},{5,6},{6,7},{7,4},{8,9},{9,10},{10,1... | collective-permute-start | bytes 786440 | tf_op jit(solution)/shard_map/ppermute | solution.py:26
  9.5 47.1 %copy-start.20 = (s32[1,3,16]{2,0,1:T(1,128)S(1)}, s32[1,3,16]{2,0,1:T(1,128)}, u32[]{:S(2)}) copy-start(s32[1,3,16]{2,0,1:T(1,128)} %param.20) | copy-start | bytes 580
  13.0 57.2 %collective-permute-start.11 = (bf16[16,128,256]{2,1,0:T(8,128)(2,1)}, bf16[16,128,256]{2,1,0:T(8,128)(2,1)S(1)}, u32[]{:S(2)}, u32[]{:S(2)}) collective-permute-start(bf16[16,128,256]{2,1,0:T(8,128)(2,1)} %shard_map.128), channel_id=1, source_target_pairs={{0,4},{4,0},{8,12},{12,8},{16,20},{20,16},{24,28},{28,24},{32,36},... | collective-permute-start | bytes 3145736 | tf_op jit(solution)/shard_map/ppermute | solution.py:21
  16.5 53.7 %collective-permute-start.12 = (bf16[16,128,256]{2,1,0:T(8,128)(2,1)}, bf16[16,128,256]{2,1,0:T(8,128)(2,1)}, u32[]{:S(2)}, u32[]{:S(2)}) collective-permute-start(bf16[16,128,256]{2,1,0:T(8,128)(2,1)} %shard_map.129), channel_id=1, source_target_pairs={{0,16},{4,20},{8,24},{12,28},{16,0},{20,4},{24,8},{28,12},{32,48},... | collective-permute-start | bytes 3145736 | tf_op jit(solution)/shard_map/ppermute | solution.py:21
  16.5 23.2 %collective-permute-start.1 = (bf16[8,128,256]{2,1,0:T(8,128)(2,1)S(1)}, bf16[8,128,256]{2,1,0:T(8,128)(2,1)S(1)}, u32[]{:S(2)}, u32[]{:S(2)}) collective-permute-start(bf16[8,128,256]{2,1,0:T(8,128)(2,1)S(1)} %bitcast.28), channel_id=1, source_target_pairs={{0,1},{1,2},{2,3},{3,0},{4,5},{5,6},{6,7},{7,4},{8,9},{9,10},{10,1... | collective-permute-start | bytes 1572872 | tf_op jit(solution)/shard_map/ppermute | solution.py:26
  17.4 24.7 %collective-permute-start = (bf16[8,128,256]{2,1,0:T(8,128)(2,1)S(1)}, bf16[8,128,256]{2,1,0:T(8,128)(2,1)S(1)}, u32[]{:S(2)}, u32[]{:S(2)}) collective-permute-start(bf16[8,128,256]{2,1,0:T(8,128)(2,1)S(1)} %bitcast.29), channel_id=1, source_target_pairs={{0,3},{1,0},{2,1},{3,2},{4,7},{5,4},{6,5},{7,6},{8,11},{9,8},{10,9... | collective-permute-start | bytes 1572872 | tf_op jit(solution)/shard_map/ppermute | solution.py:26
  18.6 17.4 %copy-start.9 = (bf16[4,128,256]{2,1,0:T(8,128)(2,1)}, bf16[4,128,256]{2,1,0:T(8,128)(2,1)S(1)}, u32[]{:S(2)}) copy-start(bf16[4,128,256]{2,1,0:T(8,128)(2,1)S(1)} %collective-permute-done.13.from_left.a_left) | copy-start | bytes 786436
  18.6 17.4 %collective-permute-start.14 = (bf16[4,128,256]{2,1,0:T(8,128)(2,1)S(1)}, bf16[4,128,256]{2,1,0:T(8,128)(2,1)S(1)}, u32[]{:S(2)}, u32[]{:S(2)}) collective-permute-start(bf16[4,128,256]{2,1,0:T(8,128)(2,1)S(1)} %copy-done.21), channel_id=1, source_target_pairs={{0,3},{1,0},{2,1},{3,2},{4,7},{5,4},{6,5},{7,6},{8,11},{9,8},{10,9... | collective-permute-start | bytes 786440 | tf_op jit(solution)/shard_map/ppermute | solution.py:26
  36.0 0.7 copy-start.10
  38.6 6.6 %collective-permute-start.15 = (bf16[2,128,256]{2,1,0:T(8,128)(2,1)}, bf16[2,128,256]{2,1,0:T(8,128)(2,1)S(1)}, u32[]{:S(2)}, u32[]{:S(2)}) collective-permute-start(bf16[2,128,256]{2,1,0:T(8,128)(2,1)} %get-tuple-element.29), channel_id=1, source_target_pairs={{0,1},{1,2},{2,3},{3,0},{4,5},{5,6},{6,7},{7,4},{8,9},{9,10},{10,1... | collective-permute-start | bytes 393224 | tf_op jit(solution)/shard_map/ppermute | solution.py:26
  39.7 17.5 %copy-start = (bf16[8,128,256]{2,1,0:T(8,128)(2,1)}, bf16[8,128,256]{2,1,0:T(8,128)(2,1)S(1)}, u32[]{:S(2)}) copy-start(bf16[8,128,256]{2,1,0:T(8,128)(2,1)S(1)} %collective-permute-done.1.p4) | copy-start | bytes 1572868
  39.7 17.4 %collective-permute-start.2 = (bf16[4,128,256]{2,1,0:T(8,128)(2,1)S(1)}, bf16[4,128,256]{2,1,0:T(8,128)(2,1)S(1)}, u32[]{:S(2)}, u32[]{:S(2)}) collective-permute-start(bf16[4,128,256]{2,1,0:T(8,128)(2,1)S(1)} %slice.16), channel_id=1, source_target_pairs={{0,1},{1,2},{2,3},{3,0},{4,5},{5,6},{6,7},{7,4},{8,9},{9,10},{10,1... | collective-permute-start | bytes 786440 | tf_op jit(solution)/shard_map/ppermute | solution.py:26
  42.1 15.0 %copy-start.1 = (bf16[8,128,256]{2,1,0:T(8,128)(2,1)}, bf16[8,128,256]{2,1,0:T(8,128)(2,1)S(1)}, u32[]{:S(2)}) copy-start(bf16[8,128,256]{2,1,0:T(8,128)(2,1)S(1)} %collective-permute-done.p1) | copy-start | bytes 1572868
  42.2 15.0 %collective-permute-start.3 = (bf16[4,128,256]{2,1,0:T(8,128)(2,1)S(1)}, bf16[4,128,256]{2,1,0:T(8,128)(2,1)S(1)}, u32[]{:S(2)}, u32[]{:S(2)}) collective-permute-start(bf16[4,128,256]{2,1,0:T(8,128)(2,1)S(1)} %slice.17), channel_id=1, source_target_pairs={{0,3},{1,0},{2,1},{3,2},{4,7},{5,4},{6,5},{7,6},{8,11},{9,8},{10,9... | collective-permute-start | bytes 786440 | tf_op jit(solution)/shard_map/ppermute | solution.py:26
  45.2 6.9 %copy-start.18 = (bf16[2,128,256]{2,1,0:T(8,128)(2,1)}, bf16[2,128,256]{2,1,0:T(8,128)(2,1)S(1)}, u32[]{:S(2)}) copy-start(bf16[2,128,256]{2,1,0:T(8,128)(2,1)S(1)} %collective-permute-done.15.b_left) | copy-start | bytes 393220
  45.2 6.9 %collective-permute-start.16 = (bf16[2,128,256]{2,1,0:T(8,128)(2,1)}, bf16[2,128,256]{2,1,0:T(8,128)(2,1)S(1)}, u32[]{:S(2)}, u32[]{:S(2)}) collective-permute-start(bf16[2,128,256]{2,1,0:T(8,128)(2,1)} %get-tuple-element.30), channel_id=1, source_target_pairs={{0,3},{1,0},{2,1},{3,2},{4,7},{5,4},{6,5},{7,6},{8,11},{9,8},{10,9... | collective-permute-start | bytes 393224 | tf_op jit(solution)/shard_map/ppermute | solution.py:26
  52.1 0.6 copy-start.19
  54.8 15.4 %collective-permute-start.17 = (bf16[4,128,256]{2,1,0:T(8,128)(2,1)}, bf16[4,128,256]{2,1,0:T(8,128)(2,1)S(1)}, u32[]{:S(2)}, u32[]{:S(2)}) collective-permute-start(bf16[4,128,256]{2,1,0:T(8,128)(2,1)} %shard_map.131), channel_id=1, source_target_pairs={{0,64},{4,68},{8,72},{12,76},{16,80},{20,84},{24,88},{28,92},{32,9... | collective-permute-start | bytes 786440 | tf_op jit(solution)/shard_map/ppermute | solution.py:21
  57.2 0.7 copy-start.4
  57.2 0.8 copy-start.5
  62.0 61.3 %collective-permute-start.10 = (bf16[16,128,256]{2,1,0:T(8,128)(2,1)}, bf16[16,128,256]{2,1,0:T(8,128)(2,1)}, u32[]{:S(2)}, u32[]{:S(2)}) collective-permute-start(bf16[16,128,256]{2,1,0:T(8,128)(2,1)} %get-tuple-element.21), channel_id=1, source_target_pairs={{0,4},{4,0},{8,12},{12,8},{16,20},{20,16},{24,28},{28,24},{32,36},... | collective-permute-start | bytes 3145736 | tf_op jit(solution)/shard_map/ppermute | solution.py:21
  62.1 68.3 %collective-permute-start.9 = (bf16[16,128,256]{2,1,0:T(8,128)(2,1)}, bf16[16,128,256]{2,1,0:T(8,128)(2,1)}, u32[]{:S(2)}, u32[]{:S(2)}) collective-permute-start(bf16[16,128,256]{2,1,0:T(8,128)(2,1)} %get-tuple-element.20), channel_id=1, source_target_pairs={{0,16},{4,20},{8,24},{12,28},{16,0},{20,4},{24,8},{28,12},{32,48},... | collective-permute-start | bytes 3145736 | tf_op jit(solution)/shard_map/ppermute | solution.py:21
  70.2 0.7 copy-start.8
  70.2 1.0 copy-start.3
  76.2 25.0 %collective-permute-start.18 = (bf16[8,128,256]{2,1,0:T(8,128)(2,1)}, bf16[8,128,256]{2,1,0:T(8,128)(2,1)S(1)}, u32[]{:S(2)}, u32[]{:S(2)}) collective-permute-start(bf16[8,128,256]{2,1,0:T(8,128)(2,1)} %get-tuple-element.32), channel_id=1, source_target_pairs={{0,1},{1,2},{2,3},{3,0},{4,5},{5,6},{6,7},{7,4},{8,9},{9,10},{10,1... | collective-permute-start | bytes 1572872 | tf_op jit(solution)/shard_map/ppermute | solution.py:26
  77.0 26.3 %collective-permute-start.19 = (bf16[8,128,256]{2,1,0:T(8,128)(2,1)}, bf16[8,128,256]{2,1,0:T(8,128)(2,1)S(1)}, u32[]{:S(2)}, u32[]{:S(2)}) collective-permute-start(bf16[8,128,256]{2,1,0:T(8,128)(2,1)} %get-tuple-element.33), channel_id=1, source_target_pairs={{0,3},{1,0},{2,1},{3,2},{4,7},{5,4},{6,5},{7,6},{8,11},{9,8},{10,9... | collective-permute-start | bytes 1572872 | tf_op jit(solution)/shard_map/ppermute | solution.py:26
  80.7 14.5 %collective-permute-start.4 = (bf16[4,128,256]{2,1,0:T(8,128)(2,1)}, bf16[4,128,256]{2,1,0:T(8,128)(2,1)S(1)}, u32[]{:S(2)}, u32[]{:S(2)}) collective-permute-start(bf16[4,128,256]{2,1,0:T(8,128)(2,1)} %shard_map.122), channel_id=1, source_target_pairs={{0,64},{4,68},{8,72},{12,76},{16,80},{20,84},{24,88},{28,92},{32,9... | collective-permute-start | bytes 786440 | tf_op jit(solution)/shard_map/ppermute | solution.py:21
  95.2 11.3 %copy-start.13 = (bf16[4,128,256]{2,1,0:T(8,128)(2,1)}, bf16[4,128,256]{2,1,0:T(8,128)(2,1)S(1)}, u32[]{:S(2)}) copy-start(bf16[4,128,256]{2,1,0:T(8,128)(2,1)S(1)} %collective-permute-done.4.p0) | copy-start | bytes 786436
  95.2 11.3 %collective-permute-start.6 = (bf16[4,128,256]{2,1,0:T(8,128)(2,1)S(1)}, bf16[4,128,256]{2,1,0:T(8,128)(2,1)S(1)}, u32[]{:S(2)}, u32[]{:S(2)}) collective-permute-start(bf16[4,128,256]{2,1,0:T(8,128)(2,1)S(1)} %collective-permute-done.4.p0), channel_id=1, source_target_pairs={{0,1},{1,2},{2,3},{3,0},{4,5},{5,6},{6,7},{7,4},{8,9},{9,10},{10,1... | collective-permute-start | bytes 786440 | tf_op jit(solution)/shard_map/ppermute | solution.py:26
  101.2 2.2 %copy-start.6 = (bf16[8,128,256]{2,1,0:T(8,128)(2,1)}, bf16[8,128,256]{2,1,0:T(8,128)(2,1)S(1)}, u32[]{:S(2)}) copy-start(bf16[8,128,256]{2,1,0:T(8,128)(2,1)S(1)} %collective-permute-done.18.from_left.a_left) | copy-start | bytes 1572868
  101.2 8.6 %collective-permute-start.5 = (bf16[4,128,256]{2,1,0:T(8,128)(2,1)S(1)}, bf16[4,128,256]{2,1,0:T(8,128)(2,1)S(1)}, u32[]{:S(2)}, u32[]{:S(2)}) collective-permute-start(bf16[4,128,256]{2,1,0:T(8,128)(2,1)S(1)} %collective-permute-done.4.p0), channel_id=1, source_target_pairs={{0,3},{1,0},{2,1},{3,2},{4,7},{5,4},{6,5},{7,6},{8,11},{9,8},{10,9... | collective-permute-start | bytes 786440 | tf_op jit(solution)/shard_map/ppermute | solution.py:26
  103.4 0.8 copy-start.7
  106.5 10.5 %collective-permute-start.20 = (bf16[4,128,256]{2,1,0:T(8,128)(2,1)}, bf16[4,128,256]{2,1,0:T(8,128)(2,1)S(1)}, u32[]{:S(2)}, u32[]{:S(2)}) collective-permute-start(bf16[4,128,256]{2,1,0:T(8,128)(2,1)} %get-tuple-element.36), channel_id=1, source_target_pairs={{0,1},{1,2},{2,3},{3,0},{4,5},{5,6},{6,7},{7,4},{8,9},{9,10},{10,1... | collective-permute-start | bytes 786440 | tf_op jit(solution)/shard_map/ppermute | solution.py:26
  106.6 23.8 %copy-start.11 = (bf16[4,128,256]{2,1,0:T(8,128)(2,1)}, bf16[4,128,256]{2,1,0:T(8,128)(2,1)S(1)}, u32[]{:S(2)}) copy-start(bf16[4,128,256]{2,1,0:T(8,128)(2,1)S(1)} %collective-permute-done.6.p4) | copy-start | bytes 786436
  106.6 13.4 %collective-permute-start.21 = (bf16[4,128,256]{2,1,0:T(8,128)(2,1)}, bf16[4,128,256]{2,1,0:T(8,128)(2,1)S(1)}, u32[]{:S(2)}, u32[]{:S(2)}) collective-permute-start(bf16[4,128,256]{2,1,0:T(8,128)(2,1)} %get-tuple-element.37), channel_id=1, source_target_pairs={{0,3},{1,0},{2,1},{3,2},{4,7},{5,4},{6,5},{7,6},{8,11},{9,8},{10,9... | collective-permute-start | bytes 786440 | tf_op jit(solution)/shard_map/ppermute | solution.py:26
  109.8 20.5 %copy-start.12 = (bf16[4,128,256]{2,1,0:T(8,128)(2,1)}, bf16[4,128,256]{2,1,0:T(8,128)(2,1)S(1)}, u32[]{:S(2)}) copy-start(bf16[4,128,256]{2,1,0:T(8,128)(2,1)S(1)} %collective-permute-done.5.p1) | copy-start | bytes 786436
  109.8 20.5 %collective-permute-start.7 = (bf16[2,128,256]{2,1,0:T(8,128)(2,1)S(1)}, bf16[2,128,256]{2,1,0:T(8,128)(2,1)S(1)}, u32[]{:S(2)}, u32[]{:S(2)}) collective-permute-start(bf16[2,128,256]{2,1,0:T(8,128)(2,1)S(1)} %slice.18), channel_id=1, source_target_pairs={{0,1},{1,2},{2,3},{3,0},{4,5},{5,6},{6,7},{7,4},{8,9},{9,10},{10,1... | collective-permute-start | bytes 393224 | tf_op jit(solution)/shard_map/ppermute | solution.py:26
  117.0 3.0 %copy-start.14 = (bf16[4,128,256]{2,1,0:T(8,128)(2,1)}, bf16[4,128,256]{2,1,0:T(8,128)(2,1)S(1)}, u32[]{:S(2)}) copy-start(bf16[4,128,256]{2,1,0:T(8,128)(2,1)S(1)} %collective-permute-done.20.b_left) | copy-start | bytes 786436
  117.0 13.3 %collective-permute-start.8 = (bf16[2,128,256]{2,1,0:T(8,128)(2,1)S(1)}, bf16[2,128,256]{2,1,0:T(8,128)(2,1)S(1)}, u32[]{:S(2)}, u32[]{:S(2)}) collective-permute-start(bf16[2,128,256]{2,1,0:T(8,128)(2,1)S(1)} %slice.19), channel_id=1, source_target_pairs={{0,3},{1,0},{2,1},{3,2},{4,7},{5,4},{6,5},{7,6},{8,11},{9,8},{10,9... | collective-permute-start | bytes 393224 | tf_op jit(solution)/shard_map/ppermute | solution.py:26
  120.0 0.7 copy-start.15
  130.4 0.7 copy-start.16
  130.4 0.7 copy-start.17

commit v3 on v1

v3 whole, which is shorter than its diff:
```python
import jax
import jax.numpy as jnp
from jax import lax
from jax.experimental import pallas as pl
from jax.experimental.pallas import tpu as pltpu
from jax.sharding import PartitionSpec as P


UNROLL = 4
F32 = jnp.float32
BF16 = jnp.bfloat16
SMEM = pl.BlockSpec(memory_space=pltpu.SMEM)
VMEM = pl.BlockSpec(memory_space=pltpu.VMEM)
ANY = pl.BlockSpec(memory_space=pl.ANY)


def swapped(array, bit):
    return lax.ppermute(array, "node", [(i, i ^ 1 << bit) for i in range(lax.axis_size("node"))])


def shifted(array, step):
    size = lax.axis_size("feat")
    return lax.ppermute(array, "feat", [(i, (i + step) % size) for i in range(size)])


def spread_relayed(mine):
    half = mine.shape[0] // 2
    before = shifted(mine, 1)
    after = shifted(mine, -1)
    far_low = shifted(before[:half], 1)
    far_high = shifted(after[half:], -1)
    return (mine, after, far_low, far_high, before)


def spread_direct(mine):
    before = shifted(mine, 1)
    after = shifted(mine, -1)
    far = shifted(mine, 2)
    return (mine, after, far, before)


def scattered(to_next, to_far, to_before):
    return shifted(to_next, 1), shifted(to_far, 2), shifted(to_before, -1)


def start_all(pairs, sems):
    copies = [pltpu.make_async_copy(a, b, sems.at[i]) for i, (a, b) in enumerate(pairs)]
    for copy in copies:
        copy.start()
    return copies


def wait_all(copies):
    for copy in copies:
        copy.wait()


def pieces_into(pieces, dst, base):
    pairs = []
    for piece in pieces:
        pairs.append((piece, dst.at[pl.ds(base, piece.shape[0])]))
        base += piece.shape[0]
    return pairs


def for_live(count, step):
    def group(k, carry):
        for u in range(UNROLL):
            t = k * UNROLL + u
            step(t, t < count)
        return carry

    lax.fori_loop(0, pl.cdiv(count, UNROLL), group, 0)


def forward_tiles(count, base, vals, row_of, source_of, acc):
    trash = acc.shape[0] - 1

    def step(t, live):
        row = jnp.where(live, row_of(t), trash)
        acc[row] += jnp.dot(vals[base + t], source_of(t), preferred_element_type=F32)

    for_live(count, step)


def backward_tiles(count, base, vals, row_of, target_of, grads, acc):
    trash = acc.shape[0] - 1

    def step(t, live):
        target = jnp.where(live, target_of(t), trash)
        acc[target] += lax.dot_general(
            vals[base + t], grads[row_of(t)], (((0,), (0,)), ((), ())), preferred_element_type=F32
        )

    for_live(count, step)


def degree_kernel(counts, lrows, rrows, rslots, me, lv_hbm, rv_hbm, go_hbm, w_ref,
                  deg_ref, gh_ref, next_ref, far_ref, before_ref, own_ref, out_b, out_a,
                  lv, rv, go, dacc, acc, sems):
    copies = start_all([(lv_hbm, lv), (rv_hbm, rv), (go_hbm, go)], sems)
    own = deg_ref.shape[0]
    cap = rrows.shape[1]
    dacc[...] = jnp.zeros_like(dacc)
    acc[...] = jnp.zeros_like(acc)
    copies[0].wait()

    def add_rows(vals, base, row_of):
        def step(t, live):
            row = jnp.where(live, row_of(t), own)
            dacc[row] += vals[base + t].astype(F32)

        return step

    for_live(counts[0], add_rows(lv, 0, lambda t: lrows[t]))
    copies[1].wait()
    for r in range(rrows.shape[0]):
        for_live(counts[r + 1], add_rows(rv, r * cap, lambda t: rrows[r, t]))
    copies[2].wait()
    for b in range(own):
        degree = 1.0 + jnp.broadcast_to(jnp.sum(dacc[b], axis=1, keepdims=True), dacc.shape[1:])
        deg_ref[b] = degree
        dense = lax.dot_general(go[b], w_ref[...], (((1,), (1,)), ((), ())), preferred_element_type=F32)
        width = degree.shape[1]
        for k in range(dense.shape[1] // width):
            gh_ref[b, :, k * width:(k + 1) * width] = (
                dense[:, k * width:(k + 1) * width] / degree
            ).astype(BF16)
    share = own_ref.shape[0]
    shift = me[0] * share
    backward_tiles(
        counts[3], 2 * cap, rv, lambda t: rrows[2, t],
        lambda t: lax.rem(rslots[2, t] - shift + cap, cap), gh_ref, acc,
    )
    split_out(acc, share, next_ref, far_ref, before_ref, own_ref)
    for r, out in ((1, out_b), (0, out_a)):
        acc[...] = jnp.zeros_like(acc)
        backward_tiles(
            counts[r + 1], r * cap, rv, lambda t: rrows[r, t], lambda t: rslots[r, t], gh_ref, acc
        )
        out[...] = acc[:cap].astype(BF16)


def split_out(acc, n, next_ref, far_ref, before_ref, own_ref):
    next_ref[...] = acc[n:2 * n].astype(BF16)
    far_ref[...] = acc[2 * n:3 * n].astype(BF16)
    before_ref[...] = acc[3 * n:4 * n].astype(BF16)
    own_ref[...] = acc[:n]


def merge_kernel(counts, lrows, lcols, sends, me, lv_hbm, gh_hbm, a_hbm, b_hbm, c_hbm,
                 next_ref, far_ref, before_ref, own_ref, lv, gh, got_a, got_b, got_c, acc, sems):
    copies = start_all([(lv_hbm, lv), (gh_hbm, gh), (a_hbm, got_a), (b_hbm, got_b), (c_hbm, got_c)], sems)
    own = gh.shape[0]
    total = acc.shape[0] - 1
    acc[own:] = jnp.zeros((total + 1 - own,) + acc.shape[1:], F32)
    wait_all(copies[:2])
    acc[:own] = gh[...].astype(F32)
    shift = me[0] * own
    backward_tiles(
        counts[0], 0, lv, lambda t: lrows[t],
        lambda t: lax.rem(lcols[t] - shift + total, total), gh, acc,
    )
    wait_all(copies[2:])
    for r, (got, base) in enumerate(((got_a, 0), (got_b, 0), (got_c, me[0] * got_c.shape[0]))):
        for s in range(got.shape[0]):
            acc[lax.rem(sends[r, base + s] - shift + total, total)] += got[s].astype(F32)
    split_out(acc, own, next_ref, far_ref, before_ref, own_ref)


def finish_kernel(own, a, b, c, out):
    out[...] = (own[...] + a[...].astype(F32) + b[...].astype(F32) + c[...].astype(F32)).astype(BF16)


def feat_kernel(counts, lrows, lcols, sends, me, p0, p1, p2, p3, p4, lv_hbm, out_a, out_b, out_c, near_ref,
                src, lv, acc, sems, sems_a, sems_b, sems_c):
    copies = start_all(pieces_into((p0, p1, p2, p3, p4), src, 0) + [(lv_hbm, lv)], sems)
    total = src.shape[0]
    own = near_ref.shape[0]
    shift = me[0] * own
    wait_all(copies[:5])
    picks = (
        (out_c, 2, me[0] * out_c.shape[0], sems_c), (out_b, 1, 0, sems_b), (out_a, 0, 0, sems_a)
    )

    def begin(out, r, base, marks):
        def one(s, carry):
            at = lax.rem(sends[r, base + s] - shift + total, total)
            pltpu.make_async_copy(src.at[at], out.at[s], marks.at[s]).start()
            return carry

        lax.fori_loop(0, out.shape[0], one, 0)

    def end(out, r, base, marks):
        def one(s, carry):
            pltpu.make_async_copy(src.at[0], out.at[s], marks.at[s]).wait()
            return carry

        lax.fori_loop(0, out.shape[0], one, 0)

    for pick in picks:
        begin(*pick)
    acc[:own] = src[:own].astype(F32)
    copies[5].wait()
    forward_tiles(
        counts[0], 0, lv, lambda t: lrows[t], lambda t: src[lax.rem(lcols[t] - shift + total, total)], acc
    )
    near_ref[...] = acc[:own]
    for pick in picks:
        end(*pick)


def far_kernel(counts, rrows, rslots, me, a_hbm, b_hbm, p0, p1, p2, p3, rv_hbm, near_hbm, deg_hbm, w_ref,
               out_ref, src, vals, acc, deg, sems):
    total = out_ref.shape[0]
    cap = rrows.shape[1]
    pairs = [(near_hbm, acc.at[pl.ds(0, total)]), (rv_hbm, vals)]
    pairs += pieces_into((a_hbm, b_hbm, p0, p1, p2, p3), src, 0) + [(deg_hbm, deg)]
    wait_all(start_all(pairs, sems))
    for r in range(2):
        forward_tiles(
            counts[r + 1], r * cap, vals, lambda t: rrows[r, t], lambda t: src[r * cap + rslots[r, t]], acc
        )
    shift = me[0] * p0.shape[0]
    forward_tiles(
        counts[3], 2 * cap, vals, lambda t: rrows[2, t],
        lambda t: src[2 * cap + lax.rem(rslots[2, t] - shift + cap, cap)], acc,
    )
    width = deg.shape[2]
    for b in range(total):
        hidden = jnp.concatenate(
            [acc[b, :, k:k + width] / deg[b] for k in range(0, acc.shape[2], width)], axis=1
        ).astype(BF16)
        out_ref[b] = jnp.dot(hidden, w_ref[...], preferred_element_type=F32).astype(BF16)


def body(
    features,
    weight,
    grad_out,
    local_rows,
    local_cols,
    local_values,
    remote_rows,
    remote_slots,
    remote_values,
    send_blocks,
    tile_counts,
):
    rows_dev, width = features.shape
    lcap, rows = local_values.shape[2:4]
    own = rows_dev // rows
    rounds, cap = remote_rows.shape[2:]
    slices = lax.axis_size("feat")
    part = own * slices
    share = cap // slices
    log_nodes = lax.axis_size("node").bit_length() - 1
    bits = [r * log_nodes // rounds for r in range(rounds)]
    tail = (rows, width)

    me = lax.axis_index("feat").astype(jnp.int32).reshape(1)
    counts = tile_counts[0, 0]
    lrows, lcols = local_rows[0, 0], local_cols[0, 0]
    rrows, rslots = remote_rows[0, 0], remote_slots[0, 0]
    sends = send_blocks[0]
    lv = local_values.reshape(lcap, rows, rows)
    rv = remote_values.reshape(rounds * cap, rows, rows)
    feats = features.reshape((own,) + tail)
    go = grad_out.reshape((own,) + tail)

    def blocks(n, kind):
        return jax.ShapeDtypeStruct((n,) + tail, kind)

    def room(n, kind):
        return pltpu.VMEM((n,) + tail, kind)

    def tiles(n, kind=BF16):
        return pltpu.VMEM((n, rows, rows), kind)

    def call(kernel, scalars, args, outs, scratch, flops, in_place=(), out_place=()):
        size = sum(a.size * a.dtype.itemsize for a in args)
        size += sum(o.size * o.dtype.itemsize for o in outs)
        return pl.pallas_call(
            kernel,
            out_shape=tuple(outs),
            in_specs=[SMEM] * len(scalars) + [VMEM if i in in_place else ANY for i in range(len(args))],
            out_specs=tuple(ANY if i in out_place else VMEM for i in range(len(outs))),
            scratch_shapes=scratch,
            cost_estimate=pl.CostEstimate(flops=flops, bytes_accessed=size, transcendentals=0),
        )(*scalars, *args)

    def sems(n):
        return pltpu.SemaphoreType.DMA((n,))

    tile_flops = 2 * rows * rows * width

    def split_shapes(n):
        return [blocks(n, BF16), blocks(n, BF16), blocks(n, BF16), blocks(n, F32)]

    def finished(own_part, arrived):
        n = own_part.shape[0]
        return call(finish_kernel, (), (own_part,) + arrived, [blocks(n, BF16)], [], 0, range(4))[0]

    part_feats = spread_relayed(feats)

    deg, gh, z_next, z_far, z_before, z_own, back_b, back_a = call(
        degree_kernel, (counts, lrows, rrows, rslots, me), (lv, rv, go, weight),
        [jax.ShapeDtypeStruct((own, rows, rows), F32), blocks(own, BF16)] + split_shapes(share)
        + [blocks(cap, BF16), blocks(cap, BF16)],
        [tiles(lcap), tiles(rounds * cap), room(own, BF16), tiles(own + 1, F32), room(cap + 1, F32), sems(3)],
        rounds * cap * tile_flops, (3,),
    )
    z_arrived = scattered(z_next, z_far, z_before)
    got_back_b = swapped(back_b, bits[1])
    got_back_a = swapped(back_a, bits[0])
    got_back_c = swapped(finished(z_own, z_arrived), bits[2])

    need_a, need_b, need_c, near = call(
        feat_kernel, (counts, lrows, lcols, sends, me), part_feats + (lv,),
        [blocks(cap, BF16), blocks(cap, BF16), blocks(share, BF16), blocks(own, F32)],
        [room(part, BF16), tiles(lcap), room(own + 1, F32), sems(6), sems(cap), sems(cap), sems(share)],
        lcap * tile_flops, (), range(3),
    )
    got_c = swapped(need_c, bits[2])
    got_b = swapped(need_b, bits[1])
    got_a = swapped(need_a, bits[0])

    to_next, to_far, to_before, own_part = call(
        merge_kernel, (counts, lrows, lcols, sends, me), (lv, gh, got_back_a, got_back_b, got_back_c),
        split_shapes(own),
        [tiles(lcap), room(own, BF16), room(cap, BF16), room(cap, BF16), room(share, BF16), room(part + 1, F32), sems(5)],
        lcap * tile_flops,
    )
    grad_features = finished(own_part, scattered(to_next, to_far, to_before))

    output = call(
        far_kernel, (counts, rrows, rslots, me),
        (got_a, got_b) + spread_direct(got_c) + (rv, near, deg, weight), [blocks(own, BF16)],
        [room(rounds * cap, BF16), tiles(rounds * cap), room(own + 1, F32), tiles(own, F32), sems(9)],
        rounds * cap * tile_flops, (9,),
    )[0]
    return (output.reshape(rows_dev, width), grad_features.reshape(rows_dev, width))


def solution(mesh):
    in_specs = (
        P(("node", "feat"), None),
        P(),
        P(("node", "feat"), None),
        P("node", "feat", None),
        P("node", "feat", None),
        P("node", "feat", None, None, None),
        P("node", "feat", None, None),
        P("node", "feat", None, None),
        P("node", "feat", None, None, None, None),
        P("node", None, None),
        P("node", "feat", None),
    )
    out_specs = (P(("node", "feat"), None), P(("node", "feat"), None))
    return jax.shard_map(body, mesh=mesh, in_specs=in_specs, out_specs=out_specs, check_vma=False)
```

time: 130 us -> 116 us (0.89)
  the two profiles are of different devices: /device:TPU:146 before, /device:TPU:1 now
where the time goes in v3:
time: 116 us; the launch traced here: 115 us
  waiting for transfers between devices  43 us (37%)
  starting transfers between devices  32.6 us (28%)
  Pallas kernels  31.7 us (27%)
  local copies, waits for them, and re-layouts  7.08 us (6%)
    ppermute x13, waiting for transfers between devices, shifted(): lax.ppermute(array, 'feat', [(i, (i + step) % size) for i in range(size)])  43 us
    pallas_call x6, Pallas kernels, call(): pl.pallas_call(kernel, out_shape=tuple(outs), in_specs=[SMEM] * len(scala...  31.7 us
    ppermute x13, starting transfers between devices, shifted(): lax.ppermute(array, 'feat', [(i, (i + step) % size) for i in range(size)])  16.8 us
    ppermute x6, starting transfers between devices, swapped(): lax.ppermute(array, 'node', [(i, i ^ 1 << bit) for i in range(lax.axis_si...  15.8 us
    unnamed x28, local copies, waits for them, and re-layouts  5.65 us
  transfers between devices with their start and end apart: 19, of which 8 were waited for; matrix products, arithmetic and copies ran while one was open for 3% of the time, Pallas kernels for 22%

profile of v3, /device:TPU:1, one launch (start us, length us, event | category | flops | bytes accessed | tf_op | source)
XLA Modules:
  0.0 115.4 jit_solution(6206263680345964321)
XLA Ops:
  0.6 2.1 %collective-permute-start.1 = (bf16[8,128,256]{2,1,0:T(8,128)(2,1)}, bf16[8,128,256]{2,1,0:T(8,128)(2,1)S(1)}, u32[]{:S(2)}, u32[]{:S(2)}) collective-permute-start(bf16[8,128,256]{2,1,0:T(8,128)(2,1)} %bitcast.24), channel_id=1, source_target_pairs={{0,1},{1,2},{2,3},{3,0},{4,5},{5,6},{6,7},{7,4},{8,9},{9,10},{10,1... | collective-permute-start | bytes 1572872 | tf_op jit(solution)/shard_map/ppermute | solution.py:23
  2.7 1.4 %collective-permute-start = (bf16[8,128,256]{2,1,0:T(8,128)(2,1)}, bf16[8,128,256]{2,1,0:T(8,128)(2,1)S(1)}, u32[]{:S(2)}, u32[]{:S(2)}) collective-permute-start(bf16[8,128,256]{2,1,0:T(8,128)(2,1)} %bitcast.25), channel_id=1, source_target_pairs={{0,3},{1,0},{2,1},{3,2},{4,7},{5,4},{6,5},{7,6},{8,11},{9,8},{10,9... | collective-permute-start | bytes 1572872 | tf_op jit(solution)/shard_map/ppermute | solution.py:23
  4.1 1.3 %copy_bitcast_fusion.1 = (s32[3,16]{1,0:T(4,128)}, s32[3,16]{1,0:T(4,128)}) fusion(s32[1,1,3,16]{3,1,2,0:T(1,128)} %param.18, s32[1,1,3,16]{3,1,2,0:T(1,128)} %param.17), kind=kLoop, calls=%fused_computation.1 | loop fusion | bytes 768
  5.4 7.8 %shard_map.123 = (f32[8,128,128]{2,1,0:T(8,128)}, bf16[8,128,256]{2,1,0:T(8,128)(2,1)}, bf16[4,128,256]{2,1,0:T(8,128)(2,1)}, bf16[4,128,256]{2,1,0:T(8,128)(2,1...) custom-call(s32[4]{0:T(128)} %bitcast.30, ...), custom_call_target="tpu_custom_call" | custom-call | flops 402653184 | bytes 7733248 | tf_op jit(solution)/shard_map/pallas_call | solution.py:283
  13.2 0.0 copy-start.12
  13.2 3.1 %collective-permute-start.10 = (bf16[16,128,256]{2,1,0:T(8,128)(2,1)}, bf16[16,128,256]{2,1,0:T(8,128)(2,1)S(1)}, u32[]{:S(2)}, u32[]{:S(2)}) collective-permute-start(bf16[16,128,256]{2,1,0:T(8,128)(2,1)} %get-tuple-element.24), channel_id=1, source_target_pairs={{0,4},{4,0},{8,12},{12,8},{16,20},{20,16},{24,28},{28,24},{32,36},... | collective-permute-start | bytes 3145736 | tf_op jit(solution)/shard_map/ppermute | solution.py:18
  16.4 1.5 %collective-permute-start.11 = (bf16[16,128,256]{2,1,0:T(8,128)(2,1)}, bf16[16,128,256]{2,1,0:T(8,128)(2,1)S(1)}, u32[]{:S(2)}, u32[]{:S(2)}) collective-permute-start(bf16[16,128,256]{2,1,0:T(8,128)(2,1)} %get-tuple-element.25), channel_id=1, source_target_pairs={{0,16},{4,20},{8,24},{12,28},{16,0},{20,4},{24,8},{28,12},{32,48},... | collective-permute-start | bytes 3145736 | tf_op jit(solution)/shard_map/ppermute | solution.py:18
  17.9 1.2 %collective-permute-start.12 = (bf16[4,128,256]{2,1,0:T(8,128)(2,1)}, bf16[4,128,256]{2,1,0:T(8,128)(2,1)}, u32[]{:S(2)}, u32[]{:S(2)}) collective-permute-start(bf16[4,128,256]{2,1,0:T(8,128)(2,1)} %get-tuple-element.27), channel_id=1, source_target_pairs={{0,1},{1,2},{2,3},{3,0},{4,5},{5,6},{6,7},{7,4},{8,9},{9,10},{10,1... | collective-permute-start | bytes 786440 | tf_op jit(solution)/shard_map/ppermute | solution.py:23
  19.1 0.0 collective-permute-done.1.p4
  19.1 1.3 %collective-permute-start.13 = (bf16[4,128,256]{2,1,0:T(8,128)(2,1)}, bf16[4,128,256]{2,1,0:T(8,128)(2,1)}, u32[]{:S(2)}, u32[]{:S(2)}) collective-permute-start(bf16[4,128,256]{2,1,0:T(8,128)(2,1)} %get-tuple-element.28), channel_id=1, source_target_pairs={{0,2},{1,3},{2,0},{3,1},{4,6},{5,7},{6,4},{7,5},{8,10},{9,11},{10,... | collective-permute-start | bytes 786440 | tf_op jit(solution)/shard_map/ppermute | solution.py:23
  20.3 0.0 collective-permute-done.p1
  20.3 1.4 %collective-permute-start.14 = (bf16[4,128,256]{2,1,0:T(8,128)(2,1)}, bf16[4,128,256]{2,1,0:T(8,128)(2,1)}, u32[]{:S(2)}, u32[]{:S(2)}) collective-permute-start(bf16[4,128,256]{2,1,0:T(8,128)(2,1)} %get-tuple-element.29), channel_id=1, source_target_pairs={{0,3},{1,0},{2,1},{3,2},{4,7},{5,4},{6,5},{7,6},{8,11},{9,8},{10,9... | collective-permute-start | bytes 786440 | tf_op jit(solution)/shard_map/ppermute | solution.py:23
  21.8 0.7 slice.8
  22.5 0.7 slice.9
  23.2 3.9 %collective-permute-done.12.a = bf16[4,128,256]{2,1,0:T(8,128)(2,1)} collective-permute-done((bf16[4,128,256]{2,1,0:T(8,128)(2,1)}, bf16[4,128,256]{2,1,0:T(8,128)(2,1)}, u32[]{:S(2)}, u32[]{:S(2)}) %collective-permute-start.12) | collective-permute-done | bytes 262176 | tf_op jit(solution)/shard_map/ppermute | solution.py:23
  27.1 0.0 collective-permute-start.2
  27.1 5.2 %collective-permute-done.13.b = bf16[4,128,256]{2,1,0:T(8,128)(2,1)} collective-permute-done((bf16[4,128,256]{2,1,0:T(8,128)(2,1)}, bf16[4,128,256]{2,1,0:T(8,128)(2,1)}, u32[]{:S(2)}, u32[]{:S(2)}) %collective-permute-start.13) | collective-permute-done | bytes 262176 | tf_op jit(solution)/shard_map/ppermute | solution.py:23
  32.3 0.0 collective-permute-start.3
  32.3 0.5 collective-permute-done.14.c
  32.8 2.1 %shard_map.125 = bf16[4,128,256]{2,1,0:T(8,128)(2,1)} custom-call(f32[4,128,256]{2,1,0:T(8,128)} %get-tuple-element.26.own, bf16[4,128,256]{2,1,0:T(8,128)(2,1)} %collective-permute-done.12.a, bf16[4,128,256]{2,1,0:T(8,128)(2,1)} %collective-permute-done.13.b, bf16[4,128,256]{2,1,0:T(8,128)(2,1)} %collective-permute-done.14.c), custom_call_target="tpu_custom_call" | custom-call | bytes 1572864 | tf_op jit(solution)/shard_map/pallas_call | solution.py:283
  35.0 3.0 %collective-permute-start.15 = (bf16[4,128,256]{2,1,0:T(8,128)(2,1)}, bf16[4,128,256]{2,1,0:T(8,128)(2,1)}, u32[]{:S(2)}, u32[]{:S(2)}) collective-permute-start(bf16[4,128,256]{2,1,0:T(8,128)(2,1)} %shard_map.125), channel_id=1, source_target_pairs={{0,64},{4,68},{8,72},{12,76},{16,80},{20,84},{24,88},{28,92},{32,9... | collective-permute-start | bytes 786440 | tf_op jit(solution)/shard_map/ppermute | solution.py:18
  38.0 0.6 copy.19
  38.5 0.0 collective-permute-done.2.p2
  38.5 0.0 collective-permute-done.3.p3
  38.6 0.7 copy-done.11
  39.2 6.1 %shard_map.122 = (bf16[16,128,256]{2,1,0:T(8,128)(2,1)}, bf16[16,128,256]{2,1,0:T(8,128)(2,1)}, bf16[4,128,256]{2,1,0:T(8,128)(2,1)}, f32[8,128,256]{2,1,0:T(8,128)}) custom-call(s32[4]{0:T(128)} %bitcast.31, s32[32]{0:T(128)} %bitcast.35, s32[32]{0:T(128)} %bitcast.37, s32[3,16]{1,0:T(4,128)} %bitcast.28, s32[1]{0:T(128)} %bitcast.1.me, ...), custom_call_target="tpu_custom_call" | custom-call | flops 268435456 | bytes 6553600 | tf_op jit(solution)/shard_map/pallas_call | solution.py:283
  45.3 1.4 %collective-permute-start.6 = (bf16[4,128,256]{2,1,0:T(8,128)(2,1)}, bf16[4,128,256]{2,1,0:T(8,128)(2,1)S(1)}, u32[]{:S(2)}, u32[]{:S(2)}) collective-permute-start(bf16[4,128,256]{2,1,0:T(8,128)(2,1)} %get-tuple-element.20), channel_id=1, source_target_pairs={{0,64},{4,68},{8,72},{12,76},{16,80},{20,84},{24,88},{28,92},{32,9... | collective-permute-start | bytes 786440 | tf_op jit(solution)/shard_map/ppermute | solution.py:18
  46.7 3.5 %collective-permute-start.4 = (bf16[16,128,256]{2,1,0:T(8,128)(2,1)}, bf16[16,128,256]{2,1,0:T(8,128)(2,1)S(1)}, u32[]{:S(2)}, u32[]{:S(2)}) collective-permute-start(bf16[16,128,256]{2,1,0:T(8,128)(2,1)} %get-tuple-element.18), channel_id=1, source_target_pairs={{0,4},{4,0},{8,12},{12,8},{16,20},{20,16},{24,28},{28,24},{32,36},... | collective-permute-start | bytes 3145736 | tf_op jit(solution)/shard_map/ppermute | solution.py:18
  50.2 3.3 %collective-permute-start.5 = (bf16[16,128,256]{2,1,0:T(8,128)(2,1)}, bf16[16,128,256]{2,1,0:T(8,128)(2,1)}, u32[]{:S(2)}, u32[]{:S(2)}) collective-permute-start(bf16[16,128,256]{2,1,0:T(8,128)(2,1)} %get-tuple-element.19), channel_id=1, source_target_pairs={{0,16},{4,20},{8,24},{12,28},{16,0},{20,4},{24,8},{28,12},{32,48},... | collective-permute-start | bytes 3145736 | tf_op jit(solution)/shard_map/ppermute | solution.py:18
  53.5 0.0 collective-permute-done.11.b_hbm
  53.5 1.0 copy-done.2
  54.5 0.3 copy-done.3
  54.8 6.5 %shard_map.126 = (bf16[8,128,256]{2,1,0:T(8,128)(2,1)}, bf16[8,128,256]{2,1,0:T(8,128)(2,1)}, bf16[8,128,256]{2,1,0:T(8,128)(2,1)}, f32[8,128,256]{2,1,0:T(8,128)}) custom-call(s32[4]{0:T(128)} %bitcast.32, s32[32]{0:T(128)} %bitcast.36, s32[32]{0:T(128)} %bitcast.38, s32[3,16]{1,0:T(4,128)} %bitcast.29, s32[1]{0:T(128)} %bitcast.1.me, ...), custom_call_target="tpu_custom_call" | custom-call | flops 268435456 | bytes 6553600 | tf_op jit(solution)/shard_map/pallas_call | solution.py:283
  61.3 3.4 %collective-permute-start.16 = (bf16[8,128,256]{2,1,0:T(8,128)(2,1)}, bf16[8,128,256]{2,1,0:T(8,128)(2,1)S(1)}, u32[]{:S(2)}, u32[]{:S(2)}) collective-permute-start(bf16[8,128,256]{2,1,0:T(8,128)(2,1)} %get-tuple-element.31), channel_id=1, source_target_pairs={{0,1},{1,2},{2,3},{3,0},{4,5},{5,6},{6,7},{7,4},{8,9},{9,10},{10,1... | collective-permute-start | bytes 1572872 | tf_op jit(solution)/shard_map/ppermute | solution.py:23
  64.7 4.7 %collective-permute-start.17 = (bf16[8,128,256]{2,1,0:T(8,128)(2,1)}, bf16[8,128,256]{2,1,0:T(8,128)(2,1)S(1)}, u32[]{:S(2)}, u32[]{:S(2)}) collective-permute-start(bf16[8,128,256]{2,1,0:T(8,128)(2,1)} %get-tuple-element.32), channel_id=1, source_target_pairs={{0,2},{1,3},{2,0},{3,1},{4,6},{5,7},{6,4},{7,5},{8,10},{9,11},{10,... | collective-permute-start | bytes 1572872 | tf_op jit(solution)/shard_map/ppermute | solution.py:23
  69.4 0.0 collective-permute-done.6.p0
  69.4 11.1 %collective-permute-done.16.a = bf16[8,128,256]{2,1,0:T(8,128)(2,1)S(1)} collective-permute-done((bf16[8,128,256]{2,1,0:T(8,128)(2,1)}, bf16[8,128,256]{2,1,0:T(8,128)(2,1)S(1)}, u32[]{:S(2)}, u32[]{:S(2)}) %collective-permute-start.16) | collective-permute-done | bytes 524320 | tf_op jit(solution)/shard_map/ppermute | solution.py:23
  80.5 1.3 %collective-permute-start.7 = (bf16[4,128,256]{2,1,0:T(8,128)(2,1)S(1)}, bf16[4,128,256]{2,1,0:T(8,128)(2,1)S(1)}, u32[]{:S(2)}, u32[]{:S(2)}) collective-permute-start(bf16[4,128,256]{2,1,0:T(8,128)(2,1)S(1)} %collective-permute-done.6.p0), channel_id=1, source_target_pairs={{0,3},{1,0},{2,1},{3,2},{4,7},{5,4},{6,5},{7,6},{8,11},{9,8},{10,9... | collective-permute-start | bytes 786440 | tf_op jit(solution)/shard_map/ppermute | solution.py:23
  81.8 10.8 %collective-permute-done.17.b = bf16[8,128,256]{2,1,0:T(8,128)(2,1)S(1)} collective-permute-done((bf16[8,128,256]{2,1,0:T(8,128)(2,1)}, bf16[8,128,256]{2,1,0:T(8,128)(2,1)S(1)}, u32[]{:S(2)}, u32[]{:S(2)}) %collective-permute-start.17) | collective-permute-done | bytes 524320 | tf_op jit(solution)/shard_map/ppermute | solution.py:23
  92.7 0.1 collective-permute-start.9
  92.8 0.7 copy-done.6
  93.5 0.2 copy-done.7
  93.6 2.7 %shard_map.127 = bf16[8,128,256]{2,1,0:T(8,128)(2,1)} custom-call(f32[8,128,256]{2,1,0:T(8,128)} %get-tuple-element.30.own, bf16[8,128,256]{2,1,0:T(8,128)(2,1)} %copy-done.5, bf16[8,128,256]{2,1,0:T(8,128)(2,1)} %copy-done.6, bf16[8,128,256]{2,1,0:T(8,128)(2,1)} %copy-done.7), custom_call_target="tpu_custom_call" | custom-call | bytes 3145728 | tf_op jit(solution)/shard_map/pallas_call | solution.py:283
  96.3 1.5 %collective-permute-done.7.p1 = bf16[4,128,256]{2,1,0:T(8,128)(2,1)S(1)} collective-permute-done((bf16[4,128,256]{2,1,0:T(8,128)(2,1)S(1)}, bf16[4,128,256]{2,1,0:T(8,128)(2,1)S(1)}, u32[]{:S(2)}, u32[]{:S(2)}) %collective-permute-start.7) | collective-permute-done | bytes 262176 | tf_op jit(solution)/shard_map/ppermute | solution.py:23
  97.8 3.2 %collective-permute-done.8.p2 = bf16[4,128,256]{2,1,0:T(8,128)(2,1)S(1)} collective-permute-done((bf16[4,128,256]{2,1,0:T(8,128)(2,1)S(1)}, bf16[4,128,256]{2,1,0:T(8,128)(2,1)S(1)}, u32[]{:S(2)}, u32[]{:S(2)}) %collective-permute-start.8) | collective-permute-done | bytes 262176 | tf_op jit(solution)/shard_map/ppermute | solution.py:23
  101.1 6.7 %collective-permute-done.9.p3 = bf16[4,128,256]{2,1,0:T(8,128)(2,1)} collective-permute-done((bf16[4,128,256]{2,1,0:T(8,128)(2,1)S(1)}, bf16[4,128,256]{2,1,0:T(8,128)(2,1)}, u32[]{:S(2)}, u32[]{:S(2)}) %collective-permute-start.9) | collective-permute-done | bytes 262176 | tf_op jit(solution)/shard_map/ppermute | solution.py:23
  107.8 0.9 copy-done.4
  108.7 6.5 %shard_map.124 = bf16[8,128,256]{2,1,0:T(8,128)(2,1)} custom-call(s32[4]{0:T(128)} %bitcast.33, s32[3,16]{1,0:T(4,128)} %get-tuple-element.35.rrows, s32[3,16]{1,0:T(4,128)} %get-tuple-element.34.rslots, s32[1]{0:T(128)} %bitcast.1.me, bf16[16,128,256]{2,1,0:T(8,128)(2,1)} %copy-done.4, bf16[16,128,256]{2,1,0:T(8,128)(2,1)} %collective-permute-done.5.b_hbm, ...), custom_call_target="tpu_custom_call" | custom-call | flops 402653184 | bytes 6946816 | tf_op jit(solution)/shard_map/pallas_call | solution.py:283
  (26 shorter events, 0.1 us)
Async XLA Ops:
  0.6 18.4 %collective-permute-start.1 = (bf16[8,128,256]{2,1,0:T(8,128)(2,1)}, bf16[8,128,256]{2,1,0:T(8,128)(2,1)S(1)}, u32[]{:S(2)}, u32[]{:S(2)}) collective-permute-start(bf16[8,128,256]{2,1,0:T(8,128)(2,1)} %bitcast.24), channel_id=1, source_target_pairs={{0,1},{1,2},{2,3},{3,0},{4,5},{5,6},{6,7},{7,4},{8,9},{9,10},{10,1... | collective-permute-start | bytes 1572872 | tf_op jit(solution)/shard_map/ppermute | solution.py:23
  2.7 17.6 %collective-permute-start = (bf16[8,128,256]{2,1,0:T(8,128)(2,1)}, bf16[8,128,256]{2,1,0:T(8,128)(2,1)S(1)}, u32[]{:S(2)}, u32[]{:S(2)}) collective-permute-start(bf16[8,128,256]{2,1,0:T(8,128)(2,1)} %bitcast.25), channel_id=1, source_target_pairs={{0,3},{1,0},{2,1},{3,2},{4,7},{5,4},{6,5},{7,6},{8,11},{9,8},{10,9... | collective-permute-start | bytes 1572872 | tf_op jit(solution)/shard_map/ppermute | solution.py:23
  13.2 24.7 %copy-start.12 = (s32[1,3,16]{2,0,1:T(1,128)S(1)}, s32[1,3,16]{2,0,1:T(1,128)}, u32[]{:S(2)}) copy-start(s32[1,3,16]{2,0,1:T(1,128)} %param.20) | copy-start | bytes 580
  13.2 40.3 %collective-permute-start.10 = (bf16[16,128,256]{2,1,0:T(8,128)(2,1)}, bf16[16,128,256]{2,1,0:T(8,128)(2,1)S(1)}, u32[]{:S(2)}, u32[]{:S(2)}) collective-permute-start(bf16[16,128,256]{2,1,0:T(8,128)(2,1)} %get-tuple-element.24), channel_id=1, source_target_pairs={{0,4},{4,0},{8,12},{12,8},{16,20},{20,16},{24,28},{28,24},{32,36},... | collective-permute-start | bytes 3145736 | tf_op jit(solution)/shard_map/ppermute | solution.py:18
  16.4 37.1 %collective-permute-start.11 = (bf16[16,128,256]{2,1,0:T(8,128)(2,1)}, bf16[16,128,256]{2,1,0:T(8,128)(2,1)S(1)}, u32[]{:S(2)}, u32[]{:S(2)}) collective-permute-start(bf16[16,128,256]{2,1,0:T(8,128)(2,1)} %get-tuple-element.25), channel_id=1, source_target_pairs={{0,16},{4,20},{8,24},{12,28},{16,0},{20,4},{24,8},{28,12},{32,48},... | collective-permute-start | bytes 3145736 | tf_op jit(solution)/shard_map/ppermute | solution.py:18
  17.9 9.2 %collective-permute-start.12 = (bf16[4,128,256]{2,1,0:T(8,128)(2,1)}, bf16[4,128,256]{2,1,0:T(8,128)(2,1)}, u32[]{:S(2)}, u32[]{:S(2)}) collective-permute-start(bf16[4,128,256]{2,1,0:T(8,128)(2,1)} %get-tuple-element.27), channel_id=1, source_target_pairs={{0,1},{1,2},{2,3},{3,0},{4,5},{5,6},{6,7},{7,4},{8,9},{9,10},{10,1... | collective-permute-start | bytes 786440 | tf_op jit(solution)/shard_map/ppermute | solution.py:23
  19.1 19.5 %copy-start = (bf16[8,128,256]{2,1,0:T(8,128)(2,1)}, bf16[8,128,256]{2,1,0:T(8,128)(2,1)S(1)}, u32[]{:S(2)}) copy-start(bf16[8,128,256]{2,1,0:T(8,128)(2,1)S(1)} %collective-permute-done.1.p4) | copy-start | bytes 1572868
  19.1 13.2 %collective-permute-start.13 = (bf16[4,128,256]{2,1,0:T(8,128)(2,1)}, bf16[4,128,256]{2,1,0:T(8,128)(2,1)}, u32[]{:S(2)}, u32[]{:S(2)}) collective-permute-start(bf16[4,128,256]{2,1,0:T(8,128)(2,1)} %get-tuple-element.28), channel_id=1, source_target_pairs={{0,2},{1,3},{2,0},{3,1},{4,6},{5,7},{6,4},{7,5},{8,10},{9,11},{10,... | collective-permute-start | bytes 786440 | tf_op jit(solution)/shard_map/ppermute | solution.py:23
  20.3 18.2 %copy-start.1 = (bf16[8,128,256]{2,1,0:T(8,128)(2,1)}, bf16[8,128,256]{2,1,0:T(8,128)(2,1)S(1)}, u32[]{:S(2)}) copy-start(bf16[8,128,256]{2,1,0:T(8,128)(2,1)S(1)} %collective-permute-done.p1) | copy-start | bytes 1572868
  20.3 12.5 %collective-permute-start.14 = (bf16[4,128,256]{2,1,0:T(8,128)(2,1)}, bf16[4,128,256]{2,1,0:T(8,128)(2,1)}, u32[]{:S(2)}, u32[]{:S(2)}) collective-permute-start(bf16[4,128,256]{2,1,0:T(8,128)(2,1)} %get-tuple-element.29), channel_id=1, source_target_pairs={{0,3},{1,0},{2,1},{3,2},{4,7},{5,4},{6,5},{7,6},{8,11},{9,8},{10,9... | collective-permute-start | bytes 786440 | tf_op jit(solution)/shard_map/ppermute | solution.py:23
  27.1 11.4 %collective-permute-start.2 = (bf16[4,128,256]{2,1,0:T(8,128)(2,1)}, bf16[4,128,256]{2,1,0:T(8,128)(2,1)S(1)}, u32[]{:S(2)}, u32[]{:S(2)}) collective-permute-start(bf16[4,128,256]{2,1,0:T(8,128)(2,1)} %slice.8), channel_id=1, source_target_pairs={{0,1},{1,2},{2,3},{3,0},{4,5},{5,6},{6,7},{7,4},{8,9},{9,10},{10,1... | collective-permute-start | bytes 786440 | tf_op jit(solution)/shard_map/ppermute | solution.py:23
  32.3 6.2 %collective-permute-start.3 = (bf16[4,128,256]{2,1,0:T(8,128)(2,1)}, bf16[4,128,256]{2,1,0:T(8,128)(2,1)}, u32[]{:S(2)}, u32[]{:S(2)}) collective-permute-start(bf16[4,128,256]{2,1,0:T(8,128)(2,1)} %slice.9), channel_id=1, source_target_pairs={{0,3},{1,0},{2,1},{3,2},{4,7},{5,4},{6,5},{7,6},{8,11},{9,8},{10,9... | collective-permute-start | bytes 786440 | tf_op jit(solution)/shard_map/ppermute | solution.py:23
  35.0 15.3 %collective-permute-start.15 = (bf16[4,128,256]{2,1,0:T(8,128)(2,1)}, bf16[4,128,256]{2,1,0:T(8,128)(2,1)}, u32[]{:S(2)}, u32[]{:S(2)}) collective-permute-start(bf16[4,128,256]{2,1,0:T(8,128)(2,1)} %shard_map.125), channel_id=1, source_target_pairs={{0,64},{4,68},{8,72},{12,76},{16,80},{20,84},{24,88},{28,92},{32,9... | collective-permute-start | bytes 786440 | tf_op jit(solution)/shard_map/ppermute | solution.py:18
  38.5 0.7 copy-start.11
  45.3 24.1 %collective-permute-start.6 = (bf16[4,128,256]{2,1,0:T(8,128)(2,1)}, bf16[4,128,256]{2,1,0:T(8,128)(2,1)S(1)}, u32[]{:S(2)}, u32[]{:S(2)}) collective-permute-start(bf16[4,128,256]{2,1,0:T(8,128)(2,1)} %get-tuple-element.20), channel_id=1, source_target_pairs={{0,64},{4,68},{8,72},{12,76},{16,80},{20,84},{24,88},{28,92},{32,9... | collective-permute-start | bytes 786440 | tf_op jit(solution)/shard_map/ppermute | solution.py:18
  46.7 61.1 %collective-permute-start.4 = (bf16[16,128,256]{2,1,0:T(8,128)(2,1)}, bf16[16,128,256]{2,1,0:T(8,128)(2,1)S(1)}, u32[]{:S(2)}, u32[]{:S(2)}) collective-permute-start(bf16[16,128,256]{2,1,0:T(8,128)(2,1)} %get-tuple-element.18), channel_id=1, source_target_pairs={{0,4},{4,0},{8,12},{12,8},{16,20},{20,16},{24,28},{28,24},{32,36},... | collective-permute-start | bytes 3145736 | tf_op jit(solution)/shard_map/ppermute | solution.py:18
  50.2 57.5 %collective-permute-start.5 = (bf16[16,128,256]{2,1,0:T(8,128)(2,1)}, bf16[16,128,256]{2,1,0:T(8,128)(2,1)}, u32[]{:S(2)}, u32[]{:S(2)}) collective-permute-start(bf16[16,128,256]{2,1,0:T(8,128)(2,1)} %get-tuple-element.19), channel_id=1, source_target_pairs={{0,16},{4,20},{8,24},{12,28},{16,0},{20,4},{24,8},{28,12},{32,48},... | collective-permute-start | bytes 3145736 | tf_op jit(solution)/shard_map/ppermute | solution.py:18
  53.5 1.0 copy-start.2
  53.5 1.3 %copy-start.3 = (bf16[16,128,256]{2,1,0:T(8,128)(2,1)}, bf16[16,128,256]{2,1,0:T(8,128)(2,1)S(1)}, u32[]{:S(2)}) copy-start(bf16[16,128,256]{2,1,0:T(8,128)(2,1)S(1)} %collective-permute-done.11.b_hbm) | copy-start | bytes 3145732
  61.3 19.2 %collective-permute-start.16 = (bf16[8,128,256]{2,1,0:T(8,128)(2,1)}, bf16[8,128,256]{2,1,0:T(8,128)(2,1)S(1)}, u32[]{:S(2)}, u32[]{:S(2)}) collective-permute-start(bf16[8,128,256]{2,1,0:T(8,128)(2,1)} %get-tuple-element.31), channel_id=1, source_target_pairs={{0,1},{1,2},{2,3},{3,0},{4,5},{5,6},{6,7},{7,4},{8,9},{9,10},{10,1... | collective-permute-start | bytes 1572872 | tf_op jit(solution)/shard_map/ppermute | solution.py:23
  64.7 27.9 %collective-permute-start.17 = (bf16[8,128,256]{2,1,0:T(8,128)(2,1)}, bf16[8,128,256]{2,1,0:T(8,128)(2,1)S(1)}, u32[]{:S(2)}, u32[]{:S(2)}) collective-permute-start(bf16[8,128,256]{2,1,0:T(8,128)(2,1)} %get-tuple-element.32), channel_id=1, source_target_pairs={{0,2},{1,3},{2,0},{3,1},{4,6},{5,7},{6,4},{7,5},{8,10},{9,11},{10,... | collective-permute-start | bytes 1572872 | tf_op jit(solution)/shard_map/ppermute | solution.py:23
  69.4 38.3 %copy-start.8 = (bf16[4,128,256]{2,1,0:T(8,128)(2,1)}, bf16[4,128,256]{2,1,0:T(8,128)(2,1)S(1)}, u32[]{:S(2)}) copy-start(bf16[4,128,256]{2,1,0:T(8,128)(2,1)S(1)} %collective-permute-done.6.p0) | copy-start | bytes 786436
  69.4 23.3 %collective-permute-start.18 = (bf16[8,128,256]{2,1,0:T(8,128)(2,1)}, bf16[8,128,256]{2,1,0:T(8,128)(2,1)S(1)}, u32[]{:S(2)}, u32[]{:S(2)}) collective-permute-start(bf16[8,128,256]{2,1,0:T(8,128)(2,1)} %get-tuple-element.33), channel_id=1, source_target_pairs={{0,3},{1,0},{2,1},{3,2},{4,7},{5,4},{6,5},{7,6},{8,11},{9,8},{10,9... | collective-permute-start | bytes 1572872 | tf_op jit(solution)/shard_map/ppermute | solution.py:23
  80.5 12.3 %copy-start.5 = (bf16[8,128,256]{2,1,0:T(8,128)(2,1)}, bf16[8,128,256]{2,1,0:T(8,128)(2,1)S(1)}, u32[]{:S(2)}) copy-start(bf16[8,128,256]{2,1,0:T(8,128)(2,1)S(1)} %collective-permute-done.16.a) | copy-start | bytes 1572868
  80.5 17.3 %collective-permute-start.7 = (bf16[4,128,256]{2,1,0:T(8,128)(2,1)S(1)}, bf16[4,128,256]{2,1,0:T(8,128)(2,1)S(1)}, u32[]{:S(2)}, u32[]{:S(2)}) collective-permute-start(bf16[4,128,256]{2,1,0:T(8,128)(2,1)S(1)} %collective-permute-done.6.p0), channel_id=1, source_target_pairs={{0,3},{1,0},{2,1},{3,2},{4,7},{5,4},{6,5},{7,6},{8,11},{9,8},{10,9... | collective-permute-start | bytes 786440 | tf_op jit(solution)/shard_map/ppermute | solution.py:23
  92.7 0.8 copy-start.6
  92.7 8.4 %collective-permute-start.8 = (bf16[4,128,256]{2,1,0:T(8,128)(2,1)S(1)}, bf16[4,128,256]{2,1,0:T(8,128)(2,1)S(1)}, u32[]{:S(2)}, u32[]{:S(2)}) collective-permute-start(bf16[4,128,256]{2,1,0:T(8,128)(2,1)S(1)} %collective-permute-done.6.p0), channel_id=1, source_target_pairs={{0,2},{1,3},{2,0},{3,1},{4,6},{5,7},{6,4},{7,5},{8,10},{9,11},{10,... | collective-permute-start | bytes 786440 | tf_op jit(solution)/shard_map/ppermute | solution.py:23
  92.7 0.9 copy-start.7
  92.7 15.0 %collective-permute-start.9 = (bf16[4,128,256]{2,1,0:T(8,128)(2,1)S(1)}, bf16[4,128,256]{2,1,0:T(8,128)(2,1)}, u32[]{:S(2)}, u32[]{:S(2)}) collective-permute-start(bf16[4,128,256]{2,1,0:T(8,128)(2,1)S(1)} %collective-permute-done.6.p0), channel_id=1, source_target_pairs={{0,1},{1,2},{2,3},{3,0},{4,5},{5,6},{6,7},{7,4},{8,9},{9,10},{10,1... | collective-permute-start | bytes 786440 | tf_op jit(solution)/shard_map/ppermute | solution.py:23
  97.8 9.9 %copy-start.9 = (bf16[4,128,256]{2,1,0:T(8,128)(2,1)}, bf16[4,128,256]{2,1,0:T(8,128)(2,1)S(1)}, u32[]{:S(2)}) copy-start(bf16[4,128,256]{2,1,0:T(8,128)(2,1)S(1)} %collective-permute-done.7.p1) | copy-start | bytes 786436
  101.1 6.7 %copy-start.10 = (bf16[4,128,256]{2,1,0:T(8,128)(2,1)}, bf16[4,128,256]{2,1,0:T(8,128)(2,1)S(1)}, u32[]{:S(2)}) copy-start(bf16[4,128,256]{2,1,0:T(8,128)(2,1)S(1)} %collective-permute-done.8.p2) | copy-start | bytes 786436
  107.7 1.0 copy-start.4

commit v4 on v3

--- a/solution.py
+++ b/solution.py
@@ -100,7 +100,7 @@
                   lv, rv, go, dacc, acc, sems):
     copies = start_all([(lv_hbm, lv), (rv_hbm, rv), (go_hbm, go)], sems)
     own = deg_ref.shape[0]
-    cap = rrows.shape[1]
+    cap = rrows.shape[2]
     dacc[...] = jnp.zeros_like(dacc)
     acc[...] = jnp.zeros_like(acc)
     copies[0].wait()
@@ -115,7 +115,7 @@
     for_live(counts[0], add_rows(lv, 0, lambda t: lrows[t]))
     copies[1].wait()
     for r in range(rrows.shape[0]):
-        for_live(counts[r + 1], add_rows(rv, r * cap, lambda t: rrows[r, t]))
+        for_live(counts[r + 1], add_rows(rv, r * cap, lambda t: rrows[r, 0, t]))
     copies[2].wait()
     for b in range(own):
         degree = 1.0 + jnp.broadcast_to(jnp.sum(dacc[b], axis=1, keepdims=True), dacc.shape[1:])
@@ -129,14 +129,14 @@
     share = own_ref.shape[0]
     shift = me[0] * share
     backward_tiles(
-        counts[3], 2 * cap, rv, lambda t: rrows[2, t],
-        lambda t: lax.rem(rslots[2, t] - shift + cap, cap), gh_ref, acc,
+        counts[3], 2 * cap, rv, lambda t: rrows[2, 0, t],
+        lambda t: lax.rem(rslots[2, 0, t] - shift + cap, cap), gh_ref, acc,
     )
     split_out(acc, share, next_ref, far_ref, before_ref, own_ref)
     for r, out in ((1, out_b), (0, out_a)):
         acc[...] = jnp.zeros_like(acc)
         backward_tiles(
-            counts[r + 1], r * cap, rv, lambda t: rrows[r, t], lambda t: rslots[r, t], gh_ref, acc
+            counts[r + 1], r * cap, rv, lambda t: rrows[r, 0, t], lambda t: rslots[r, 0, t], gh_ref, acc
         )
         out[...] = acc[:cap].astype(BF16)
 
@@ -149,7 +149,7 @@
 
 
 def merge_kernel(counts, lrows, lcols, sends, me, lv_hbm, gh_hbm, a_hbm, b_hbm, c_hbm,
-                 next_ref, far_ref, before_ref, own_ref, lv, gh, got_a, got_b, got_c, acc, sems):
+                 right_ref, left_ref, keep_r_ref, keep_l_ref, own_ref, lv, gh, got_a, got_b, got_c, acc, sems):
     copies = start_all([(lv_hbm, lv), (gh_hbm, gh), (a_hbm, got_a), (b_hbm, got_b), (c_hbm, got_c)], sems)
     own = gh.shape[0]
     total = acc.shape[0] - 1
@@ -164,8 +164,26 @@
     wait_all(copies[2:])
     for r, (got, base) in enumerate(((got_a, 0), (got_b, 0), (got_c, me[0] * got_c.shape[0]))):
         for s in range(got.shape[0]):
-            acc[lax.rem(sends[r, base + s] - shift + total, total)] += got[s].astype(F32)
-    split_out(acc, own, next_ref, far_ref, before_ref, own_ref)
+            acc[lax.rem(sends[r, 0, base + s] - shift + total, total)] += got[s].astype(F32)
+    n, h = own, own // 2
+    right_ref[:h] = acc[2 * n:2 * n + h].astype(BF16)
+    right_ref[h:] = acc[n + h:2 * n].astype(BF16)
+    left_ref[:h] = acc[2 * n + h:3 * n].astype(BF16)
+    left_ref[h:] = acc[3 * n:3 * n + h].astype(BF16)
+    keep_r_ref[...] = acc[n:n + h]
+    keep_l_ref[...] = acc[3 * n + h:4 * n]
+    own_ref[...] = acc[:n]
+
+
+def combine_kernel(keep_r, keep_l, from_left, from_right, out_r, out_l):
+    out_r[...] = (keep_r[...] + from_left[...].astype(F32)).astype(BF16)
+    out_l[...] = (keep_l[...] + from_right[...].astype(F32)).astype(BF16)
+
+
+def relay_finish_kernel(own, a_left, a_right, b_left, b_right, out):
+    h = own.shape[0] // 2
+    out[:h] = (own[:h] + a_right[...].astype(F32) + b_left[...].astype(F32)).astype(BF16)
+    out[h:] = (own[h:] + a_left[...].astype(F32) + b_right[...].astype(F32)).astype(BF16)
 
 
 def finish_kernel(own, a, b, c, out):
@@ -185,7 +203,7 @@
 
     def begin(out, r, base, marks):
         def one(s, carry):
-            at = lax.rem(sends[r, base + s] - shift + total, total)
+            at = lax.rem(sends[r, 0, base + s] - shift + total, total)
             pltpu.make_async_copy(src.at[at], out.at[s], marks.at[s]).start()
             return carry
 
@@ -213,18 +231,18 @@
 def far_kernel(counts, rrows, rslots, me, a_hbm, b_hbm, p0, p1, p2, p3, rv_hbm, near_hbm, deg_hbm, w_ref,
                out_ref, src, vals, acc, deg, sems):
     total = out_ref.shape[0]
-    cap = rrows.shape[1]
+    cap = rrows.shape[2]
     pairs = [(near_hbm, acc.at[pl.ds(0, total)]), (rv_hbm, vals)]
     pairs += pieces_into((a_hbm, b_hbm, p0, p1, p2, p3), src, 0) + [(deg_hbm, deg)]
     wait_all(start_all(pairs, sems))
     for r in range(2):
         forward_tiles(
-            counts[r + 1], r * cap, vals, lambda t: rrows[r, t], lambda t: src[r * cap + rslots[r, t]], acc
+            counts[r + 1], r * cap, vals, lambda t: rrows[r, 0, t], lambda t: src[r * cap + rslots[r, 0, t]], acc
         )
     shift = me[0] * p0.shape[0]
     forward_tiles(
-        counts[3], 2 * cap, vals, lambda t: rrows[2, t],
-        lambda t: src[2 * cap + lax.rem(rslots[2, t] - shift + cap, cap)], acc,
+        counts[3], 2 * cap, vals, lambda t: rrows[2, 0, t],
+        lambda t: src[2 * cap + lax.rem(rslots[2, 0, t] - shift + cap, cap)], acc,
     )
     width = deg.shape[2]
     for b in range(total):
@@ -254,6 +272,7 @@
     slices = lax.axis_size("feat")
     part = own * slices
     share = cap // slices
+    half = own // 2
     log_nodes = lax.axis_size("node").bit_length() - 1
     bits = [r * log_nodes // rounds for r in range(rounds)]
     tail = (rows, width)
@@ -261,8 +280,7 @@
     me = lax.axis_index("feat").astype(jnp.int32).reshape(1)
     counts = tile_counts[0, 0]
     lrows, lcols = local_rows[0, 0], local_cols[0, 0]
-    rrows, rslots = remote_rows[0, 0], remote_slots[0, 0]
-    sends = send_blocks[0]
+    rrows, rslots, sends = (a.reshape(rounds, 1, cap) for a in (remote_rows, remote_slots, send_blocks))
     lv = local_values.reshape(lcap, rows, rows)
     rv = remote_values.reshape(rounds * cap, rows, rows)
     feats = features.reshape((own,) + tail)
@@ -325,13 +343,36 @@
     got_b = swapped(need_b, bits[1])
     got_a = swapped(need_a, bits[0])
 
-    to_next, to_far, to_before, own_part = call(
+    right, left, keep_r, keep_l, own_part = call(
         merge_kernel, (counts, lrows, lcols, sends, me), (lv, gh, got_back_a, got_back_b, got_back_c),
-        split_shapes(own),
+        [blocks(own, BF16), blocks(own, BF16), blocks(half, F32), blocks(half, F32), blocks(own, F32)],
         [tiles(lcap), room(own, BF16), room(cap, BF16), room(cap, BF16), room(share, BF16), room(part + 1, F32), sems(5)],
         lcap * tile_flops,
     )
-    grad_features = finished(own_part, scattered(to_next, to_far, to_before))
+    a_left = shifted(right, 1)
+    a_right = shifted(left, -1)
+
+    def halves(start):
+        return pl.BlockSpec((half,) + tail, lambda i: (start, 0, 0))
+
+    out_r, out_l = pl.pallas_call(
+        combine_kernel,
+        out_shape=(blocks(half, BF16), blocks(half, BF16)),
+        grid=(1,),
+        in_specs=[halves(0)] * 4,
+        out_specs=(halves(0), halves(0)),
+        cost_estimate=pl.CostEstimate(flops=0, bytes_accessed=8 * half * rows * width, transcendentals=0),
+    )(keep_r, keep_l, a_left, a_right)
+    b_left = shifted(out_r, 1)
+    b_right = shifted(out_l, -1)
+    grad_features = pl.pallas_call(
+        relay_finish_kernel,
+        out_shape=blocks(own, BF16),
+        grid=(1,),
+        in_specs=[pl.BlockSpec((own,) + tail, lambda i: (0, 0, 0)), halves(1), halves(1), halves(0), halves(0)],
+        out_specs=pl.BlockSpec((own,) + tail, lambda i: (0, 0, 0)),
+        cost_estimate=pl.CostEstimate(flops=0, bytes_accessed=10 * own * rows * width, transcendentals=0),
+    )(own_part, a_left, a_right, b_left, b_right)
 
     output = call(
         far_kernel, (counts, rrows, rslots, me),

time: 116 us -> 115 us (level)
  the two profiles are of different devices: /device:TPU:1 before, /device:TPU:225 now
where the time goes in v4:
time: 115 us
  starting transfers between devices  39.2 us (34%)
  waiting for transfers between devices  39.1 us (34%)
  Pallas kernels  30.7 us (27%)
  local copies, waits for them, and re-layouts  5.29 us (5%)
    ppermute x14, waiting for transfers between devices, shifted(): lax.ppermute(array, 'feat', [(i, (i + step) % size) for i in range(size)])  35.8 us
    ppermute x14, starting transfers between devices, shifted(): lax.ppermute(array, 'feat', [(i, (i + step) % size) for i in range(size)])  26.7 us
    pallas_call x5, Pallas kernels, call(): pl.pallas_call(kernel, out_shape=tuple(outs), in_specs=[SMEM] * len(scala...  26 us
    ppermute x6, starting transfers between devices, swapped(): lax.ppermute(array, 'node', [(i, i ^ 1 << bit) for i in range(lax.axis_si...  12.5 us
    unnamed x30, local copies, waits for them, and re-layouts  3.74 us
    ppermute x6, waiting for transfers between devices, swapped(): lax.ppermute(array, 'node', [(i, i ^ 1 << bit) for i in range(lax.axis_si...  3.33 us
    pallas_call x1, Pallas kernels, body(): pl.pallas_call(relay_finish_kernel, out_shape=blocks(own, BF16), grid=(1,...  2.45 us
  transfers between devices with their start and end apart: 20, of which 9 were waited for; matrix products, arithmetic and copies ran while one was open for 1% of the time, Pallas kernels for 15%

profile of v4, /device:TPU:225, one launch (start us, length us, event | category | flops | bytes accessed | tf_op | source)
XLA Modules:
  0.0 115.2 jit_solution(10993087352135259985)
XLA Ops:
  0.6 7.2 %shard_map.123 = (f32[8,128,128]{2,1,0:T(8,128)}, bf16[8,128,256]{2,1,0:T(8,128)(2,1)}, bf16[4,128,256]{2,1,0:T(8,128)(2,1)}, bf16[4,128,256]{2,1,0:T(8,128)(2,1...) custom-call(s32[4]{0:T(128)} %bitcast.21, ...), custom_call_target="tpu_custom_call" | custom-call | flops 402653184 | bytes 7733248 | tf_op jit(solution)/shard_map/pallas_call | solution.py:301
  7.9 0.5 collective-permute-start.10
  8.3 4.7 %collective-permute-start.11 = (bf16[16,128,256]{2,1,0:T(8,128)(2,1)}, bf16[16,128,256]{2,1,0:T(8,128)(2,1)S(1)}, u32[]{:S(2)}, u32[]{:S(2)}) collective-permute-start(bf16[16,128,256]{2,1,0:T(8,128)(2,1)} %get-tuple-element.28), channel_id=1, source_target_pairs={{0,16},{4,20},{8,24},{12,28},{16,0},{20,4},{24,8},{28,12},{32,48},... | collective-permute-start | bytes 3145736 | tf_op jit(solution)/shard_map/ppermute | solution.py:18
  13.0 0.9 collective-permute-start.12
  13.9 1.3 %collective-permute-start.13 = (bf16[4,128,256]{2,1,0:T(8,128)(2,1)}, bf16[4,128,256]{2,1,0:T(8,128)(2,1)}, u32[]{:S(2)}, u32[]{:S(2)}) collective-permute-start(bf16[4,128,256]{2,1,0:T(8,128)(2,1)} %get-tuple-element.31), channel_id=1, source_target_pairs={{0,2},{1,3},{2,0},{3,1},{4,6},{5,7},{6,4},{7,5},{8,10},{9,11},{10,... | collective-permute-start | bytes 786440 | tf_op jit(solution)/shard_map/ppermute | solution.py:23
  15.2 1.1 collective-permute-start.1
  16.3 6.1 %collective-permute-done.12.a = bf16[4,128,256]{2,1,0:T(8,128)(2,1)S(1)} collective-permute-done((bf16[4,128,256]{2,1,0:T(8,128)(2,1)}, bf16[4,128,256]{2,1,0:T(8,128)(2,1)S(1)}, u32[]{:S(2)}, u32[]{:S(2)}) %collective-permute-start.12) | collective-permute-done | bytes 262176 | tf_op jit(solution)/shard_map/ppermute | solution.py:23
  22.4 4.8 %collective-permute-done.13.b = bf16[4,128,256]{2,1,0:T(8,128)(2,1)} collective-permute-done((bf16[4,128,256]{2,1,0:T(8,128)(2,1)}, bf16[4,128,256]{2,1,0:T(8,128)(2,1)}, u32[]{:S(2)}, u32[]{:S(2)}) %collective-permute-start.13) | collective-permute-done | bytes 262176 | tf_op jit(solution)/shard_map/ppermute | solution.py:23
  27.2 0.0 collective-permute-start.14
  27.2 7.3 %collective-permute-done.14.c = bf16[4,128,256]{2,1,0:T(8,128)(2,1)} collective-permute-done((bf16[4,128,256]{2,1,0:T(8,128)(2,1)}, bf16[4,128,256]{2,1,0:T(8,128)(2,1)}, u32[]{:S(2)}, u32[]{:S(2)}) %collective-permute-start.14) | collective-permute-done | bytes 262176 | tf_op jit(solution)/shard_map/ppermute | solution.py:23
  34.6 2.1 %shard_map.125 = bf16[4,128,256]{2,1,0:T(8,128)(2,1)} custom-call(f32[4,128,256]{2,1,0:T(8,128)} %get-tuple-element.29.own, bf16[4,128,256]{2,1,0:T(8,128)(2,1)} %copy-done.14, bf16[4,128,256]{2,1,0:T(8,128)(2,1)} %collective-permute-done.13.b, bf16[4,128,256]{2,1,0:T(8,128)(2,1)} %collective-permute-done.14.c), custom_call_target="tpu_custom_call" | custom-call | bytes 1572864 | tf_op jit(solution)/shard_map/pallas_call | solution.py:301
  36.6 4.9 %collective-permute-start.15 = (bf16[4,128,256]{2,1,0:T(8,128)(2,1)}, bf16[4,128,256]{2,1,0:T(8,128)(2,1)S(1)}, u32[]{:S(2)}, u32[]{:S(2)}) collective-permute-start(bf16[4,128,256]{2,1,0:T(8,128)(2,1)} %shard_map.125), channel_id=1, source_target_pairs={{0,64},{4,68},{8,72},{12,76},{16,80},{20,84},{24,88},{28,92},{32,9... | collective-permute-start | bytes 786440 | tf_op jit(solution)/shard_map/ppermute | solution.py:18
  41.5 0.0 collective-permute-done.1.p4
  41.5 0.8 slice.8
  42.3 6.4 %collective-permute-start.2 = (bf16[4,128,256]{2,1,0:T(8,128)(2,1)}, bf16[4,128,256]{2,1,0:T(8,128)(2,1)}, u32[]{:S(2)}, u32[]{:S(2)}) collective-permute-start(bf16[4,128,256]{2,1,0:T(8,128)(2,1)} %slice.8), channel_id=1, source_target_pairs={{0,1},{1,2},{2,3},{3,0},{4,5},{5,6},{6,7},{7,4},{8,9},{9,10},{10,1... | collective-permute-start | bytes 786440 | tf_op jit(solution)/shard_map/ppermute | solution.py:23
  48.7 0.0 collective-permute-done.p1
  48.7 0.8 slice.9
  49.5 0.0 collective-permute-start.3
  49.5 0.0 collective-permute-done.15.c_hbm
  49.5 0.0 collective-permute-done.10.a_hbm
  49.5 0.7 copy-done.11
  50.2 0.4 copy-done.6
  50.6 0.3 copy-done.7
  50.9 5.5 %shard_map.126 = (bf16[8,128,256]{2,1,0:T(8,128)(2,1)}, bf16[8,128,256]{2,1,0:T(8,128)(2,1)}, f32[4,128,256]{2,1,0:T(8,128)}, f32[4,128,256]{2,1,0:T(8,128)}, f32[8,128,256]{2,1,0:T(8,128)}) custom-call(s32[4]{0:T(128)} %bitcast.22, s32[32]{0:T(128)} %bitcast.32, s32[32]{0:T(128)} %bitcast.34, s32[3,1,16]{2,1,0:T(1,128)} %bitcast.29, s32[1]{0:T(128)} %bitcast.3.me, ...), custom_call_target="tpu_custom_call" | custom-call | flops 268435456 | bytes 7077888 | tf_op jit(solution)/shard_map/pallas_call | solution.py:301
  56.5 7.7 %collective-permute-start.16 = (bf16[8,128,256]{2,1,0:T(8,128)(2,1)}, bf16[8,128,256]{2,1,0:T(8,128)(2,1)S(1)}, u32[]{:S(2)}, u32[]{:S(2)}) collective-permute-start(bf16[8,128,256]{2,1,0:T(8,128)(2,1)} %get-tuple-element.34), channel_id=1, source_target_pairs={{0,1},{1,2},{2,3},{3,0},{4,5},{5,6},{6,7},{7,4},{8,9},{9,10},{10,1... | collective-permute-start | bytes 1572872 | tf_op jit(solution)/shard_map/ppermute | solution.py:23
  64.2 3.2 %collective-permute-start.17 = (bf16[8,128,256]{2,1,0:T(8,128)(2,1)}, bf16[8,128,256]{2,1,0:T(8,128)(2,1)S(1)}, u32[]{:S(2)}, u32[]{:S(2)}) collective-permute-start(bf16[8,128,256]{2,1,0:T(8,128)(2,1)} %get-tuple-element.35), channel_id=1, source_target_pairs={{0,3},{1,0},{2,1},{3,2},{4,7},{5,4},{6,5},{7,6},{8,11},{9,8},{10,9... | collective-permute-start | bytes 1572872 | tf_op jit(solution)/shard_map/ppermute | solution.py:23
  67.4 5.1 %shard_map.122 = (bf16[16,128,256]{2,1,0:T(8,128)(2,1)}, bf16[16,128,256]{2,1,0:T(8,128)(2,1)}, bf16[4,128,256]{2,1,0:T(8,128)(2,1)}, f32[8,128,256]{2,1,0:T(8,128)}) custom-call(s32[4]{0:T(128)} %bitcast.23, s32[32]{0:T(128)} %bitcast.33, s32[32]{0:T(128)} %bitcast.35, s32[3,1,16]{2,1,0:T(1,128)} %bitcast.30, s32[1]{0:T(128)} %bitcast.3.me, ...), custom_call_target="tpu_custom_call" | custom-call | flops 268435456 | bytes 6553600 | tf_op jit(solution)/shard_map/pallas_call | solution.py:301
  72.5 0.3 collective-permute-start.4
  72.8 2.2 %collective-permute-start.5 = (bf16[16,128,256]{2,1,0:T(8,128)(2,1)}, bf16[16,128,256]{2,1,0:T(8,128)(2,1)S(1)}, u32[]{:S(2)}, u32[]{:S(2)}) collective-permute-start(bf16[16,128,256]{2,1,0:T(8,128)(2,1)} %get-tuple-element.22), channel_id=1, source_target_pairs={{0,16},{4,20},{8,24},{12,28},{16,0},{20,4},{24,8},{28,12},{32,48},... | collective-permute-start | bytes 3145736 | tf_op jit(solution)/shard_map/ppermute | solution.py:18
  75.0 4.4 %collective-permute-done.16.from_left.a_left = bf16[8,128,256]{2,1,0:T(8,128)(2,1)S(1)} collective-permute-done((bf16[8,128,256]{2,1,0:T(8,128)(2,1)}, bf16[8,128,256]{2,1,0:T(8,128)(2,1)S(1)}, u32[]{:S(2)}, u32[]{:S(2)}) %collective-permute-start.16) | collective-permute-done | bytes 524320 | tf_op jit(solution)/shard_map/ppermute | solution.py:23
  79.4 0.8 copy-done
  80.2 0.2 copy-done.1
  80.4 2.2 %shard_map.127 = (bf16[4,128,256]{2,1,0:T(8,128)(2,1)}, bf16[4,128,256]{2,1,0:T(8,128)(2,1)}) custom-call(f32[4,128,256]{2,1,0:T(8,128)} %get-tuple-element.36.keep_r, f32[4,128,256]{2,1,0:T(8,128)} %get-tuple-element.37.keep_l, bf16[8,128,256]{2,1,0:T(8,128)(2,1)} %copy-done, bf16[8,128,256]{2,1,0:T(8,128)(2,1)} %copy-done.1), custom_call_target="tpu_custom_call" | custom-call | bytes 1048576 | tf_op jit(solution)/shard_map/pallas_call | solution.py:358
  82.6 1.2 %collective-permute-start.18 = (bf16[4,128,256]{2,1,0:T(8,128)(2,1)}, bf16[4,128,256]{2,1,0:T(8,128)(2,1)S(1)}, u32[]{:S(2)}, u32[]{:S(2)}) collective-permute-start(bf16[4,128,256]{2,1,0:T(8,128)(2,1)} %get-tuple-element.38), channel_id=1, source_target_pairs={{0,1},{1,2},{2,3},{3,0},{4,5},{5,6},{6,7},{7,4},{8,9},{9,10},{10,1... | collective-permute-start | bytes 786440 | tf_op jit(solution)/shard_map/ppermute | solution.py:23
  83.8 1.7 %collective-permute-start.19 = (bf16[4,128,256]{2,1,0:T(8,128)(2,1)}, bf16[4,128,256]{2,1,0:T(8,128)(2,1)}, u32[]{:S(2)}, u32[]{:S(2)}) collective-permute-start(bf16[4,128,256]{2,1,0:T(8,128)(2,1)} %get-tuple-element.39), channel_id=1, source_target_pairs={{0,3},{1,0},{2,1},{3,2},{4,7},{5,4},{6,5},{7,6},{8,11},{9,8},{10,9... | collective-permute-start | bytes 786440 | tf_op jit(solution)/shard_map/ppermute | solution.py:23
  85.5 3.3 %collective-permute-done.6.p0 = bf16[4,128,256]{2,1,0:T(8,128)(2,1)S(1)} collective-permute-done((bf16[4,128,256]{2,1,0:T(8,128)(2,1)}, bf16[4,128,256]{2,1,0:T(8,128)(2,1)S(1)}, u32[]{:S(2)}, u32[]{:S(2)}) %collective-permute-start.6) | collective-permute-done | bytes 262176 | tf_op jit(solution)/shard_map/ppermute | solution.py:18
  88.8 1.4 %collective-permute-start.7 = (bf16[4,128,256]{2,1,0:T(8,128)(2,1)S(1)}, bf16[4,128,256]{2,1,0:T(8,128)(2,1)S(1)}, u32[]{:S(2)}, u32[]{:S(2)}) collective-permute-start(bf16[4,128,256]{2,1,0:T(8,128)(2,1)S(1)} %collective-permute-done.6.p0), channel_id=1, source_target_pairs={{0,3},{1,0},{2,1},{3,2},{4,7},{5,4},{6,5},{7,6},{8,11},{9,8},{10,9... | collective-permute-start | bytes 786440 | tf_op jit(solution)/shard_map/ppermute | solution.py:23
  90.2 2.1 %collective-permute-done.18.b_left = bf16[4,128,256]{2,1,0:T(8,128)(2,1)S(1)} collective-permute-done((bf16[4,128,256]{2,1,0:T(8,128)(2,1)}, bf16[4,128,256]{2,1,0:T(8,128)(2,1)S(1)}, u32[]{:S(2)}, u32[]{:S(2)}) %collective-permute-start.18) | collective-permute-done | bytes 262176 | tf_op jit(solution)/shard_map/ppermute | solution.py:23
  92.2 1.1 collective-permute-start.8
  93.4 0.7 collective-permute-start.9
  94.1 2.5 %shard_map.128 = bf16[8,128,256]{2,1,0:T(8,128)(2,1)} custom-call(f32[8,128,256]{2,1,0:T(8,128)} %get-tuple-element.33.own, bf16[8,128,256]{2,1,0:T(8,128)(2,1)} %copy-done, bf16[8,128,256]{2,1,0:T(8,128)(2,1)} %copy-done.1, bf16[4,128,256]{2,1,0:T(8,128)(2,1)} %copy-done.13, bf16[4,128,256]{2,1,0:T(8,128)(2,1)} %collective-permute-done.19.b_right), custom_call_target="tpu_custom_call" | custom-call | bytes 2621440 | tf_op jit(solution)/shard_map/pallas_call | solution.py:368
  96.6 0.6 collective-permute-done.7.p1
  97.1 3.8 %collective-permute-done.8.p2 = bf16[4,128,256]{2,1,0:T(8,128)(2,1)S(1)} collective-permute-done((bf16[4,128,256]{2,1,0:T(8,128)(2,1)S(1)}, bf16[4,128,256]{2,1,0:T(8,128)(2,1)S(1)}, u32[]{:S(2)}, u32[]{:S(2)}) %collective-permute-start.8) | collective-permute-done | bytes 262176 | tf_op jit(solution)/shard_map/ppermute | solution.py:23
  101.0 6.6 %collective-permute-done.9.p3 = bf16[4,128,256]{2,1,0:T(8,128)(2,1)S(1)} collective-permute-done((bf16[4,128,256]{2,1,0:T(8,128)(2,1)S(1)}, bf16[4,128,256]{2,1,0:T(8,128)(2,1)S(1)}, u32[]{:S(2)}, u32[]{:S(2)}) %collective-permute-start.9) | collective-permute-done | bytes 262176 | tf_op jit(solution)/shard_map/ppermute | solution.py:23
  107.6 0.6 copy-done.12
  108.3 0.4 copy-done.4
  108.7 0.3 copy-done.5
  109.0 6.1 %shard_map.124 = bf16[8,128,256]{2,1,0:T(8,128)(2,1)} custom-call(s32[4]{0:T(128)} %bitcast.24, s32[3,1,16]{2,1,0:T(1,128)} %bitcast.26, s32[3,1,16]{2,1,0:T(1,128)} %bitcast.28, s32[1]{0:T(128)} %bitcast.3.me, bf16[16,128,256]{2,1,0:T(8,128)(2,1)} %copy-done.4, bf16[16,128,256]{2,1,0:T(8,128)(2,1)} %copy-done.5, bf16[4,128,256]{2,1,0:T(8,128)(2,1)} %copy-done.8, ...), custom_call_target="tpu_custom_call" | custom-call | flops 402653184 | bytes 6946816 | tf_op jit(solution)/shard_map/pallas_call | solution.py:301
  (31 shorter events, 0.1 us)
Async XLA Ops:
  7.9 41.6 %collective-permute-start.10 = (bf16[16,128,256]{2,1,0:T(8,128)(2,1)}, bf16[16,128,256]{2,1,0:T(8,128)(2,1)S(1)}, u32[]{:S(2)}, u32[]{:S(2)}) collective-permute-start(bf16[16,128,256]{2,1,0:T(8,128)(2,1)} %get-tuple-element.27), channel_id=1, source_target_pairs={{0,4},{4,0},{8,12},{12,8},{16,20},{20,16},{24,28},{28,24},{32,36},... | collective-permute-start | bytes 3145736 | tf_op jit(solution)/shard_map/ppermute | solution.py:18
  8.3 41.2 %collective-permute-start.11 = (bf16[16,128,256]{2,1,0:T(8,128)(2,1)}, bf16[16,128,256]{2,1,0:T(8,128)(2,1)S(1)}, u32[]{:S(2)}, u32[]{:S(2)}) collective-permute-start(bf16[16,128,256]{2,1,0:T(8,128)(2,1)} %get-tuple-element.28), channel_id=1, source_target_pairs={{0,16},{4,20},{8,24},{12,28},{16,0},{20,4},{24,8},{28,12},{32,48},... | collective-permute-start | bytes 3145736 | tf_op jit(solution)/shard_map/ppermute | solution.py:18
  13.0 9.4 %collective-permute-start.12 = (bf16[4,128,256]{2,1,0:T(8,128)(2,1)}, bf16[4,128,256]{2,1,0:T(8,128)(2,1)S(1)}, u32[]{:S(2)}, u32[]{:S(2)}) collective-permute-start(bf16[4,128,256]{2,1,0:T(8,128)(2,1)} %get-tuple-element.30), channel_id=1, source_target_pairs={{0,1},{1,2},{2,3},{3,0},{4,5},{5,6},{6,7},{7,4},{8,9},{9,10},{10,1... | collective-permute-start | bytes 786440 | tf_op jit(solution)/shard_map/ppermute | solution.py:23
  13.9 13.3 %collective-permute-start.13 = (bf16[4,128,256]{2,1,0:T(8,128)(2,1)}, bf16[4,128,256]{2,1,0:T(8,128)(2,1)}, u32[]{:S(2)}, u32[]{:S(2)}) collective-permute-start(bf16[4,128,256]{2,1,0:T(8,128)(2,1)} %get-tuple-element.31), channel_id=1, source_target_pairs={{0,2},{1,3},{2,0},{3,1},{4,6},{5,7},{6,4},{7,5},{8,10},{9,11},{10,... | collective-permute-start | bytes 786440 | tf_op jit(solution)/shard_map/ppermute | solution.py:23
  15.2 26.3 %collective-permute-start.1 = (bf16[8,128,256]{2,1,0:T(8,128)(2,1)}, bf16[8,128,256]{2,1,0:T(8,128)(2,1)S(1)}, u32[]{:S(2)}, u32[]{:S(2)}) collective-permute-start(bf16[8,128,256]{2,1,0:T(8,128)(2,1)} %bitcast.7.p0), channel_id=1, source_target_pairs={{0,1},{1,2},{2,3},{3,0},{4,5},{5,6},{6,7},{7,4},{8,9},{9,10},{10,1... | collective-permute-start | bytes 1572872 | tf_op jit(solution)/shard_map/ppermute | solution.py:23
  22.4 12.1 %copy-start.14 = (bf16[4,128,256]{2,1,0:T(8,128)(2,1)}, bf16[4,128,256]{2,1,0:T(8,128)(2,1)S(1)}, u32[]{:S(2)}) copy-start(bf16[4,128,256]{2,1,0:T(8,128)(2,1)S(1)} %collective-permute-done.12.a) | copy-start | bytes 786436
  22.4 26.3 %collective-permute-start = (bf16[8,128,256]{2,1,0:T(8,128)(2,1)}, bf16[8,128,256]{2,1,0:T(8,128)(2,1)S(1)}, u32[]{:S(2)}, u32[]{:S(2)}) collective-permute-start(bf16[8,128,256]{2,1,0:T(8,128)(2,1)} %bitcast.7.p0), channel_id=1, source_target_pairs={{0,3},{1,0},{2,1},{3,2},{4,7},{5,4},{6,5},{7,6},{8,11},{9,8},{10,9... | collective-permute-start | bytes 1572872 | tf_op jit(solution)/shard_map/ppermute | solution.py:23
  27.2 7.3 %collective-permute-start.14 = (bf16[4,128,256]{2,1,0:T(8,128)(2,1)}, bf16[4,128,256]{2,1,0:T(8,128)(2,1)}, u32[]{:S(2)}, u32[]{:S(2)}) collective-permute-start(bf16[4,128,256]{2,1,0:T(8,128)(2,1)} %get-tuple-element.32), channel_id=1, source_target_pairs={{0,3},{1,0},{2,1},{3,2},{4,7},{5,4},{6,5},{7,6},{8,11},{9,8},{10,9... | collective-permute-start | bytes 786440 | tf_op jit(solution)/shard_map/ppermute | solution.py:23
  36.6 12.9 %collective-permute-start.15 = (bf16[4,128,256]{2,1,0:T(8,128)(2,1)}, bf16[4,128,256]{2,1,0:T(8,128)(2,1)S(1)}, u32[]{:S(2)}, u32[]{:S(2)}) collective-permute-start(bf16[4,128,256]{2,1,0:T(8,128)(2,1)} %shard_map.125), channel_id=1, source_target_pairs={{0,64},{4,68},{8,72},{12,76},{16,80},{20,84},{24,88},{28,92},{32,9... | collective-permute-start | bytes 786440 | tf_op jit(solution)/shard_map/ppermute | solution.py:18
  41.5 15.0 %copy-start.2 = (bf16[8,128,256]{2,1,0:T(8,128)(2,1)}, bf16[8,128,256]{2,1,0:T(8,128)(2,1)S(1)}, u32[]{:S(2)}) copy-start(bf16[8,128,256]{2,1,0:T(8,128)(2,1)S(1)} %collective-permute-done.1.p4) | copy-start | bytes 1572868
  42.3 25.1 %collective-permute-start.2 = (bf16[4,128,256]{2,1,0:T(8,128)(2,1)}, bf16[4,128,256]{2,1,0:T(8,128)(2,1)}, u32[]{:S(2)}, u32[]{:S(2)}) collective-permute-start(bf16[4,128,256]{2,1,0:T(8,128)(2,1)} %slice.8), channel_id=1, source_target_pairs={{0,1},{1,2},{2,3},{3,0},{4,5},{5,6},{6,7},{7,4},{8,9},{9,10},{10,1... | collective-permute-start | bytes 786440 | tf_op jit(solution)/shard_map/ppermute | solution.py:23
  48.7 7.8 %copy-start.3 = (bf16[8,128,256]{2,1,0:T(8,128)(2,1)}, bf16[8,128,256]{2,1,0:T(8,128)(2,1)S(1)}, u32[]{:S(2)}) copy-start(bf16[8,128,256]{2,1,0:T(8,128)(2,1)S(1)} %collective-permute-done.p1) | copy-start | bytes 1572868
  49.5 17.9 %collective-permute-start.3 = (bf16[4,128,256]{2,1,0:T(8,128)(2,1)}, bf16[4,128,256]{2,1,0:T(8,128)(2,1)}, u32[]{:S(2)}, u32[]{:S(2)}) collective-permute-start(bf16[4,128,256]{2,1,0:T(8,128)(2,1)} %slice.9), channel_id=1, source_target_pairs={{0,3},{1,0},{2,1},{3,2},{4,7},{5,4},{6,5},{7,6},{8,11},{9,8},{10,9... | collective-permute-start | bytes 786440 | tf_op jit(solution)/shard_map/ppermute | solution.py:23
  49.5 0.7 copy-start.11
  49.5 1.1 copy-start.6
  49.5 1.4 %copy-start.7 = (bf16[16,128,256]{2,1,0:T(8,128)(2,1)}, bf16[16,128,256]{2,1,0:T(8,128)(2,1)S(1)}, u32[]{:S(2)}) copy-start(bf16[16,128,256]{2,1,0:T(8,128)(2,1)S(1)} %collective-permute-done.11.b_hbm) | copy-start | bytes 3145732
  56.5 23.0 %collective-permute-start.16 = (bf16[8,128,256]{2,1,0:T(8,128)(2,1)}, bf16[8,128,256]{2,1,0:T(8,128)(2,1)S(1)}, u32[]{:S(2)}, u32[]{:S(2)}) collective-permute-start(bf16[8,128,256]{2,1,0:T(8,128)(2,1)} %get-tuple-element.34), channel_id=1, source_target_pairs={{0,1},{1,2},{2,3},{3,0},{4,5},{5,6},{6,7},{7,4},{8,9},{9,10},{10,1... | collective-permute-start | bytes 1572872 | tf_op jit(solution)/shard_map/ppermute | solution.py:23
  64.2 15.3 %collective-permute-start.17 = (bf16[8,128,256]{2,1,0:T(8,128)(2,1)}, bf16[8,128,256]{2,1,0:T(8,128)(2,1)S(1)}, u32[]{:S(2)}, u32[]{:S(2)}) collective-permute-start(bf16[8,128,256]{2,1,0:T(8,128)(2,1)} %get-tuple-element.35), channel_id=1, source_target_pairs={{0,3},{1,0},{2,1},{3,2},{4,7},{5,4},{6,5},{7,6},{8,11},{9,8},{10,9... | collective-permute-start | bytes 1572872 | tf_op jit(solution)/shard_map/ppermute | solution.py:23
  72.5 35.1 %collective-permute-start.4 = (bf16[16,128,256]{2,1,0:T(8,128)(2,1)}, bf16[16,128,256]{2,1,0:T(8,128)(2,1)S(1)}, u32[]{:S(2)}, u32[]{:S(2)}) collective-permute-start(bf16[16,128,256]{2,1,0:T(8,128)(2,1)} %get-tuple-element.21), channel_id=1, source_target_pairs={{0,4},{4,0},{8,12},{12,8},{16,20},{20,16},{24,28},{28,24},{32,36},... | collective-permute-start | bytes 3145736 | tf_op jit(solution)/shard_map/ppermute | solution.py:18
  72.8 34.8 %collective-permute-start.5 = (bf16[16,128,256]{2,1,0:T(8,128)(2,1)}, bf16[16,128,256]{2,1,0:T(8,128)(2,1)S(1)}, u32[]{:S(2)}, u32[]{:S(2)}) collective-permute-start(bf16[16,128,256]{2,1,0:T(8,128)(2,1)} %get-tuple-element.22), channel_id=1, source_target_pairs={{0,16},{4,20},{8,24},{12,28},{16,0},{20,4},{24,8},{28,12},{32,48},... | collective-permute-start | bytes 3145736 | tf_op jit(solution)/shard_map/ppermute | solution.py:18
  75.0 13.8 %collective-permute-start.6 = (bf16[4,128,256]{2,1,0:T(8,128)(2,1)}, bf16[4,128,256]{2,1,0:T(8,128)(2,1)S(1)}, u32[]{:S(2)}, u32[]{:S(2)}) collective-permute-start(bf16[4,128,256]{2,1,0:T(8,128)(2,1)} %get-tuple-element.23), channel_id=1, source_target_pairs={{0,64},{4,68},{8,72},{12,76},{16,80},{20,84},{24,88},{28,92},{32,9... | collective-permute-start | bytes 786440 | tf_op jit(solution)/shard_map/ppermute | solution.py:18
  79.4 0.8 copy-start
  79.4 1.0 copy-start.1
  82.6 9.6 %collective-permute-start.18 = (bf16[4,128,256]{2,1,0:T(8,128)(2,1)}, bf16[4,128,256]{2,1,0:T(8,128)(2,1)S(1)}, u32[]{:S(2)}, u32[]{:S(2)}) collective-permute-start(bf16[4,128,256]{2,1,0:T(8,128)(2,1)} %get-tuple-element.38), channel_id=1, source_target_pairs={{0,1},{1,2},{2,3},{3,0},{4,5},{5,6},{6,7},{7,4},{8,9},{9,10},{10,1... | collective-permute-start | bytes 786440 | tf_op jit(solution)/shard_map/ppermute | solution.py:23
  83.8 9.6 %collective-permute-start.19 = (bf16[4,128,256]{2,1,0:T(8,128)(2,1)}, bf16[4,128,256]{2,1,0:T(8,128)(2,1)}, u32[]{:S(2)}, u32[]{:S(2)}) collective-permute-start(bf16[4,128,256]{2,1,0:T(8,128)(2,1)} %get-tuple-element.39), channel_id=1, source_target_pairs={{0,3},{1,0},{2,1},{3,2},{4,7},{5,4},{6,5},{7,6},{8,11},{9,8},{10,9... | collective-permute-start | bytes 786440 | tf_op jit(solution)/shard_map/ppermute | solution.py:23
  88.8 7.8 %copy-start.8 = (bf16[4,128,256]{2,1,0:T(8,128)(2,1)}, bf16[4,128,256]{2,1,0:T(8,128)(2,1)S(1)}, u32[]{:S(2)}) copy-start(bf16[4,128,256]{2,1,0:T(8,128)(2,1)S(1)} %collective-permute-done.6.p0) | copy-start | bytes 786436
  88.8 8.3 %collective-permute-start.7 = (bf16[4,128,256]{2,1,0:T(8,128)(2,1)S(1)}, bf16[4,128,256]{2,1,0:T(8,128)(2,1)S(1)}, u32[]{:S(2)}, u32[]{:S(2)}) collective-permute-start(bf16[4,128,256]{2,1,0:T(8,128)(2,1)S(1)} %collective-permute-done.6.p0), channel_id=1, source_target_pairs={{0,3},{1,0},{2,1},{3,2},{4,7},{5,4},{6,5},{7,6},{8,11},{9,8},{10,9... | collective-permute-start | bytes 786440 | tf_op jit(solution)/shard_map/ppermute | solution.py:23
  92.2 1.9 %copy-start.13 = (bf16[4,128,256]{2,1,0:T(8,128)(2,1)}, bf16[4,128,256]{2,1,0:T(8,128)(2,1)S(1)}, u32[]{:S(2)}) copy-start(bf16[4,128,256]{2,1,0:T(8,128)(2,1)S(1)} %collective-permute-done.18.b_left) | copy-start | bytes 786436
  92.2 8.7 %collective-permute-start.8 = (bf16[4,128,256]{2,1,0:T(8,128)(2,1)S(1)}, bf16[4,128,256]{2,1,0:T(8,128)(2,1)S(1)}, u32[]{:S(2)}, u32[]{:S(2)}) collective-permute-start(bf16[4,128,256]{2,1,0:T(8,128)(2,1)S(1)} %collective-permute-done.6.p0), channel_id=1, source_target_pairs={{0,2},{1,3},{2,0},{3,1},{4,6},{5,7},{6,4},{7,5},{8,10},{9,11},{10,... | collective-permute-start | bytes 786440 | tf_op jit(solution)/shard_map/ppermute | solution.py:23
  93.4 14.2 %collective-permute-start.9 = (bf16[4,128,256]{2,1,0:T(8,128)(2,1)S(1)}, bf16[4,128,256]{2,1,0:T(8,128)(2,1)S(1)}, u32[]{:S(2)}, u32[]{:S(2)}) collective-permute-start(bf16[4,128,256]{2,1,0:T(8,128)(2,1)S(1)} %collective-permute-done.6.p0), channel_id=1, source_target_pairs={{0,1},{1,2},{2,3},{3,0},{4,5},{5,6},{6,7},{7,4},{8,9},{9,10},{10,1... | collective-permute-start | bytes 786440 | tf_op jit(solution)/shard_map/ppermute | solution.py:23
  97.1 10.5 %copy-start.9 = (bf16[4,128,256]{2,1,0:T(8,128)(2,1)}, bf16[4,128,256]{2,1,0:T(8,128)(2,1)S(1)}, u32[]{:S(2)}) copy-start(bf16[4,128,256]{2,1,0:T(8,128)(2,1)S(1)} %collective-permute-done.7.p1) | copy-start | bytes 786436
  101.0 6.7 %copy-start.10 = (bf16[4,128,256]{2,1,0:T(8,128)(2,1)}, bf16[4,128,256]{2,1,0:T(8,128)(2,1)S(1)}, u32[]{:S(2)}) copy-start(bf16[4,128,256]{2,1,0:T(8,128)(2,1)S(1)} %collective-permute-done.8.p2) | copy-start | bytes 786436
  107.6 0.7 copy-start.12
  107.6 1.1 copy-start.4
  107.6 1.4 %copy-start.5 = (bf16[16,128,256]{2,1,0:T(8,128)(2,1)}, bf16[16,128,256]{2,1,0:T(8,128)(2,1)S(1)}, u32[]{:S(2)}) copy-start(bf16[16,128,256]{2,1,0:T(8,128)(2,1)S(1)} %collective-permute-done.5.b_hbm) | copy-start | bytes 3145732

commit v5 on v4

--- a/solution.py
+++ b/solution.py
@@ -96,7 +96,7 @@
 
 
 def degree_kernel(counts, lrows, rrows, rslots, me, lv_hbm, rv_hbm, go_hbm, w_ref,
-                  deg_ref, gh_ref, next_ref, far_ref, before_ref, own_ref, out_b, out_a,
+                  deg_ref, gh_ref, next_ref, far_ref, before_ref, own_ref,
                   lv, rv, go, dacc, acc, sems):
     copies = start_all([(lv_hbm, lv), (rv_hbm, rv), (go_hbm, go)], sems)
     own = deg_ref.shape[0]
@@ -133,12 +133,20 @@
         lambda t: lax.rem(rslots[2, 0, t] - shift + cap, cap), gh_ref, acc,
     )
     split_out(acc, share, next_ref, far_ref, before_ref, own_ref)
+
+
+def parcels_kernel(counts, rrows, rslots, rv_hbm, gh_hbm, out_b, out_a, rv, gh, acc, sems):
+    cap = rrows.shape[2]
+    copies = start_all([(rv_hbm.at[pl.ds(0, 2 * cap)], rv), (gh_hbm, gh)], sems)
+    acc[...] = jnp.zeros_like(acc)
+    wait_all(copies)
     for r, out in ((1, out_b), (0, out_a)):
-        acc[...] = jnp.zeros_like(acc)
         backward_tiles(
-            counts[r + 1], r * cap, rv, lambda t: rrows[r, 0, t], lambda t: rslots[r, 0, t], gh_ref, acc
+            counts[r + 1], r * cap, rv, lambda t: rrows[r, 0, t], lambda t: rslots[r, 0, t], gh, acc
         )
         out[...] = acc[:cap].astype(BF16)
+        if r:
+            acc[...] = jnp.zeros_like(acc)
 
 
 def split_out(acc, n, next_ref, far_ref, before_ref, own_ref):
@@ -190,26 +198,24 @@
     out[...] = (own[...] + a[...].astype(F32) + b[...].astype(F32) + c[...].astype(F32)).astype(BF16)
 
 
-def feat_kernel(counts, lrows, lcols, sends, me, p0, p1, p2, p3, p4, lv_hbm, out_a, out_b, out_c, near_ref,
-                src, lv, acc, sems, sems_a, sems_b, sems_c):
+def feat_kernel(counts, lrows, lcols, sends, me, p0, p1, p2, p3, p4, lv_hbm, out_a, out_b, near_ref,
+                src, lv, acc, sems, sems_a, sems_b):
     copies = start_all(pieces_into((p0, p1, p2, p3, p4), src, 0) + [(lv_hbm, lv)], sems)
     total = src.shape[0]
     own = near_ref.shape[0]
     shift = me[0] * own
     wait_all(copies[:5])
-    picks = (
-        (out_c, 2, me[0] * out_c.shape[0], sems_c), (out_b, 1, 0, sems_b), (out_a, 0, 0, sems_a)
-    )
-
-    def begin(out, r, base, marks):
+    picks = ((out_b, 1, sems_b), (out_a, 0, sems_a))
+
+    def begin(out, r, marks):
         def one(s, carry):
-            at = lax.rem(sends[r, 0, base + s] - shift + total, total)
+            at = lax.rem(sends[r, 0, s] - shift + total, total)
             pltpu.make_async_copy(src.at[at], out.at[s], marks.at[s]).start()
             return carry
 
         lax.fori_loop(0, out.shape[0], one, 0)
 
-    def end(out, r, base, marks):
+    def end(out, r, marks):
         def one(s, carry):
             pltpu.make_async_copy(src.at[0], out.at[s], marks.at[s]).wait()
             return carry
@@ -228,7 +234,7 @@
         end(*pick)
 
 
-def far_kernel(counts, rrows, rslots, me, a_hbm, b_hbm, p0, p1, p2, p3, rv_hbm, near_hbm, deg_hbm, w_ref,
+def far_kernel(counts, rrows, rslots, ids, me, a_hbm, b_hbm, p0, p1, p2, p3, rv_hbm, near_hbm, deg_hbm, w_ref,
                out_ref, src, vals, acc, deg, sems):
     total = out_ref.shape[0]
     cap = rrows.shape[2]
@@ -239,10 +245,11 @@
         forward_tiles(
             counts[r + 1], r * cap, vals, lambda t: rrows[r, 0, t], lambda t: src[r * cap + rslots[r, 0, t]], acc
         )
+    part = src.shape[0] - 2 * cap
     shift = me[0] * p0.shape[0]
     forward_tiles(
         counts[3], 2 * cap, vals, lambda t: rrows[2, 0, t],
-        lambda t: src[2 * cap + lax.rem(rslots[2, 0, t] - shift + cap, cap)], acc,
+        lambda t: src[2 * cap + lax.rem(ids[0, rslots[2, 0, t]] - shift + part, part)], acc,
     )
     width = deg.shape[2]
     for b in range(total):
@@ -320,26 +327,30 @@
         return call(finish_kernel, (), (own_part,) + arrived, [blocks(n, BF16)], [], 0, range(4))[0]
 
     part_feats = spread_relayed(feats)
-
-    deg, gh, z_next, z_far, z_before, z_own, back_b, back_a = call(
+    partner_feats = spread_direct(swapped(feats, bits[2]))
+    ids = swapped(sends[2], bits[2])
+
+    deg, gh, z_next, z_far, z_before, z_own = call(
         degree_kernel, (counts, lrows, rrows, rslots, me), (lv, rv, go, weight),
-        [jax.ShapeDtypeStruct((own, rows, rows), F32), blocks(own, BF16)] + split_shapes(share)
-        + [blocks(cap, BF16), blocks(cap, BF16)],
+        [jax.ShapeDtypeStruct((own, rows, rows), F32), blocks(own, BF16)] + split_shapes(share),
         [tiles(lcap), tiles(rounds * cap), room(own, BF16), tiles(own + 1, F32), room(cap + 1, F32), sems(3)],
-        rounds * cap * tile_flops, (3,),
+        cap * tile_flops, (3,),
+    )
+    back_b, back_a = call(
+        parcels_kernel, (counts, rrows, rslots), (rv, gh), [blocks(cap, BF16), blocks(cap, BF16)],
+        [tiles(2 * cap), room(own, BF16), room(cap + 1, F32), sems(2)], 2 * cap * tile_flops,
     )
     z_arrived = scattered(z_next, z_far, z_before)
     got_back_b = swapped(back_b, bits[1])
     got_back_a = swapped(back_a, bits[0])
     got_back_c = swapped(finished(z_own, z_arrived), bits[2])
 
-    need_a, need_b, need_c, near = call(
+    need_a, need_b, near = call(
         feat_kernel, (counts, lrows, lcols, sends, me), part_feats + (lv,),
-        [blocks(cap, BF16), blocks(cap, BF16), blocks(share, BF16), blocks(own, F32)],
-        [room(part, BF16), tiles(lcap), room(own + 1, F32), sems(6), sems(cap), sems(cap), sems(share)],
-        lcap * tile_flops, (), range(3),
-    )
-    got_c = swapped(need_c, bits[2])
+        [blocks(cap, BF16), blocks(cap, BF16), blocks(own, F32)],
+        [room(part, BF16), tiles(lcap), room(own + 1, F32), sems(6), sems(cap), sems(cap)],
+        lcap * tile_flops, (), range(2),
+    )
     got_b = swapped(need_b, bits[1])
     got_a = swapped(need_a, bits[0])
 
@@ -375,9 +386,9 @@
     )(own_part, a_left, a_right, b_left, b_right)
 
     output = call(
-        far_kernel, (counts, rrows, rslots, me),
-        (got_a, got_b) + spread_direct(got_c) + (rv, near, deg, weight), [blocks(own, BF16)],
-        [room(rounds * cap, BF16), tiles(rounds * cap), room(own + 1, F32), tiles(own, F32), sems(9)],
+        far_kernel, (counts, rrows, rslots, ids, me),
+        (got_a, got_b) + partner_feats + (rv, near, deg, weight), [blocks(own, BF16)],
+        [room(2 * cap + part, BF16), tiles(rounds * cap), room(own + 1, F32), tiles(own, F32), sems(9)],
         rounds * cap * tile_flops, (9,),
     )[0]
     return (output.reshape(rows_dev, width), grad_features.reshape(rows_dev, width))

time: 115 us -> 134 us (1.17)
  the two profiles are of different devices: /device:TPU:225 before, /device:TPU:146 now
where the time goes in v5:
time: 134 us; the launch traced here: 132 us
  waiting for transfers between devices  57.3 us (43%)
  Pallas kernels  38 us (28%)
  starting transfers between devices  29.6 us (22%)
  local copies, waits for them, and re-layouts  5.66 us (4%)
    ppermute x14, waiting for transfers between devices, shifted(): lax.ppermute(array, 'feat', [(i, (i + step) % size) for i in range(size)])  42.1 us
    pallas_call x6, Pallas kernels, call(): pl.pallas_call(kernel, out_shape=tuple(outs), in_specs=[SMEM] * len(scala...  33.4 us
    ppermute x14, starting transfers between devices, shifted(): lax.ppermute(array, 'feat', [(i, (i + step) % size) for i in range(size)])  23.1 us
    ppermute x7, waiting for transfers between devices, swapped(): lax.ppermute(array, 'node', [(i, i ^ 1 << bit) for i in range(lax.axis_si...  15.2 us
    ppermute x7, starting transfers between devices, swapped(): lax.ppermute(array, 'node', [(i, i ^ 1 << bit) for i in range(lax.axis_si...  6.53 us
    unnamed x30, local copies, waits for them, and re-layouts  3.47 us
  transfers between devices with their start and end apart: 21, of which 10 were waited for; matrix products, arithmetic and copies ran while one was open for 2% of the time, Pallas kernels for 15%

profile of v5, /device:TPU:146, one launch (start us, length us, event | category | flops | bytes accessed | tf_op | source)
XLA Modules:
  0.0 131.6 jit_solution(10861707923334596926)
XLA Ops:
  0.6 5.4 %shard_map.123 = (f32[8,128,128]{2,1,0:T(8,128)}, bf16[8,128,256]{2,1,0:T(8,128)(2,1)}, bf16[4,128,256]{2,1,0:T(8,128)(2,1)}, bf16[4,128,256]{2,1,0:T(8,128)(2,1...) custom-call(s32[4]{0:T(128)} %bitcast.30, s32[32]{0:T(128)} %bitcast.37, s32[3,1,16]{2,1,0:T(1,128)} %bitcast.24, ...), custom_call_target="tpu_custom_call" | custom-call | flops 134217728 | bytes 5636096 | tf_op jit(solution)/shard_map/pallas_call | solution.py:308
  6.1 0.0 copy-start.14
  6.1 5.9 %shard_map.125 = (bf16[16,128,256]{2,1,0:T(8,128)(2,1)}, bf16[16,128,256]{2,1,0:T(8,128)(2,1)}) custom-call(s32[4]{0:T(128)} %bitcast.31, s32[3,1,16]{2,1,0:T(1,128)} %bitcast.25, s32[3,1,16]{2,1,0:T(1,128)} %bitcast.28, bf16[48,128,128]{2,1,0:T(8,128)(2,1)} %bitcast.16, bf16[8,128,256]{2,1,0:T(8,128)(2,1)} %get-tuple-element.24.gh_hbm), custom_call_target="tpu_custom_call" | custom-call | flops 268435456 | bytes 4194304 | tf_op jit(solution)/shard_map/pallas_call | solution.py:308
  12.0 0.1 collective-permute-start.11
  12.1 0.1 collective-permute-start.12
  12.2 0.9 collective-permute-start.13
  13.1 2.1 %collective-permute-start.14 = (bf16[4,128,256]{2,1,0:T(8,128)(2,1)}, bf16[4,128,256]{2,1,0:T(8,128)(2,1)}, u32[]{:S(2)}, u32[]{:S(2)}) collective-permute-start(bf16[4,128,256]{2,1,0:T(8,128)(2,1)} %get-tuple-element.29), channel_id=1, source_target_pairs={{0,2},{1,3},{2,0},{3,1},{4,6},{5,7},{6,4},{7,5},{8,10},{9,11},{10,... | collective-permute-start | bytes 786440 | tf_op jit(solution)/shard_map/ppermute | solution.py:23
  15.3 0.6 collective-permute-start.2
  15.8 5.7 %collective-permute-done.13.a = bf16[4,128,256]{2,1,0:T(8,128)(2,1)S(1)} collective-permute-done((bf16[4,128,256]{2,1,0:T(8,128)(2,1)S(1)}, bf16[4,128,256]{2,1,0:T(8,128)(2,1)S(1)}, u32[]{:S(2)}, u32[]{:S(2)}) %collective-permute-start.13) | collective-permute-done | bytes 262176 | tf_op jit(solution)/shard_map/ppermute | solution.py:23
  21.5 2.3 %collective-permute-start.1 = (bf16[8,128,256]{2,1,0:T(8,128)(2,1)}, bf16[8,128,256]{2,1,0:T(8,128)(2,1)S(1)}, u32[]{:S(2)}, u32[]{:S(2)}) collective-permute-start(bf16[8,128,256]{2,1,0:T(8,128)(2,1)} %bitcast.8.p0), channel_id=1, source_target_pairs={{0,3},{1,0},{2,1},{3,2},{4,7},{5,4},{6,5},{7,6},{8,11},{9,8},{10,9... | collective-permute-start | bytes 1572872 | tf_op jit(solution)/shard_map/ppermute | solution.py:23
  23.8 0.0 collective-permute-done.14.b
  23.8 7.0 %collective-permute-start.15 = (bf16[4,128,256]{2,1,0:T(8,128)(2,1)}, bf16[4,128,256]{2,1,0:T(8,128)(2,1)}, u32[]{:S(2)}, u32[]{:S(2)}) collective-permute-start(bf16[4,128,256]{2,1,0:T(8,128)(2,1)} %get-tuple-element.30), channel_id=1, source_target_pairs={{0,3},{1,0},{2,1},{3,2},{4,7},{5,4},{6,5},{7,6},{8,11},{9,8},{10,9... | collective-permute-start | bytes 786440 | tf_op jit(solution)/shard_map/ppermute | solution.py:23
  30.8 9.3 %collective-permute-done.15.c = bf16[4,128,256]{2,1,0:T(8,128)(2,1)} collective-permute-done((bf16[4,128,256]{2,1,0:T(8,128)(2,1)}, bf16[4,128,256]{2,1,0:T(8,128)(2,1)}, u32[]{:S(2)}, u32[]{:S(2)}) %collective-permute-start.15) | collective-permute-done | bytes 262176 | tf_op jit(solution)/shard_map/ppermute | solution.py:23
  40.2 2.1 %shard_map.126 = bf16[4,128,256]{2,1,0:T(8,128)(2,1)} custom-call(f32[4,128,256]{2,1,0:T(8,128)} %get-tuple-element.27.own, bf16[4,128,256]{2,1,0:T(8,128)(2,1)} %copy-done.12, bf16[4,128,256]{2,1,0:T(8,128)(2,1)} %collective-permute-done.14.b, bf16[4,128,256]{2,1,0:T(8,128)(2,1)} %collective-permute-done.15.c), custom_call_target="tpu_custom_call" | custom-call | bytes 1572864 | tf_op jit(solution)/shard_map/pallas_call | solution.py:308
  42.2 6.1 %collective-permute-start.16 = (bf16[4,128,256]{2,1,0:T(8,128)(2,1)}, bf16[4,128,256]{2,1,0:T(8,128)(2,1)S(1)}, u32[]{:S(2)}, u32[]{:S(2)}) collective-permute-start(bf16[4,128,256]{2,1,0:T(8,128)(2,1)} %shard_map.126), channel_id=1, source_target_pairs={{0,64},{4,68},{8,72},{12,76},{16,80},{20,84},{24,88},{28,92},{32,9... | collective-permute-start | bytes 786440 | tf_op jit(solution)/shard_map/ppermute | solution.py:18
  48.4 0.8 slice.13
  49.2 1.7 %collective-permute-start.3 = (bf16[4,128,256]{2,1,0:T(8,128)(2,1)}, bf16[4,128,256]{2,1,0:T(8,128)(2,1)}, u32[]{:S(2)}, u32[]{:S(2)}) collective-permute-start(bf16[4,128,256]{2,1,0:T(8,128)(2,1)} %slice.13), channel_id=1, source_target_pairs={{0,1},{1,2},{2,3},{3,0},{4,5},{5,6},{6,7},{7,4},{8,9},{9,10},{10,1... | collective-permute-start | bytes 786440 | tf_op jit(solution)/shard_map/ppermute | solution.py:23
  50.9 0.8 slice.14
  51.7 0.3 collective-permute-start.4
  52.0 6.4 %collective-permute-done.16.c_hbm = bf16[4,128,256]{2,1,0:T(8,128)(2,1)S(1)} collective-permute-done((bf16[4,128,256]{2,1,0:T(8,128)(2,1)}, bf16[4,128,256]{2,1,0:T(8,128)(2,1)S(1)}, u32[]{:S(2)}, u32[]{:S(2)}) %collective-permute-start.16) | collective-permute-done | bytes 262176 | tf_op jit(solution)/shard_map/ppermute | solution.py:18
  58.4 0.7 copy-done.10
  59.1 0.4 copy-done.6
  59.4 0.3 copy-done.7
  59.7 6.5 %shard_map.127 = (bf16[8,128,256]{2,1,0:T(8,128)(2,1)}, bf16[8,128,256]{2,1,0:T(8,128)(2,1)}, f32[4,128,256]{2,1,0:T(8,128)}, f32[4,128,256]{2,1,0:T(8,128)}, f32[8,128,256]{2,1,0:T(8,128)}) custom-call(s32[4]{0:T(128)} %bitcast.32, s32[32]{0:T(128)} %bitcast.38, s32[32]{0:T(128)} %bitcast.40, s32[3,1,16]{2,1,0:T(1,128)} %bitcast.35, s32[1]{0:T(128)} %bitcast.4.me, ...), custom_call_target="tpu_custom_call" | custom-call | flops 268435456 | bytes 7077888 | tf_op jit(solution)/shard_map/pallas_call | solution.py:308
  66.2 1.5 %collective-permute-start.17 = (bf16[8,128,256]{2,1,0:T(8,128)(2,1)}, bf16[8,128,256]{2,1,0:T(8,128)(2,1)S(1)}, u32[]{:S(2)}, u32[]{:S(2)}) collective-permute-start(bf16[8,128,256]{2,1,0:T(8,128)(2,1)} %get-tuple-element.32), channel_id=1, source_target_pairs={{0,1},{1,2},{2,3},{3,0},{4,5},{5,6},{6,7},{7,4},{8,9},{9,10},{10,1... | collective-permute-start | bytes 1572872 | tf_op jit(solution)/shard_map/ppermute | solution.py:23
  67.8 0.6 collective-permute-start.18
  68.3 0.0 collective-permute-start.7
  68.3 6.0 %shard_map.122 = (bf16[16,128,256]{2,1,0:T(8,128)(2,1)}, bf16[16,128,256]{2,1,0:T(8,128)(2,1)}, f32[8,128,256]{2,1,0:T(8,128)}) custom-call(s32[4]{0:T(128)} %bitcast.33, s32[32]{0:T(128)} %bitcast.39, s32[32]{0:T(128)} %bitcast.41, s32[3,1,16]{2,1,0:T(1,128)} %bitcast.36, s32[1]{0:T(128)} %bitcast.4.me, bf16[8,128,256]{2,1,0:T(8,128)(2,1)} %bitcast.8.p0, ...), custom_call_target="tpu_custom_call" | custom-call | flops 268435456 | bytes 6291456 | tf_op jit(solution)/shard_map/pallas_call | solution.py:308
  74.4 0.1 collective-permute-start.5
  74.5 0.1 collective-permute-start.6
  74.6 0.7 slice_bitcast_fusion
  75.2 2.0 %collective-permute-done.17.from_left.a_left = bf16[8,128,256]{2,1,0:T(8,128)(2,1)S(1)} collective-permute-done((bf16[8,128,256]{2,1,0:T(8,128)(2,1)}, bf16[8,128,256]{2,1,0:T(8,128)(2,1)S(1)}, u32[]{:S(2)}, u32[]{:S(2)}) %collective-permute-start.17) | collective-permute-done | bytes 524320 | tf_op jit(solution)/shard_map/ppermute | solution.py:23
  77.2 2.1 %collective-permute-done.18.from_right.a_right = bf16[8,128,256]{2,1,0:T(8,128)(2,1)S(1)} collective-permute-done((bf16[8,128,256]{2,1,0:T(8,128)(2,1)}, bf16[8,128,256]{2,1,0:T(8,128)(2,1)S(1)}, u32[]{:S(2)}, u32[]{:S(2)}) %collective-permute-start.18) | collective-permute-done | bytes 524320 | tf_op jit(solution)/shard_map/ppermute | solution.py:23
  79.3 0.8 copy-done.1
  80.1 2.2 %shard_map.128 = (bf16[4,128,256]{2,1,0:T(8,128)(2,1)}, bf16[4,128,256]{2,1,0:T(8,128)(2,1)}) custom-call(f32[4,128,256]{2,1,0:T(8,128)} %get-tuple-element.34.keep_r, f32[4,128,256]{2,1,0:T(8,128)} %get-tuple-element.35.keep_l, bf16[8,128,256]{2,1,0:T(8,128)(2,1)} %copy-done, bf16[8,128,256]{2,1,0:T(8,128)(2,1)} %copy-done.1), custom_call_target="tpu_custom_call" | custom-call | bytes 1048576 | tf_op jit(solution)/shard_map/pallas_call | solution.py:369
  82.3 0.5 collective-permute-start.19
  82.7 8.8 %collective-permute-done.ids = s32[1,16]{1,0:T(1,128)S(1)} collective-permute-done((s32[1,16]{1,0:T(1,128)S(1)}, s32[1,16]{1,0:T(1,128)S(1)}, u32[]{:S(2)}, u32[]{:S(2)}) %collective-permute-start) | collective-permute-done | bytes 96 | tf_op jit(solution)/shard_map/ppermute | solution.py:18
  91.6 2.0 %collective-permute-start.10 = (bf16[8,128,256]{2,1,0:T(8,128)(2,1)}, bf16[8,128,256]{2,1,0:T(8,128)(2,1)S(1)}, u32[]{:S(2)}, u32[]{:S(2)}) collective-permute-start(bf16[8,128,256]{2,1,0:T(8,128)(2,1)} %collective-permute-done.7.p0), channel_id=1, source_target_pairs={{0,1},{1,2},{2,3},{3,0},{4,5},{5,6},{6,7},{7,4},{8,9},{9,10},{10,1... | collective-permute-start | bytes 1572872 | tf_op jit(solution)/shard_map/ppermute | solution.py:23
  93.6 0.8 collective-permute-start.8
  94.4 6.7 %collective-permute-done.20.b_right = bf16[4,128,256]{2,1,0:T(8,128)(2,1)} collective-permute-done((bf16[4,128,256]{2,1,0:T(8,128)(2,1)}, bf16[4,128,256]{2,1,0:T(8,128)(2,1)}, u32[]{:S(2)}, u32[]{:S(2)}) %collective-permute-start.20) | collective-permute-done | bytes 262176 | tf_op jit(solution)/shard_map/ppermute | solution.py:23
  101.0 2.8 %collective-permute-start.9 = (bf16[8,128,256]{2,1,0:T(8,128)(2,1)}, bf16[8,128,256]{2,1,0:T(8,128)(2,1)}, u32[]{:S(2)}, u32[]{:S(2)}) collective-permute-start(bf16[8,128,256]{2,1,0:T(8,128)(2,1)} %collective-permute-done.7.p0), channel_id=1, source_target_pairs={{0,2},{1,3},{2,0},{3,1},{4,6},{5,7},{6,4},{7,5},{8,10},{9,11},{10,... | collective-permute-start | bytes 1572872 | tf_op jit(solution)/shard_map/ppermute | solution.py:23
  103.8 2.5 %shard_map.129 = bf16[8,128,256]{2,1,0:T(8,128)(2,1)} custom-call(f32[8,128,256]{2,1,0:T(8,128)} %get-tuple-element.31.own, bf16[8,128,256]{2,1,0:T(8,128)(2,1)} %copy-done, bf16[8,128,256]{2,1,0:T(8,128)(2,1)} %copy-done.1, bf16[4,128,256]{2,1,0:T(8,128)(2,1)} %copy-done.11, bf16[4,128,256]{2,1,0:T(8,128)(2,1)} %collective-permute-done.20.b_right), custom_call_target="tpu_custom_call" | custom-call | bytes 2621440 | tf_op jit(solution)/shard_map/pallas_call | solution.py:379
  106.3 1.0 collective-permute-done.10.p3
  107.3 3.7 %collective-permute-done.8.p1 = bf16[8,128,256]{2,1,0:T(8,128)(2,1)S(1)} collective-permute-done((bf16[8,128,256]{2,1,0:T(8,128)(2,1)}, bf16[8,128,256]{2,1,0:T(8,128)(2,1)S(1)}, u32[]{:S(2)}, u32[]{:S(2)}) %collective-permute-start.8) | collective-permute-done | bytes 524320 | tf_op jit(solution)/shard_map/ppermute | solution.py:23
  111.0 11.6 %collective-permute-done.9.p2 = bf16[8,128,256]{2,1,0:T(8,128)(2,1)} collective-permute-done((bf16[8,128,256]{2,1,0:T(8,128)(2,1)}, bf16[8,128,256]{2,1,0:T(8,128)(2,1)}, u32[]{:S(2)}, u32[]{:S(2)}) %collective-permute-start.9) | collective-permute-done | bytes 524320 | tf_op jit(solution)/shard_map/ppermute | solution.py:23
  122.7 0.9 copy-done.4
  123.6 0.3 copy-done.5
  123.9 7.5 %shard_map.124 = bf16[8,128,256]{2,1,0:T(8,128)(2,1)} custom-call(s32[4]{0:T(128)} %bitcast.34, s32[3,1,16]{2,1,0:T(1,128)} %bitcast.26, s32[3,1,16]{2,1,0:T(1,128)} %bitcast.29, s32[1,16]{1,0:T(1,128)} %copy-done.13, s32[1]{0:T(128)} %bitcast.4.me, bf16[16,128,256]{2,1,0:T(8,128)(2,1)} %copy-done.4, bf16[16,128,256]{2,1,0:T(8,128)(2,1)} %copy-done.5, ...), custom_call_target="tpu_custom_call" | custom-call | flops 402653184 | bytes 7995392 | tf_op jit(solution)/shard_map/pallas_call | solution.py:308
  (35 shorter events, 0.1 us)
Async XLA Ops:
  6.1 6.1 %copy-start.14 = (bf16[4,128,256]{2,1,0:T(8,128)(2,1)S(1)}, bf16[4,128,256]{2,1,0:T(8,128)(2,1)}, u32[]{:S(2)}) copy-start(bf16[4,128,256]{2,1,0:T(8,128)(2,1)} %get-tuple-element.28) | copy-start | bytes 786436
  12.0 46.3 %collective-permute-start.11 = (bf16[16,128,256]{2,1,0:T(8,128)(2,1)}, bf16[16,128,256]{2,1,0:T(8,128)(2,1)S(1)}, u32[]{:S(2)}, u32[]{:S(2)}) collective-permute-start(bf16[16,128,256]{2,1,0:T(8,128)(2,1)} %get-tuple-element.25), channel_id=1, source_target_pairs={{0,4},{4,0},{8,12},{12,8},{16,20},{20,16},{24,28},{28,24},{32,36},... | collective-permute-start | bytes 3145736 | tf_op jit(solution)/shard_map/ppermute | solution.py:18
  12.1 46.2 %collective-permute-start.12 = (bf16[16,128,256]{2,1,0:T(8,128)(2,1)}, bf16[16,128,256]{2,1,0:T(8,128)(2,1)S(1)}, u32[]{:S(2)}, u32[]{:S(2)}) collective-permute-start(bf16[16,128,256]{2,1,0:T(8,128)(2,1)} %get-tuple-element.26), channel_id=1, source_target_pairs={{0,16},{4,20},{8,24},{12,28},{16,0},{20,4},{24,8},{28,12},{32,48},... | collective-permute-start | bytes 3145736 | tf_op jit(solution)/shard_map/ppermute | solution.py:18
  12.2 9.3 %collective-permute-start.13 = (bf16[4,128,256]{2,1,0:T(8,128)(2,1)S(1)}, bf16[4,128,256]{2,1,0:T(8,128)(2,1)S(1)}, u32[]{:S(2)}, u32[]{:S(2)}) collective-permute-start(bf16[4,128,256]{2,1,0:T(8,128)(2,1)S(1)} %copy-done.14), channel_id=1, source_target_pairs={{0,1},{1,2},{2,3},{3,0},{4,5},{5,6},{6,7},{7,4},{8,9},{9,10},{10,1... | collective-permute-start | bytes 786440 | tf_op jit(solution)/shard_map/ppermute | solution.py:23
  13.1 10.7 %collective-permute-start.14 = (bf16[4,128,256]{2,1,0:T(8,128)(2,1)}, bf16[4,128,256]{2,1,0:T(8,128)(2,1)}, u32[]{:S(2)}, u32[]{:S(2)}) collective-permute-start(bf16[4,128,256]{2,1,0:T(8,128)(2,1)} %get-tuple-element.29), channel_id=1, source_target_pairs={{0,2},{1,3},{2,0},{3,1},{4,6},{5,7},{6,4},{7,5},{8,10},{9,11},{10,... | collective-permute-start | bytes 786440 | tf_op jit(solution)/shard_map/ppermute | solution.py:23
  15.3 33.1 %collective-permute-start.2 = (bf16[8,128,256]{2,1,0:T(8,128)(2,1)}, bf16[8,128,256]{2,1,0:T(8,128)(2,1)S(1)}, u32[]{:S(2)}, u32[]{:S(2)}) collective-permute-start(bf16[8,128,256]{2,1,0:T(8,128)(2,1)} %bitcast.8.p0), channel_id=1, source_target_pairs={{0,1},{1,2},{2,3},{3,0},{4,5},{5,6},{6,7},{7,4},{8,9},{9,10},{10,1... | collective-permute-start | bytes 1572872 | tf_op jit(solution)/shard_map/ppermute | solution.py:23
  21.5 18.7 %copy-start.12 = (bf16[4,128,256]{2,1,0:T(8,128)(2,1)}, bf16[4,128,256]{2,1,0:T(8,128)(2,1)S(1)}, u32[]{:S(2)}) copy-start(bf16[4,128,256]{2,1,0:T(8,128)(2,1)S(1)} %collective-permute-done.13.a) | copy-start | bytes 786436
  21.5 29.4 %collective-permute-start.1 = (bf16[8,128,256]{2,1,0:T(8,128)(2,1)}, bf16[8,128,256]{2,1,0:T(8,128)(2,1)S(1)}, u32[]{:S(2)}, u32[]{:S(2)}) collective-permute-start(bf16[8,128,256]{2,1,0:T(8,128)(2,1)} %bitcast.8.p0), channel_id=1, source_target_pairs={{0,3},{1,0},{2,1},{3,2},{4,7},{5,4},{6,5},{7,6},{8,11},{9,8},{10,9... | collective-permute-start | bytes 1572872 | tf_op jit(solution)/shard_map/ppermute | solution.py:23
  23.8 16.3 %collective-permute-start.15 = (bf16[4,128,256]{2,1,0:T(8,128)(2,1)}, bf16[4,128,256]{2,1,0:T(8,128)(2,1)}, u32[]{:S(2)}, u32[]{:S(2)}) collective-permute-start(bf16[4,128,256]{2,1,0:T(8,128)(2,1)} %get-tuple-element.30), channel_id=1, source_target_pairs={{0,3},{1,0},{2,1},{3,2},{4,7},{5,4},{6,5},{7,6},{8,11},{9,8},{10,9... | collective-permute-start | bytes 786440 | tf_op jit(solution)/shard_map/ppermute | solution.py:23
  42.2 16.1 %collective-permute-start.16 = (bf16[4,128,256]{2,1,0:T(8,128)(2,1)}, bf16[4,128,256]{2,1,0:T(8,128)(2,1)S(1)}, u32[]{:S(2)}, u32[]{:S(2)}) collective-permute-start(bf16[4,128,256]{2,1,0:T(8,128)(2,1)} %shard_map.126), channel_id=1, source_target_pairs={{0,64},{4,68},{8,72},{12,76},{16,80},{20,84},{24,88},{28,92},{32,9... | collective-permute-start | bytes 786440 | tf_op jit(solution)/shard_map/ppermute | solution.py:18
  48.4 17.8 %copy-start.2 = (bf16[8,128,256]{2,1,0:T(8,128)(2,1)}, bf16[8,128,256]{2,1,0:T(8,128)(2,1)S(1)}, u32[]{:S(2)}) copy-start(bf16[8,128,256]{2,1,0:T(8,128)(2,1)S(1)} %collective-permute-done.2.p4) | copy-start | bytes 1572868
  49.2 19.2 %collective-permute-start.3 = (bf16[4,128,256]{2,1,0:T(8,128)(2,1)}, bf16[4,128,256]{2,1,0:T(8,128)(2,1)}, u32[]{:S(2)}, u32[]{:S(2)}) collective-permute-start(bf16[4,128,256]{2,1,0:T(8,128)(2,1)} %slice.13), channel_id=1, source_target_pairs={{0,1},{1,2},{2,3},{3,0},{4,5},{5,6},{6,7},{7,4},{8,9},{9,10},{10,1... | collective-permute-start | bytes 786440 | tf_op jit(solution)/shard_map/ppermute | solution.py:23
  50.9 15.3 %copy-start.3 = (bf16[8,128,256]{2,1,0:T(8,128)(2,1)}, bf16[8,128,256]{2,1,0:T(8,128)(2,1)S(1)}, u32[]{:S(2)}) copy-start(bf16[8,128,256]{2,1,0:T(8,128)(2,1)S(1)} %collective-permute-done.1.p1) | copy-start | bytes 1572868
  51.7 16.7 %collective-permute-start.4 = (bf16[4,128,256]{2,1,0:T(8,128)(2,1)}, bf16[4,128,256]{2,1,0:T(8,128)(2,1)}, u32[]{:S(2)}, u32[]{:S(2)}) collective-permute-start(bf16[4,128,256]{2,1,0:T(8,128)(2,1)} %slice.14), channel_id=1, source_target_pairs={{0,3},{1,0},{2,1},{3,2},{4,7},{5,4},{6,5},{7,6},{8,11},{9,8},{10,9... | collective-permute-start | bytes 786440 | tf_op jit(solution)/shard_map/ppermute | solution.py:23
  58.3 0.7 copy-start.10
  58.3 1.1 copy-start.6
  58.4 1.4 %copy-start.7 = (bf16[16,128,256]{2,1,0:T(8,128)(2,1)}, bf16[16,128,256]{2,1,0:T(8,128)(2,1)S(1)}, u32[]{:S(2)}) copy-start(bf16[16,128,256]{2,1,0:T(8,128)(2,1)S(1)} %collective-permute-done.12.b_hbm) | copy-start | bytes 3145732
  66.2 11.0 %collective-permute-start.17 = (bf16[8,128,256]{2,1,0:T(8,128)(2,1)}, bf16[8,128,256]{2,1,0:T(8,128)(2,1)S(1)}, u32[]{:S(2)}, u32[]{:S(2)}) collective-permute-start(bf16[8,128,256]{2,1,0:T(8,128)(2,1)} %get-tuple-element.32), channel_id=1, source_target_pairs={{0,1},{1,2},{2,3},{3,0},{4,5},{5,6},{6,7},{7,4},{8,9},{9,10},{10,1... | collective-permute-start | bytes 1572872 | tf_op jit(solution)/shard_map/ppermute | solution.py:23
  67.8 11.5 %collective-permute-start.18 = (bf16[8,128,256]{2,1,0:T(8,128)(2,1)}, bf16[8,128,256]{2,1,0:T(8,128)(2,1)S(1)}, u32[]{:S(2)}, u32[]{:S(2)}) collective-permute-start(bf16[8,128,256]{2,1,0:T(8,128)(2,1)} %get-tuple-element.33), channel_id=1, source_target_pairs={{0,3},{1,0},{2,1},{3,2},{4,7},{5,4},{6,5},{7,6},{8,11},{9,8},{10,9... | collective-permute-start | bytes 1572872 | tf_op jit(solution)/shard_map/ppermute | solution.py:23
  68.3 23.2 %collective-permute-start.7 = (bf16[8,128,256]{2,1,0:T(8,128)(2,1)}, bf16[8,128,256]{2,1,0:T(8,128)(2,1)}, u32[]{:S(2)}, u32[]{:S(2)}) collective-permute-start(bf16[8,128,256]{2,1,0:T(8,128)(2,1)} %bitcast.8.p0), channel_id=1, source_target_pairs={{0,64},{4,68},{8,72},{12,76},{16,80},{20,84},{24,88},{28,92},{32,9... | collective-permute-start | bytes 1572872 | tf_op jit(solution)/shard_map/ppermute | solution.py:18
  74.4 48.3 %collective-permute-start.5 = (bf16[16,128,256]{2,1,0:T(8,128)(2,1)}, bf16[16,128,256]{2,1,0:T(8,128)(2,1)S(1)}, u32[]{:S(2)}, u32[]{:S(2)}) collective-permute-start(bf16[16,128,256]{2,1,0:T(8,128)(2,1)} %get-tuple-element.20), channel_id=1, source_target_pairs={{0,4},{4,0},{8,12},{12,8},{16,20},{20,16},{24,28},{28,24},{32,36},... | collective-permute-start | bytes 3145736 | tf_op jit(solution)/shard_map/ppermute | solution.py:18
  74.5 48.2 %collective-permute-start.6 = (bf16[16,128,256]{2,1,0:T(8,128)(2,1)}, bf16[16,128,256]{2,1,0:T(8,128)(2,1)S(1)}, u32[]{:S(2)}, u32[]{:S(2)}) collective-permute-start(bf16[16,128,256]{2,1,0:T(8,128)(2,1)} %get-tuple-element.21), channel_id=1, source_target_pairs={{0,16},{4,20},{8,24},{12,28},{16,0},{20,4},{24,8},{28,12},{32,48},... | collective-permute-start | bytes 3145736 | tf_op jit(solution)/shard_map/ppermute | solution.py:18
  77.2 2.1 %copy-start = (bf16[8,128,256]{2,1,0:T(8,128)(2,1)}, bf16[8,128,256]{2,1,0:T(8,128)(2,1)S(1)}, u32[]{:S(2)}) copy-start(bf16[8,128,256]{2,1,0:T(8,128)(2,1)S(1)} %collective-permute-done.17.from_left.a_left) | copy-start | bytes 1572868
  77.2 14.4 %collective-permute-start = (s32[1,16]{1,0:T(1,128)S(1)}, s32[1,16]{1,0:T(1,128)S(1)}, u32[]{:S(2)}, u32[]{:S(2)}) collective-permute-start(s32[1,16]{1,0:T(1,128)S(1)} %slice_bitcast_fusion), channel_id=1, source_target_pairs={{0,64},{4,68},{8,72},{12,76},{16,80},{20,84},{24,88},{28,92},{32,9... | collective-permute-start | bytes 200 | tf_op jit(solution)/shard_map/ppermute | solution.py:18
  79.3 0.8 copy-start.1
  82.3 11.3 %collective-permute-start.19 = (bf16[4,128,256]{2,1,0:T(8,128)(2,1)}, bf16[4,128,256]{2,1,0:T(8,128)(2,1)S(1)}, u32[]{:S(2)}, u32[]{:S(2)}) collective-permute-start(bf16[4,128,256]{2,1,0:T(8,128)(2,1)} %get-tuple-element.36), channel_id=1, source_target_pairs={{0,1},{1,2},{2,3},{3,0},{4,5},{5,6},{6,7},{7,4},{8,9},{9,10},{10,1... | collective-permute-start | bytes 786440 | tf_op jit(solution)/shard_map/ppermute | solution.py:23
  91.5 14.7 %copy-start.13 = (s32[1,16]{1,0:T(1,128)}, s32[1,16]{1,0:T(1,128)S(1)}, u32[]{:S(2)}) copy-start(s32[1,16]{1,0:T(1,128)S(1)} %collective-permute-done.ids) | copy-start | bytes 196
  91.5 9.5 %collective-permute-start.20 = (bf16[4,128,256]{2,1,0:T(8,128)(2,1)}, bf16[4,128,256]{2,1,0:T(8,128)(2,1)}, u32[]{:S(2)}, u32[]{:S(2)}) collective-permute-start(bf16[4,128,256]{2,1,0:T(8,128)(2,1)} %get-tuple-element.37), channel_id=1, source_target_pairs={{0,3},{1,0},{2,1},{3,2},{4,7},{5,4},{6,5},{7,6},{8,11},{9,8},{10,9... | collective-permute-start | bytes 786440 | tf_op jit(solution)/shard_map/ppermute | solution.py:23
  91.6 15.7 %collective-permute-start.10 = (bf16[8,128,256]{2,1,0:T(8,128)(2,1)}, bf16[8,128,256]{2,1,0:T(8,128)(2,1)S(1)}, u32[]{:S(2)}, u32[]{:S(2)}) collective-permute-start(bf16[8,128,256]{2,1,0:T(8,128)(2,1)} %collective-permute-done.7.p0), channel_id=1, source_target_pairs={{0,1},{1,2},{2,3},{3,0},{4,5},{5,6},{6,7},{7,4},{8,9},{9,10},{10,1... | collective-permute-start | bytes 1572872 | tf_op jit(solution)/shard_map/ppermute | solution.py:23
  93.6 10.2 %copy-start.11 = (bf16[4,128,256]{2,1,0:T(8,128)(2,1)}, bf16[4,128,256]{2,1,0:T(8,128)(2,1)S(1)}, u32[]{:S(2)}) copy-start(bf16[4,128,256]{2,1,0:T(8,128)(2,1)S(1)} %collective-permute-done.19.b_left) | copy-start | bytes 786436
  93.6 17.4 %collective-permute-start.8 = (bf16[8,128,256]{2,1,0:T(8,128)(2,1)}, bf16[8,128,256]{2,1,0:T(8,128)(2,1)S(1)}, u32[]{:S(2)}, u32[]{:S(2)}) collective-permute-start(bf16[8,128,256]{2,1,0:T(8,128)(2,1)} %collective-permute-done.7.p0), channel_id=1, source_target_pairs={{0,3},{1,0},{2,1},{3,2},{4,7},{5,4},{6,5},{7,6},{8,11},{9,8},{10,9... | collective-permute-start | bytes 1572872 | tf_op jit(solution)/shard_map/ppermute | solution.py:23
  101.0 21.6 %collective-permute-start.9 = (bf16[8,128,256]{2,1,0:T(8,128)(2,1)}, bf16[8,128,256]{2,1,0:T(8,128)(2,1)}, u32[]{:S(2)}, u32[]{:S(2)}) collective-permute-start(bf16[8,128,256]{2,1,0:T(8,128)(2,1)} %collective-permute-done.7.p0), channel_id=1, source_target_pairs={{0,2},{1,3},{2,0},{3,1},{4,6},{5,7},{6,4},{7,5},{8,10},{9,11},{10,... | collective-permute-start | bytes 1572872 | tf_op jit(solution)/shard_map/ppermute | solution.py:23
  107.3 15.4 %copy-start.8 = (bf16[8,128,256]{2,1,0:T(8,128)(2,1)}, bf16[8,128,256]{2,1,0:T(8,128)(2,1)S(1)}, u32[]{:S(2)}) copy-start(bf16[8,128,256]{2,1,0:T(8,128)(2,1)S(1)} %collective-permute-done.10.p3) | copy-start | bytes 1572868
  111.0 11.7 %copy-start.9 = (bf16[8,128,256]{2,1,0:T(8,128)(2,1)}, bf16[8,128,256]{2,1,0:T(8,128)(2,1)S(1)}, u32[]{:S(2)}) copy-start(bf16[8,128,256]{2,1,0:T(8,128)(2,1)S(1)} %collective-permute-done.8.p1) | copy-start | bytes 1572868
  122.6 1.0 copy-start.4
  122.6 1.3 copy-start.5

commit v6 on v5

--- a/solution.py
+++ b/solution.py
@@ -30,13 +30,6 @@
     far_low = shifted(before[:half], 1)
     far_high = shifted(after[half:], -1)
     return (mine, after, far_low, far_high, before)
-
-
-def spread_direct(mine):
-    before = shifted(mine, 1)
-    after = shifted(mine, -1)
-    far = shifted(mine, 2)
-    return (mine, after, far, before)
 
 
 def scattered(to_next, to_far, to_before):
@@ -234,12 +227,12 @@
         end(*pick)
 
 
-def far_kernel(counts, rrows, rslots, ids, me, a_hbm, b_hbm, p0, p1, p2, p3, rv_hbm, near_hbm, deg_hbm, w_ref,
+def far_kernel(counts, rrows, rslots, ids, me, a_hbm, b_hbm, p0, p1, p2, p3, p4, rv_hbm, near_hbm, deg_hbm, w_ref,
                out_ref, src, vals, acc, deg, sems):
     total = out_ref.shape[0]
     cap = rrows.shape[2]
     pairs = [(near_hbm, acc.at[pl.ds(0, total)]), (rv_hbm, vals)]
-    pairs += pieces_into((a_hbm, b_hbm, p0, p1, p2, p3), src, 0) + [(deg_hbm, deg)]
+    pairs += pieces_into((a_hbm, b_hbm, p0, p1, p2, p3, p4), src, 0) + [(deg_hbm, deg)]
     wait_all(start_all(pairs, sems))
     for r in range(2):
         forward_tiles(
@@ -327,7 +320,7 @@
         return call(finish_kernel, (), (own_part,) + arrived, [blocks(n, BF16)], [], 0, range(4))[0]
 
     part_feats = spread_relayed(feats)
-    partner_feats = spread_direct(swapped(feats, bits[2]))
+    partner_feats = spread_relayed(swapped(feats, bits[2]))
     ids = swapped(sends[2], bits[2])
 
     deg, gh, z_next, z_far, z_before, z_own = call(
@@ -388,8 +381,8 @@
     output = call(
         far_kernel, (counts, rrows, rslots, ids, me),
         (got_a, got_b) + partner_feats + (rv, near, deg, weight), [blocks(own, BF16)],
-        [room(2 * cap + part, BF16), tiles(rounds * cap), room(own + 1, F32), tiles(own, F32), sems(9)],
-        rounds * cap * tile_flops, (9,),
+        [room(2 * cap + part, BF16), tiles(rounds * cap), room(own + 1, F32), tiles(own, F32), sems(10)],
+        rounds * cap * tile_flops, (10,),
     )[0]
     return (output.reshape(rows_dev, width), grad_features.reshape(rows_dev, width))
 

time: 134 us -> 130 us (0.970); the launches traced: 132 us -> 129 us
  waiting for transfers between devices: 57.3 us -> 47.8 us
  starting transfers between devices: 29.6 us -> 35 us
  local copies, waits for them, and re-layouts: 5.66 us -> 7.11 us
    ppermute x14 -> x15, waiting for transfers between devices: 42.1 us -> 26.3 us  [shifted(): lax.ppermute(array, 'feat', [(i, (i + step) % size) for i in range(size)])]
    ppermute x7, waiting for transfers between devices: 15.2 us -> 21.5 us  [swapped(): lax.ppermute(array, 'node', [(i, i ^ 1 << bit) for i in range(lax.axis_si...]
    ppermute x14 -> x15, starting transfers between devices: 23.1 us -> 26.4 us  [shifted(): lax.ppermute(array, 'feat', [(i, (i + step) % size) for i in range(size)])]
    ppermute x7, starting transfers between devices: 6.53 us -> 8.59 us  [swapped(): lax.ppermute(array, 'node', [(i, i ^ 1 << bit) for i in range(lax.axis_si...]
    unnamed x30 -> x34, local copies, waits for them, and re-layouts: 3.47 us -> 4.16 us
  transfers between devices with their start and end apart: 21 -> 22, of which waited for: 10 -> 6; matrix products, arithmetic and copies ran while one was open for 2% -> 2% of each run, Pallas kernels for 15% -> 15%
where the time goes in v6:
time: 130 us; the launch traced here: 129 us
  waiting for transfers between devices  47.8 us (37%)
  Pallas kernels  38.2 us (29%)
  starting transfers between devices  35 us (27%)
  local copies, waits for them, and re-layouts  7.11 us (5%)
    pallas_call x6, Pallas kernels, call(): pl.pallas_call(kernel, out_shape=tuple(outs), in_specs=[SMEM] * len(scala...  33.5 us
    ppermute x15, starting transfers between devices, shifted(): lax.ppermute(array, 'feat', [(i, (i + step) % size) for i in range(size)])  26.4 us
    ppermute x15, waiting for transfers between devices, shifted(): lax.ppermute(array, 'feat', [(i, (i + step) % size) for i in range(size)])  26.3 us
    ppermute x7, waiting for transfers between devices, swapped(): lax.ppermute(array, 'node', [(i, i ^ 1 << bit) for i in range(lax.axis_si...  21.5 us
    ppermute x7, starting transfers between devices, swapped(): lax.ppermute(array, 'node', [(i, i ^ 1 << bit) for i in range(lax.axis_si...  8.59 us
    unnamed x34, local copies, waits for them, and re-layouts  4.16 us
  transfers between devices with their start and end apart: 22, of which 6 were waited for; matrix products, arithmetic and copies ran while one was open for 2% of the time, Pallas kernels for 15%

profile of v6, /device:TPU:146, one launch (start us, length us, event | category | flops | bytes accessed | tf_op | source)
XLA Modules:
  0.0 129.0 jit_solution(18429592777976810603)
XLA Ops:
  0.6 5.4 %shard_map.123 = (f32[8,128,128]{2,1,0:T(8,128)}, bf16[8,128,256]{2,1,0:T(8,128)(2,1)}, bf16[4,128,256]{2,1,0:T(8,128)(2,1)}, bf16[4,128,256]{2,1,0:T(8,128)(2,1...) custom-call(s32[4]{0:T(128)} %bitcast.30, s32[32]{0:T(128)} %bitcast.37, s32[3,1,16]{2,1,0:T(1,128)} %bitcast.24, ...), custom_call_target="tpu_custom_call" | custom-call | flops 134217728 | bytes 5636096 | tf_op jit(solution)/shard_map/pallas_call | solution.py:301
  6.1 0.0 copy-start.16
  6.1 5.9 %shard_map.125 = (bf16[16,128,256]{2,1,0:T(8,128)(2,1)}, bf16[16,128,256]{2,1,0:T(8,128)(2,1)}) custom-call(s32[4]{0:T(128)} %bitcast.31, s32[3,1,16]{2,1,0:T(1,128)} %bitcast.25, s32[3,1,16]{2,1,0:T(1,128)} %bitcast.28, bf16[48,128,128]{2,1,0:T(8,128)(2,1)} %bitcast.16, bf16[8,128,256]{2,1,0:T(8,128)(2,1)} %get-tuple-element.24.gh_hbm), custom_call_target="tpu_custom_call" | custom-call | flops 268435456 | bytes 4194304 | tf_op jit(solution)/shard_map/pallas_call | solution.py:301
  12.0 0.1 collective-permute-start.12
  12.1 0.1 collective-permute-start.13
  12.2 0.9 collective-permute-start.14
  13.1 2.1 %collective-permute-start.15 = (bf16[4,128,256]{2,1,0:T(8,128)(2,1)}, bf16[4,128,256]{2,1,0:T(8,128)(2,1)}, u32[]{:S(2)}, u32[]{:S(2)}) collective-permute-start(bf16[4,128,256]{2,1,0:T(8,128)(2,1)} %get-tuple-element.29), channel_id=1, source_target_pairs={{0,2},{1,3},{2,0},{3,1},{4,6},{5,7},{6,4},{7,5},{8,10},{9,11},{10,... | collective-permute-start | bytes 786440 | tf_op jit(solution)/shard_map/ppermute | solution.py:23
  15.3 0.6 collective-permute-start.2
  15.8 5.7 %collective-permute-done.14.a = bf16[4,128,256]{2,1,0:T(8,128)(2,1)S(1)} collective-permute-done((bf16[4,128,256]{2,1,0:T(8,128)(2,1)S(1)}, bf16[4,128,256]{2,1,0:T(8,128)(2,1)S(1)}, u32[]{:S(2)}, u32[]{:S(2)}) %collective-permute-start.14) | collective-permute-done | bytes 262176 | tf_op jit(solution)/shard_map/ppermute | solution.py:23
  21.5 2.3 %collective-permute-start.1 = (bf16[8,128,256]{2,1,0:T(8,128)(2,1)}, bf16[8,128,256]{2,1,0:T(8,128)(2,1)S(1)}, u32[]{:S(2)}, u32[]{:S(2)}) collective-permute-start(bf16[8,128,256]{2,1,0:T(8,128)(2,1)} %bitcast.8.p0), channel_id=1, source_target_pairs={{0,3},{1,0},{2,1},{3,2},{4,7},{5,4},{6,5},{7,6},{8,11},{9,8},{10,9... | collective-permute-start | bytes 1572872 | tf_op jit(solution)/shard_map/ppermute | solution.py:23
  23.8 7.0 %collective-permute-start.16 = (bf16[4,128,256]{2,1,0:T(8,128)(2,1)}, bf16[4,128,256]{2,1,0:T(8,128)(2,1)}, u32[]{:S(2)}, u32[]{:S(2)}) collective-permute-start(bf16[4,128,256]{2,1,0:T(8,128)(2,1)} %get-tuple-element.30), channel_id=1, source_target_pairs={{0,3},{1,0},{2,1},{3,2},{4,7},{5,4},{6,5},{7,6},{8,11},{9,8},{10,9... | collective-permute-start | bytes 786440 | tf_op jit(solution)/shard_map/ppermute | solution.py:23
  30.8 9.3 %collective-permute-done.16.c = bf16[4,128,256]{2,1,0:T(8,128)(2,1)} collective-permute-done((bf16[4,128,256]{2,1,0:T(8,128)(2,1)}, bf16[4,128,256]{2,1,0:T(8,128)(2,1)}, u32[]{:S(2)}, u32[]{:S(2)}) %collective-permute-start.16) | collective-permute-done | bytes 262176 | tf_op jit(solution)/shard_map/ppermute | solution.py:23
  40.2 2.1 %shard_map.126 = bf16[4,128,256]{2,1,0:T(8,128)(2,1)} custom-call(f32[4,128,256]{2,1,0:T(8,128)} %get-tuple-element.27.own, bf16[4,128,256]{2,1,0:T(8,128)(2,1)} %copy-done.14, bf16[4,128,256]{2,1,0:T(8,128)(2,1)} %collective-permute-done.15.b, bf16[4,128,256]{2,1,0:T(8,128)(2,1)} %collective-permute-done.16.c), custom_call_target="tpu_custom_call" | custom-call | bytes 1572864 | tf_op jit(solution)/shard_map/pallas_call | solution.py:301
  42.3 6.1 %collective-permute-start.17 = (bf16[4,128,256]{2,1,0:T(8,128)(2,1)}, bf16[4,128,256]{2,1,0:T(8,128)(2,1)S(1)}, u32[]{:S(2)}, u32[]{:S(2)}) collective-permute-start(bf16[4,128,256]{2,1,0:T(8,128)(2,1)} %shard_map.126), channel_id=1, source_target_pairs={{0,64},{4,68},{8,72},{12,76},{16,80},{20,84},{24,88},{28,92},{32,9... | collective-permute-start | bytes 786440 | tf_op jit(solution)/shard_map/ppermute | solution.py:18
  48.4 0.1 collective-permute-start.7
  48.5 0.8 slice.21
  49.3 0.0 collective-permute-done.1.p1
  49.3 1.7 %collective-permute-start.3 = (bf16[4,128,256]{2,1,0:T(8,128)(2,1)}, bf16[4,128,256]{2,1,0:T(8,128)(2,1)}, u32[]{:S(2)}, u32[]{:S(2)}) collective-permute-start(bf16[4,128,256]{2,1,0:T(8,128)(2,1)} %slice.21), channel_id=1, source_target_pairs={{0,1},{1,2},{2,3},{3,0},{4,5},{5,6},{6,7},{7,4},{8,9},{9,10},{10,1... | collective-permute-start | bytes 786440 | tf_op jit(solution)/shard_map/ppermute | solution.py:23
  51.0 0.7 slice.22
  51.8 20.2 %collective-permute-done.17.c_hbm = bf16[4,128,256]{2,1,0:T(8,128)(2,1)S(1)} collective-permute-done((bf16[4,128,256]{2,1,0:T(8,128)(2,1)}, bf16[4,128,256]{2,1,0:T(8,128)(2,1)S(1)}, u32[]{:S(2)}, u32[]{:S(2)}) %collective-permute-start.17) | collective-permute-done | bytes 262176 | tf_op jit(solution)/shard_map/ppermute | solution.py:18
  72.0 0.7 copy-done.11
  72.7 0.4 copy-done.7
  73.0 0.4 copy-done.8
  73.4 6.5 %shard_map.127 = (bf16[8,128,256]{2,1,0:T(8,128)(2,1)}, bf16[8,128,256]{2,1,0:T(8,128)(2,1)}, f32[4,128,256]{2,1,0:T(8,128)}, f32[4,128,256]{2,1,0:T(8,128)}, f32[8,128,256]{2,1,0:T(8,128)}) custom-call(s32[4]{0:T(128)} %bitcast.32, s32[32]{0:T(128)} %bitcast.38, s32[32]{0:T(128)} %bitcast.40, s32[3,1,16]{2,1,0:T(1,128)} %bitcast.35, s32[1]{0:T(128)} %bitcast.4.me, ...), custom_call_target="tpu_custom_call" | custom-call | flops 268435456 | bytes 7077888 | tf_op jit(solution)/shard_map/pallas_call | solution.py:301
  79.9 2.0 %collective-permute-start.18 = (bf16[8,128,256]{2,1,0:T(8,128)(2,1)}, bf16[8,128,256]{2,1,0:T(8,128)(2,1)S(1)}, u32[]{:S(2)}, u32[]{:S(2)}) collective-permute-start(bf16[8,128,256]{2,1,0:T(8,128)(2,1)} %get-tuple-element.32), channel_id=1, source_target_pairs={{0,1},{1,2},{2,3},{3,0},{4,5},{5,6},{6,7},{7,4},{8,9},{9,10},{10,1... | collective-permute-start | bytes 1572872 | tf_op jit(solution)/shard_map/ppermute | solution.py:23
  81.9 0.1 collective-permute-start.19
  82.0 6.0 %shard_map.122 = (bf16[16,128,256]{2,1,0:T(8,128)(2,1)}, bf16[16,128,256]{2,1,0:T(8,128)(2,1)}, f32[8,128,256]{2,1,0:T(8,128)}) custom-call(s32[4]{0:T(128)} %bitcast.33, s32[32]{0:T(128)} %bitcast.39, s32[32]{0:T(128)} %bitcast.41, s32[3,1,16]{2,1,0:T(1,128)} %bitcast.36, s32[1]{0:T(128)} %bitcast.4.me, bf16[8,128,256]{2,1,0:T(8,128)(2,1)} %bitcast.8.p0, ...), custom_call_target="tpu_custom_call" | custom-call | flops 268435456 | bytes 6291456 | tf_op jit(solution)/shard_map/pallas_call | solution.py:301
  88.1 0.1 collective-permute-start.5
  88.2 2.1 %collective-permute-start.6 = (bf16[16,128,256]{2,1,0:T(8,128)(2,1)}, bf16[16,128,256]{2,1,0:T(8,128)(2,1)}, u32[]{:S(2)}, u32[]{:S(2)}) collective-permute-start(bf16[16,128,256]{2,1,0:T(8,128)(2,1)} %get-tuple-element.21), channel_id=1, source_target_pairs={{0,16},{4,20},{8,24},{12,28},{16,0},{20,4},{24,8},{28,12},{32,48},... | collective-permute-start | bytes 3145736 | tf_op jit(solution)/shard_map/ppermute | solution.py:18
  90.2 0.5 collective-permute-start.9
  90.7 2.6 %collective-permute-start.8 = (bf16[8,128,256]{2,1,0:T(8,128)(2,1)}, bf16[8,128,256]{2,1,0:T(8,128)(2,1)S(1)}, u32[]{:S(2)}, u32[]{:S(2)}) collective-permute-start(bf16[8,128,256]{2,1,0:T(8,128)(2,1)} %collective-permute-done.7.p0), channel_id=1, source_target_pairs={{0,3},{1,0},{2,1},{3,2},{4,7},{5,4},{6,5},{7,6},{8,11},{9,8},{10,9... | collective-permute-start | bytes 1572872 | tf_op jit(solution)/shard_map/ppermute | solution.py:23
  93.3 0.8 copy-done.1
  94.1 2.2 %shard_map.128 = (bf16[4,128,256]{2,1,0:T(8,128)(2,1)}, bf16[4,128,256]{2,1,0:T(8,128)(2,1)}) custom-call(f32[4,128,256]{2,1,0:T(8,128)} %get-tuple-element.34.keep_r, f32[4,128,256]{2,1,0:T(8,128)} %get-tuple-element.35.keep_l, bf16[8,128,256]{2,1,0:T(8,128)(2,1)} %copy-done, bf16[8,128,256]{2,1,0:T(8,128)(2,1)} %copy-done.1), custom_call_target="tpu_custom_call" | custom-call | bytes 1048576 | tf_op jit(solution)/shard_map/pallas_call | solution.py:362
  96.4 9.8 %collective-permute-done.9.p4 = bf16[8,128,256]{2,1,0:T(8,128)(2,1)S(1)} collective-permute-done((bf16[8,128,256]{2,1,0:T(8,128)(2,1)}, bf16[8,128,256]{2,1,0:T(8,128)(2,1)S(1)}, u32[]{:S(2)}, u32[]{:S(2)}) %collective-permute-start.9) | collective-permute-done | bytes 524320 | tf_op jit(solution)/shard_map/ppermute | solution.py:23
  106.2 3.2 %collective-permute-start.21 = (bf16[4,128,256]{2,1,0:T(8,128)(2,1)}, bf16[4,128,256]{2,1,0:T(8,128)(2,1)S(1)}, u32[]{:S(2)}, u32[]{:S(2)}) collective-permute-start(bf16[4,128,256]{2,1,0:T(8,128)(2,1)} %get-tuple-element.37), channel_id=1, source_target_pairs={{0,3},{1,0},{2,1},{3,2},{4,7},{5,4},{6,5},{7,6},{8,11},{9,8},{10,9... | collective-permute-start | bytes 786440 | tf_op jit(solution)/shard_map/ppermute | solution.py:23
  109.5 0.1 collective-permute-start.10
  109.6 0.8 slice.24
  110.4 1.4 %collective-permute-done.20.b_left = bf16[4,128,256]{2,1,0:T(8,128)(2,1)S(1)} collective-permute-done((bf16[4,128,256]{2,1,0:T(8,128)(2,1)}, bf16[4,128,256]{2,1,0:T(8,128)(2,1)S(1)}, u32[]{:S(2)}, u32[]{:S(2)}) %collective-permute-start.20) | collective-permute-done | bytes 262176 | tf_op jit(solution)/shard_map/ppermute | solution.py:23
  111.8 3.2 %collective-permute-start.11 = (bf16[4,128,256]{2,1,0:T(8,128)(2,1)}, bf16[4,128,256]{2,1,0:T(8,128)(2,1)S(1)}, u32[]{:S(2)}, u32[]{:S(2)}) collective-permute-start(bf16[4,128,256]{2,1,0:T(8,128)(2,1)} %slice.24), channel_id=1, source_target_pairs={{0,3},{1,0},{2,1},{3,2},{4,7},{5,4},{6,5},{7,6},{8,11},{9,8},{10,9... | collective-permute-start | bytes 786440 | tf_op jit(solution)/shard_map/ppermute | solution.py:23
  115.0 0.7 slice_bitcast_fusion
  115.7 0.7 copy-done.13
  116.4 2.5 %shard_map.129 = bf16[8,128,256]{2,1,0:T(8,128)(2,1)} custom-call(f32[8,128,256]{2,1,0:T(8,128)} %get-tuple-element.31.own, bf16[8,128,256]{2,1,0:T(8,128)(2,1)} %copy-done, bf16[8,128,256]{2,1,0:T(8,128)(2,1)} %copy-done.1, bf16[4,128,256]{2,1,0:T(8,128)(2,1)} %copy-done.12, bf16[4,128,256]{2,1,0:T(8,128)(2,1)} %copy-done.13), custom_call_target="tpu_custom_call" | custom-call | bytes 2621440 | tf_op jit(solution)/shard_map/pallas_call | solution.py:372
  118.9 1.3 collective-permute-done.ids
  120.2 0.5 copy-done.15
  120.7 0.1 copy-done.9
  120.9 0.1 copy-done.10
  121.0 0.4 copy-done.6
  121.3 7.5 %shard_map.124 = bf16[8,128,256]{2,1,0:T(8,128)(2,1)} custom-call(s32[4]{0:T(128)} %bitcast.34, s32[3,1,16]{2,1,0:T(1,128)} %bitcast.26, s32[3,1,16]{2,1,0:T(1,128)} %bitcast.29, s32[1,16]{1,0:T(1,128)} %copy-done.15, s32[1]{0:T(128)} %bitcast.4.me, bf16[16,128,256]{2,1,0:T(8,128)(2,1)} %copy-done.6, bf16[16,128,256]{2,1,0:T(8,128)(2,1)} %collective-permute-done.6.b_hbm, ...), custom_call_target="tpu_custom_call" | custom-call | flops 402653184 | bytes 7995392 | tf_op jit(solution)/shard_map/pallas_call | solution.py:301
  (43 shorter events, 0.1 us)
Async XLA Ops:
  6.1 6.1 %copy-start.16 = (bf16[4,128,256]{2,1,0:T(8,128)(2,1)S(1)}, bf16[4,128,256]{2,1,0:T(8,128)(2,1)}, u32[]{:S(2)}) copy-start(bf16[4,128,256]{2,1,0:T(8,128)(2,1)} %get-tuple-element.28) | copy-start | bytes 786436
  12.0 59.9 %collective-permute-start.12 = (bf16[16,128,256]{2,1,0:T(8,128)(2,1)}, bf16[16,128,256]{2,1,0:T(8,128)(2,1)S(1)}, u32[]{:S(2)}, u32[]{:S(2)}) collective-permute-start(bf16[16,128,256]{2,1,0:T(8,128)(2,1)} %get-tuple-element.25), channel_id=1, source_target_pairs={{0,4},{4,0},{8,12},{12,8},{16,20},{20,16},{24,28},{28,24},{32,36},... | collective-permute-start | bytes 3145736 | tf_op jit(solution)/shard_map/ppermute | solution.py:18
  12.1 59.9 %collective-permute-start.13 = (bf16[16,128,256]{2,1,0:T(8,128)(2,1)}, bf16[16,128,256]{2,1,0:T(8,128)(2,1)S(1)}, u32[]{:S(2)}, u32[]{:S(2)}) collective-permute-start(bf16[16,128,256]{2,1,0:T(8,128)(2,1)} %get-tuple-element.26), channel_id=1, source_target_pairs={{0,16},{4,20},{8,24},{12,28},{16,0},{20,4},{24,8},{28,12},{32,48},... | collective-permute-start | bytes 3145736 | tf_op jit(solution)/shard_map/ppermute | solution.py:18
  12.2 9.3 %collective-permute-start.14 = (bf16[4,128,256]{2,1,0:T(8,128)(2,1)S(1)}, bf16[4,128,256]{2,1,0:T(8,128)(2,1)S(1)}, u32[]{:S(2)}, u32[]{:S(2)}) collective-permute-start(bf16[4,128,256]{2,1,0:T(8,128)(2,1)S(1)} %copy-done.16), channel_id=1, source_target_pairs={{0,1},{1,2},{2,3},{3,0},{4,5},{5,6},{6,7},{7,4},{8,9},{9,10},{10,1... | collective-permute-start | bytes 786440 | tf_op jit(solution)/shard_map/ppermute | solution.py:23
  13.1 10.7 %collective-permute-start.15 = (bf16[4,128,256]{2,1,0:T(8,128)(2,1)}, bf16[4,128,256]{2,1,0:T(8,128)(2,1)}, u32[]{:S(2)}, u32[]{:S(2)}) collective-permute-start(bf16[4,128,256]{2,1,0:T(8,128)(2,1)} %get-tuple-element.29), channel_id=1, source_target_pairs={{0,2},{1,3},{2,0},{3,1},{4,6},{5,7},{6,4},{7,5},{8,10},{9,11},{10,... | collective-permute-start | bytes 786440 | tf_op jit(solution)/shard_map/ppermute | solution.py:23
  15.3 33.2 %collective-permute-start.2 = (bf16[8,128,256]{2,1,0:T(8,128)(2,1)}, bf16[8,128,256]{2,1,0:T(8,128)(2,1)S(1)}, u32[]{:S(2)}, u32[]{:S(2)}) collective-permute-start(bf16[8,128,256]{2,1,0:T(8,128)(2,1)} %bitcast.8.p0), channel_id=1, source_target_pairs={{0,1},{1,2},{2,3},{3,0},{4,5},{5,6},{6,7},{7,4},{8,9},{9,10},{10,1... | collective-permute-start | bytes 1572872 | tf_op jit(solution)/shard_map/ppermute | solution.py:23
  21.5 18.7 %copy-start.14 = (bf16[4,128,256]{2,1,0:T(8,128)(2,1)}, bf16[4,128,256]{2,1,0:T(8,128)(2,1)S(1)}, u32[]{:S(2)}) copy-start(bf16[4,128,256]{2,1,0:T(8,128)(2,1)S(1)} %collective-permute-done.14.a) | copy-start | bytes 786436
  21.5 27.8 %collective-permute-start.1 = (bf16[8,128,256]{2,1,0:T(8,128)(2,1)}, bf16[8,128,256]{2,1,0:T(8,128)(2,1)S(1)}, u32[]{:S(2)}, u32[]{:S(2)}) collective-permute-start(bf16[8,128,256]{2,1,0:T(8,128)(2,1)} %bitcast.8.p0), channel_id=1, source_target_pairs={{0,3},{1,0},{2,1},{3,2},{4,7},{5,4},{6,5},{7,6},{8,11},{9,8},{10,9... | collective-permute-start | bytes 1572872 | tf_op jit(solution)/shard_map/ppermute | solution.py:23
  23.8 16.3 %collective-permute-start.16 = (bf16[4,128,256]{2,1,0:T(8,128)(2,1)}, bf16[4,128,256]{2,1,0:T(8,128)(2,1)}, u32[]{:S(2)}, u32[]{:S(2)}) collective-permute-start(bf16[4,128,256]{2,1,0:T(8,128)(2,1)} %get-tuple-element.30), channel_id=1, source_target_pairs={{0,3},{1,0},{2,1},{3,2},{4,7},{5,4},{6,5},{7,6},{8,11},{9,8},{10,9... | collective-permute-start | bytes 786440 | tf_op jit(solution)/shard_map/ppermute | solution.py:23
  42.3 29.7 %collective-permute-start.17 = (bf16[4,128,256]{2,1,0:T(8,128)(2,1)}, bf16[4,128,256]{2,1,0:T(8,128)(2,1)S(1)}, u32[]{:S(2)}, u32[]{:S(2)}) collective-permute-start(bf16[4,128,256]{2,1,0:T(8,128)(2,1)} %shard_map.126), channel_id=1, source_target_pairs={{0,64},{4,68},{8,72},{12,76},{16,80},{20,84},{24,88},{28,92},{32,9... | collective-permute-start | bytes 786440 | tf_op jit(solution)/shard_map/ppermute | solution.py:18
  48.4 31.5 %copy-start.4 = (bf16[8,128,256]{2,1,0:T(8,128)(2,1)}, bf16[8,128,256]{2,1,0:T(8,128)(2,1)S(1)}, u32[]{:S(2)}) copy-start(bf16[8,128,256]{2,1,0:T(8,128)(2,1)S(1)} %collective-permute-done.2.p4) | copy-start | bytes 1572868
  48.4 41.8 %collective-permute-start.7 = (bf16[8,128,256]{2,1,0:T(8,128)(2,1)}, bf16[8,128,256]{2,1,0:T(8,128)(2,1)}, u32[]{:S(2)}, u32[]{:S(2)}) collective-permute-start(bf16[8,128,256]{2,1,0:T(8,128)(2,1)} %bitcast.8.p0), channel_id=1, source_target_pairs={{0,64},{4,68},{8,72},{12,76},{16,80},{20,84},{24,88},{28,92},{32,9... | collective-permute-start | bytes 1572872 | tf_op jit(solution)/shard_map/ppermute | solution.py:18
  49.3 30.6 %copy-start.5 = (bf16[8,128,256]{2,1,0:T(8,128)(2,1)}, bf16[8,128,256]{2,1,0:T(8,128)(2,1)S(1)}, u32[]{:S(2)}) copy-start(bf16[8,128,256]{2,1,0:T(8,128)(2,1)S(1)} %collective-permute-done.1.p1) | copy-start | bytes 1572868
  49.3 32.7 %collective-permute-start.3 = (bf16[4,128,256]{2,1,0:T(8,128)(2,1)}, bf16[4,128,256]{2,1,0:T(8,128)(2,1)}, u32[]{:S(2)}, u32[]{:S(2)}) collective-permute-start(bf16[4,128,256]{2,1,0:T(8,128)(2,1)} %slice.21), channel_id=1, source_target_pairs={{0,1},{1,2},{2,3},{3,0},{4,5},{5,6},{6,7},{7,4},{8,9},{9,10},{10,1... | collective-permute-start | bytes 786440 | tf_op jit(solution)/shard_map/ppermute | solution.py:23
  72.0 0.7 copy-start.11
  72.0 10.1 %collective-permute-start.4 = (bf16[4,128,256]{2,1,0:T(8,128)(2,1)}, bf16[4,128,256]{2,1,0:T(8,128)(2,1)}, u32[]{:S(2)}, u32[]{:S(2)}) collective-permute-start(bf16[4,128,256]{2,1,0:T(8,128)(2,1)} %slice.22), channel_id=1, source_target_pairs={{0,3},{1,0},{2,1},{3,2},{4,7},{5,4},{6,5},{7,6},{8,11},{9,8},{10,9... | collective-permute-start | bytes 786440 | tf_op jit(solution)/shard_map/ppermute | solution.py:23
  72.0 1.1 copy-start.7
  72.0 1.4 %copy-start.8 = (bf16[16,128,256]{2,1,0:T(8,128)(2,1)}, bf16[16,128,256]{2,1,0:T(8,128)(2,1)S(1)}, u32[]{:S(2)}) copy-start(bf16[16,128,256]{2,1,0:T(8,128)(2,1)S(1)} %collective-permute-done.13.b_hbm) | copy-start | bytes 3145732
  79.9 10.8 %collective-permute-start.18 = (bf16[8,128,256]{2,1,0:T(8,128)(2,1)}, bf16[8,128,256]{2,1,0:T(8,128)(2,1)S(1)}, u32[]{:S(2)}, u32[]{:S(2)}) collective-permute-start(bf16[8,128,256]{2,1,0:T(8,128)(2,1)} %get-tuple-element.32), channel_id=1, source_target_pairs={{0,1},{1,2},{2,3},{3,0},{4,5},{5,6},{6,7},{7,4},{8,9},{9,10},{10,1... | collective-permute-start | bytes 1572872 | tf_op jit(solution)/shard_map/ppermute | solution.py:23
  81.9 11.4 %collective-permute-start.19 = (bf16[8,128,256]{2,1,0:T(8,128)(2,1)}, bf16[8,128,256]{2,1,0:T(8,128)(2,1)S(1)}, u32[]{:S(2)}, u32[]{:S(2)}) collective-permute-start(bf16[8,128,256]{2,1,0:T(8,128)(2,1)} %get-tuple-element.33), channel_id=1, source_target_pairs={{0,3},{1,0},{2,1},{3,2},{4,7},{5,4},{6,5},{7,6},{8,11},{9,8},{10,9... | collective-permute-start | bytes 1572872 | tf_op jit(solution)/shard_map/ppermute | solution.py:23
  88.1 32.1 %collective-permute-start.5 = (bf16[16,128,256]{2,1,0:T(8,128)(2,1)}, bf16[16,128,256]{2,1,0:T(8,128)(2,1)S(1)}, u32[]{:S(2)}, u32[]{:S(2)}) collective-permute-start(bf16[16,128,256]{2,1,0:T(8,128)(2,1)} %get-tuple-element.20), channel_id=1, source_target_pairs={{0,4},{4,0},{8,12},{12,8},{16,20},{20,16},{24,28},{28,24},{32,36},... | collective-permute-start | bytes 3145736 | tf_op jit(solution)/shard_map/ppermute | solution.py:18
  88.2 32.0 %collective-permute-start.6 = (bf16[16,128,256]{2,1,0:T(8,128)(2,1)}, bf16[16,128,256]{2,1,0:T(8,128)(2,1)}, u32[]{:S(2)}, u32[]{:S(2)}) collective-permute-start(bf16[16,128,256]{2,1,0:T(8,128)(2,1)} %get-tuple-element.21), channel_id=1, source_target_pairs={{0,16},{4,20},{8,24},{12,28},{16,0},{20,4},{24,8},{28,12},{32,48},... | collective-permute-start | bytes 3145736 | tf_op jit(solution)/shard_map/ppermute | solution.py:18
  90.2 15.9 %collective-permute-start.9 = (bf16[8,128,256]{2,1,0:T(8,128)(2,1)}, bf16[8,128,256]{2,1,0:T(8,128)(2,1)S(1)}, u32[]{:S(2)}, u32[]{:S(2)}) collective-permute-start(bf16[8,128,256]{2,1,0:T(8,128)(2,1)} %collective-permute-done.7.p0), channel_id=1, source_target_pairs={{0,1},{1,2},{2,3},{3,0},{4,5},{5,6},{6,7},{7,4},{8,9},{9,10},{10,1... | collective-permute-start | bytes 1572872 | tf_op jit(solution)/shard_map/ppermute | solution.py:23
  90.7 2.6 %copy-start = (bf16[8,128,256]{2,1,0:T(8,128)(2,1)}, bf16[8,128,256]{2,1,0:T(8,128)(2,1)S(1)}, u32[]{:S(2)}) copy-start(bf16[8,128,256]{2,1,0:T(8,128)(2,1)S(1)} %collective-permute-done.18.from_left.a_left) | copy-start | bytes 1572868
  90.7 18.7 %collective-permute-start.8 = (bf16[8,128,256]{2,1,0:T(8,128)(2,1)}, bf16[8,128,256]{2,1,0:T(8,128)(2,1)S(1)}, u32[]{:S(2)}, u32[]{:S(2)}) collective-permute-start(bf16[8,128,256]{2,1,0:T(8,128)(2,1)} %collective-permute-done.7.p0), channel_id=1, source_target_pairs={{0,3},{1,0},{2,1},{3,2},{4,7},{5,4},{6,5},{7,6},{8,11},{9,8},{10,9... | collective-permute-start | bytes 1572872 | tf_op jit(solution)/shard_map/ppermute | solution.py:23
  93.3 0.8 copy-start.1
  96.4 15.4 %collective-permute-start.20 = (bf16[4,128,256]{2,1,0:T(8,128)(2,1)}, bf16[4,128,256]{2,1,0:T(8,128)(2,1)S(1)}, u32[]{:S(2)}, u32[]{:S(2)}) collective-permute-start(bf16[4,128,256]{2,1,0:T(8,128)(2,1)} %get-tuple-element.36), channel_id=1, source_target_pairs={{0,1},{1,2},{2,3},{3,0},{4,5},{5,6},{6,7},{7,4},{8,9},{9,10},{10,1... | collective-permute-start | bytes 786440 | tf_op jit(solution)/shard_map/ppermute | solution.py:23
  106.2 12.7 %copy-start.2 = (bf16[8,128,256]{2,1,0:T(8,128)(2,1)}, bf16[8,128,256]{2,1,0:T(8,128)(2,1)S(1)}, u32[]{:S(2)}) copy-start(bf16[8,128,256]{2,1,0:T(8,128)(2,1)S(1)} %collective-permute-done.9.p4) | copy-start | bytes 1572868
  106.2 9.5 %collective-permute-start.21 = (bf16[4,128,256]{2,1,0:T(8,128)(2,1)}, bf16[4,128,256]{2,1,0:T(8,128)(2,1)S(1)}, u32[]{:S(2)}, u32[]{:S(2)}) collective-permute-start(bf16[4,128,256]{2,1,0:T(8,128)(2,1)} %get-tuple-element.37), channel_id=1, source_target_pairs={{0,3},{1,0},{2,1},{3,2},{4,7},{5,4},{6,5},{7,6},{8,11},{9,8},{10,9... | collective-permute-start | bytes 786440 | tf_op jit(solution)/shard_map/ppermute | solution.py:23
  109.5 9.4 %copy-start.3 = (bf16[8,128,256]{2,1,0:T(8,128)(2,1)}, bf16[8,128,256]{2,1,0:T(8,128)(2,1)S(1)}, u32[]{:S(2)}) copy-start(bf16[8,128,256]{2,1,0:T(8,128)(2,1)S(1)} %collective-permute-done.8.p1) | copy-start | bytes 1572868
  109.5 10.7 %collective-permute-start.10 = (bf16[4,128,256]{2,1,0:T(8,128)(2,1)S(1)}, bf16[4,128,256]{2,1,0:T(8,128)(2,1)S(1)}, u32[]{:S(2)}, u32[]{:S(2)}) collective-permute-start(bf16[4,128,256]{2,1,0:T(8,128)(2,1)S(1)} %slice.23), channel_id=1, source_target_pairs={{0,1},{1,2},{2,3},{3,0},{4,5},{5,6},{6,7},{7,4},{8,9},{9,10},{10,1... | collective-permute-start | bytes 786440 | tf_op jit(solution)/shard_map/ppermute | solution.py:23
  111.8 3.9 %copy-start.12 = (bf16[4,128,256]{2,1,0:T(8,128)(2,1)}, bf16[4,128,256]{2,1,0:T(8,128)(2,1)S(1)}, u32[]{:S(2)}) copy-start(bf16[4,128,256]{2,1,0:T(8,128)(2,1)S(1)} %collective-permute-done.20.b_left) | copy-start | bytes 786436
  111.8 8.4 %collective-permute-start.11 = (bf16[4,128,256]{2,1,0:T(8,128)(2,1)}, bf16[4,128,256]{2,1,0:T(8,128)(2,1)S(1)}, u32[]{:S(2)}, u32[]{:S(2)}) collective-permute-start(bf16[4,128,256]{2,1,0:T(8,128)(2,1)} %slice.24), channel_id=1, source_target_pairs={{0,3},{1,0},{2,1},{3,2},{4,7},{5,4},{6,5},{7,6},{8,11},{9,8},{10,9... | collective-permute-start | bytes 786440 | tf_op jit(solution)/shard_map/ppermute | solution.py:23
  115.7 0.7 copy-start.13
  115.7 4.5 %collective-permute-start = (s32[1,16]{1,0:T(1,128)S(1)}, s32[1,16]{1,0:T(1,128)S(1)}, u32[]{:S(2)}, u32[]{:S(2)}) collective-permute-start(s32[1,16]{1,0:T(1,128)S(1)} %slice_bitcast_fusion), channel_id=1, source_target_pairs={{0,64},{4,68},{8,72},{12,76},{16,80},{20,84},{24,88},{28,92},{32,9... | collective-permute-start | bytes 200 | tf_op jit(solution)/shard_map/ppermute | solution.py:18
  120.2 0.6 copy-start.15
  120.2 0.7 copy-start.9
  120.2 0.8 copy-start.10
  120.2 1.1 copy-start.6

commit v7 on v6

--- a/solution.py
+++ b/solution.py
@@ -227,23 +227,33 @@
         end(*pick)
 
 
-def far_kernel(counts, rrows, rslots, ids, me, a_hbm, b_hbm, p0, p1, p2, p3, p4, rv_hbm, near_hbm, deg_hbm, w_ref,
-               out_ref, src, vals, acc, deg, sems):
+def mid_kernel(counts, rrows, rslots, ids, me, a_hbm, p0, p1, p2, p3, p4, rv_hbm, near_hbm,
+               out_ref, src, vals, acc, sems):
     total = out_ref.shape[0]
     cap = rrows.shape[2]
-    pairs = [(near_hbm, acc.at[pl.ds(0, total)]), (rv_hbm, vals)]
-    pairs += pieces_into((a_hbm, b_hbm, p0, p1, p2, p3, p4), src, 0) + [(deg_hbm, deg)]
+    part = src.shape[0] - cap
+    pairs = [(near_hbm, acc.at[pl.ds(0, total)])]
+    pairs += [(rv_hbm.at[pl.ds(0, cap)], vals.at[pl.ds(0, cap)])]
+    pairs += [(rv_hbm.at[pl.ds(2 * cap, cap)], vals.at[pl.ds(cap, cap)])]
+    pairs += pieces_into((a_hbm, p0, p1, p2, p3, p4), src, 0)
     wait_all(start_all(pairs, sems))
-    for r in range(2):
-        forward_tiles(
-            counts[r + 1], r * cap, vals, lambda t: rrows[r, 0, t], lambda t: src[r * cap + rslots[r, 0, t]], acc
-        )
-    part = src.shape[0] - 2 * cap
+    forward_tiles(counts[1], 0, vals, lambda t: rrows[0, 0, t], lambda t: src[rslots[0, 0, t]], acc)
     shift = me[0] * p0.shape[0]
     forward_tiles(
-        counts[3], 2 * cap, vals, lambda t: rrows[2, 0, t],
-        lambda t: src[2 * cap + lax.rem(ids[0, rslots[2, 0, t]] - shift + part, part)], acc,
-    )
+        counts[3], cap, vals, lambda t: rrows[2, 0, t],
+        lambda t: src[cap + lax.rem(ids[2, 0, rslots[2, 0, t]] - shift + part, part)], acc,
+    )
+    out_ref[...] = acc[:total]
+
+
+def far_kernel(counts, rrows, rslots, b_hbm, rv_hbm, near_hbm, deg_hbm, w_ref, out_ref, src, vals, acc, deg, sems):
+    total = out_ref.shape[0]
+    cap = rrows.shape[2]
+    pairs = [
+        (near_hbm, acc.at[pl.ds(0, total)]), (rv_hbm.at[pl.ds(cap, cap)], vals), (b_hbm, src), (deg_hbm, deg)
+    ]
+    wait_all(start_all(pairs, sems))
+    forward_tiles(counts[2], 0, vals, lambda t: rrows[1, 0, t], lambda t: src[rslots[1, 0, t]], acc)
     width = deg.shape[2]
     for b in range(total):
         hidden = jnp.concatenate(
@@ -321,7 +331,7 @@
 
     part_feats = spread_relayed(feats)
     partner_feats = spread_relayed(swapped(feats, bits[2]))
-    ids = swapped(sends[2], bits[2])
+    ids = swapped(sends, bits[2])
 
     deg, gh, z_next, z_far, z_before, z_own = call(
         degree_kernel, (counts, lrows, rrows, rslots, me), (lv, rv, go, weight),
@@ -378,11 +388,14 @@
         cost_estimate=pl.CostEstimate(flops=0, bytes_accessed=10 * own * rows * width, transcendentals=0),
     )(own_part, a_left, a_right, b_left, b_right)
 
+    mid = call(
+        mid_kernel, (counts, rrows, rslots, ids, me), (got_a,) + partner_feats + (rv, near),
+        [blocks(own, F32)],
+        [room(cap + part, BF16), tiles(2 * cap), room(own + 1, F32), sems(9)], 2 * cap * tile_flops,
+    )[0]
     output = call(
-        far_kernel, (counts, rrows, rslots, ids, me),
-        (got_a, got_b) + partner_feats + (rv, near, deg, weight), [blocks(own, BF16)],
-        [room(2 * cap + part, BF16), tiles(rounds * cap), room(own + 1, F32), tiles(own, F32), sems(10)],
-        rounds * cap * tile_flops, (10,),
+        far_kernel, (counts, rrows, rslots), (got_b, rv, mid, deg, weight), [blocks(own, BF16)],
+        [room(cap, BF16), tiles(cap), room(own + 1, F32), tiles(own, F32), sems(4)], cap * tile_flops, (4,),
     )[0]
     return (output.reshape(rows_dev, width), grad_features.reshape(rows_dev, width))
 

time: 130 us -> 132 us (1.015)
  Pallas kernels: 38.2 us -> 41.2 us
    pallas_call x6 -> x7, Pallas kernels: 33.5 us -> 36.5 us  [call(): pl.pallas_call(kernel, out_shape=tuple(outs), in_specs=[SMEM] * len(scala...]
    ppermute x7, starting transfers between devices: 8.59 us -> 7.17 us  [swapped(): lax.ppermute(array, 'node', [(i, i ^ 1 << bit) for i in range(lax.axis_si...]
  transfers between devices with their start and end apart: 22 -> 22, of which waited for: 6 -> 8; matrix products, arithmetic and copies ran while one was open for 2% -> 1% of each run, Pallas kernels for 15% -> 19%
where the time goes in v7:
time: 132 us; the launch traced here: 131 us
  waiting for transfers between devices  48.5 us (37%)
  Pallas kernels  41.2 us (31%)
  starting transfers between devices  34.1 us (26%)
  local copies, waits for them, and re-layouts  6.01 us (5%)
    pallas_call x7, Pallas kernels, call(): pl.pallas_call(kernel, out_shape=tuple(outs), in_specs=[SMEM] * len(scala...  36.5 us
    ppermute x15, starting transfers between devices, shifted(): lax.ppermute(array, 'feat', [(i, (i + step) % size) for i in range(size)])  27 us
    ppermute x15, waiting for transfers between devices, shifted(): lax.ppermute(array, 'feat', [(i, (i + step) % size) for i in range(size)])  26.4 us
    ppermute x7, waiting for transfers between devices, swapped(): lax.ppermute(array, 'node', [(i, i ^ 1 << bit) for i in range(lax.axis_si...  22.1 us
    ppermute x7, starting transfers between devices, swapped(): lax.ppermute(array, 'node', [(i, i ^ 1 << bit) for i in range(lax.axis_si...  7.17 us
    unnamed x34, local copies, waits for them, and re-layouts  4.5 us
  transfers between devices with their start and end apart: 22, of which 8 were waited for; matrix products, arithmetic and copies ran while one was open for 1% of the time, Pallas kernels for 19%

profile of v7, /device:TPU:146, one launch (start us, length us, event | category | flops | bytes accessed | tf_op | source)
XLA Modules:
  0.0 130.8 jit_solution(10426595871360314970)
XLA Ops:
  0.6 5.4 %shard_map.124 = (f32[8,128,128]{2,1,0:T(8,128)}, bf16[8,128,256]{2,1,0:T(8,128)(2,1)}, bf16[4,128,256]{2,1,0:T(8,128)(2,1)}, bf16[4,128,256]{2,1,0:T(8,128)(2,1...) custom-call(s32[4]{0:T(128)} %bitcast.31, s32[32]{0:T(128)} %bitcast.40, s32[3,1,16]{2,1,0:T(1,128)} %bitcast.23, ...), custom_call_target="tpu_custom_call" | custom-call | flops 134217728 | bytes 5636096 | tf_op jit(solution)/shard_map/pallas_call | solution.py:311
  6.1 5.9 %shard_map.126 = (bf16[16,128,256]{2,1,0:T(8,128)(2,1)}, bf16[16,128,256]{2,1,0:T(8,128)(2,1)}) custom-call(s32[4]{0:T(128)} %bitcast.32, s32[3,1,16]{2,1,0:T(1,128)} %bitcast.24, s32[3,1,16]{2,1,0:T(1,128)} %bitcast.28, bf16[48,128,128]{2,1,0:T(8,128)(2,1)} %bitcast.14, bf16[8,128,256]{2,1,0:T(8,128)(2,1)} %get-tuple-element.24.gh_hbm), custom_call_target="tpu_custom_call" | custom-call | flops 268435456 | bytes 4194304 | tf_op jit(solution)/shard_map/pallas_call | solution.py:311
  12.0 0.1 collective-permute-start.12
  12.1 0.1 collective-permute-start.13
  12.2 0.9 collective-permute-start.14
  13.1 2.1 %collective-permute-start.15 = (bf16[4,128,256]{2,1,0:T(8,128)(2,1)}, bf16[4,128,256]{2,1,0:T(8,128)(2,1)}, u32[]{:S(2)}, u32[]{:S(2)}) collective-permute-start(bf16[4,128,256]{2,1,0:T(8,128)(2,1)} %get-tuple-element.29), channel_id=1, source_target_pairs={{0,2},{1,3},{2,0},{3,1},{4,6},{5,7},{6,4},{7,5},{8,10},{9,11},{10,... | collective-permute-start | bytes 786440 | tf_op jit(solution)/shard_map/ppermute | solution.py:23
  15.3 2.6 %collective-permute-start = (bf16[8,128,256]{2,1,0:T(8,128)(2,1)}, bf16[8,128,256]{2,1,0:T(8,128)(2,1)S(1)}, u32[]{:S(2)}, u32[]{:S(2)}) collective-permute-start(bf16[8,128,256]{2,1,0:T(8,128)(2,1)} %bitcast.7.p0), channel_id=1, source_target_pairs={{0,3},{1,0},{2,1},{3,2},{4,7},{5,4},{6,5},{7,6},{8,11},{9,8},{10,9... | collective-permute-start | bytes 1572872 | tf_op jit(solution)/shard_map/ppermute | solution.py:23
  17.9 3.6 %collective-permute-done.14.a = bf16[4,128,256]{2,1,0:T(8,128)(2,1)S(1)} collective-permute-done((bf16[4,128,256]{2,1,0:T(8,128)(2,1)S(1)}, bf16[4,128,256]{2,1,0:T(8,128)(2,1)S(1)}, u32[]{:S(2)}, u32[]{:S(2)}) %collective-permute-start.14) | collective-permute-done | bytes 262176 | tf_op jit(solution)/shard_map/ppermute | solution.py:23
  21.5 1.0 collective-permute-start.1
  22.5 1.7 %collective-permute-done.15.b = bf16[4,128,256]{2,1,0:T(8,128)(2,1)} collective-permute-done((bf16[4,128,256]{2,1,0:T(8,128)(2,1)}, bf16[4,128,256]{2,1,0:T(8,128)(2,1)}, u32[]{:S(2)}, u32[]{:S(2)}) %collective-permute-start.15) | collective-permute-done | bytes 262176 | tf_op jit(solution)/shard_map/ppermute | solution.py:23
  24.2 6.6 %collective-permute-start.16 = (bf16[4,128,256]{2,1,0:T(8,128)(2,1)}, bf16[4,128,256]{2,1,0:T(8,128)(2,1)}, u32[]{:S(2)}, u32[]{:S(2)}) collective-permute-start(bf16[4,128,256]{2,1,0:T(8,128)(2,1)} %get-tuple-element.30), channel_id=1, source_target_pairs={{0,3},{1,0},{2,1},{3,2},{4,7},{5,4},{6,5},{7,6},{8,11},{9,8},{10,9... | collective-permute-start | bytes 786440 | tf_op jit(solution)/shard_map/ppermute | solution.py:23
  30.8 9.1 %collective-permute-done.16.c = bf16[4,128,256]{2,1,0:T(8,128)(2,1)} collective-permute-done((bf16[4,128,256]{2,1,0:T(8,128)(2,1)}, bf16[4,128,256]{2,1,0:T(8,128)(2,1)}, u32[]{:S(2)}, u32[]{:S(2)}) %collective-permute-start.16) | collective-permute-done | bytes 262176 | tf_op jit(solution)/shard_map/ppermute | solution.py:23
  39.9 2.1 %shard_map.127 = bf16[4,128,256]{2,1,0:T(8,128)(2,1)} custom-call(f32[4,128,256]{2,1,0:T(8,128)} %get-tuple-element.27.own, bf16[4,128,256]{2,1,0:T(8,128)(2,1)} %copy-done.12, bf16[4,128,256]{2,1,0:T(8,128)(2,1)} %collective-permute-done.15.b, bf16[4,128,256]{2,1,0:T(8,128)(2,1)} %collective-permute-done.16.c), custom_call_target="tpu_custom_call" | custom-call | bytes 1572864 | tf_op jit(solution)/shard_map/pallas_call | solution.py:311
  42.0 1.7 %collective-permute-start.17 = (bf16[4,128,256]{2,1,0:T(8,128)(2,1)}, bf16[4,128,256]{2,1,0:T(8,128)(2,1)S(1)}, u32[]{:S(2)}, u32[]{:S(2)}) collective-permute-start(bf16[4,128,256]{2,1,0:T(8,128)(2,1)} %shard_map.127), channel_id=1, source_target_pairs={{0,64},{4,68},{8,72},{12,76},{16,80},{20,84},{24,88},{28,92},{32,9... | collective-permute-start | bytes 786440 | tf_op jit(solution)/shard_map/ppermute | solution.py:18
  43.7 1.2 collective-permute-start.7
  44.9 0.7 slice.16
  45.6 0.6 collective-permute-start.2
  46.2 0.7 slice.17
  47.0 20.7 %collective-permute-done.17.c_hbm = bf16[4,128,256]{2,1,0:T(8,128)(2,1)S(1)} collective-permute-done((bf16[4,128,256]{2,1,0:T(8,128)(2,1)}, bf16[4,128,256]{2,1,0:T(8,128)(2,1)S(1)}, u32[]{:S(2)}, u32[]{:S(2)}) %collective-permute-start.17) | collective-permute-done | bytes 262176 | tf_op jit(solution)/shard_map/ppermute | solution.py:18
  67.7 0.5 collective-permute-start.3
  68.2 0.2 copy-done.9
  68.4 0.8 copy-done.7
  69.2 0.4 copy-done.8
  69.6 6.5 %shard_map.128 = (bf16[8,128,256]{2,1,0:T(8,128)(2,1)}, bf16[8,128,256]{2,1,0:T(8,128)(2,1)}, f32[4,128,256]{2,1,0:T(8,128)}, f32[4,128,256]{2,1,0:T(8,128)}, f32[8,128,256]{2,1,0:T(8,128)}) custom-call(s32[4]{0:T(128)} %bitcast.33, s32[32]{0:T(128)} %bitcast.41, s32[32]{0:T(128)} %bitcast.43, s32[3,1,16]{2,1,0:T(1,128)} %bitcast.37, s32[1]{0:T(128)} %bitcast.6.me, ...), custom_call_target="tpu_custom_call" | custom-call | flops 268435456 | bytes 7077888 | tf_op jit(solution)/shard_map/pallas_call | solution.py:311
  76.1 1.7 %collective-permute-start.18 = (bf16[8,128,256]{2,1,0:T(8,128)(2,1)}, bf16[8,128,256]{2,1,0:T(8,128)(2,1)S(1)}, u32[]{:S(2)}, u32[]{:S(2)}) collective-permute-start(bf16[8,128,256]{2,1,0:T(8,128)(2,1)} %get-tuple-element.32), channel_id=1, source_target_pairs={{0,1},{1,2},{2,3},{3,0},{4,5},{5,6},{6,7},{7,4},{8,9},{9,10},{10,1... | collective-permute-start | bytes 1572872 | tf_op jit(solution)/shard_map/ppermute | solution.py:23
  77.7 1.3 collective-permute-start.19
  79.0 6.0 %shard_map.122 = (bf16[16,128,256]{2,1,0:T(8,128)(2,1)}, bf16[16,128,256]{2,1,0:T(8,128)(2,1)}, f32[8,128,256]{2,1,0:T(8,128)}) custom-call(s32[4]{0:T(128)} %bitcast.34, s32[32]{0:T(128)} %bitcast.42, s32[32]{0:T(128)} %bitcast.44, s32[3,1,16]{2,1,0:T(1,128)} %bitcast.38, s32[1]{0:T(128)} %bitcast.6.me, bf16[8,128,256]{2,1,0:T(8,128)(2,1)} %bitcast.7.p0, ...), custom_call_target="tpu_custom_call" | custom-call | flops 268435456 | bytes 6291456 | tf_op jit(solution)/shard_map/pallas_call | solution.py:311
  85.0 0.1 collective-permute-start.6
  85.1 3.9 %collective-permute-start.4 = (bf16[16,128,256]{2,1,0:T(8,128)(2,1)}, bf16[16,128,256]{2,1,0:T(8,128)(2,1)S(1)}, u32[]{:S(2)}, u32[]{:S(2)}) collective-permute-start(bf16[16,128,256]{2,1,0:T(8,128)(2,1)} %get-tuple-element.20), channel_id=1, source_target_pairs={{0,16},{4,20},{8,24},{12,28},{16,0},{20,4},{24,8},{28,12},{32,48},... | collective-permute-start | bytes 3145736 | tf_op jit(solution)/shard_map/ppermute | solution.py:18
  89.0 0.0 collective-permute-start.9
  89.1 2.6 %collective-permute-done.18.from_left.a_left = bf16[8,128,256]{2,1,0:T(8,128)(2,1)S(1)} collective-permute-done((bf16[8,128,256]{2,1,0:T(8,128)(2,1)}, bf16[8,128,256]{2,1,0:T(8,128)(2,1)S(1)}, u32[]{:S(2)}, u32[]{:S(2)}) %collective-permute-start.18) | collective-permute-done | bytes 524320 | tf_op jit(solution)/shard_map/ppermute | solution.py:23
  91.7 3.0 %collective-permute-start.8 = (bf16[8,128,256]{2,1,0:T(8,128)(2,1)}, bf16[8,128,256]{2,1,0:T(8,128)(2,1)S(1)}, u32[]{:S(2)}, u32[]{:S(2)}) collective-permute-start(bf16[8,128,256]{2,1,0:T(8,128)(2,1)} %collective-permute-done.7.p0), channel_id=1, source_target_pairs={{0,3},{1,0},{2,1},{3,2},{4,7},{5,4},{6,5},{7,6},{8,11},{9,8},{10,9... | collective-permute-start | bytes 1572872 | tf_op jit(solution)/shard_map/ppermute | solution.py:23
  94.6 0.8 copy-done.1
  95.5 2.2 %shard_map.129 = (bf16[4,128,256]{2,1,0:T(8,128)(2,1)}, bf16[4,128,256]{2,1,0:T(8,128)(2,1)}) custom-call(f32[4,128,256]{2,1,0:T(8,128)} %get-tuple-element.34.keep_r, f32[4,128,256]{2,1,0:T(8,128)} %get-tuple-element.35.keep_l, bf16[8,128,256]{2,1,0:T(8,128)(2,1)} %copy-done, bf16[8,128,256]{2,1,0:T(8,128)(2,1)} %copy-done.1), custom_call_target="tpu_custom_call" | custom-call | bytes 1048576 | tf_op jit(solution)/shard_map/pallas_call | solution.py:372
  97.7 7.3 %collective-permute-done.9.p4 = bf16[8,128,256]{2,1,0:T(8,128)(2,1)S(1)} collective-permute-done((bf16[8,128,256]{2,1,0:T(8,128)(2,1)}, bf16[8,128,256]{2,1,0:T(8,128)(2,1)S(1)}, u32[]{:S(2)}, u32[]{:S(2)}) %collective-permute-start.9) | collective-permute-done | bytes 524320 | tf_op jit(solution)/shard_map/ppermute | solution.py:23
  105.0 3.2 %collective-permute-start.21 = (bf16[4,128,256]{2,1,0:T(8,128)(2,1)}, bf16[4,128,256]{2,1,0:T(8,128)(2,1)S(1)}, u32[]{:S(2)}, u32[]{:S(2)}) collective-permute-start(bf16[4,128,256]{2,1,0:T(8,128)(2,1)} %get-tuple-element.37), channel_id=1, source_target_pairs={{0,3},{1,0},{2,1},{3,2},{4,7},{5,4},{6,5},{7,6},{8,11},{9,8},{10,9... | collective-permute-start | bytes 786440 | tf_op jit(solution)/shard_map/ppermute | solution.py:23
  108.2 0.1 collective-permute-start.10
  108.4 2.2 %collective-permute-done.20.b_left = bf16[4,128,256]{2,1,0:T(8,128)(2,1)S(1)} collective-permute-done((bf16[4,128,256]{2,1,0:T(8,128)(2,1)}, bf16[4,128,256]{2,1,0:T(8,128)(2,1)S(1)}, u32[]{:S(2)}, u32[]{:S(2)}) %collective-permute-start.20) | collective-permute-done | bytes 262176 | tf_op jit(solution)/shard_map/ppermute | solution.py:23
  110.6 3.2 %collective-permute-start.11 = (bf16[4,128,256]{2,1,0:T(8,128)(2,1)S(1)}, bf16[4,128,256]{2,1,0:T(8,128)(2,1)}, u32[]{:S(2)}, u32[]{:S(2)}) collective-permute-start(bf16[4,128,256]{2,1,0:T(8,128)(2,1)S(1)} %slice.19), channel_id=1, source_target_pairs={{0,3},{1,0},{2,1},{3,2},{4,7},{5,4},{6,5},{7,6},{8,11},{9,8},{10,9... | collective-permute-start | bytes 786440 | tf_op jit(solution)/shard_map/ppermute | solution.py:23
  113.8 0.1 collective-permute-start.5
  113.9 0.6 copy-done.11
  114.6 2.5 %shard_map.130 = bf16[8,128,256]{2,1,0:T(8,128)(2,1)} custom-call(f32[8,128,256]{2,1,0:T(8,128)} %get-tuple-element.31.own, bf16[8,128,256]{2,1,0:T(8,128)(2,1)} %copy-done, bf16[8,128,256]{2,1,0:T(8,128)(2,1)} %copy-done.1, bf16[4,128,256]{2,1,0:T(8,128)(2,1)} %copy-done.10, bf16[4,128,256]{2,1,0:T(8,128)(2,1)} %copy-done.11), custom_call_target="tpu_custom_call" | custom-call | bytes 2621440 | tf_op jit(solution)/shard_map/pallas_call | solution.py:382
  117.0 1.4 %collective-permute-done.5.ids = s32[3,1,16]{2,1,0:T(1,128)S(1)} collective-permute-done((s32[3,1,16]{2,1,0:T(1,128)S(1)}, s32[3,1,16]{2,1,0:T(1,128)S(1)}, u32[]{:S(2)}, u32[]{:S(2)}) %collective-permute-start.5) | collective-permute-done | bytes 224 | tf_op jit(solution)/shard_map/ppermute | solution.py:18
  118.4 0.6 copy-done.15
  119.0 0.1 copy-done.13
  119.1 5.8 %shard_map.123.near_hbm = f32[8,128,256]{2,1,0:T(8,128)} custom-call(s32[4]{0:T(128)} %bitcast.35, s32[3,1,16]{2,1,0:T(1,128)} %bitcast.25, s32[3,1,16]{2,1,0:T(1,128)} %bitcast.29, s32[3,1,16]{2,1,0:T(1,128)} %copy-done.15, s32[1]{0:T(128)} %bitcast.6.me, bf16[16,128,256]{2,1,0:T(8,128)(2,1)} %collective-permute-done.6.a_hbm, ...), custom_call_target="tpu_custom_call" | custom-call | flops 268435456 | bytes 6815744 | tf_op jit(solution)/shard_map/pallas_call | solution.py:311
  124.9 1.0 copy-done.6
  125.9 4.8 %shard_map.125 = bf16[8,128,256]{2,1,0:T(8,128)(2,1)} custom-call(s32[4]{0:T(128)} %bitcast.36, s32[3,1,16]{2,1,0:T(1,128)} %bitcast.26, s32[3,1,16]{2,1,0:T(1,128)} %bitcast.30, bf16[16,128,256]{2,1,0:T(8,128)(2,1)} %copy-done.6, bf16[48,128,128]{2,1,0:T(8,128)(2,1)} %bitcast.16, f32[8,128,256]{2,1,0:T(8,128)} %shard_map.123.near_hbm, ...), custom_call_target="tpu_custom_call" | custom-call | flops 134217728 | bytes 4849664 | tf_op jit(solution)/shard_map/pallas_call | solution.py:311
  (43 shorter events, 0.1 us)
Async XLA Ops:
  6.1 6.1 %copy-start.16 = (bf16[4,128,256]{2,1,0:T(8,128)(2,1)S(1)}, bf16[4,128,256]{2,1,0:T(8,128)(2,1)}, u32[]{:S(2)}) copy-start(bf16[4,128,256]{2,1,0:T(8,128)(2,1)} %get-tuple-element.28) | copy-start | bytes 786436
  12.0 56.2 %collective-permute-start.12 = (bf16[16,128,256]{2,1,0:T(8,128)(2,1)}, bf16[16,128,256]{2,1,0:T(8,128)(2,1)S(1)}, u32[]{:S(2)}, u32[]{:S(2)}) collective-permute-start(bf16[16,128,256]{2,1,0:T(8,128)(2,1)} %get-tuple-element.25), channel_id=1, source_target_pairs={{0,4},{4,0},{8,12},{12,8},{16,20},{20,16},{24,28},{28,24},{32,36},... | collective-permute-start | bytes 3145736 | tf_op jit(solution)/shard_map/ppermute | solution.py:18
  12.1 56.1 %collective-permute-start.13 = (bf16[16,128,256]{2,1,0:T(8,128)(2,1)}, bf16[16,128,256]{2,1,0:T(8,128)(2,1)S(1)}, u32[]{:S(2)}, u32[]{:S(2)}) collective-permute-start(bf16[16,128,256]{2,1,0:T(8,128)(2,1)} %get-tuple-element.26), channel_id=1, source_target_pairs={{0,16},{4,20},{8,24},{12,28},{16,0},{20,4},{24,8},{28,12},{32,48},... | collective-permute-start | bytes 3145736 | tf_op jit(solution)/shard_map/ppermute | solution.py:18
  12.2 9.3 %collective-permute-start.14 = (bf16[4,128,256]{2,1,0:T(8,128)(2,1)S(1)}, bf16[4,128,256]{2,1,0:T(8,128)(2,1)S(1)}, u32[]{:S(2)}, u32[]{:S(2)}) collective-permute-start(bf16[4,128,256]{2,1,0:T(8,128)(2,1)S(1)} %copy-done.16), channel_id=1, source_target_pairs={{0,1},{1,2},{2,3},{3,0},{4,5},{5,6},{6,7},{7,4},{8,9},{9,10},{10,1... | collective-permute-start | bytes 786440 | tf_op jit(solution)/shard_map/ppermute | solution.py:23
  13.1 11.0 %collective-permute-start.15 = (bf16[4,128,256]{2,1,0:T(8,128)(2,1)}, bf16[4,128,256]{2,1,0:T(8,128)(2,1)}, u32[]{:S(2)}, u32[]{:S(2)}) collective-permute-start(bf16[4,128,256]{2,1,0:T(8,128)(2,1)} %get-tuple-element.29), channel_id=1, source_target_pairs={{0,2},{1,3},{2,0},{3,1},{4,6},{5,7},{6,4},{7,5},{8,10},{9,11},{10,... | collective-permute-start | bytes 786440 | tf_op jit(solution)/shard_map/ppermute | solution.py:23
  15.3 30.3 %collective-permute-start = (bf16[8,128,256]{2,1,0:T(8,128)(2,1)}, bf16[8,128,256]{2,1,0:T(8,128)(2,1)S(1)}, u32[]{:S(2)}, u32[]{:S(2)}) collective-permute-start(bf16[8,128,256]{2,1,0:T(8,128)(2,1)} %bitcast.7.p0), channel_id=1, source_target_pairs={{0,3},{1,0},{2,1},{3,2},{4,7},{5,4},{6,5},{7,6},{8,11},{9,8},{10,9... | collective-permute-start | bytes 1572872 | tf_op jit(solution)/shard_map/ppermute | solution.py:23
  21.5 18.4 %copy-start.12 = (bf16[4,128,256]{2,1,0:T(8,128)(2,1)}, bf16[4,128,256]{2,1,0:T(8,128)(2,1)S(1)}, u32[]{:S(2)}) copy-start(bf16[4,128,256]{2,1,0:T(8,128)(2,1)S(1)} %collective-permute-done.14.a) | copy-start | bytes 786436
  21.5 22.2 %collective-permute-start.1 = (bf16[8,128,256]{2,1,0:T(8,128)(2,1)}, bf16[8,128,256]{2,1,0:T(8,128)(2,1)S(1)}, u32[]{:S(2)}, u32[]{:S(2)}) collective-permute-start(bf16[8,128,256]{2,1,0:T(8,128)(2,1)} %bitcast.7.p0), channel_id=1, source_target_pairs={{0,1},{1,2},{2,3},{3,0},{4,5},{5,6},{6,7},{7,4},{8,9},{9,10},{10,1... | collective-permute-start | bytes 1572872 | tf_op jit(solution)/shard_map/ppermute | solution.py:23
  24.2 15.7 %collective-permute-start.16 = (bf16[4,128,256]{2,1,0:T(8,128)(2,1)}, bf16[4,128,256]{2,1,0:T(8,128)(2,1)}, u32[]{:S(2)}, u32[]{:S(2)}) collective-permute-start(bf16[4,128,256]{2,1,0:T(8,128)(2,1)} %get-tuple-element.30), channel_id=1, source_target_pairs={{0,3},{1,0},{2,1},{3,2},{4,7},{5,4},{6,5},{7,6},{8,11},{9,8},{10,9... | collective-permute-start | bytes 786440 | tf_op jit(solution)/shard_map/ppermute | solution.py:23
  42.0 25.7 %collective-permute-start.17 = (bf16[4,128,256]{2,1,0:T(8,128)(2,1)}, bf16[4,128,256]{2,1,0:T(8,128)(2,1)S(1)}, u32[]{:S(2)}, u32[]{:S(2)}) collective-permute-start(bf16[4,128,256]{2,1,0:T(8,128)(2,1)} %shard_map.127), channel_id=1, source_target_pairs={{0,64},{4,68},{8,72},{12,76},{16,80},{20,84},{24,88},{28,92},{32,9... | collective-permute-start | bytes 786440 | tf_op jit(solution)/shard_map/ppermute | solution.py:18
  43.7 32.4 %copy-start.3 = (bf16[8,128,256]{2,1,0:T(8,128)(2,1)}, bf16[8,128,256]{2,1,0:T(8,128)(2,1)S(1)}, u32[]{:S(2)}) copy-start(bf16[8,128,256]{2,1,0:T(8,128)(2,1)S(1)} %collective-permute-done.1.p4) | copy-start | bytes 1572868
  43.7 45.4 %collective-permute-start.7 = (bf16[8,128,256]{2,1,0:T(8,128)(2,1)}, bf16[8,128,256]{2,1,0:T(8,128)(2,1)}, u32[]{:S(2)}, u32[]{:S(2)}) collective-permute-start(bf16[8,128,256]{2,1,0:T(8,128)(2,1)} %bitcast.7.p0), channel_id=1, source_target_pairs={{0,64},{4,68},{8,72},{12,76},{16,80},{20,84},{24,88},{28,92},{32,9... | collective-permute-start | bytes 1572872 | tf_op jit(solution)/shard_map/ppermute | solution.py:18
  45.6 30.4 %copy-start.2 = (bf16[8,128,256]{2,1,0:T(8,128)(2,1)}, bf16[8,128,256]{2,1,0:T(8,128)(2,1)S(1)}, u32[]{:S(2)}) copy-start(bf16[8,128,256]{2,1,0:T(8,128)(2,1)S(1)} %collective-permute-done.p1) | copy-start | bytes 1572868
  45.6 33.4 %collective-permute-start.2 = (bf16[4,128,256]{2,1,0:T(8,128)(2,1)}, bf16[4,128,256]{2,1,0:T(8,128)(2,1)}, u32[]{:S(2)}, u32[]{:S(2)}) collective-permute-start(bf16[4,128,256]{2,1,0:T(8,128)(2,1)} %slice.16), channel_id=1, source_target_pairs={{0,1},{1,2},{2,3},{3,0},{4,5},{5,6},{6,7},{7,4},{8,9},{9,10},{10,1... | collective-permute-start | bytes 786440 | tf_op jit(solution)/shard_map/ppermute | solution.py:23
  67.7 0.7 copy-start.9
  67.7 11.3 %collective-permute-start.3 = (bf16[4,128,256]{2,1,0:T(8,128)(2,1)}, bf16[4,128,256]{2,1,0:T(8,128)(2,1)}, u32[]{:S(2)}, u32[]{:S(2)}) collective-permute-start(bf16[4,128,256]{2,1,0:T(8,128)(2,1)} %slice.17), channel_id=1, source_target_pairs={{0,3},{1,0},{2,1},{3,2},{4,7},{5,4},{6,5},{7,6},{8,11},{9,8},{10,9... | collective-permute-start | bytes 786440 | tf_op jit(solution)/shard_map/ppermute | solution.py:23
  68.2 1.0 copy-start.7
  68.2 1.3 %copy-start.8 = (bf16[16,128,256]{2,1,0:T(8,128)(2,1)}, bf16[16,128,256]{2,1,0:T(8,128)(2,1)S(1)}, u32[]{:S(2)}) copy-start(bf16[16,128,256]{2,1,0:T(8,128)(2,1)S(1)} %collective-permute-done.13.b_hbm) | copy-start | bytes 3145732
  76.1 15.6 %collective-permute-start.18 = (bf16[8,128,256]{2,1,0:T(8,128)(2,1)}, bf16[8,128,256]{2,1,0:T(8,128)(2,1)S(1)}, u32[]{:S(2)}, u32[]{:S(2)}) collective-permute-start(bf16[8,128,256]{2,1,0:T(8,128)(2,1)} %get-tuple-element.32), channel_id=1, source_target_pairs={{0,1},{1,2},{2,3},{3,0},{4,5},{5,6},{6,7},{7,4},{8,9},{9,10},{10,1... | collective-permute-start | bytes 1572872 | tf_op jit(solution)/shard_map/ppermute | solution.py:23
  77.7 16.9 %collective-permute-start.19 = (bf16[8,128,256]{2,1,0:T(8,128)(2,1)}, bf16[8,128,256]{2,1,0:T(8,128)(2,1)S(1)}, u32[]{:S(2)}, u32[]{:S(2)}) collective-permute-start(bf16[8,128,256]{2,1,0:T(8,128)(2,1)} %get-tuple-element.33), channel_id=1, source_target_pairs={{0,3},{1,0},{2,1},{3,2},{4,7},{5,4},{6,5},{7,6},{8,11},{9,8},{10,9... | collective-permute-start | bytes 1572872 | tf_op jit(solution)/shard_map/ppermute | solution.py:23
  85.0 33.4 %collective-permute-start.6 = (bf16[16,128,256]{2,1,0:T(8,128)(2,1)}, bf16[16,128,256]{2,1,0:T(8,128)(2,1)}, u32[]{:S(2)}, u32[]{:S(2)}) collective-permute-start(bf16[16,128,256]{2,1,0:T(8,128)(2,1)} %get-tuple-element.21), channel_id=1, source_target_pairs={{0,4},{4,0},{8,12},{12,8},{16,20},{20,16},{24,28},{28,24},{32,36},... | collective-permute-start | bytes 3145736 | tf_op jit(solution)/shard_map/ppermute | solution.py:18
  85.1 39.7 %collective-permute-start.4 = (bf16[16,128,256]{2,1,0:T(8,128)(2,1)}, bf16[16,128,256]{2,1,0:T(8,128)(2,1)S(1)}, u32[]{:S(2)}, u32[]{:S(2)}) collective-permute-start(bf16[16,128,256]{2,1,0:T(8,128)(2,1)} %get-tuple-element.20), channel_id=1, source_target_pairs={{0,16},{4,20},{8,24},{12,28},{16,0},{20,4},{24,8},{28,12},{32,48},... | collective-permute-start | bytes 3145736 | tf_op jit(solution)/shard_map/ppermute | solution.py:18
  89.0 15.9 %collective-permute-start.9 = (bf16[8,128,256]{2,1,0:T(8,128)(2,1)}, bf16[8,128,256]{2,1,0:T(8,128)(2,1)S(1)}, u32[]{:S(2)}, u32[]{:S(2)}) collective-permute-start(bf16[8,128,256]{2,1,0:T(8,128)(2,1)} %collective-permute-done.7.p0), channel_id=1, source_target_pairs={{0,1},{1,2},{2,3},{3,0},{4,5},{5,6},{6,7},{7,4},{8,9},{9,10},{10,1... | collective-permute-start | bytes 1572872 | tf_op jit(solution)/shard_map/ppermute | solution.py:23
  91.7 3.0 %copy-start = (bf16[8,128,256]{2,1,0:T(8,128)(2,1)}, bf16[8,128,256]{2,1,0:T(8,128)(2,1)S(1)}, u32[]{:S(2)}) copy-start(bf16[8,128,256]{2,1,0:T(8,128)(2,1)S(1)} %collective-permute-done.18.from_left.a_left) | copy-start | bytes 1572868
  91.7 16.6 %collective-permute-start.8 = (bf16[8,128,256]{2,1,0:T(8,128)(2,1)}, bf16[8,128,256]{2,1,0:T(8,128)(2,1)S(1)}, u32[]{:S(2)}, u32[]{:S(2)}) collective-permute-start(bf16[8,128,256]{2,1,0:T(8,128)(2,1)} %collective-permute-done.7.p0), channel_id=1, source_target_pairs={{0,3},{1,0},{2,1},{3,2},{4,7},{5,4},{6,5},{7,6},{8,11},{9,8},{10,9... | collective-permute-start | bytes 1572872 | tf_op jit(solution)/shard_map/ppermute | solution.py:23
  94.6 0.9 copy-start.1
  95.5 18.4 %copy-start.14 = (s32[1,3,16]{2,0,1:T(1,128)S(1)}, s32[1,3,16]{2,0,1:T(1,128)}, u32[]{:S(2)}) copy-start(s32[1,3,16]{2,0,1:T(1,128)} %param.20) | copy-start | bytes 580
  97.7 12.9 %collective-permute-start.20 = (bf16[4,128,256]{2,1,0:T(8,128)(2,1)}, bf16[4,128,256]{2,1,0:T(8,128)(2,1)S(1)}, u32[]{:S(2)}, u32[]{:S(2)}) collective-permute-start(bf16[4,128,256]{2,1,0:T(8,128)(2,1)} %get-tuple-element.36), channel_id=1, source_target_pairs={{0,1},{1,2},{2,3},{3,0},{4,5},{5,6},{6,7},{7,4},{8,9},{9,10},{10,1... | collective-permute-start | bytes 786440 | tf_op jit(solution)/shard_map/ppermute | solution.py:23
  105.0 12.0 %copy-start.4 = (bf16[8,128,256]{2,1,0:T(8,128)(2,1)}, bf16[8,128,256]{2,1,0:T(8,128)(2,1)S(1)}, u32[]{:S(2)}) copy-start(bf16[8,128,256]{2,1,0:T(8,128)(2,1)S(1)} %collective-permute-done.9.p4) | copy-start | bytes 1572868
  105.0 8.9 %collective-permute-start.21 = (bf16[4,128,256]{2,1,0:T(8,128)(2,1)}, bf16[4,128,256]{2,1,0:T(8,128)(2,1)S(1)}, u32[]{:S(2)}, u32[]{:S(2)}) collective-permute-start(bf16[4,128,256]{2,1,0:T(8,128)(2,1)} %get-tuple-element.37), channel_id=1, source_target_pairs={{0,3},{1,0},{2,1},{3,2},{4,7},{5,4},{6,5},{7,6},{8,11},{9,8},{10,9... | collective-permute-start | bytes 786440 | tf_op jit(solution)/shard_map/ppermute | solution.py:23
  108.2 8.8 %copy-start.5 = (bf16[8,128,256]{2,1,0:T(8,128)(2,1)}, bf16[8,128,256]{2,1,0:T(8,128)(2,1)S(1)}, u32[]{:S(2)}) copy-start(bf16[8,128,256]{2,1,0:T(8,128)(2,1)S(1)} %collective-permute-done.8.p1) | copy-start | bytes 1572868
  108.2 10.1 %collective-permute-start.10 = (bf16[4,128,256]{2,1,0:T(8,128)(2,1)S(1)}, bf16[4,128,256]{2,1,0:T(8,128)(2,1)S(1)}, u32[]{:S(2)}, u32[]{:S(2)}) collective-permute-start(bf16[4,128,256]{2,1,0:T(8,128)(2,1)S(1)} %slice.18), channel_id=1, source_target_pairs={{0,1},{1,2},{2,3},{3,0},{4,5},{5,6},{6,7},{7,4},{8,9},{9,10},{10,1... | collective-permute-start | bytes 786440 | tf_op jit(solution)/shard_map/ppermute | solution.py:23
  110.6 3.3 %copy-start.10 = (bf16[4,128,256]{2,1,0:T(8,128)(2,1)}, bf16[4,128,256]{2,1,0:T(8,128)(2,1)S(1)}, u32[]{:S(2)}) copy-start(bf16[4,128,256]{2,1,0:T(8,128)(2,1)S(1)} %collective-permute-done.20.b_left) | copy-start | bytes 786436
  110.6 7.8 %collective-permute-start.11 = (bf16[4,128,256]{2,1,0:T(8,128)(2,1)S(1)}, bf16[4,128,256]{2,1,0:T(8,128)(2,1)}, u32[]{:S(2)}, u32[]{:S(2)}) collective-permute-start(bf16[4,128,256]{2,1,0:T(8,128)(2,1)S(1)} %slice.19), channel_id=1, source_target_pairs={{0,3},{1,0},{2,1},{3,2},{4,7},{5,4},{6,5},{7,6},{8,11},{9,8},{10,9... | collective-permute-start | bytes 786440 | tf_op jit(solution)/shard_map/ppermute | solution.py:23
  113.8 0.7 copy-start.11
  113.8 4.6 %collective-permute-start.5 = (s32[3,1,16]{2,1,0:T(1,128)S(1)}, s32[3,1,16]{2,1,0:T(1,128)S(1)}, u32[]{:S(2)}, u32[]{:S(2)}) collective-permute-start(s32[3,1,16]{2,1,0:T(1,128)S(1)} %bitcast.39), channel_id=1, source_target_pairs={{0,64},{4,68},{8,72},{12,76},{16,80},{20,84},{24,88},{28,92},{32,9... | collective-permute-start | bytes 584 | tf_op jit(solution)/shard_map/ppermute | solution.py:18
  118.4 0.6 copy-start.15
  118.4 0.7 copy-start.13
  124.9 1.0 copy-start.6

commit v8 on v6

--- a/solution.py
+++ b/solution.py
@@ -7,11 +7,13 @@
 
 
 UNROLL = 4
+VMEM_ALL = 67_043_328
 F32 = jnp.float32
 BF16 = jnp.bfloat16
 SMEM = pl.BlockSpec(memory_space=pltpu.SMEM)
 VMEM = pl.BlockSpec(memory_space=pltpu.VMEM)
 ANY = pl.BlockSpec(memory_space=pl.ANY)
+HBM = pl.BlockSpec(memory_space=pltpu.HBM)
 
 
 def swapped(array, bit):
@@ -176,28 +178,33 @@
     own_ref[...] = acc[:n]
 
 
-def combine_kernel(keep_r, keep_l, from_left, from_right, out_r, out_l):
-    out_r[...] = (keep_r[...] + from_left[...].astype(F32)).astype(BF16)
-    out_l[...] = (keep_l[...] + from_right[...].astype(F32)).astype(BF16)
-
-
-def relay_finish_kernel(own, a_left, a_right, b_left, b_right, out):
-    h = own.shape[0] // 2
-    out[:h] = (own[:h] + a_right[...].astype(F32) + b_left[...].astype(F32)).astype(BF16)
-    out[h:] = (own[h:] + a_left[...].astype(F32) + b_right[...].astype(F32)).astype(BF16)
-
-
-def finish_kernel(own, a, b, c, out):
+def combine_kernel(keep_r, keep_l, from_left, from_right, out_r, out_l, keep, came, sems):
+    h = keep_r.shape[0]
+    pairs = pieces_into((keep_r, keep_l), keep, 0)
+    pairs += pieces_into((from_left.at[pl.ds(0, h)], from_right.at[pl.ds(0, h)]), came, 0)
+    wait_all(start_all(pairs, sems))
+    out_r[...] = (keep[:h] + came[:h].astype(F32)).astype(BF16)
+    out_l[...] = (keep[h:] + came[h:].astype(F32)).astype(BF16)
+
+
+def relay_finish_kernel(own_hbm, a_left, a_right, b_left, b_right, out, own, first, second, sems):
+    h = out.shape[0] // 2
+    pairs = [(own_hbm, own)]
+    pairs += pieces_into((a_right.at[pl.ds(h, h)], a_left.at[pl.ds(h, h)]), first, 0)
+    pairs += pieces_into((b_left, b_right), second, 0)
+    wait_all(start_all(pairs, sems))
+    out[...] = (own[...] + first[...].astype(F32) + second[...].astype(F32)).astype(BF16)
+
+
+def finish_kernel(own_hbm, a_hbm, b_hbm, c_hbm, out, own, a, b, c, sems):
+    wait_all(start_all([(own_hbm, own), (a_hbm, a), (b_hbm, b), (c_hbm, c)], sems))
     out[...] = (own[...] + a[...].astype(F32) + b[...].astype(F32) + c[...].astype(F32)).astype(BF16)
 
 
-def feat_kernel(counts, lrows, lcols, sends, me, p0, p1, p2, p3, p4, lv_hbm, out_a, out_b, near_ref,
-                src, lv, acc, sems, sems_a, sems_b):
-    copies = start_all(pieces_into((p0, p1, p2, p3, p4), src, 0) + [(lv_hbm, lv)], sems)
+def pick_kernel(sends, me, p0, p1, p2, p3, p4, out_a, out_b, src, sems, sems_a, sems_b):
+    wait_all(start_all(pieces_into((p0, p1, p2, p3, p4), src, 0), sems))
     total = src.shape[0]
-    own = near_ref.shape[0]
-    shift = me[0] * own
-    wait_all(copies[:5])
+    shift = me[0] * p0.shape[0]
     picks = ((out_b, 1, sems_b), (out_a, 0, sems_a))
 
     def begin(out, r, marks):
@@ -217,32 +224,40 @@
 
     for pick in picks:
         begin(*pick)
-    acc[:own] = src[:own].astype(F32)
-    copies[5].wait()
-    forward_tiles(
-        counts[0], 0, lv, lambda t: lrows[t], lambda t: src[lax.rem(lcols[t] - shift + total, total)], acc
-    )
-    near_ref[...] = acc[:own]
     for pick in picks:
         end(*pick)
 
 
-def far_kernel(counts, rrows, rslots, ids, me, a_hbm, b_hbm, p0, p1, p2, p3, p4, rv_hbm, near_hbm, deg_hbm, w_ref,
+def near_kernel(counts, lrows, lcols, rrows, rslots, me, a_hbm, p0, p1, p2, p3, p4, lv_hbm, rv_hbm,
+                out_ref, src, vals, acc, sems):
+    own = out_ref.shape[0]
+    cap = rrows.shape[2]
+    lcap = vals.shape[0] - cap
+    part = src.shape[0] - cap
+    pairs = [(lv_hbm, vals.at[pl.ds(0, lcap)]), (rv_hbm.at[pl.ds(0, cap)], vals.at[pl.ds(lcap, cap)])]
+    wait_all(start_all(pairs + pieces_into((p0, p1, p2, p3, p4, a_hbm), src, 0), sems))
+    acc[:own] = src[:own].astype(F32)
+    shift = me[0] * own
+    forward_tiles(
+        counts[0], 0, vals, lambda t: lrows[t], lambda t: src[lax.rem(lcols[t] - shift + part, part)], acc
+    )
+    forward_tiles(counts[1], lcap, vals, lambda t: rrows[0, 0, t], lambda t: src[part + rslots[0, 0, t]], acc)
+    out_ref[...] = acc[:own]
+
+
+def far_kernel(counts, rrows, rslots, ids, me, b_hbm, p0, p1, p2, p3, p4, rv_hbm, near_hbm, deg_hbm, w_ref,
                out_ref, src, vals, acc, deg, sems):
     total = out_ref.shape[0]
     cap = rrows.shape[2]
-    pairs = [(near_hbm, acc.at[pl.ds(0, total)]), (rv_hbm, vals)]
-    pairs += pieces_into((a_hbm, b_hbm, p0, p1, p2, p3, p4), src, 0) + [(deg_hbm, deg)]
+    part = src.shape[0] - cap
+    pairs = [(near_hbm, acc.at[pl.ds(0, total)]), (rv_hbm.at[pl.ds(cap, 2 * cap)], vals)]
+    pairs += pieces_into((b_hbm, p0, p1, p2, p3, p4), src, 0) + [(deg_hbm, deg)]
     wait_all(start_all(pairs, sems))
-    for r in range(2):
-        forward_tiles(
-            counts[r + 1], r * cap, vals, lambda t: rrows[r, 0, t], lambda t: src[r * cap + rslots[r, 0, t]], acc
-        )
-    part = src.shape[0] - 2 * cap
+    forward_tiles(counts[2], 0, vals, lambda t: rrows[1, 0, t], lambda t: src[rslots[1, 0, t]], acc)
     shift = me[0] * p0.shape[0]
     forward_tiles(
-        counts[3], 2 * cap, vals, lambda t: rrows[2, 0, t],
-        lambda t: src[2 * cap + lax.rem(ids[0, rslots[2, 0, t]] - shift + part, part)], acc,
+        counts[3], cap, vals, lambda t: rrows[2, 0, t],
+        lambda t: src[cap + lax.rem(ids[2, 0, rslots[2, 0, t]] - shift + part, part)], acc,
     )
     width = deg.shape[2]
     for b in range(total):
@@ -295,15 +310,16 @@
     def tiles(n, kind=BF16):
         return pltpu.VMEM((n, rows, rows), kind)
 
-    def call(kernel, scalars, args, outs, scratch, flops, in_place=(), out_place=()):
+    def call(kernel, scalars, args, outs, scratch, flops, in_place=(), out_place=(), held=()):
         size = sum(a.size * a.dtype.itemsize for a in args)
         size += sum(o.size * o.dtype.itemsize for o in outs)
         return pl.pallas_call(
             kernel,
             out_shape=tuple(outs),
-            in_specs=[SMEM] * len(scalars) + [VMEM if i in in_place else ANY for i in range(len(args))],
+            in_specs=[SMEM] * len(scalars) + [VMEM if i in in_place else HBM if i in held else ANY for i in range(len(args))],
             out_specs=tuple(ANY if i in out_place else VMEM for i in range(len(outs))),
             scratch_shapes=scratch,
+            compiler_params=pltpu.CompilerParams(vmem_limit_bytes=VMEM_ALL),
             cost_estimate=pl.CostEstimate(flops=flops, bytes_accessed=size, transcendentals=0),
         )(*scalars, *args)
 
@@ -317,11 +333,14 @@
 
     def finished(own_part, arrived):
         n = own_part.shape[0]
-        return call(finish_kernel, (), (own_part,) + arrived, [blocks(n, BF16)], [], 0, range(4))[0]
+        return call(
+            finish_kernel, (), (own_part,) + arrived, [blocks(n, BF16)],
+            [room(n, F32), room(n, BF16), room(n, BF16), room(n, BF16), sems(4)], 0, held=range(4),
+        )[0]
 
     part_feats = spread_relayed(feats)
     partner_feats = spread_relayed(swapped(feats, bits[2]))
-    ids = swapped(sends[2], bits[2])
+    ids = swapped(sends, bits[2])
 
     deg, gh, z_next, z_far, z_before, z_own = call(
         degree_kernel, (counts, lrows, rrows, rslots, me), (lv, rv, go, weight),
@@ -338,11 +357,9 @@
     got_back_a = swapped(back_a, bits[0])
     got_back_c = swapped(finished(z_own, z_arrived), bits[2])
 
-    need_a, need_b, near = call(
-        feat_kernel, (counts, lrows, lcols, sends, me), part_feats + (lv,),
-        [blocks(cap, BF16), blocks(cap, BF16), blocks(own, F32)],
-        [room(part, BF16), tiles(lcap), room(own + 1, F32), sems(6), sems(cap), sems(cap)],
-        lcap * tile_flops, (), range(2),
+    need_a, need_b = call(
+        pick_kernel, (sends, me), part_feats, [blocks(cap, BF16), blocks(cap, BF16)],
+        [room(part, BF16), sems(5), sems(cap), sems(cap)], 0, out_place=range(2),
     )
     got_b = swapped(need_b, bits[1])
     got_a = swapped(need_a, bits[0])
@@ -351,38 +368,32 @@
         merge_kernel, (counts, lrows, lcols, sends, me), (lv, gh, got_back_a, got_back_b, got_back_c),
         [blocks(own, BF16), blocks(own, BF16), blocks(half, F32), blocks(half, F32), blocks(own, F32)],
         [tiles(lcap), room(own, BF16), room(cap, BF16), room(cap, BF16), room(share, BF16), room(part + 1, F32), sems(5)],
-        lcap * tile_flops,
+        lcap * tile_flops, held=range(5),
     )
     a_left = shifted(right, 1)
     a_right = shifted(left, -1)
 
-    def halves(start):
-        return pl.BlockSpec((half,) + tail, lambda i: (start, 0, 0))
-
-    out_r, out_l = pl.pallas_call(
-        combine_kernel,
-        out_shape=(blocks(half, BF16), blocks(half, BF16)),
-        grid=(1,),
-        in_specs=[halves(0)] * 4,
-        out_specs=(halves(0), halves(0)),
-        cost_estimate=pl.CostEstimate(flops=0, bytes_accessed=8 * half * rows * width, transcendentals=0),
-    )(keep_r, keep_l, a_left, a_right)
+    out_r, out_l = call(
+        combine_kernel, (), (keep_r, keep_l, a_left, a_right), [blocks(half, BF16), blocks(half, BF16)],
+        [room(own, F32), room(own, BF16), sems(4)], 0, held=range(4),
+    )
     b_left = shifted(out_r, 1)
     b_right = shifted(out_l, -1)
-    grad_features = pl.pallas_call(
-        relay_finish_kernel,
-        out_shape=blocks(own, BF16),
-        grid=(1,),
-        in_specs=[pl.BlockSpec((own,) + tail, lambda i: (0, 0, 0)), halves(1), halves(1), halves(0), halves(0)],
-        out_specs=pl.BlockSpec((own,) + tail, lambda i: (0, 0, 0)),
-        cost_estimate=pl.CostEstimate(flops=0, bytes_accessed=10 * own * rows * width, transcendentals=0),
-    )(own_part, a_left, a_right, b_left, b_right)
-
+    grad_features = call(
+        relay_finish_kernel, (), (own_part, a_left, a_right, b_left, b_right), [blocks(own, BF16)],
+        [room(own, F32), room(own, BF16), room(own, BF16), sems(5)], 0, held=range(5),
+    )[0]
+
+    near = call(
+        near_kernel, (counts, lrows, lcols, rrows, rslots, me), (got_a,) + part_feats + (lv, rv),
+        [blocks(own, F32)],
+        [room(part + cap, BF16), tiles(lcap + cap), room(own + 1, F32), sems(8)], (lcap + cap) * tile_flops,
+    )[0]
     output = call(
-        far_kernel, (counts, rrows, rslots, ids, me),
-        (got_a, got_b) + partner_feats + (rv, near, deg, weight), [blocks(own, BF16)],
-        [room(2 * cap + part, BF16), tiles(rounds * cap), room(own + 1, F32), tiles(own, F32), sems(10)],
-        rounds * cap * tile_flops, (10,),
+        far_kernel, (counts, rrows, rslots, ids, me), (got_b,) + partner_feats + (rv, near, deg, weight),
+        [blocks(own, BF16)],
+        [room(cap + part, BF16), tiles(2 * cap), room(own + 1, F32), tiles(own, F32), sems(9)],
+        2 * cap * tile_flops, (9,),
     )[0]
     return (output.reshape(rows_dev, width), grad_features.reshape(rows_dev, width))
 

time: 130 us -> 141 us (1.085)
  the two profiles are of different devices: /device:TPU:146 before, /device:TPU:192 now
where the time goes in v8:
time: 141 us; the launch traced here: 140 us
  waiting for transfers between devices  55.4 us (39%)
  Pallas kernels  41.5 us (29%)
  starting transfers between devices  35.8 us (25%)
  local copies, waits for them, and re-layouts  6.69 us (5%)
    ppermute x15, waiting for transfers between devices, shifted(): lax.ppermute(array, 'feat', [(i, (i + step) % size) for i in range(size)])  41.6 us
    pallas_call x9, Pallas kernels, call(): pl.pallas_call(kernel, out_shape=tuple(outs), in_specs=[SMEM] * len(scala...  41.5 us
    ppermute x15, starting transfers between devices, shifted(): lax.ppermute(array, 'feat', [(i, (i + step) % size) for i in range(size)])  26.3 us
    ppermute x7, waiting for transfers between devices, swapped(): lax.ppermute(array, 'node', [(i, i ^ 1 << bit) for i in range(lax.axis_si...  13.8 us
    ppermute x7, starting transfers between devices, swapped(): lax.ppermute(array, 'node', [(i, i ^ 1 << bit) for i in range(lax.axis_si...  9.49 us
    slice x2, local copies, waits for them, and re-layouts, spread_relayed(): far_high = shifted(after[half:], -1)  3.35 us
    slice x2, local copies, waits for them, and re-layouts, spread_relayed(): far_low = shifted(before[:half], 1)  3.34 us
  transfers between devices with their start and end apart: 22, of which 8 were waited for; matrix products, arithmetic and copies ran while one was open for 5% of the time, Pallas kernels for 17%

profile of v8, /device:TPU:192, one launch (start us, length us, event | category | flops | bytes accessed | tf_op | source)
XLA Modules:
  0.0 140.4 jit_solution(17958280335146964197)
XLA Ops:
  0.6 5.4 %shard_map.124 = (f32[8,128,128]{2,1,0:T(8,128)}, bf16[8,128,256]{2,1,0:T(8,128)(2,1)}, bf16[4,128,256]{2,1,0:T(8,128)(2,1)}, bf16[4,128,256]{2,1,0:T(8,128)(2,1...) custom-call(s32[4]{0:T(128)} %bitcast.36, s32[32]{0:T(128)} %bitcast.44, s32[3,1,16]{2,1,0:T(1,128)} %bitcast.28, ...), custom_call_target="tpu_custom_call" | custom-call | flops 134217728 | bytes 5636096 | tf_op jit(solution)/shard_map/pallas_call | solution.py:316
  6.1 5.7 %shard_map.126 = (bf16[16,128,256]{2,1,0:T(8,128)(2,1)}, bf16[16,128,256]{2,1,0:T(8,128)(2,1)}) custom-call(s32[4]{0:T(128)} %bitcast.37, s32[3,1,16]{2,1,0:T(1,128)} %bitcast.29, s32[3,1,16]{2,1,0:T(1,128)} %bitcast.33, bf16[48,128,128]{2,1,0:T(8,128)(2,1)} %bitcast.14, bf16[8,128,256]{2,1,0:T(8,128)(2,1)} %get-tuple-element.22.gh_hbm), custom_call_target="tpu_custom_call" | custom-call | flops 268435456 | bytes 4194304 | tf_op jit(solution)/shard_map/pallas_call | solution.py:316
  11.8 0.1 collective-permute-start.12
  11.9 2.4 %collective-permute-start.13 = (bf16[16,128,256]{2,1,0:T(8,128)(2,1)}, bf16[16,128,256]{2,1,0:T(8,128)(2,1)}, u32[]{:S(2)}, u32[]{:S(2)}) collective-permute-start(bf16[16,128,256]{2,1,0:T(8,128)(2,1)} %get-tuple-element.24), channel_id=1, source_target_pairs={{0,16},{4,20},{8,24},{12,28},{16,0},{20,4},{24,8},{28,12},{32,48},... | collective-permute-start | bytes 3145736 | tf_op jit(solution)/shard_map/ppermute | solution.py:20
  14.3 1.8 %collective-permute-start.14 = (bf16[4,128,256]{2,1,0:T(8,128)(2,1)}, bf16[4,128,256]{2,1,0:T(8,128)(2,1)}, u32[]{:S(2)}, u32[]{:S(2)}) collective-permute-start(bf16[4,128,256]{2,1,0:T(8,128)(2,1)} %get-tuple-element.26), channel_id=1, source_target_pairs={{0,1},{1,2},{2,3},{3,0},{4,5},{5,6},{6,7},{7,4},{8,9},{9,10},{10,1... | collective-permute-start | bytes 786440 | tf_op jit(solution)/shard_map/ppermute | solution.py:25
  16.1 3.3 %collective-permute-start.15 = (bf16[4,128,256]{2,1,0:T(8,128)(2,1)}, bf16[4,128,256]{2,1,0:T(8,128)(2,1)}, u32[]{:S(2)}, u32[]{:S(2)}) collective-permute-start(bf16[4,128,256]{2,1,0:T(8,128)(2,1)} %get-tuple-element.27), channel_id=1, source_target_pairs={{0,2},{1,3},{2,0},{3,1},{4,6},{5,7},{6,4},{7,5},{8,10},{9,11},{10,... | collective-permute-start | bytes 786440 | tf_op jit(solution)/shard_map/ppermute | solution.py:25
  19.4 0.0 collective-permute-start.2
  19.4 6.2 %collective-permute-done.14.a_hbm = bf16[4,128,256]{2,1,0:T(8,128)(2,1)} collective-permute-done((bf16[4,128,256]{2,1,0:T(8,128)(2,1)}, bf16[4,128,256]{2,1,0:T(8,128)(2,1)}, u32[]{:S(2)}, u32[]{:S(2)}) %collective-permute-start.14) | collective-permute-done | bytes 262176 | tf_op jit(solution)/shard_map/ppermute | solution.py:25
  25.6 1.8 %collective-permute-start.1 = (bf16[8,128,256]{2,1,0:T(8,128)(2,1)}, bf16[8,128,256]{2,1,0:T(8,128)(2,1)}, u32[]{:S(2)}, u32[]{:S(2)}) collective-permute-start(bf16[8,128,256]{2,1,0:T(8,128)(2,1)} %bitcast.21), channel_id=1, source_target_pairs={{0,3},{1,0},{2,1},{3,2},{4,7},{5,4},{6,5},{7,6},{8,11},{9,8},{10,9... | collective-permute-start | bytes 1572872 | tf_op jit(solution)/shard_map/ppermute | solution.py:25
  27.5 5.1 %collective-permute-done.15.b_hbm = bf16[4,128,256]{2,1,0:T(8,128)(2,1)} collective-permute-done((bf16[4,128,256]{2,1,0:T(8,128)(2,1)}, bf16[4,128,256]{2,1,0:T(8,128)(2,1)}, u32[]{:S(2)}, u32[]{:S(2)}) %collective-permute-start.15) | collective-permute-done | bytes 262176 | tf_op jit(solution)/shard_map/ppermute | solution.py:25
  32.6 1.3 collective-permute-start.16
  33.9 10.3 %collective-permute-done.16.c_hbm = bf16[4,128,256]{2,1,0:T(8,128)(2,1)} collective-permute-done((bf16[4,128,256]{2,1,0:T(8,128)(2,1)}, bf16[4,128,256]{2,1,0:T(8,128)(2,1)}, u32[]{:S(2)}, u32[]{:S(2)}) %collective-permute-start.16) | collective-permute-done | bytes 262176 | tf_op jit(solution)/shard_map/ppermute | solution.py:25
  44.2 2.1 %shard_map.127 = bf16[4,128,256]{2,1,0:T(8,128)(2,1)} custom-call(f32[4,128,256]{2,1,0:T(8,128)} %get-tuple-element.25.own_hbm, bf16[4,128,256]{2,1,0:T(8,128)(2,1)} %collective-permute-done.14.a_hbm, bf16[4,128,256]{2,1,0:T(8,128)(2,1)} %collective-permute-done.15.b_hbm, bf16[4,128,256]{2,1,0:T(8,128)(2,1)} %collective-permute-done.16.c_hbm), custom_call_target="tpu_custom_call" | custom-call | bytes 1572864 | tf_op jit(solution)/shard_map/pallas_call | solution.py:316
  46.3 1.3 collective-permute-start.17
  47.6 1.7 %collective-permute-start.6 = (bf16[8,128,256]{2,1,0:T(8,128)(2,1)}, bf16[8,128,256]{2,1,0:T(8,128)(2,1)}, u32[]{:S(2)}, u32[]{:S(2)}) collective-permute-start(bf16[8,128,256]{2,1,0:T(8,128)(2,1)} %bitcast.22), channel_id=1, source_target_pairs={{0,64},{4,68},{8,72},{12,76},{16,80},{20,84},{24,88},{28,92},{32,9... | collective-permute-start | bytes 1572872 | tf_op jit(solution)/shard_map/ppermute | solution.py:20
  49.3 1.7 %slice.16 = bf16[4,128,256]{2,1,0:T(8,128)(2,1)} slice(bf16[8,128,256]{2,1,0:T(8,128)(2,1)} %collective-permute-done.2.p4), slice={[0:4], [0:128], [0:256]} | slice | bytes 524288 | tf_op jit(solution)/shard_map/slice | solution.py:32
  51.0 1.1 collective-permute-start.3
  52.1 1.7 %slice.17 = bf16[4,128,256]{2,1,0:T(8,128)(2,1)} slice(bf16[8,128,256]{2,1,0:T(8,128)(2,1)} %collective-permute-done.1.p1), slice={[4:8], [0:128], [0:256]} | slice | bytes 524288 | tf_op jit(solution)/shard_map/slice | solution.py:33
  53.8 13.8 %collective-permute-done.17.c_hbm = bf16[4,128,256]{2,1,0:T(8,128)(2,1)} collective-permute-done((bf16[4,128,256]{2,1,0:T(8,128)(2,1)}, bf16[4,128,256]{2,1,0:T(8,128)(2,1)}, u32[]{:S(2)}, u32[]{:S(2)}) %collective-permute-start.17) | collective-permute-done | bytes 262176 | tf_op jit(solution)/shard_map/ppermute | solution.py:20
  67.6 5.6 %collective-permute-start.4 = (bf16[4,128,256]{2,1,0:T(8,128)(2,1)}, bf16[4,128,256]{2,1,0:T(8,128)(2,1)}, u32[]{:S(2)}, u32[]{:S(2)}) collective-permute-start(bf16[4,128,256]{2,1,0:T(8,128)(2,1)} %slice.17), channel_id=1, source_target_pairs={{0,3},{1,0},{2,1},{3,2},{4,7},{5,4},{6,5},{7,6},{8,11},{9,8},{10,9... | collective-permute-start | bytes 786440 | tf_op jit(solution)/shard_map/ppermute | solution.py:25
  73.2 0.0 collective-permute-done.12.a_hbm
  73.2 6.5 %shard_map.128 = (bf16[8,128,256]{2,1,0:T(8,128)(2,1)}, bf16[8,128,256]{2,1,0:T(8,128)(2,1)}, f32[4,128,256]{2,1,0:T(8,128)}, f32[4,128,256]{2,1,0:T(8,128)}, f32[8,128,256]{2,1,0:T(8,128)}) custom-call(s32[4]{0:T(128)} %bitcast.38, s32[32]{0:T(128)} %bitcast.45, s32[32]{0:T(128)} %bitcast.47, s32[3,1,16]{2,1,0:T(1,128)} %bitcast.41, s32[1]{0:T(128)} %bitcast.4.me, ...), custom_call_target="tpu_custom_call" | custom-call | flops 268435456 | bytes 7077888 | tf_op jit(solution)/shard_map/pallas_call | solution.py:316
  79.7 0.1 collective-permute-start.18
  79.8 0.0 collective-permute-done.4.p3
  79.8 3.9 %shard_map.122 = (bf16[16,128,256]{2,1,0:T(8,128)(2,1)}, bf16[16,128,256]{2,1,0:T(8,128)(2,1)}) custom-call(s32[3,1,16]{2,1,0:T(1,128)} %bitcast.42, s32[1]{0:T(128)} %bitcast.4.me, bf16[8,128,256]{2,1,0:T(8,128)(2,1)} %bitcast.23, bf16[8,128,256]{2,1,0:T(8,128)(2,1)} %collective-permute-done.1.p1, bf16[4,128,256]{2,1,0:T(8,128)(2,1)} %collective-permute-done.3.p2, ...), custom_call_target="tpu_custom_call" | custom-call | bytes 4194304 | tf_op jit(solution)/shard_map/pallas_call | solution.py:316
  83.7 0.1 collective-permute-start.11
  83.8 3.5 %collective-permute-start.19 = (bf16[8,128,256]{2,1,0:T(8,128)(2,1)}, bf16[8,128,256]{2,1,0:T(8,128)(2,1)}, u32[]{:S(2)}, u32[]{:S(2)}) collective-permute-start(bf16[8,128,256]{2,1,0:T(8,128)(2,1)} %get-tuple-element.31), channel_id=1, source_target_pairs={{0,3},{1,0},{2,1},{3,2},{4,7},{5,4},{6,5},{7,6},{8,11},{9,8},{10,9... | collective-permute-start | bytes 1572872 | tf_op jit(solution)/shard_map/ppermute | solution.py:25
  87.3 0.5 collective-permute-start.5
  87.8 0.0 collective-permute-done.6.p0
  87.8 2.0 %collective-permute-start.7 = (bf16[8,128,256]{2,1,0:T(8,128)(2,1)}, bf16[8,128,256]{2,1,0:T(8,128)(2,1)}, u32[]{:S(2)}, u32[]{:S(2)}) collective-permute-start(bf16[8,128,256]{2,1,0:T(8,128)(2,1)} %collective-permute-done.6.p0), channel_id=1, source_target_pairs={{0,3},{1,0},{2,1},{3,2},{4,7},{5,4},{6,5},{7,6},{8,11},{9,8},{10,9... | collective-permute-start | bytes 1572872 | tf_op jit(solution)/shard_map/ppermute | solution.py:25
  89.8 0.7 collective-permute-done.18.from_left.a_left
  90.5 0.0 collective-permute-start.8
  90.5 9.4 %collective-permute-done.19.from_right.a_right = bf16[8,128,256]{2,1,0:T(8,128)(2,1)} collective-permute-done((bf16[8,128,256]{2,1,0:T(8,128)(2,1)}, bf16[8,128,256]{2,1,0:T(8,128)(2,1)}, u32[]{:S(2)}, u32[]{:S(2)}) %collective-permute-start.19) | collective-permute-done | bytes 524320 | tf_op jit(solution)/shard_map/ppermute | solution.py:25
  99.9 2.2 %shard_map.129 = (bf16[4,128,256]{2,1,0:T(8,128)(2,1)}, bf16[4,128,256]{2,1,0:T(8,128)(2,1)}) custom-call(f32[4,128,256]{2,1,0:T(8,128)} %get-tuple-element.32.keep_r, f32[4,128,256]{2,1,0:T(8,128)} %get-tuple-element.33.keep_l, bf16[8,128,256]{2,1,0:T(8,128)(2,1)} %collective-permute-done.18.from_left.a_left, ...), custom_call_target="tpu_custom_call" | custom-call | bytes 2621440 | tf_op jit(solution)/shard_map/pallas_call | solution.py:316
  102.1 0.1 collective-permute-start.20
  102.2 8.2 %collective-permute-done.7.p1 = bf16[8,128,256]{2,1,0:T(8,128)(2,1)} collective-permute-done((bf16[8,128,256]{2,1,0:T(8,128)(2,1)}, bf16[8,128,256]{2,1,0:T(8,128)(2,1)}, u32[]{:S(2)}, u32[]{:S(2)}) %collective-permute-start.7) | collective-permute-done | bytes 524320 | tf_op jit(solution)/shard_map/ppermute | solution.py:25
  110.4 3.7 %collective-permute-start.21 = (bf16[4,128,256]{2,1,0:T(8,128)(2,1)}, bf16[4,128,256]{2,1,0:T(8,128)(2,1)}, u32[]{:S(2)}, u32[]{:S(2)}) collective-permute-start(bf16[4,128,256]{2,1,0:T(8,128)(2,1)} %get-tuple-element.35), channel_id=1, source_target_pairs={{0,3},{1,0},{2,1},{3,2},{4,7},{5,4},{6,5},{7,6},{8,11},{9,8},{10,9... | collective-permute-start | bytes 786440 | tf_op jit(solution)/shard_map/ppermute | solution.py:25
  114.1 1.7 %slice.19 = bf16[4,128,256]{2,1,0:T(8,128)(2,1)} slice(bf16[8,128,256]{2,1,0:T(8,128)(2,1)} %collective-permute-done.7.p1), slice={[4:8], [0:128], [0:256]} | slice | bytes 524288 | tf_op jit(solution)/shard_map/slice | solution.py:33
  115.8 0.0 collective-permute-done.8.p4
  115.8 0.0 collective-permute-start.10
  115.8 1.7 %slice.18 = bf16[4,128,256]{2,1,0:T(8,128)(2,1)} slice(bf16[8,128,256]{2,1,0:T(8,128)(2,1)} %collective-permute-done.8.p4), slice={[0:4], [0:128], [0:256]} | slice | bytes 524288 | tf_op jit(solution)/shard_map/slice | solution.py:32
  117.5 2.0 %collective-permute-start.9 = (bf16[4,128,256]{2,1,0:T(8,128)(2,1)}, bf16[4,128,256]{2,1,0:T(8,128)(2,1)}, u32[]{:S(2)}, u32[]{:S(2)}) collective-permute-start(bf16[4,128,256]{2,1,0:T(8,128)(2,1)} %slice.18), channel_id=1, source_target_pairs={{0,1},{1,2},{2,3},{3,0},{4,5},{5,6},{6,7},{7,4},{8,9},{9,10},{10,1... | collective-permute-start | bytes 786440 | tf_op jit(solution)/shard_map/ppermute | solution.py:25
  119.5 1.6 %collective-permute-done.21.b_right = bf16[4,128,256]{2,1,0:T(8,128)(2,1)} collective-permute-done((bf16[4,128,256]{2,1,0:T(8,128)(2,1)}, bf16[4,128,256]{2,1,0:T(8,128)(2,1)}, u32[]{:S(2)}, u32[]{:S(2)}) %collective-permute-start.21) | collective-permute-done | bytes 262176 | tf_op jit(solution)/shard_map/ppermute | solution.py:25
  121.1 3.4 %collective-permute-start = (s32[3,1,16]{2,1,0:T(1,128)}, s32[3,1,16]{2,1,0:T(1,128)}, u32[]{:S(2)}, u32[]{:S(2)}) collective-permute-start(s32[3,1,16]{2,1,0:T(1,128)} %bitcast.43), channel_id=1, source_target_pairs={{0,64},{4,68},{8,72},{12,76},{16,80},{20,84},{24,88},{28,92},{32,9... | collective-permute-start | bytes 584 | tf_op jit(solution)/shard_map/ppermute | solution.py:20
  124.5 2.5 %shard_map.130 = bf16[8,128,256]{2,1,0:T(8,128)(2,1)} custom-call(f32[8,128,256]{2,1,0:T(8,128)} %get-tuple-element.29.own_hbm, bf16[8,128,256]{2,1,0:T(8,128)(2,1)} %collective-permute-done.18.from_left.a_left, bf16[8,128,256]{2,1,0:T(8,128)(2,1)} %collective-permute-done.19.from_right.a_right, bf16[4,128,256]{2,1,0:T(8,128)(2,1)} %collective-permute-done.20.b_left, ...), custom_call_target="tpu_custom_call" | custom-call | bytes 3145728 | tf_op jit(solution)/shard_map/pallas_call | solution.py:316
  127.0 0.0 collective-permute-done.11.a_hbm
  127.0 7.0 %shard_map.123.near_hbm = f32[8,128,256]{2,1,0:T(8,128)} custom-call(s32[4]{0:T(128)} %bitcast.39, s32[32]{0:T(128)} %bitcast.46, s32[32]{0:T(128)} %bitcast.48, s32[3,1,16]{2,1,0:T(1,128)} %bitcast.30, s32[3,1,16]{2,1,0:T(1,128)} %bitcast.34, s32[1]{0:T(128)} %bitcast.4.me, bf16[16,128,256]{2,1,0:T(8,128)(2,1)} %collective-permute-done.11.a_hbm, ...), custom_call_target="tpu_custom_call" | custom-call | flops 402653184 | bytes 6815744 | tf_op jit(solution)/shard_map/pallas_call | solution.py:316
  134.1 6.1 %shard_map.125 = bf16[8,128,256]{2,1,0:T(8,128)(2,1)} custom-call(s32[4]{0:T(128)} %bitcast.40, s32[3,1,16]{2,1,0:T(1,128)} %bitcast.31, s32[3,1,16]{2,1,0:T(1,128)} %bitcast.35, s32[3,1,16]{2,1,0:T(1,128)} %collective-permute-done.ids, s32[1]{0:T(128)} %bitcast.4.me, bf16[16,128,256]{2,1,0:T(8,128)(2,1)} %collective-permute-done.5.b_hbm, ...), custom_call_target="tpu_custom_call" | custom-call | flops 268435456 | bytes 6946816 | tf_op jit(solution)/shard_map/pallas_call | solution.py:316
  (9 shorter events, 0.0 us)
Async XLA Ops:
  11.8 61.4 %collective-permute-start.12 = (bf16[16,128,256]{2,1,0:T(8,128)(2,1)}, bf16[16,128,256]{2,1,0:T(8,128)(2,1)}, u32[]{:S(2)}, u32[]{:S(2)}) collective-permute-start(bf16[16,128,256]{2,1,0:T(8,128)(2,1)} %get-tuple-element.23), channel_id=1, source_target_pairs={{0,4},{4,0},{8,12},{12,8},{16,20},{20,16},{24,28},{28,24},{32,36},... | collective-permute-start | bytes 3145736 | tf_op jit(solution)/shard_map/ppermute | solution.py:20
  11.9 61.3 %collective-permute-start.13 = (bf16[16,128,256]{2,1,0:T(8,128)(2,1)}, bf16[16,128,256]{2,1,0:T(8,128)(2,1)}, u32[]{:S(2)}, u32[]{:S(2)}) collective-permute-start(bf16[16,128,256]{2,1,0:T(8,128)(2,1)} %get-tuple-element.24), channel_id=1, source_target_pairs={{0,16},{4,20},{8,24},{12,28},{16,0},{20,4},{24,8},{28,12},{32,48},... | collective-permute-start | bytes 3145736 | tf_op jit(solution)/shard_map/ppermute | solution.py:20
  14.3 11.3 %collective-permute-start.14 = (bf16[4,128,256]{2,1,0:T(8,128)(2,1)}, bf16[4,128,256]{2,1,0:T(8,128)(2,1)}, u32[]{:S(2)}, u32[]{:S(2)}) collective-permute-start(bf16[4,128,256]{2,1,0:T(8,128)(2,1)} %get-tuple-element.26), channel_id=1, source_target_pairs={{0,1},{1,2},{2,3},{3,0},{4,5},{5,6},{6,7},{7,4},{8,9},{9,10},{10,1... | collective-permute-start | bytes 786440 | tf_op jit(solution)/shard_map/ppermute | solution.py:25
  16.1 16.4 %collective-permute-start.15 = (bf16[4,128,256]{2,1,0:T(8,128)(2,1)}, bf16[4,128,256]{2,1,0:T(8,128)(2,1)}, u32[]{:S(2)}, u32[]{:S(2)}) collective-permute-start(bf16[4,128,256]{2,1,0:T(8,128)(2,1)} %get-tuple-element.27), channel_id=1, source_target_pairs={{0,2},{1,3},{2,0},{3,1},{4,6},{5,7},{6,4},{7,5},{8,10},{9,11},{10,... | collective-permute-start | bytes 786440 | tf_op jit(solution)/shard_map/ppermute | solution.py:25
  19.4 28.2 %collective-permute-start.2 = (bf16[8,128,256]{2,1,0:T(8,128)(2,1)}, bf16[8,128,256]{2,1,0:T(8,128)(2,1)}, u32[]{:S(2)}, u32[]{:S(2)}) collective-permute-start(bf16[8,128,256]{2,1,0:T(8,128)(2,1)} %bitcast.20), channel_id=1, source_target_pairs={{0,1},{1,2},{2,3},{3,0},{4,5},{5,6},{6,7},{7,4},{8,9},{9,10},{10,1... | collective-permute-start | bytes 1572872 | tf_op jit(solution)/shard_map/ppermute | solution.py:25
  25.6 25.4 %collective-permute-start.1 = (bf16[8,128,256]{2,1,0:T(8,128)(2,1)}, bf16[8,128,256]{2,1,0:T(8,128)(2,1)}, u32[]{:S(2)}, u32[]{:S(2)}) collective-permute-start(bf16[8,128,256]{2,1,0:T(8,128)(2,1)} %bitcast.21), channel_id=1, source_target_pairs={{0,3},{1,0},{2,1},{3,2},{4,7},{5,4},{6,5},{7,6},{8,11},{9,8},{10,9... | collective-permute-start | bytes 1572872 | tf_op jit(solution)/shard_map/ppermute | solution.py:25
  32.6 11.6 %collective-permute-start.16 = (bf16[4,128,256]{2,1,0:T(8,128)(2,1)}, bf16[4,128,256]{2,1,0:T(8,128)(2,1)}, u32[]{:S(2)}, u32[]{:S(2)}) collective-permute-start(bf16[4,128,256]{2,1,0:T(8,128)(2,1)} %get-tuple-element.28), channel_id=1, source_target_pairs={{0,3},{1,0},{2,1},{3,2},{4,7},{5,4},{6,5},{7,6},{8,11},{9,8},{10,9... | collective-permute-start | bytes 786440 | tf_op jit(solution)/shard_map/ppermute | solution.py:25
  46.3 21.3 %collective-permute-start.17 = (bf16[4,128,256]{2,1,0:T(8,128)(2,1)}, bf16[4,128,256]{2,1,0:T(8,128)(2,1)}, u32[]{:S(2)}, u32[]{:S(2)}) collective-permute-start(bf16[4,128,256]{2,1,0:T(8,128)(2,1)} %shard_map.127), channel_id=1, source_target_pairs={{0,64},{4,68},{8,72},{12,76},{16,80},{20,84},{24,88},{28,92},{32,9... | collective-permute-start | bytes 786440 | tf_op jit(solution)/shard_map/ppermute | solution.py:20
  47.6 40.2 %collective-permute-start.6 = (bf16[8,128,256]{2,1,0:T(8,128)(2,1)}, bf16[8,128,256]{2,1,0:T(8,128)(2,1)}, u32[]{:S(2)}, u32[]{:S(2)}) collective-permute-start(bf16[8,128,256]{2,1,0:T(8,128)(2,1)} %bitcast.22), channel_id=1, source_target_pairs={{0,64},{4,68},{8,72},{12,76},{16,80},{20,84},{24,88},{28,92},{32,9... | collective-permute-start | bytes 1572872 | tf_op jit(solution)/shard_map/ppermute | solution.py:20
  51.0 28.8 %collective-permute-start.3 = (bf16[4,128,256]{2,1,0:T(8,128)(2,1)}, bf16[4,128,256]{2,1,0:T(8,128)(2,1)}, u32[]{:S(2)}, u32[]{:S(2)}) collective-permute-start(bf16[4,128,256]{2,1,0:T(8,128)(2,1)} %slice.16), channel_id=1, source_target_pairs={{0,1},{1,2},{2,3},{3,0},{4,5},{5,6},{6,7},{7,4},{8,9},{9,10},{10,1... | collective-permute-start | bytes 786440 | tf_op jit(solution)/shard_map/ppermute | solution.py:25
  67.6 12.2 %collective-permute-start.4 = (bf16[4,128,256]{2,1,0:T(8,128)(2,1)}, bf16[4,128,256]{2,1,0:T(8,128)(2,1)}, u32[]{:S(2)}, u32[]{:S(2)}) collective-permute-start(bf16[4,128,256]{2,1,0:T(8,128)(2,1)} %slice.17), channel_id=1, source_target_pairs={{0,3},{1,0},{2,1},{3,2},{4,7},{5,4},{6,5},{7,6},{8,11},{9,8},{10,9... | collective-permute-start | bytes 786440 | tf_op jit(solution)/shard_map/ppermute | solution.py:25
  79.7 10.8 %collective-permute-start.18 = (bf16[8,128,256]{2,1,0:T(8,128)(2,1)}, bf16[8,128,256]{2,1,0:T(8,128)(2,1)}, u32[]{:S(2)}, u32[]{:S(2)}) collective-permute-start(bf16[8,128,256]{2,1,0:T(8,128)(2,1)} %get-tuple-element.30), channel_id=1, source_target_pairs={{0,1},{1,2},{2,3},{3,0},{4,5},{5,6},{6,7},{7,4},{8,9},{9,10},{10,1... | collective-permute-start | bytes 1572872 | tf_op jit(solution)/shard_map/ppermute | solution.py:25
  83.7 43.3 %collective-permute-start.11 = (bf16[16,128,256]{2,1,0:T(8,128)(2,1)}, bf16[16,128,256]{2,1,0:T(8,128)(2,1)}, u32[]{:S(2)}, u32[]{:S(2)}) collective-permute-start(bf16[16,128,256]{2,1,0:T(8,128)(2,1)} %get-tuple-element.20), channel_id=1, source_target_pairs={{0,4},{4,0},{8,12},{12,8},{16,20},{20,16},{24,28},{28,24},{32,36},... | collective-permute-start | bytes 3145736 | tf_op jit(solution)/shard_map/ppermute | solution.py:20
  83.8 16.1 %collective-permute-start.19 = (bf16[8,128,256]{2,1,0:T(8,128)(2,1)}, bf16[8,128,256]{2,1,0:T(8,128)(2,1)}, u32[]{:S(2)}, u32[]{:S(2)}) collective-permute-start(bf16[8,128,256]{2,1,0:T(8,128)(2,1)} %get-tuple-element.31), channel_id=1, source_target_pairs={{0,3},{1,0},{2,1},{3,2},{4,7},{5,4},{6,5},{7,6},{8,11},{9,8},{10,9... | collective-permute-start | bytes 1572872 | tf_op jit(solution)/shard_map/ppermute | solution.py:25
  87.3 46.8 %collective-permute-start.5 = (bf16[16,128,256]{2,1,0:T(8,128)(2,1)}, bf16[16,128,256]{2,1,0:T(8,128)(2,1)}, u32[]{:S(2)}, u32[]{:S(2)}) collective-permute-start(bf16[16,128,256]{2,1,0:T(8,128)(2,1)} %get-tuple-element.19), channel_id=1, source_target_pairs={{0,16},{4,20},{8,24},{12,28},{16,0},{20,4},{24,8},{28,12},{32,48},... | collective-permute-start | bytes 3145736 | tf_op jit(solution)/shard_map/ppermute | solution.py:20
  87.8 22.6 %collective-permute-start.7 = (bf16[8,128,256]{2,1,0:T(8,128)(2,1)}, bf16[8,128,256]{2,1,0:T(8,128)(2,1)}, u32[]{:S(2)}, u32[]{:S(2)}) collective-permute-start(bf16[8,128,256]{2,1,0:T(8,128)(2,1)} %collective-permute-done.6.p0), channel_id=1, source_target_pairs={{0,3},{1,0},{2,1},{3,2},{4,7},{5,4},{6,5},{7,6},{8,11},{9,8},{10,9... | collective-permute-start | bytes 1572872 | tf_op jit(solution)/shard_map/ppermute | solution.py:25
  90.5 25.3 %collective-permute-start.8 = (bf16[8,128,256]{2,1,0:T(8,128)(2,1)}, bf16[8,128,256]{2,1,0:T(8,128)(2,1)}, u32[]{:S(2)}, u32[]{:S(2)}) collective-permute-start(bf16[8,128,256]{2,1,0:T(8,128)(2,1)} %collective-permute-done.6.p0), channel_id=1, source_target_pairs={{0,1},{1,2},{2,3},{3,0},{4,5},{5,6},{6,7},{7,4},{8,9},{9,10},{10,1... | collective-permute-start | bytes 1572872 | tf_op jit(solution)/shard_map/ppermute | solution.py:25
  102.1 15.3 %collective-permute-start.20 = (bf16[4,128,256]{2,1,0:T(8,128)(2,1)}, bf16[4,128,256]{2,1,0:T(8,128)(2,1)}, u32[]{:S(2)}, u32[]{:S(2)}) collective-permute-start(bf16[4,128,256]{2,1,0:T(8,128)(2,1)} %get-tuple-element.34), channel_id=1, source_target_pairs={{0,1},{1,2},{2,3},{3,0},{4,5},{5,6},{6,7},{7,4},{8,9},{9,10},{10,1... | collective-permute-start | bytes 786440 | tf_op jit(solution)/shard_map/ppermute | solution.py:25
  110.4 10.7 %collective-permute-start.21 = (bf16[4,128,256]{2,1,0:T(8,128)(2,1)}, bf16[4,128,256]{2,1,0:T(8,128)(2,1)}, u32[]{:S(2)}, u32[]{:S(2)}) collective-permute-start(bf16[4,128,256]{2,1,0:T(8,128)(2,1)} %get-tuple-element.35), channel_id=1, source_target_pairs={{0,3},{1,0},{2,1},{3,2},{4,7},{5,4},{6,5},{7,6},{8,11},{9,8},{10,9... | collective-permute-start | bytes 786440 | tf_op jit(solution)/shard_map/ppermute | solution.py:25
  115.8 18.2 %collective-permute-start.10 = (bf16[4,128,256]{2,1,0:T(8,128)(2,1)}, bf16[4,128,256]{2,1,0:T(8,128)(2,1)}, u32[]{:S(2)}, u32[]{:S(2)}) collective-permute-start(bf16[4,128,256]{2,1,0:T(8,128)(2,1)} %slice.19), channel_id=1, source_target_pairs={{0,3},{1,0},{2,1},{3,2},{4,7},{5,4},{6,5},{7,6},{8,11},{9,8},{10,9... | collective-permute-start | bytes 786440 | tf_op jit(solution)/shard_map/ppermute | solution.py:25
  117.5 16.6 %collective-permute-start.9 = (bf16[4,128,256]{2,1,0:T(8,128)(2,1)}, bf16[4,128,256]{2,1,0:T(8,128)(2,1)}, u32[]{:S(2)}, u32[]{:S(2)}) collective-permute-start(bf16[4,128,256]{2,1,0:T(8,128)(2,1)} %slice.18), channel_id=1, source_target_pairs={{0,1},{1,2},{2,3},{3,0},{4,5},{5,6},{6,7},{7,4},{8,9},{9,10},{10,1... | collective-permute-start | bytes 786440 | tf_op jit(solution)/shard_map/ppermute | solution.py:25
  121.1 12.9 %collective-permute-start = (s32[3,1,16]{2,1,0:T(1,128)}, s32[3,1,16]{2,1,0:T(1,128)}, u32[]{:S(2)}, u32[]{:S(2)}) collective-permute-start(s32[3,1,16]{2,1,0:T(1,128)} %bitcast.43), channel_id=1, source_target_pairs={{0,64},{4,68},{8,72},{12,76},{16,80},{20,84},{24,88},{28,92},{32,9... | collective-permute-start | bytes 584 | tf_op jit(solution)/shard_map/ppermute | solution.py:20

commit v9 on v8

--- a/solution.py
+++ b/solution.py
@@ -6,7 +6,7 @@
 from jax.sharding import PartitionSpec as P
 
 
-UNROLL = 4
+UNROLL = 8
 VMEM_ALL = 67_043_328
 F32 = jnp.float32
 BF16 = jnp.bfloat16
@@ -25,13 +25,12 @@
     return lax.ppermute(array, "feat", [(i, (i + step) % size) for i in range(size)])
 
 
-def spread_relayed(mine):
-    half = mine.shape[0] // 2
-    before = shifted(mine, 1)
-    after = shifted(mine, -1)
-    far_low = shifted(before[:half], 1)
-    far_high = shifted(after[half:], -1)
-    return (mine, after, far_low, far_high, before)
+def relay_begun(mine):
+    return shifted(mine, 1), shifted(mine, -1)
+
+
+def relayed(mine, before, after, low, high):
+    return (mine, after, shifted(low, 1), shifted(high, -1), before)
 
 
 def scattered(to_next, to_far, to_before):
@@ -151,8 +150,19 @@
     own_ref[...] = acc[:n]
 
 
-def merge_kernel(counts, lrows, lcols, sends, me, lv_hbm, gh_hbm, a_hbm, b_hbm, c_hbm,
-                 right_ref, left_ref, keep_r_ref, keep_l_ref, own_ref, lv, gh, got_a, got_b, got_c, acc, sems):
+def halves(before, after, low, high):
+    h = low.shape[0]
+    return [(before.at[pl.ds(0, h)], low), (after.at[pl.ds(h, h)], high)]
+
+
+def cut_kernel(before, after, low, high, sems):
+    wait_all(start_all(halves(before, after, low, high), sems))
+
+
+def merge_kernel(counts, lrows, lcols, sends, me, lv_hbm, gh_hbm, a_hbm, b_hbm, c_hbm, before, after,
+                 right_ref, left_ref, keep_r_ref, keep_l_ref, own_ref, low, high,
+                 lv, gh, got_a, got_b, got_c, acc, sems, sems_cut):
+    cuts = start_all(halves(before, after, low, high), sems_cut)
     copies = start_all([(lv_hbm, lv), (gh_hbm, gh), (a_hbm, got_a), (b_hbm, got_b), (c_hbm, got_c)], sems)
     own = gh.shape[0]
     total = acc.shape[0] - 1
@@ -176,6 +186,7 @@
     keep_r_ref[...] = acc[n:n + h]
     keep_l_ref[...] = acc[3 * n + h:4 * n]
     own_ref[...] = acc[:n]
+    wait_all(cuts)
 
 
 def combine_kernel(keep_r, keep_l, from_left, from_right, out_r, out_l, keep, came, sems):
@@ -338,8 +349,13 @@
             [room(n, F32), room(n, BF16), room(n, BF16), room(n, BF16), sems(4)], 0, held=range(4),
         )[0]
 
-    part_feats = spread_relayed(feats)
-    partner_feats = spread_relayed(swapped(feats, bits[2]))
+    before, after = relay_begun(feats)
+    low, high = call(
+        cut_kernel, (), (before, after), [blocks(half, BF16), blocks(half, BF16)], [sems(2)], 0, held=range(2)
+    )
+    part_feats = relayed(feats, before, after, low, high)
+    partner = swapped(feats, bits[2])
+    partner_before, partner_after = relay_begun(partner)
     ids = swapped(sends, bits[2])
 
     deg, gh, z_next, z_far, z_before, z_own = call(
@@ -364,12 +380,15 @@
     got_b = swapped(need_b, bits[1])
     got_a = swapped(need_a, bits[0])
 
-    right, left, keep_r, keep_l, own_part = call(
-        merge_kernel, (counts, lrows, lcols, sends, me), (lv, gh, got_back_a, got_back_b, got_back_c),
-        [blocks(own, BF16), blocks(own, BF16), blocks(half, F32), blocks(half, F32), blocks(own, F32)],
-        [tiles(lcap), room(own, BF16), room(cap, BF16), room(cap, BF16), room(share, BF16), room(part + 1, F32), sems(5)],
-        lcap * tile_flops, held=range(5),
-    )
+    right, left, keep_r, keep_l, own_part, low, high = call(
+        merge_kernel, (counts, lrows, lcols, sends, me),
+        (lv, gh, got_back_a, got_back_b, got_back_c, partner_before, partner_after),
+        [blocks(own, BF16), blocks(own, BF16), blocks(half, F32), blocks(half, F32), blocks(own, F32)]
+        + [blocks(half, BF16), blocks(half, BF16)],
+        [tiles(lcap), room(own, BF16), room(cap, BF16), room(cap, BF16), room(share, BF16), room(part + 1, F32), sems(5), sems(2)],
+        lcap * tile_flops, held=range(7),
+    )
+    partner_feats = relayed(partner, partner_before, partner_after, low, high)
     a_left = shifted(right, 1)
     a_right = shifted(left, -1)
 

time: 141 us -> 116 us (0.82)
  the two profiles are of different devices: /device:TPU:192 before, /device:TPU:32 now
where the time goes in v9:
time: 116 us
  waiting for transfers between devices  41 us (35%)
  Pallas kernels  38.7 us (33%)
  starting transfers between devices  35.4 us (31%)
    pallas_call x10, Pallas kernels, call(): pl.pallas_call(kernel, out_shape=tuple(outs), in_specs=[SMEM] * len(scala...  38.7 us
    ppermute x15, waiting for transfers between devices, shifted(): lax.ppermute(array, 'feat', [(i, (i + step) % size) for i in range(size)])  36.7 us
    ppermute x15, starting transfers between devices, shifted(): lax.ppermute(array, 'feat', [(i, (i + step) % size) for i in range(size)])  22.7 us
    ppermute x7, starting transfers between devices, swapped(): lax.ppermute(array, 'node', [(i, i ^ 1 << bit) for i in range(lax.axis_si...  12.7 us
    ppermute x7, waiting for transfers between devices, swapped(): lax.ppermute(array, 'node', [(i, i ^ 1 << bit) for i in range(lax.axis_si...  4.26 us
  transfers between devices with their start and end apart: 22, of which 7 were waited for; matrix products, arithmetic and copies ran while one was open for 0% of the time, Pallas kernels for 28%

profile of v9, /device:TPU:32, one launch (start us, length us, event | category | flops | bytes accessed | tf_op | source)
XLA Modules:
  0.0 116.1 jit_solution(14724932989076830070)
XLA Ops:
  0.6 2.8 %collective-permute-start.1 = (bf16[8,128,256]{2,1,0:T(8,128)(2,1)}, bf16[8,128,256]{2,1,0:T(8,128)(2,1)}, u32[]{:S(2)}, u32[]{:S(2)}) collective-permute-start(bf16[8,128,256]{2,1,0:T(8,128)(2,1)} %bitcast.20), channel_id=1, source_target_pairs={{0,3},{1,0},{2,1},{3,2},{4,7},{5,4},{6,5},{7,6},{8,11},{9,8},{10,9... | collective-permute-start | bytes 1572872 | tf_op jit(solution)/shard_map/ppermute | solution.py:25
  3.5 0.0 collective-permute-start.2
  3.5 5.5 %shard_map.124 = (f32[8,128,128]{2,1,0:T(8,128)}, bf16[8,128,256]{2,1,0:T(8,128)(2,1)}, bf16[4,128,256]{2,1,0:T(8,128)(2,1)}, bf16[4,128,256]{2,1,0:T(8,128)(2,1...) custom-call(s32[4]{0:T(128)} %bitcast.36, s32[32]{0:T(128)} %bitcast.44, s32[3,1,16]{2,1,0:T(1,128)} %bitcast.28, ...), custom_call_target="tpu_custom_call" | custom-call | flops 134217728 | bytes 5636096 | tf_op jit(solution)/shard_map/pallas_call | solution.py:327
  9.0 0.9 collective-permute-start.10
  9.9 2.8 %collective-permute-start.6 = (bf16[8,128,256]{2,1,0:T(8,128)(2,1)}, bf16[8,128,256]{2,1,0:T(8,128)(2,1)}, u32[]{:S(2)}, u32[]{:S(2)}) collective-permute-start(bf16[8,128,256]{2,1,0:T(8,128)(2,1)} %bitcast.22), channel_id=1, source_target_pairs={{0,64},{4,68},{8,72},{12,76},{16,80},{20,84},{24,88},{28,92},{32,9... | collective-permute-start | bytes 1572872 | tf_op jit(solution)/shard_map/ppermute | solution.py:20
  12.7 4.0 %collective-permute-start.11 = (bf16[4,128,256]{2,1,0:T(8,128)(2,1)}, bf16[4,128,256]{2,1,0:T(8,128)(2,1)}, u32[]{:S(2)}, u32[]{:S(2)}) collective-permute-start(bf16[4,128,256]{2,1,0:T(8,128)(2,1)} %get-tuple-element.31), channel_id=1, source_target_pairs={{0,2},{1,3},{2,0},{3,1},{4,6},{5,7},{6,4},{7,5},{8,10},{9,11},{10,... | collective-permute-start | bytes 786440 | tf_op jit(solution)/shard_map/ppermute | solution.py:25
  16.7 4.3 %shard_map.125 = (bf16[16,128,256]{2,1,0:T(8,128)(2,1)}, bf16[16,128,256]{2,1,0:T(8,128)(2,1)}) custom-call(s32[4]{0:T(128)} %bitcast.37, s32[3,1,16]{2,1,0:T(1,128)} %bitcast.29, s32[3,1,16]{2,1,0:T(1,128)} %bitcast.33, bf16[48,128,128]{2,1,0:T(8,128)(2,1)} %bitcast.14, bf16[8,128,256]{2,1,0:T(8,128)(2,1)} %get-tuple-element.26.gh_hbm), custom_call_target="tpu_custom_call" | custom-call | flops 268435456 | bytes 4194304 | tf_op jit(solution)/shard_map/pallas_call | solution.py:327
  21.0 8.6 %collective-permute-done.10.a_hbm = bf16[4,128,256]{2,1,0:T(8,128)(2,1)} collective-permute-done((bf16[4,128,256]{2,1,0:T(8,128)(2,1)}, bf16[4,128,256]{2,1,0:T(8,128)(2,1)}, u32[]{:S(2)}, u32[]{:S(2)}) %collective-permute-start.10) | collective-permute-done | bytes 262176 | tf_op jit(solution)/shard_map/ppermute | solution.py:25
  29.6 0.0 collective-permute-start.8
  29.6 0.0 collective-permute-done.1.after.p1
  29.6 3.2 %collective-permute-start.9 = (bf16[16,128,256]{2,1,0:T(8,128)(2,1)}, bf16[16,128,256]{2,1,0:T(8,128)(2,1)}, u32[]{:S(2)}, u32[]{:S(2)}) collective-permute-start(bf16[16,128,256]{2,1,0:T(8,128)(2,1)} %get-tuple-element.28), channel_id=1, source_target_pairs={{0,16},{4,20},{8,24},{12,28},{16,0},{20,4},{24,8},{28,12},{32,48},... | collective-permute-start | bytes 3145736 | tf_op jit(solution)/shard_map/ppermute | solution.py:20
  32.8 0.0 collective-permute-done.2.before.p4
  32.8 0.0 collective-permute-start.12
  32.8 1.8 %shard_map.122 = (bf16[4,128,256]{2,1,0:T(8,128)(2,1)}, bf16[4,128,256]{2,1,0:T(8,128)(2,1)}) custom-call(bf16[8,128,256]{2,1,0:T(8,128)(2,1)} %collective-permute-done.2.before.p4, bf16[8,128,256]{2,1,0:T(8,128)(2,1)} %collective-permute-done.1.after.p1), custom_call_target="tpu_custom_call" | custom-call | bytes 1572864 | tf_op jit(solution)/shard_map/pallas_call | solution.py:327
  34.7 0.0 collective-permute-done.11.b_hbm
  34.7 2.1 %collective-permute-start.3 = (bf16[4,128,256]{2,1,0:T(8,128)(2,1)}, bf16[4,128,256]{2,1,0:T(8,128)(2,1)}, u32[]{:S(2)}, u32[]{:S(2)}) collective-permute-start(bf16[4,128,256]{2,1,0:T(8,128)(2,1)} %get-tuple-element.23), channel_id=1, source_target_pairs={{0,1},{1,2},{2,3},{3,0},{4,5},{5,6},{6,7},{7,4},{8,9},{9,10},{10,1... | collective-permute-start | bytes 786440 | tf_op jit(solution)/shard_map/ppermute | solution.py:25
  36.8 4.8 %collective-permute-done.12.c_hbm = bf16[4,128,256]{2,1,0:T(8,128)(2,1)} collective-permute-done((bf16[4,128,256]{2,1,0:T(8,128)(2,1)}, bf16[4,128,256]{2,1,0:T(8,128)(2,1)}, u32[]{:S(2)}, u32[]{:S(2)}) %collective-permute-start.12) | collective-permute-done | bytes 262176 | tf_op jit(solution)/shard_map/ppermute | solution.py:25
  41.6 1.5 %collective-permute-start.4 = (bf16[4,128,256]{2,1,0:T(8,128)(2,1)}, bf16[4,128,256]{2,1,0:T(8,128)(2,1)}, u32[]{:S(2)}, u32[]{:S(2)}) collective-permute-start(bf16[4,128,256]{2,1,0:T(8,128)(2,1)} %get-tuple-element.24), channel_id=1, source_target_pairs={{0,3},{1,0},{2,1},{3,2},{4,7},{5,4},{6,5},{7,6},{8,11},{9,8},{10,9... | collective-permute-start | bytes 786440 | tf_op jit(solution)/shard_map/ppermute | solution.py:25
  43.1 0.5 collective-permute-start.14
  43.6 1.1 collective-permute-done.3.p2
  44.7 1.6 %collective-permute-start.7 = (bf16[8,128,256]{2,1,0:T(8,128)(2,1)}, bf16[8,128,256]{2,1,0:T(8,128)(2,1)}, u32[]{:S(2)}, u32[]{:S(2)}) collective-permute-start(bf16[8,128,256]{2,1,0:T(8,128)(2,1)} %collective-permute-done.6.p0), channel_id=1, source_target_pairs={{0,3},{1,0},{2,1},{3,2},{4,7},{5,4},{6,5},{7,6},{8,11},{9,8},{10,9... | collective-permute-start | bytes 1572872 | tf_op jit(solution)/shard_map/ppermute | solution.py:25
  46.3 2.1 %shard_map.126 = bf16[4,128,256]{2,1,0:T(8,128)(2,1)} custom-call(f32[4,128,256]{2,1,0:T(8,128)} %get-tuple-element.29.own_hbm, bf16[4,128,256]{2,1,0:T(8,128)(2,1)} %collective-permute-done.10.a_hbm, bf16[4,128,256]{2,1,0:T(8,128)(2,1)} %collective-permute-done.11.b_hbm, bf16[4,128,256]{2,1,0:T(8,128)(2,1)} %collective-permute-done.12.c_hbm), custom_call_target="tpu_custom_call" | custom-call | bytes 1572864 | tf_op jit(solution)/shard_map/pallas_call | solution.py:327
  48.4 2.6 %collective-permute-done.4.p3 = bf16[4,128,256]{2,1,0:T(8,128)(2,1)} collective-permute-done((bf16[4,128,256]{2,1,0:T(8,128)(2,1)}, bf16[4,128,256]{2,1,0:T(8,128)(2,1)}, u32[]{:S(2)}, u32[]{:S(2)}) %collective-permute-start.4) | collective-permute-done | bytes 262176 | tf_op jit(solution)/shard_map/ppermute | solution.py:25
  51.1 3.3 %collective-permute-start.13 = (bf16[4,128,256]{2,1,0:T(8,128)(2,1)}, bf16[4,128,256]{2,1,0:T(8,128)(2,1)}, u32[]{:S(2)}, u32[]{:S(2)}) collective-permute-start(bf16[4,128,256]{2,1,0:T(8,128)(2,1)} %shard_map.126), channel_id=1, source_target_pairs={{0,64},{4,68},{8,72},{12,76},{16,80},{20,84},{24,88},{28,92},{32,9... | collective-permute-start | bytes 786440 | tf_op jit(solution)/shard_map/ppermute | solution.py:20
  54.3 3.9 %shard_map.123 = (bf16[16,128,256]{2,1,0:T(8,128)(2,1)}, bf16[16,128,256]{2,1,0:T(8,128)(2,1)}) custom-call(s32[3,1,16]{2,1,0:T(1,128)} %bitcast.41, s32[1]{0:T(128)} %bitcast.4.me, bf16[8,128,256]{2,1,0:T(8,128)(2,1)} %bitcast.23, bf16[8,128,256]{2,1,0:T(8,128)(2,1)} %collective-permute-done.1.after.p1, bf16[4,128,256]{2,1,0:T(8,128)(2,1)} %collective-permute-done.3.p2, ...), custom_call_target="tpu_custom_call" | custom-call | bytes 4194304 | tf_op jit(solution)/shard_map/pallas_call | solution.py:327
  58.2 4.2 %collective-permute-done.13.c_hbm = bf16[4,128,256]{2,1,0:T(8,128)(2,1)} collective-permute-done((bf16[4,128,256]{2,1,0:T(8,128)(2,1)}, bf16[4,128,256]{2,1,0:T(8,128)(2,1)}, u32[]{:S(2)}, u32[]{:S(2)}) %collective-permute-start.13) | collective-permute-done | bytes 262176 | tf_op jit(solution)/shard_map/ppermute | solution.py:20
  62.5 0.0 collective-permute-start.17
  62.5 0.0 collective-permute-done.14.before.p4
  62.5 0.0 collective-permute-done.7.after.p1
  62.5 5.5 %shard_map.127 = (bf16[8,128,256]{2,1,0:T(8,128)(2,1)}, bf16[8,128,256]{2,1,0:T(8,128)(2,1)}, f32[4,128,256]{2,1,0:T(8,128)}, f32[4,128,256]{2,1,0:T(8,128)}, f3...) custom-call(s32[4]{0:T(128)} %bitcast.38, s32[32]{0:T(128)} %bitcast.45, ...), custom_call_target="tpu_custom_call" | custom-call | flops 268435456 | bytes 8650752 | tf_op jit(solution)/shard_map/pallas_call | solution.py:327
  68.0 0.1 collective-permute-start.18
  68.2 3.3 %collective-permute-start.19 = (bf16[8,128,256]{2,1,0:T(8,128)(2,1)}, bf16[8,128,256]{2,1,0:T(8,128)(2,1)}, u32[]{:S(2)}, u32[]{:S(2)}) collective-permute-start(bf16[8,128,256]{2,1,0:T(8,128)(2,1)} %get-tuple-element.39), channel_id=1, source_target_pairs={{0,3},{1,0},{2,1},{3,2},{4,7},{5,4},{6,5},{7,6},{8,11},{9,8},{10,9... | collective-permute-start | bytes 1572872 | tf_op jit(solution)/shard_map/ppermute | solution.py:25
  71.5 0.4 collective-permute-start.5
  71.9 12.2 %collective-permute-done.18.from_left.a_left = bf16[8,128,256]{2,1,0:T(8,128)(2,1)} collective-permute-done((bf16[8,128,256]{2,1,0:T(8,128)(2,1)}, bf16[8,128,256]{2,1,0:T(8,128)(2,1)}, u32[]{:S(2)}, u32[]{:S(2)}) %collective-permute-start.18) | collective-permute-done | bytes 524320 | tf_op jit(solution)/shard_map/ppermute | solution.py:25
  84.1 2.2 %shard_map.130 = (bf16[4,128,256]{2,1,0:T(8,128)(2,1)}, bf16[4,128,256]{2,1,0:T(8,128)(2,1)}) custom-call(f32[4,128,256]{2,1,0:T(8,128)} %get-tuple-element.40.keep_r, f32[4,128,256]{2,1,0:T(8,128)} %get-tuple-element.41.keep_l, bf16[8,128,256]{2,1,0:T(8,128)(2,1)} %collective-permute-done.18.from_left.a_left, ...), custom_call_target="tpu_custom_call" | custom-call | bytes 2621440 | tf_op jit(solution)/shard_map/pallas_call | solution.py:327
  86.3 1.8 %collective-permute-start.20 = (bf16[4,128,256]{2,1,0:T(8,128)(2,1)}, bf16[4,128,256]{2,1,0:T(8,128)(2,1)}, u32[]{:S(2)}, u32[]{:S(2)}) collective-permute-start(bf16[4,128,256]{2,1,0:T(8,128)(2,1)} %get-tuple-element.42), channel_id=1, source_target_pairs={{0,1},{1,2},{2,3},{3,0},{4,5},{5,6},{6,7},{7,4},{8,9},{9,10},{10,1... | collective-permute-start | bytes 786440 | tf_op jit(solution)/shard_map/ppermute | solution.py:25
  88.1 2.0 %collective-permute-start.21 = (bf16[4,128,256]{2,1,0:T(8,128)(2,1)}, bf16[4,128,256]{2,1,0:T(8,128)(2,1)}, u32[]{:S(2)}, u32[]{:S(2)}) collective-permute-start(bf16[4,128,256]{2,1,0:T(8,128)(2,1)} %get-tuple-element.43), channel_id=1, source_target_pairs={{0,3},{1,0},{2,1},{3,2},{4,7},{5,4},{6,5},{7,6},{8,11},{9,8},{10,9... | collective-permute-start | bytes 786440 | tf_op jit(solution)/shard_map/ppermute | solution.py:25
  90.1 0.0 collective-permute-start.15
  90.1 7.4 %collective-permute-done.20.b_left = bf16[4,128,256]{2,1,0:T(8,128)(2,1)} collective-permute-done((bf16[4,128,256]{2,1,0:T(8,128)(2,1)}, bf16[4,128,256]{2,1,0:T(8,128)(2,1)}, u32[]{:S(2)}, u32[]{:S(2)}) %collective-permute-start.20) | collective-permute-done | bytes 262176 | tf_op jit(solution)/shard_map/ppermute | solution.py:25
  97.5 2.0 %collective-permute-start.16 = (bf16[4,128,256]{2,1,0:T(8,128)(2,1)}, bf16[4,128,256]{2,1,0:T(8,128)(2,1)}, u32[]{:S(2)}, u32[]{:S(2)}) collective-permute-start(bf16[4,128,256]{2,1,0:T(8,128)(2,1)} %get-tuple-element.34), channel_id=1, source_target_pairs={{0,3},{1,0},{2,1},{3,2},{4,7},{5,4},{6,5},{7,6},{8,11},{9,8},{10,9... | collective-permute-start | bytes 786440 | tf_op jit(solution)/shard_map/ppermute | solution.py:25
  99.5 0.0 collective-permute-done.21.b_right
  99.5 3.0 %collective-permute-start = (s32[3,1,16]{2,1,0:T(1,128)}, s32[3,1,16]{2,1,0:T(1,128)}, u32[]{:S(2)}, u32[]{:S(2)}) collective-permute-start(s32[3,1,16]{2,1,0:T(1,128)} %bitcast.43), channel_id=1, source_target_pairs={{0,64},{4,68},{8,72},{12,76},{16,80},{20,84},{24,88},{28,92},{32,9... | collective-permute-start | bytes 584 | tf_op jit(solution)/shard_map/ppermute | solution.py:20
  102.5 2.5 %shard_map.131 = bf16[8,128,256]{2,1,0:T(8,128)(2,1)} custom-call(f32[8,128,256]{2,1,0:T(8,128)} %get-tuple-element.37.own_hbm, bf16[8,128,256]{2,1,0:T(8,128)(2,1)} %collective-permute-done.18.from_left.a_left, bf16[8,128,256]{2,1,0:T(8,128)(2,1)} %collective-permute-done.19.from_right.a_right, bf16[4,128,256]{2,1,0:T(8,128)(2,1)} %collective-permute-done.20.b_left, ...), custom_call_target="tpu_custom_call" | custom-call | bytes 3145728 | tf_op jit(solution)/shard_map/pallas_call | solution.py:327
  105.0 0.0 collective-permute-done.17.a_hbm
  105.0 5.2 %shard_map.128.near_hbm = f32[8,128,256]{2,1,0:T(8,128)} custom-call(s32[4]{0:T(128)} %bitcast.39, s32[32]{0:T(128)} %bitcast.46, s32[32]{0:T(128)} %bitcast.48, s32[3,1,16]{2,1,0:T(1,128)} %bitcast.30, s32[3,1,16]{2,1,0:T(1,128)} %bitcast.34, s32[1]{0:T(128)} %bitcast.4.me, bf16[16,128,256]{2,1,0:T(8,128)(2,1)} %collective-permute-done.17.a_hbm, ...), custom_call_target="tpu_custom_call" | custom-call | flops 402653184 | bytes 6815744 | tf_op jit(solution)/shard_map/pallas_call | solution.py:327
  110.2 0.0 collective-permute-done.15.p2
  110.2 0.0 collective-permute-done.16.p3
  110.2 5.7 %shard_map.129 = bf16[8,128,256]{2,1,0:T(8,128)(2,1)} custom-call(s32[4]{0:T(128)} %bitcast.40, s32[3,1,16]{2,1,0:T(1,128)} %bitcast.31, s32[3,1,16]{2,1,0:T(1,128)} %bitcast.35, s32[3,1,16]{2,1,0:T(1,128)} %collective-permute-done.ids, s32[1]{0:T(128)} %bitcast.4.me, bf16[16,128,256]{2,1,0:T(8,128)(2,1)} %collective-permute-done.5.b_hbm, ...), custom_call_target="tpu_custom_call" | custom-call | flops 268435456 | bytes 6946816 | tf_op jit(solution)/shard_map/pallas_call | solution.py:327
  (6 shorter events, 0.0 us)
Async XLA Ops:
  0.6 29.0 %collective-permute-start.1 = (bf16[8,128,256]{2,1,0:T(8,128)(2,1)}, bf16[8,128,256]{2,1,0:T(8,128)(2,1)}, u32[]{:S(2)}, u32[]{:S(2)}) collective-permute-start(bf16[8,128,256]{2,1,0:T(8,128)(2,1)} %bitcast.20), channel_id=1, source_target_pairs={{0,3},{1,0},{2,1},{3,2},{4,7},{5,4},{6,5},{7,6},{8,11},{9,8},{10,9... | collective-permute-start | bytes 1572872 | tf_op jit(solution)/shard_map/ppermute | solution.py:25
  3.5 29.4 %collective-permute-start.2 = (bf16[8,128,256]{2,1,0:T(8,128)(2,1)}, bf16[8,128,256]{2,1,0:T(8,128)(2,1)}, u32[]{:S(2)}, u32[]{:S(2)}) collective-permute-start(bf16[8,128,256]{2,1,0:T(8,128)(2,1)} %bitcast.21), channel_id=1, source_target_pairs={{0,1},{1,2},{2,3},{3,0},{4,5},{5,6},{6,7},{7,4},{8,9},{9,10},{10,1... | collective-permute-start | bytes 1572872 | tf_op jit(solution)/shard_map/ppermute | solution.py:25
  9.0 20.6 %collective-permute-start.10 = (bf16[4,128,256]{2,1,0:T(8,128)(2,1)}, bf16[4,128,256]{2,1,0:T(8,128)(2,1)}, u32[]{:S(2)}, u32[]{:S(2)}) collective-permute-start(bf16[4,128,256]{2,1,0:T(8,128)(2,1)} %get-tuple-element.30), channel_id=1, source_target_pairs={{0,1},{1,2},{2,3},{3,0},{4,5},{5,6},{6,7},{7,4},{8,9},{9,10},{10,1... | collective-permute-start | bytes 786440 | tf_op jit(solution)/shard_map/ppermute | solution.py:25
  9.9 33.2 %collective-permute-start.6 = (bf16[8,128,256]{2,1,0:T(8,128)(2,1)}, bf16[8,128,256]{2,1,0:T(8,128)(2,1)}, u32[]{:S(2)}, u32[]{:S(2)}) collective-permute-start(bf16[8,128,256]{2,1,0:T(8,128)(2,1)} %bitcast.22), channel_id=1, source_target_pairs={{0,64},{4,68},{8,72},{12,76},{16,80},{20,84},{24,88},{28,92},{32,9... | collective-permute-start | bytes 1572872 | tf_op jit(solution)/shard_map/ppermute | solution.py:20
  12.7 22.0 %collective-permute-start.11 = (bf16[4,128,256]{2,1,0:T(8,128)(2,1)}, bf16[4,128,256]{2,1,0:T(8,128)(2,1)}, u32[]{:S(2)}, u32[]{:S(2)}) collective-permute-start(bf16[4,128,256]{2,1,0:T(8,128)(2,1)} %get-tuple-element.31), channel_id=1, source_target_pairs={{0,2},{1,3},{2,0},{3,1},{4,6},{5,7},{6,4},{7,5},{8,10},{9,11},{10,... | collective-permute-start | bytes 786440 | tf_op jit(solution)/shard_map/ppermute | solution.py:25
  29.6 32.9 %collective-permute-start.8 = (bf16[16,128,256]{2,1,0:T(8,128)(2,1)}, bf16[16,128,256]{2,1,0:T(8,128)(2,1)}, u32[]{:S(2)}, u32[]{:S(2)}) collective-permute-start(bf16[16,128,256]{2,1,0:T(8,128)(2,1)} %get-tuple-element.27), channel_id=1, source_target_pairs={{0,4},{4,0},{8,12},{12,8},{16,20},{20,16},{24,28},{28,24},{32,36},... | collective-permute-start | bytes 3145736 | tf_op jit(solution)/shard_map/ppermute | solution.py:20
  29.6 32.9 %collective-permute-start.9 = (bf16[16,128,256]{2,1,0:T(8,128)(2,1)}, bf16[16,128,256]{2,1,0:T(8,128)(2,1)}, u32[]{:S(2)}, u32[]{:S(2)}) collective-permute-start(bf16[16,128,256]{2,1,0:T(8,128)(2,1)} %get-tuple-element.28), channel_id=1, source_target_pairs={{0,16},{4,20},{8,24},{12,28},{16,0},{20,4},{24,8},{28,12},{32,48},... | collective-permute-start | bytes 3145736 | tf_op jit(solution)/shard_map/ppermute | solution.py:20
  32.8 8.8 %collective-permute-start.12 = (bf16[4,128,256]{2,1,0:T(8,128)(2,1)}, bf16[4,128,256]{2,1,0:T(8,128)(2,1)}, u32[]{:S(2)}, u32[]{:S(2)}) collective-permute-start(bf16[4,128,256]{2,1,0:T(8,128)(2,1)} %get-tuple-element.32), channel_id=1, source_target_pairs={{0,3},{1,0},{2,1},{3,2},{4,7},{5,4},{6,5},{7,6},{8,11},{9,8},{10,9... | collective-permute-start | bytes 786440 | tf_op jit(solution)/shard_map/ppermute | solution.py:25
  34.7 10.0 %collective-permute-start.3 = (bf16[4,128,256]{2,1,0:T(8,128)(2,1)}, bf16[4,128,256]{2,1,0:T(8,128)(2,1)}, u32[]{:S(2)}, u32[]{:S(2)}) collective-permute-start(bf16[4,128,256]{2,1,0:T(8,128)(2,1)} %get-tuple-element.23), channel_id=1, source_target_pairs={{0,1},{1,2},{2,3},{3,0},{4,5},{5,6},{6,7},{7,4},{8,9},{9,10},{10,1... | collective-permute-start | bytes 786440 | tf_op jit(solution)/shard_map/ppermute | solution.py:25
  41.6 9.5 %collective-permute-start.4 = (bf16[4,128,256]{2,1,0:T(8,128)(2,1)}, bf16[4,128,256]{2,1,0:T(8,128)(2,1)}, u32[]{:S(2)}, u32[]{:S(2)}) collective-permute-start(bf16[4,128,256]{2,1,0:T(8,128)(2,1)} %get-tuple-element.24), channel_id=1, source_target_pairs={{0,3},{1,0},{2,1},{3,2},{4,7},{5,4},{6,5},{7,6},{8,11},{9,8},{10,9... | collective-permute-start | bytes 786440 | tf_op jit(solution)/shard_map/ppermute | solution.py:25
  43.1 19.4 %collective-permute-start.14 = (bf16[8,128,256]{2,1,0:T(8,128)(2,1)}, bf16[8,128,256]{2,1,0:T(8,128)(2,1)}, u32[]{:S(2)}, u32[]{:S(2)}) collective-permute-start(bf16[8,128,256]{2,1,0:T(8,128)(2,1)} %collective-permute-done.6.p0), channel_id=1, source_target_pairs={{0,1},{1,2},{2,3},{3,0},{4,5},{5,6},{6,7},{7,4},{8,9},{9,10},{10,1... | collective-permute-start | bytes 1572872 | tf_op jit(solution)/shard_map/ppermute | solution.py:25
  44.7 17.8 %collective-permute-start.7 = (bf16[8,128,256]{2,1,0:T(8,128)(2,1)}, bf16[8,128,256]{2,1,0:T(8,128)(2,1)}, u32[]{:S(2)}, u32[]{:S(2)}) collective-permute-start(bf16[8,128,256]{2,1,0:T(8,128)(2,1)} %collective-permute-done.6.p0), channel_id=1, source_target_pairs={{0,3},{1,0},{2,1},{3,2},{4,7},{5,4},{6,5},{7,6},{8,11},{9,8},{10,9... | collective-permute-start | bytes 1572872 | tf_op jit(solution)/shard_map/ppermute | solution.py:25
  51.1 11.4 %collective-permute-start.13 = (bf16[4,128,256]{2,1,0:T(8,128)(2,1)}, bf16[4,128,256]{2,1,0:T(8,128)(2,1)}, u32[]{:S(2)}, u32[]{:S(2)}) collective-permute-start(bf16[4,128,256]{2,1,0:T(8,128)(2,1)} %shard_map.126), channel_id=1, source_target_pairs={{0,64},{4,68},{8,72},{12,76},{16,80},{20,84},{24,88},{28,92},{32,9... | collective-permute-start | bytes 786440 | tf_op jit(solution)/shard_map/ppermute | solution.py:20
  62.5 42.5 %collective-permute-start.17 = (bf16[16,128,256]{2,1,0:T(8,128)(2,1)}, bf16[16,128,256]{2,1,0:T(8,128)(2,1)}, u32[]{:S(2)}, u32[]{:S(2)}) collective-permute-start(bf16[16,128,256]{2,1,0:T(8,128)(2,1)} %get-tuple-element.35), channel_id=1, source_target_pairs={{0,4},{4,0},{8,12},{12,8},{16,20},{20,16},{24,28},{28,24},{32,36},... | collective-permute-start | bytes 3145736 | tf_op jit(solution)/shard_map/ppermute | solution.py:20
  68.0 16.1 %collective-permute-start.18 = (bf16[8,128,256]{2,1,0:T(8,128)(2,1)}, bf16[8,128,256]{2,1,0:T(8,128)(2,1)}, u32[]{:S(2)}, u32[]{:S(2)}) collective-permute-start(bf16[8,128,256]{2,1,0:T(8,128)(2,1)} %get-tuple-element.38), channel_id=1, source_target_pairs={{0,1},{1,2},{2,3},{3,0},{4,5},{5,6},{6,7},{7,4},{8,9},{9,10},{10,1... | collective-permute-start | bytes 1572872 | tf_op jit(solution)/shard_map/ppermute | solution.py:25
  68.2 15.9 %collective-permute-start.19 = (bf16[8,128,256]{2,1,0:T(8,128)(2,1)}, bf16[8,128,256]{2,1,0:T(8,128)(2,1)}, u32[]{:S(2)}, u32[]{:S(2)}) collective-permute-start(bf16[8,128,256]{2,1,0:T(8,128)(2,1)} %get-tuple-element.39), channel_id=1, source_target_pairs={{0,3},{1,0},{2,1},{3,2},{4,7},{5,4},{6,5},{7,6},{8,11},{9,8},{10,9... | collective-permute-start | bytes 1572872 | tf_op jit(solution)/shard_map/ppermute | solution.py:25
  71.5 38.8 %collective-permute-start.5 = (bf16[16,128,256]{2,1,0:T(8,128)(2,1)}, bf16[16,128,256]{2,1,0:T(8,128)(2,1)}, u32[]{:S(2)}, u32[]{:S(2)}) collective-permute-start(bf16[16,128,256]{2,1,0:T(8,128)(2,1)} %get-tuple-element.25), channel_id=1, source_target_pairs={{0,16},{4,20},{8,24},{12,28},{16,0},{20,4},{24,8},{28,12},{32,48},... | collective-permute-start | bytes 3145736 | tf_op jit(solution)/shard_map/ppermute | solution.py:20
  86.3 11.1 %collective-permute-start.20 = (bf16[4,128,256]{2,1,0:T(8,128)(2,1)}, bf16[4,128,256]{2,1,0:T(8,128)(2,1)}, u32[]{:S(2)}, u32[]{:S(2)}) collective-permute-start(bf16[4,128,256]{2,1,0:T(8,128)(2,1)} %get-tuple-element.42), channel_id=1, source_target_pairs={{0,1},{1,2},{2,3},{3,0},{4,5},{5,6},{6,7},{7,4},{8,9},{9,10},{10,1... | collective-permute-start | bytes 786440 | tf_op jit(solution)/shard_map/ppermute | solution.py:25
  88.1 11.4 %collective-permute-start.21 = (bf16[4,128,256]{2,1,0:T(8,128)(2,1)}, bf16[4,128,256]{2,1,0:T(8,128)(2,1)}, u32[]{:S(2)}, u32[]{:S(2)}) collective-permute-start(bf16[4,128,256]{2,1,0:T(8,128)(2,1)} %get-tuple-element.43), channel_id=1, source_target_pairs={{0,3},{1,0},{2,1},{3,2},{4,7},{5,4},{6,5},{7,6},{8,11},{9,8},{10,9... | collective-permute-start | bytes 786440 | tf_op jit(solution)/shard_map/ppermute | solution.py:25
  90.1 20.1 %collective-permute-start.15 = (bf16[4,128,256]{2,1,0:T(8,128)(2,1)}, bf16[4,128,256]{2,1,0:T(8,128)(2,1)}, u32[]{:S(2)}, u32[]{:S(2)}) collective-permute-start(bf16[4,128,256]{2,1,0:T(8,128)(2,1)} %get-tuple-element.33), channel_id=1, source_target_pairs={{0,1},{1,2},{2,3},{3,0},{4,5},{5,6},{6,7},{7,4},{8,9},{9,10},{10,1... | collective-permute-start | bytes 786440 | tf_op jit(solution)/shard_map/ppermute | solution.py:25
  97.5 12.8 %collective-permute-start.16 = (bf16[4,128,256]{2,1,0:T(8,128)(2,1)}, bf16[4,128,256]{2,1,0:T(8,128)(2,1)}, u32[]{:S(2)}, u32[]{:S(2)}) collective-permute-start(bf16[4,128,256]{2,1,0:T(8,128)(2,1)} %get-tuple-element.34), channel_id=1, source_target_pairs={{0,3},{1,0},{2,1},{3,2},{4,7},{5,4},{6,5},{7,6},{8,11},{9,8},{10,9... | collective-permute-start | bytes 786440 | tf_op jit(solution)/shard_map/ppermute | solution.py:25
  99.5 10.7 %collective-permute-start = (s32[3,1,16]{2,1,0:T(1,128)}, s32[3,1,16]{2,1,0:T(1,128)}, u32[]{:S(2)}, u32[]{:S(2)}) collective-permute-start(s32[3,1,16]{2,1,0:T(1,128)} %bitcast.43), channel_id=1, source_target_pairs={{0,64},{4,68},{8,72},{12,76},{16,80},{20,84},{24,88},{28,92},{32,9... | collective-permute-start | bytes 584 | tf_op jit(solution)/shard_map/ppermute | solution.py:20
